TPU v7x, 32 devices: a whole 2x2x4 slice. The times are simulated.
32 devices in a mesh: row: 8 (over y, x, core), col: 4 (over z).
Axes of the slice: x: 2, y: 2, z: 4, core: 2. Of those that a mesh axis runs over, the one named last changes fastest.
Arguments:
- tokens: bfloat16 [16384, 1024], P('row'), may hold values from -6 to 6
- w_qkv: bfloat16 [3, 1024, 1024], P(None, 'row', 'col'), may hold values from -0.1875 to 0.1875
- w_out: bfloat16 [1024, 1024], P('col', 'row'), may hold values from -6 to 6
- w_router: bfloat16 [1024, 32], P('row'), may hold values from -0.09375 to 0.09375
- ln_gains: bfloat16 [2, 1024], P(None, 'row'), may hold values from 0.099609375 to 1.8984375
- ln_biases: bfloat16 [2, 1024], P(None, 'row'), may hold values from -1 to 1
- w_in: bfloat16 [32, 1024, 4096], P('row', None, 'col'), may hold values from -0.1875 to 0.1875
- w_back: bfloat16 [32, 4096, 1024], P('row', 'col'), may hold values from -12 to 12
- expert_ids: int32 [16384, 1], P('row'), may hold values from 0 to 31; in each aligned block of 2048 rows (0 to 2047, 2048 to 4095, ...) at most 128 rows name the same one
- cotangent: bfloat16 [16384, 1024], P('row'), may hold values from -6 to 6
Outputs:
- mixed_out: bfloat16 [16384, 1024], P('row')
- grad_tokens: bfloat16 [16384, 1024], P('row')
- grad_qkv: float32 [3, 1024, 1024], P(None, 'row', 'col')
- grad_out: float32 [1024, 1024], P('col', 'row')
- grad_router: float32 [1024, 32], P('row')
- grad_gains: float32 [2, 1024], P(None, 'row')
- bias_attend: float32 [1024], P('row')
- bias_expert: float32 [1024], P('row')
- grad_in: float32 [32, 1024, 4096], P('row', None, 'col')
- grad_back: float32 [32, 4096, 1024], P('row', 'col')
Inputs may be any that keep to these rules, and one draw needn't show every extreme that they name: `expert_ids`: among the 2048 tokens of one sequence (the rows of one index of row) no expert is named more than 128 times, a bound that some block reaches.
All inputs are finite; a program needn't handle non-finite values.
Results may differ from a plain program's by a relative error of at most 0.019.
Values may be sent and summed in bfloat16 or wider, within the bound.
No kernel may reach another device: no remote copies, remote signals or barrier semaphores. Data moves between devices by JAX's collectives and lax.ppermute only.
A program may use at most 320 MiB of HBM per device.

v0:
```python
import functools
import math

import jax
import jax.numpy as jnp
from jax import lax
from jax.sharding import PartitionSpec as P

HEAD_DIM = 64


EPSILON = 1e-05
MASKED = -1e30


def layer_stats(values):
    mean = jnp.mean(values, axis=-1, keepdims=True)
    centered = values - mean
    variance = jnp.mean(centered * centered, axis=-1, keepdims=True)
    inverse = lax.rsqrt(variance + EPSILON)
    return (centered * inverse, inverse)


def norm_back(grad_normed, normed, inverse, gain):
    grad_hat = grad_normed * gain
    centred_grad = grad_hat - jnp.mean(grad_hat, axis=-1, keepdims=True)
    return inverse * (centred_grad - normed * jnp.mean(grad_hat * normed, axis=-1, keepdims=True))


def causal(start, block, length):
    places = start + jnp.arange(block, dtype=jnp.int32)
    return jnp.arange(length, dtype=jnp.int32)[None, :] <= places[:, None]


def slot_layout(expert_ids, experts, cap):
    chosen = expert_ids[:, 0]
    table = (chosen[:, None] == jnp.arange(experts, dtype=jnp.int32)[None, :]).astype(jnp.int32)
    ranks = jnp.sum((jnp.cumsum(table, axis=0) - 1) * table, axis=1)
    slots = chosen * cap + ranks
    length = chosen.shape[0]
    filler = (
        jnp.full((experts * cap,), length, jnp.int32)
        .at[slots]
        .set(jnp.arange(length, dtype=jnp.int32))
    )
    return (slots, filler, table.astype(jnp.float32))


def to_experts(rows, filler, row_count, local_count, cap):
    packed = jnp.take(rows, filler, axis=0, mode="fill", fill_value=0)
    packed = packed.reshape(row_count, local_count, cap, rows.shape[1])
    moved = lax.all_to_all(packed, "row", split_axis=0, concat_axis=2, tiled=True)
    return moved[0]


def to_tokens(partial_rows, slots):
    shared = lax.psum_scatter(partial_rows[None], "col", scatter_dimension=3, tiled=True).astype(
        jnp.bfloat16
    )
    homed = lax.all_to_all(shared, "row", split_axis=2, concat_axis=0, tiled=True)
    flat_rows = homed.reshape(-1, homed.shape[3])
    own_rows = jnp.take(flat_rows, slots, axis=0)
    return lax.all_gather(own_rows, "col", axis=1, tiled=True)


def attend_forward(query, keys, values, block, head_scale):
    length = keys.shape[0]

    def one_block(start):
        rows = lax.dynamic_slice_in_dim(query, start, block, 0)
        scores = (
            jnp.einsum("qhd,khd->hqk", rows, keys, preferred_element_type=jnp.float32) * head_scale
        )
        scores = jnp.where(causal(start, block, length)[None], scores, MASKED)
        peak = jnp.max(scores, axis=-1, keepdims=True)
        raised = jnp.exp(scores - peak)
        total = jnp.sum(raised, axis=-1, keepdims=True)
        weights = (raised / total).astype(jnp.bfloat16)
        mixed = jnp.einsum("hqk,khd->qhd", weights, values, preferred_element_type=jnp.float32)
        return (mixed.astype(jnp.bfloat16), peak + jnp.log(total))

    starts = jnp.arange(length // block, dtype=jnp.int32) * block
    return (lax.map(one_block, starts), starts)


def attend_backward(query, keys, values, grad_context, logsum, starts, block, head_scale):
    length = keys.shape[0]

    def one_block(carry, inputs):
        grad_keys, grad_values = carry
        start, block_sum = inputs
        rows = lax.dynamic_slice_in_dim(query, start, block, 0)
        grad_rows = lax.dynamic_slice_in_dim(grad_context, start, block, 0)
        scores = (
            jnp.einsum("qhd,khd->hqk", rows, keys, preferred_element_type=jnp.float32) * head_scale
        )
        probs = jnp.where(causal(start, block, length)[None], jnp.exp(scores - block_sum), 0.0)
        weights = probs.astype(jnp.bfloat16)
        grad_values = grad_values + jnp.einsum(
            "hqk,qhd->khd", weights, grad_rows, preferred_element_type=jnp.float32
        )
        grad_probs = jnp.einsum(
            "qhd,khd->hqk", grad_rows, values, preferred_element_type=jnp.float32
        )
        row_dot = jnp.sum(grad_probs * probs, axis=-1, keepdims=True)
        grad_scores = (probs * (grad_probs - row_dot)).astype(jnp.bfloat16)
        grad_query = (
            jnp.einsum("hqk,khd->qhd", grad_scores, keys, preferred_element_type=jnp.float32)
            * head_scale
        )
        grad_keys = (
            grad_keys
            + jnp.einsum("hqk,qhd->khd", grad_scores, rows, preferred_element_type=jnp.float32)
            * head_scale
        )
        return ((grad_keys, grad_values), grad_query)

    zeros = jnp.zeros(keys.shape, jnp.float32)
    (grad_keys, grad_values), grad_query = lax.scan(one_block, (zeros, zeros), (starts, logsum))
    return (grad_query.reshape(keys.shape), grad_keys, grad_values)


def per_device(
    tokens, w_qkv, w_out, w_router, ln_gains, ln_biases, w_in, w_back, expert_ids, cotangent
):
    qkv_full, out_full, router_full, gains_low, biases_low = (
        lax.all_gather(w_qkv, "row", axis=1, tiled=True),
        lax.all_gather(w_out, "row", axis=1, tiled=True),
        lax.all_gather(w_router, "row", axis=0, tiled=True),
        lax.all_gather(ln_gains, "row", axis=1, tiled=True),
        lax.all_gather(ln_biases, "row", axis=1, tiled=True),
    )
    gains = gains_low.astype(jnp.float32)
    biases = biases_low.astype(jnp.float32)
    length = tokens.shape[0]
    experts = router_full.shape[1]
    row_count = lax.axis_size("row")
    local_count = w_in.shape[0]
    cap = 2 * length // experts
    block = min(512, length)
    head_scale = 1.0 / math.sqrt(HEAD_DIM)
    head_count = qkv_full.shape[2] // HEAD_DIM
    head_width = head_count * HEAD_DIM
    slots, filler, select = slot_layout(expert_ids, experts, cap)
    resid_in = tokens.astype(jnp.float32)
    normed_one, inverse_one = layer_stats(resid_in)
    normal_in = (normed_one * gains[0] + biases[0]).astype(jnp.bfloat16)
    projected = jnp.einsum(
        "td,kdc->ktc", normal_in, qkv_full, preferred_element_type=jnp.float32
    ).astype(jnp.bfloat16)
    query = projected[0].reshape(length, head_count, HEAD_DIM)
    keys = projected[1].reshape(length, head_count, HEAD_DIM)
    values = projected[2].reshape(length, head_count, HEAD_DIM)
    (mixed_blocks, logsum), starts = attend_forward(query, keys, values, block, head_scale)
    context = mixed_blocks.reshape(length, head_width)
    attention = lax.psum(jnp.dot(context, out_full, preferred_element_type=jnp.float32), "col")
    middle = resid_in + attention
    normed_two, inverse_two = layer_stats(middle)
    routed = (normed_two * gains[1] + biases[1]).astype(jnp.bfloat16)
    logits = jnp.dot(routed, router_full, preferred_element_type=jnp.float32)
    probs = jax.nn.softmax(logits, axis=-1)
    gate = jnp.sum(probs * select, axis=-1, keepdims=True)
    arrived = to_experts(routed, filler, row_count, local_count, cap)
    hidden = jnp.einsum("erd,edf->erf", arrived, w_in, preferred_element_type=jnp.float32)
    active, gelu_back = jax.vjp(functools.partial(jax.nn.gelu, approximate=True), hidden)
    active_low = active.astype(jnp.bfloat16)
    expert_rows = jnp.einsum("erf,efd->erd", active_low, w_back, preferred_element_type=jnp.float32)
    returned = to_tokens(expert_rows, slots).astype(jnp.float32)
    mixed_out = (middle + gate * returned).astype(jnp.bfloat16)
    grad_y = cotangent.astype(jnp.float32)
    grad_gate = jnp.sum(grad_y * returned, axis=-1, keepdims=True)
    grad_expert = (gate * grad_y).astype(jnp.bfloat16)
    grad_logits = (grad_gate * probs * (select - gate)).astype(jnp.bfloat16)
    grad_router = jnp.einsum("td,te->de", routed, grad_logits, preferred_element_type=jnp.float32)
    grad_from_router = jnp.einsum(
        "te,de->td", grad_logits, router_full, preferred_element_type=jnp.float32
    )
    grad_arrived = to_experts(grad_expert, filler, row_count, local_count, cap)
    grad_back = jnp.einsum(
        "erf,erd->efd", active_low, grad_arrived, preferred_element_type=jnp.float32
    )
    grad_active = jnp.einsum(
        "erd,efd->erf", grad_arrived, w_back, preferred_element_type=jnp.float32
    )
    grad_hidden = gelu_back(grad_active)[0].astype(jnp.bfloat16)
    grad_in = jnp.einsum("erd,erf->edf", arrived, grad_hidden, preferred_element_type=jnp.float32)
    grad_rows = jnp.einsum("erf,edf->erd", grad_hidden, w_in, preferred_element_type=jnp.float32)
    grad_sent = to_tokens(grad_rows, slots).astype(jnp.float32)
    grad_routed = grad_sent + grad_from_router
    gain_two = jnp.sum(grad_routed * normed_two, axis=0)
    bias_two = jnp.sum(grad_routed, axis=0)
    grad_middle = grad_y + norm_back(grad_routed, normed_two, inverse_two, gains[1])
    grad_attn = grad_middle.astype(jnp.bfloat16)
    grad_out = jnp.einsum("tc,td->cd", context, grad_attn, preferred_element_type=jnp.float32)
    grad_context = jnp.einsum(
        "td,cd->tc", grad_attn, out_full, preferred_element_type=jnp.float32
    ).astype(jnp.bfloat16)
    grad_query, grad_keys, grad_values = attend_backward(
        query,
        keys,
        values,
        grad_context.reshape(length, head_count, HEAD_DIM),
        logsum,
        starts,
        block,
        head_scale,
    )
    grad_proj = jnp.stack(
        [
            grad_query.reshape(length, head_width),
            grad_keys.reshape(length, head_width),
            grad_values.reshape(length, head_width),
        ]
    ).astype(jnp.bfloat16)
    grad_qkv = jnp.einsum("td,ktc->kdc", normal_in, grad_proj, preferred_element_type=jnp.float32)
    grad_normal = lax.psum(
        jnp.einsum("ktc,kdc->td", grad_proj, qkv_full, preferred_element_type=jnp.float32).astype(
            jnp.bfloat16
        ),
        "col",
    ).astype(jnp.float32)
    gain_one = jnp.sum(grad_normal * normed_one, axis=0)
    bias_one = jnp.sum(grad_normal, axis=0)
    grad_tokens = (grad_middle + norm_back(grad_normal, normed_one, inverse_one, gains[0])).astype(
        jnp.bfloat16
    )
    grad_gains = jnp.stack([gain_one, gain_two])
    qkv_share, out_share, router_share, gains_share, first_share, second_share = (
        lax.psum_scatter(
            grad_qkv.astype(jnp.bfloat16), "row", scatter_dimension=1, tiled=True
        ).astype(jnp.float32),
        lax.psum_scatter(
            grad_out.astype(jnp.bfloat16), "row", scatter_dimension=1, tiled=True
        ).astype(jnp.float32),
        lax.psum_scatter(
            grad_router.astype(jnp.bfloat16), "row", scatter_dimension=0, tiled=True
        ).astype(jnp.float32),
        lax.psum_scatter(
            grad_gains.astype(jnp.bfloat16), "row", scatter_dimension=1, tiled=True
        ).astype(jnp.float32),
        lax.psum_scatter(
            bias_one.astype(jnp.bfloat16), "row", scatter_dimension=0, tiled=True
        ).astype(jnp.float32),
        lax.psum_scatter(
            bias_two.astype(jnp.bfloat16), "row", scatter_dimension=0, tiled=True
        ).astype(jnp.float32),
    )
    return (
        mixed_out,
        grad_tokens,
        qkv_share,
        out_share,
        router_share,
        gains_share,
        first_share,
        second_share,
        grad_in,
        grad_back,
    )


def solution(mesh):
    return jax.shard_map(
        per_device,
        mesh=mesh,
        in_specs=(
            P("row", None),
            P(None, "row", "col"),
            P("col", "row"),
            P("row", None),
            P(None, "row"),
            P(None, "row"),
            P("row", None, "col"),
            P("row", "col", None),
            P("row", None),
            P("row", None),
        ),
        out_specs=(
            P("row", None),
            P("row", None),
            P(None, "row", "col"),
            P("col", "row"),
            P("row", None),
            P(None, "row"),
            P("row"),
            P("row"),
            P("row", None, "col"),
            P("row", "col", None),
        ),
        check_vma=False,
    )
```

profile of v0, /device:TPU:0, one launch (start us, length us, event | category | flops | bytes accessed | tf_op | source)
XLA Modules:
  0.0 2132.2 jit_solution(2631430041157021837)
XLA Ops:
  54.9 72.9 %while.27 = (s32[]{:T(128)}, bf16[4,512,4,64]{1,3,2,0:T(8,128)(2,1)}, f32[4,4,512,1]{2,1,3,0:T(4,128)}, s32[4]{0:T(128)S(1)}, bf16[2048,4,64]{0,2,1:T(8,128)(2,1...) while((s32[]{:T(128)}, ...), condition=%wide.region_5.6_spmd, body=%wide.region_2.0_spmd.sunk | while | flops 1125251584 | bytes 57217192 | solution.py:83
  155.8 273.1 %all-reduce.6.cloned.1.call-done = f32[2048,1024]{1,0:T(8,128)} async-done(((f32[2048,1024]{1,0:T(8,128)}), f32[2048,1024]{1,0:T(8,128)}) %all-reduce.6.cloned.1.call-update) | async-done | bytes 8388624 | tf_op jit(solution)/shard_map/psum | solution.py:156
  440.5 23.5 %gather_fusion = bf16[4096,1024]{1,0:T(8,128)(2,1)} fusion(bf16[2048,1024]{1,0:T(8,128)(2,1)} %add_convert_fusion, s32[4096]{0:T(1024)S(1)} %fusion.80), kind=kCustom, calls=%fused_computation.clone | custom fusion | bytes 16793600 | tf_op jit(solution)/shard_map/jit(_take)/gather | solution.py:50
  468.5 98.0 %all_to_all.60 = bf16[8,4,128,1024]{3,2,1,0:T(8,128)(2,1)} all-to-all(bf16[8,4,128,1024]{3,2,1,0:T(8,128)(2,1)S(1)} %bitcast.167), channel_id=1, replica_groups=mesh['row'=8,'col'=4] {'row'}, dimensions={0} | all-to-all | bytes 16777216 | tf_op jit(solution)/shard_map/all_to_all | solution.py:52
  574.7 16.9 fusion.92
  591.6 19.1 convolution_bitcast_fusion.1
  610.7 277.6 %reduce-scatter.15.cloned.1.call-done = f32[1,4,1024,256]{3,2,1,0:T(8,128)} async-done(((f32[1,4,1024,1024]{3,2,1,0:T(8,128)}), f32[1,4,1024,256]{3,2,1,0:T(8,128)}) %reduce-scatter.15.cloned.1.call-update) | async-done | bytes 4194320 | tf_op jit(solution)/shard_map/reduce_scatter | solution.py:57
  897.3 26.6 %all-to-all-done.1 = bf16[1,4,1024,256]{3,1,0,2:T(4,128)(2,1)S(1)} async-done(((bf16[1,4,1024,256]{3,1,0,2:T(4,128)(2,1)}), bf16[1,4,1024,256]{3,1,0,2:T(4,128)(2,1)S(1)}, u32[]{:S(2)}, u32[]{:S(2)}) %all-to-all-start.1) | async-done | bytes 2097184 | tf_op jit(solution)/shard_map/all_to_all | solution.py:60
  948.0 67.7 %all-gather.6.cloned.1.call-done = bf16[2048,1024]{1,0:T(8,128)(2,1)} async-done(((bf16[2048,256]{1,0:T(8,128)(2,1)}), bf16[2048,1024]{1,0:T(8,128)(2,1)}) %all-gather.6.cloned.1.call-update) | async-done | bytes 4194320 | tf_op jit(solution)/shard_map/all_gather | solution.py:63
  1021.4 23.5 %gather_fusion.2 = bf16[4096,1024]{1,0:T(8,128)(2,1)} fusion(bf16[2048,1024]{1,0:T(8,128)(2,1)} %get-tuple-element.224, s32[4096]{0:T(1024)S(1)} %fusion.80), kind=kCustom, calls=%fused_computation.2.clone | custom fusion | bytes 16793600 | tf_op jit(solution)/shard_map/jit(_take)/gather | solution.py:50
  1049.4 97.6 %all_to_all.61 = bf16[8,4,128,1024]{3,2,1,0:T(8,128)(2,1)} all-to-all(bf16[8,4,128,1024]{3,2,1,0:T(8,128)(2,1)S(1)} %bitcast.166), channel_id=1, replica_groups=mesh['row'=8,'col'=4] {'row'}, dimensions={0} | all-to-all | bytes 16777216 | tf_op jit(solution)/shard_map/all_to_all | solution.py:52
  1155.1 25.4 %fusion.43 = bf16[4,1024,1024]{2,1,0:T(8,128)(2,1)} fusion(f32[4,1024,1024]{2,1,0:T(8,128)} %fusion.92, bf16[4,1024,1024]{2,1,0:T(8,128)(2,1)} %bitcast.177, bf16[4,1024,1024]{2,1,0:T(8,128)(2,1)} %param.25), kind=kOutput, calls=%fused_computation.59 | convolution fusion | flops 8673820672 | bytes 41943040 | tf_op jit(solution)/shard_map/erd,efd->erf/dot_general | solution.py:182
  1180.5 17.2 convolution_bitcast_fusion
  1197.9 276.6 %reduce-scatter.17.cloned.1.call-done = f32[1,4,1024,256]{3,2,1,0:T(8,128)} async-done(((f32[1,4,1024,1024]{3,2,1,0:T(8,128)}), f32[1,4,1024,256]{3,2,1,0:T(8,128)}) %reduce-scatter.17.cloned.1.call-update) | async-done | bytes 4194320 | tf_op jit(solution)/shard_map/reduce_scatter | solution.py:57
  1478.5 30.1 %all_to_all.62 = bf16[1,4,1024,256]{3,1,0,2:T(4,128)(2,1)S(1)} all-to-all(bf16[1,4,1024,256]{3,1,0,2:T(4,128)(2,1)S(1)} %copy.58), channel_id=1, replica_groups=mesh['row'=8,'col'=4] {'row'}, dimensions={2} | all-to-all | bytes 4194304 | tf_op jit(solution)/shard_map/all_to_all | solution.py:60
  1521.7 75.6 %all-gather.8.cloned.1.call-done = bf16[2048,1024]{1,0:T(8,128)(2,1)} async-done(((bf16[2048,256]{1,0:T(8,128)(2,1)}), bf16[2048,1024]{1,0:T(8,128)(2,1)}) %all-gather.8.cloned.1.call-update) | async-done | bytes 4194320 | tf_op jit(solution)/shard_map/all_gather | solution.py:63
  1616.9 217.4 %while.28 = (s32[]{:T(128)}, f32[2048,4,64]{0,2,1:T(8,128)}, f32[2048,4,64]{0,2,1:T(8,128)}, bf16[4,512,4,64]{1,3,2,0:T(8,128)(2,1)}, s32[4]{0:T(128)S(1)}, /*in...) while((s32[]{:T(128)}, f32[2048,4,64]{0,2,1:T(8,128)}, ...), condition=%wide.region_23.26_spmd.clone, body=%wide.region_21.25_spmd.clone.sunk | while | flops 2751068672 | bytes 235467088 | solution.py:119
  1692.7 13.5 multiply_reduce_fusion.7
  1747.1 13.5 multiply_reduce_fusion.7
  1801.4 13.5 multiply_reduce_fusion.7
  1876.0 17.4 fusion.93
  1893.3 19.1 fusion.85
  1928.7 155.6 %all-reduce.8.cloned.1.call-done = bf16[2048,1024]{1,0:T(8,128)(2,1)} async-done(((bf16[2048,1024]{1,0:T(8,128)(2,1)}), bf16[2048,1024]{1,0:T(8,128)(2,1)}) %all-reduce.8.cloned.1.call-update) | async-done | bytes 4194320 | tf_op jit(solution)/shard_map/psum | solution.py:216
  2094.0 13.7 all-reduce.2
  (305 shorter events, 505.1 us)
Async XLA Ops:
  7.2 40.6 %all-gather.4.cloned.1.call-start = ((), (), s32[]{:S(2)}) async-start(), calls=%async_computation.10 | async-start | bytes 1769472 | tf_op jit(solution)/shard_map/all_gather | solution.py:127
  9.0 419.9 %all-reduce.6.cloned.1.call-start = ((), (), s32[]{:S(2)}) async-start(), calls=%async_computation.11 | async-start | bytes 16777216 | tf_op jit(solution)/shard_map/psum | solution.py:156
  137.7 750.6 %reduce-scatter.15.cloned.1.call-start = ((), (), s32[]{:S(2)}) async-start(), calls=%async_computation.12 | async-start | bytes 20971520 | tf_op jit(solution)/shard_map/reduce_scatter | solution.py:57
  435.5 28.5 %copy-start.27 = (f32[2048]{0:T(1024)}, f32[2048]{0:T(1024)S(1)}, u32[]{:S(2)}) copy-start(f32[2048]{0:T(1024)S(1)} %add_rsqrt_fusion) | copy-start | bytes 24580
  893.6 30.3 %all-to-all-start.1 = ((bf16[1,4,1024,256]{3,1,0,2:T(4,128)(2,1)}), bf16[1,4,1024,256]{3,1,0,2:T(4,128)(2,1)S(1)}, u32[]{:S(2)}, u32[]{:S(2)}) async-start(bf16[1,4,1024,256]{3,1,0,2:T(4,128)(2,1)} %copy.55), calls=%async_computation.2 | async-start | bytes 4194304 | tf_op jit(solution)/shard_map/all_to_all | solution.py:60
  897.3 118.4 %all-gather.6.cloned.1.call-start = ((), (), s32[]{:S(2)}) async-start(), calls=%async_computation.13 | async-start | bytes 5242880 | tf_op jit(solution)/shard_map/all_gather | solution.py:63
  936.0 538.5 %reduce-scatter.17.cloned.1.call-start = ((), (), s32[]{:S(2)}) async-start(), calls=%async_computation.14 | async-start | bytes 20971520 | tf_op jit(solution)/shard_map/reduce_scatter | solution.py:57
  1197.6 399.7 %all-gather.8.cloned.1.call-start = ((), (), s32[]{:S(2)}) async-start(), calls=%async_computation.15 | async-start | bytes 5242880 | tf_op jit(solution)/shard_map/all_gather | solution.py:63
  1509.0 88.4 %copy-start.24 = (f32[2048]{0:T(1024)S(1)}, f32[2048]{0:T(1024)}, u32[]{:S(2)}) copy-start(f32[2048]{0:T(1024)} %copy-done.23) | copy-start | bytes 24580
  1509.0 88.4 %copy-start.28 = (f32[2048]{0:T(1024)S(1)}, f32[2048]{0:T(1024)}, u32[]{:S(2)}) copy-start(f32[2048]{0:T(1024)} %copy-done.27) | copy-start | bytes 24580
  1509.0 88.4 %copy-start.30 = (f32[1,1024]{1,0:T(1,128)S(1)}, f32[1,1024]{1,0:T(1,128)}, u32[]{:S(2)}) copy-start(f32[1,1024]{1,0:T(1,128)} %get-tuple-element.228) | copy-start | bytes 12292
  1517.8 356.7 %reduce-scatter.23.cloned.1.call-start = ((), (), s32[]{:S(2)}) async-start(), calls=%async_computation.19 | async-start | bytes 294912
  1521.7 390.8 %reduce-scatter.21.cloned.1.call-start = ((), (), s32[]{:S(2)}) async-start(), calls=%async_computation.18 | async-start | bytes 589824
  1760.6 12.2 copy-start.15
  1834.4 14.5 copy-start.7
  1840.5 12.7 copy-start.22
  1840.5 12.7 copy-start.26
  1840.5 12.7 copy-start.32
  1840.5 12.7 copy-start.36
  1852.3 74.3 %reduce-scatter.19.cloned.1.call-start = ((), (), s32[]{:S(2)}) async-start(), calls=%async_computation.17 | async-start | bytes 1769472
  1865.6 218.7 %all-reduce.8.cloned.1.call-start = ((), (), s32[]{:S(2)}) async-start(), calls=%async_computation.16 | async-start | bytes 8388608 | tf_op jit(solution)/shard_map/psum | solution.py:216
  1873.2 250.7 %reduce-scatter.25.cloned.1.call-start = ((), (), s32[]{:S(2)}) async-start(), calls=%async_computation.20 | async-start | bytes 294912
  1893.3 19.1 copy-start.37
  1912.4 181.5 %copy-start.38 = (bf16[1024]{0:T(1024)(128)(2,1)S(1)}, bf16[1024]{0:T(1024)(128)(2,1)}, u32[]{:S(2)}) copy-start(bf16[1024]{0:T(1024)(128)(2,1)} %get-tuple-element.177) | copy-start | bytes 6148
  (45 other events, 230.9 us)
Sparse Core Ops, SparseCore 0:
  10.5 30.2 all-gather.3
  137.8 291.0 all-reduce.5
  610.8 277.4 reduce-scatter.14
  936.1 79.5 all-gather.5
  1197.8 276.6 reduce-scatter.16
  1517.9 79.4 all-gather.7
  1601.0 31.7 reduce-scatter.22
  1852.4 32.3 reduce-scatter.20
  1888.0 38.4 reduce-scatter.18
  1929.3 154.9 all-reduce.7
  2091.2 32.6 reduce-scatter.24
where the time goes:
time: 2140 us; the launch traced here: 2130 us
  waiting for transfers between devices  1170 us (55%)
  matrix products  322 us (15%)
  blocking collectives  279 us (13%)
  local copies, waits for them, and re-layouts  166 us (8%)
  other arithmetic  158 us (7%)
    reduce_scatter x2, waiting for transfers between devices, to_tokens(): lax.psum_scatter(partial_rows[None], 'col', scatter_dimension=3, tiled=True)  554 us
    psum x1, waiting for transfers between devices, per_device(): lax.psum(jnp.dot(context, out_full, preferred_element_type=jnp.float32),...  273 us
    all_to_all x2, blocking collectives, to_experts(): lax.all_to_all(packed, 'row', split_axis=0, concat_axis=2, tiled=True)  196 us
    psum x1, waiting for transfers between devices, per_device(): lax.psum(jnp.einsum('ktc,kdc->td', grad_proj, qkv_full, preferred_element...  156 us
    all_gather x2, waiting for transfers between devices, to_tokens(): return lax.all_gather(own_rows, 'col', axis=1, tiled=True)  143 us
    dot_general x4, matrix products, one_block(): jnp.einsum('qhd,khd->hqk', grad_rows, values, preferred_element_type=jnp....  54.2 us
    convert_element_type x4, other arithmetic, one_block(): grad_scores = (probs * (grad_probs - row_dot)).astype(jnp.bfloat16)  48.7 us
    gather x2, local copies, waits for them, and re-layouts, to_experts(): packed = jnp.take(rows, filler, axis=0, mode='fill', fill_value=0)  47 us
  transfers between devices with their start and end apart: 12, of which 9 were waited for; matrix products, arithmetic and copies ran while one was open for 15% of the time, Pallas kernels for 0%

commit v1 on v0

v1 whole, which is shorter than its diff:
```python
import functools, math
import jax, jax.numpy as jnp
from jax import lax
from jax.experimental import pallas as pl
from jax.experimental.pallas import tpu as pltpu
from jax.sharding import PartitionSpec as P

HEAD_DIM = 64
MASKED = -1e30
VMEM = 60 << 20


def params(*kinds):
    return pltpu.CompilerParams(dimension_semantics=kinds or None, vmem_limit_bytes=VMEM)


def dot(a, b, dims):
    return lax.dot_general(a, b, (dims, ((), ())), preferred_element_type=jnp.float32)

NN = ((1,), (0,))
NT = ((1,), (1,))
TN = ((0,), (0,))


def pack_body(base, step, slots_ref, rows_ref, out_ref):
    length = slots_ref.shape[1]
    first = base + pl.program_id(0) * step
    wanted = first + lax.broadcasted_iota(jnp.int32, (step, length), 0)
    chosen = jnp.where(slots_ref[...] == wanted, 1.0, 0.0).astype(jnp.bfloat16)
    out_ref[...] = dot(chosen, rows_ref[...], NN).astype(out_ref.dtype)


def pack(slots, rows, base, count):
    length, width = rows.shape
    step = min(512, count)
    return pl.pallas_call(
        functools.partial(pack_body, base, step),
        out_shape=jax.ShapeDtypeStruct((count, width), rows.dtype),
        grid=(count // step,),
        in_specs=[
            pl.BlockSpec((1, length), lambda i: (0, 0)),
            pl.BlockSpec((length, width), lambda i: (0, 0)),
        ],
        out_specs=pl.BlockSpec((step, width), lambda i: (i, 0)),
        compiler_params=params("arbitrary"),
        name="pack",
    )(slots.reshape(1, length), rows)


def unpack_body(slots_ref, rows_ref, out_ref):
    step = out_ref.shape[0]
    count = rows_ref.shape[0]
    held = lax.broadcasted_iota(jnp.int32, (step, count), 1)
    chosen = jnp.where(slots_ref[...] == held, 1.0, 0.0).astype(jnp.bfloat16)
    out_ref[...] = dot(chosen, rows_ref[...], NN).astype(out_ref.dtype)


def unpack(slots, rows):
    count, width = rows.shape
    length = slots.shape[0]
    step = min(256, length)
    return pl.pallas_call(
        unpack_body,
        out_shape=jax.ShapeDtypeStruct((length, width), rows.dtype),
        grid=(length // step,),
        in_specs=[
            pl.BlockSpec((step, 1), lambda i: (i, 0)),
            pl.BlockSpec((count, width), lambda i: (0, 0)),
        ],
        out_specs=pl.BlockSpec((step, width), lambda i: (i, 0)),
        compiler_params=params("arbitrary"),
        name="unpack",
    )(slots.reshape(length, 1), rows)


def forward_body(blocks, block, q_ref, k_ref, v_ref, o_ref, lse_ref):
    width = q_ref.shape[1]
    heads = width // HEAD_DIM
    lane = lax.broadcasted_iota(jnp.int32, (block, width), 1)
    hidden = lax.broadcasted_iota(jnp.int32, (block, block), 1) > lax.broadcasted_iota(
        jnp.int32, (block, block), 0
    )
    for at, i in enumerate(blocks):
        span = (i + 1) * block
        here = pl.ds(at * block, block)
        o_ref[here, :] = jnp.zeros((block, width), o_ref.dtype)

        def one_head(h, carry, here=here, span=span, i=i):
            mine = (lane >= h * HEAD_DIM) & (lane < (h + 1) * HEAD_DIM)
            query = q_ref[pl.ds(i * block, block), :].astype(jnp.float32) * 0.125
            query = jnp.where(mine, query, 0.0).astype(jnp.bfloat16)
            edge = jnp.where(hidden, MASKED, dot(query, k_ref[pl.ds(span - block, block), :], NT))
            peak = jnp.max(edge, axis=1, keepdims=True)
            if i:
                past = dot(query, k_ref[pl.ds(0, span - block), :], NT)
                peak = jnp.maximum(peak, jnp.max(past, axis=1, keepdims=True))
            edge = jnp.exp(edge - peak)
            total = jnp.sum(edge, axis=1, keepdims=True)
            if i:
                past = jnp.exp(past - peak)
                total = total + jnp.sum(past, axis=1, keepdims=True)
            share = 1.0 / total
            mixed = dot((edge * share).astype(jnp.bfloat16), v_ref[pl.ds(span - block, block), :], NN)
            if i:
                mixed = mixed + dot(
                    (past * share).astype(jnp.bfloat16), v_ref[pl.ds(0, span - block), :], NN
                )
            o_ref[here, :] = jnp.where(mine, mixed.astype(o_ref.dtype), o_ref[here, :])
            logsum = jnp.broadcast_to(peak + jnp.log(total), (block, 128))
            lse_ref[pl.ds(h, 1), here] = logsum.T[0:1, :]
            return carry

        lax.fori_loop(0, heads, one_head, 0)


def attend_forward(projected, blocks, block):
    length, triple = projected.shape
    width = triple // 3
    heads = width // HEAD_DIM
    rows = len(blocks) * block
    spec = [pl.BlockSpec((length, width), lambda i, j=j: (0, j)) for j in range(3)]
    return pl.pallas_call(
        functools.partial(forward_body, blocks, block),
        out_shape=(
            jax.ShapeDtypeStruct((rows, width), jnp.bfloat16),
            jax.ShapeDtypeStruct((heads, rows), jnp.float32),
        ),
        grid=(1,),
        in_specs=spec,
        out_specs=(
            pl.BlockSpec((rows, width), lambda i: (0, 0)),
            pl.BlockSpec((heads, rows), lambda i: (0, 0)),
        ),
        compiler_params=params("arbitrary"),
        name="attend_forward",
    )(projected, projected, projected)


def backward_body(
    block, q_ref, k_ref, v_ref, do_ref, o_ref, lse_ref, out_ref, dk_ref, dv_ref, p_ref, ds_ref, qm_ref, dom_ref
):
    length, width = q_ref.shape
    heads = width // HEAD_DIM
    count = length // block
    lane = lax.broadcasted_iota(jnp.int32, (block, width), 1)
    hidden = lax.broadcasted_iota(jnp.int32, (block, block), 0) > lax.broadcasted_iota(
        jnp.int32, (block, block), 1
    )
    for i in reversed(range(count)):
        span = (i + 1) * block
        here = pl.ds(i * block, block)

        def one_head(h, carry, here=here, span=span, i=i):
            mine = (lane >= h * HEAD_DIM) & (lane < (h + 1) * HEAD_DIM)
            query = q_ref[here, :].astype(jnp.float32) * 0.125
            query = jnp.where(mine, query, 0.0).astype(jnp.bfloat16)
            grad = jnp.where(mine, do_ref[here, :].astype(jnp.float32), 0.0)
            delta = jnp.sum(grad * o_ref[here, :].astype(jnp.float32), axis=1, keepdims=True)
            delta = jnp.broadcast_to(delta, (block, 128)).T[0:1, :]
            grad = grad.astype(jnp.bfloat16)
            logsum = lse_ref[pl.ds(h, 1), here]
            column = pl.ds(pl.multiple_of(h * block, block), block)
            qm_ref[column, :] = query
            dom_ref[column, :] = grad

            def part(rows, edge):
                scores = dot(k_ref[rows, :], query, NT)
                if edge:
                    scores = jnp.where(hidden, MASKED, scores)
                probs = jnp.exp(scores - logsum)
                p_ref[rows, column] = probs.astype(jnp.bfloat16)
                grad_probs = dot(v_ref[rows, :], grad, NT)
                ds_ref[rows, column] = (probs * (grad_probs - delta)).astype(jnp.bfloat16)

            if i:
                part(pl.ds(0, span - block), False)
            part(pl.ds(span - block, block), True)
            dq = dot(ds_ref[pl.ds(0, span), column], k_ref[pl.ds(0, span), :], TN)
            out_ref[here, pl.ds(0, width)] = jnp.where(
                mine, (dq * 0.125).astype(out_ref.dtype), out_ref[here, pl.ds(0, width)]
            )
            return carry

        lax.fori_loop(0, heads, one_head, 0)
        new_v = dot(p_ref[pl.ds(0, span), :], dom_ref[...], NN)
        new_k = dot(ds_ref[pl.ds(0, span), :], qm_ref[...], NN)
        if i == count - 1:
            dv_ref[...] = new_v
            dk_ref[...] = new_k
        else:
            dv_ref[pl.ds(0, span), :] += new_v
            dk_ref[pl.ds(0, span), :] += new_k
        out_ref[here, pl.ds(width, width)] = dk_ref[here, :].astype(out_ref.dtype)
        out_ref[here, pl.ds(2 * width, width)] = dv_ref[here, :].astype(out_ref.dtype)


def attend_backward(projected, grad_context, context, logsum, block):
    length, triple = projected.shape
    width = triple // 3
    heads = width // HEAD_DIM
    spec = [pl.BlockSpec((length, width), lambda i, j=j: (0, j)) for j in range(3)]
    whole = pl.BlockSpec((length, width), lambda i: (0, 0))
    return pl.pallas_call(
        functools.partial(backward_body, block),
        out_shape=jax.ShapeDtypeStruct((length, triple), jnp.bfloat16),
        grid=(1,),
        in_specs=spec + [whole, whole, pl.BlockSpec((heads, length), lambda i: (0, 0))],
        out_specs=pl.BlockSpec((length, triple), lambda i: (0, 0)),
        scratch_shapes=[
            pltpu.VMEM((length, width), jnp.float32),
            pltpu.VMEM((length, width), jnp.float32),
            pltpu.VMEM((length, heads * block), jnp.bfloat16),
            pltpu.VMEM((length, heads * block), jnp.bfloat16),
            pltpu.VMEM((heads * block, width), jnp.bfloat16),
            pltpu.VMEM((heads * block, width), jnp.bfloat16),
        ],
        compiler_params=params("arbitrary"),
        name="attend_backward",
    )(projected, projected, projected, grad_context, context, logsum)


ROOT = math.sqrt(2.0 / math.pi)
CUBE = 0.044715


def expert_body(given, x_ref, gy_ref, win_ref, wback_ref, *rest):
    out_ref, active_ref, slope_ref, *sent = rest[given:]
    rows, depth = x_ref.shape
    hidden = dot(x_ref[...], win_ref[...], NN)
    square = hidden * hidden
    bent = jnp.tanh(ROOT * hidden * (1.0 + CUBE * square))
    active = (0.5 * hidden * (1.0 + bent)).astype(jnp.bfloat16)
    slope = 0.5 * (1.0 + bent) + 0.5 * hidden * (1.0 - bent * bent) * (
        ROOT * (1.0 + 3.0 * CUBE * square)
    )
    active_ref[...] = active
    parts = out_ref.shape[0]
    wide = depth // parts
    made = dot(active, wback_ref[...], NN).astype(jnp.bfloat16)
    for j in range(parts):
        out_ref[j] = made[:, j * wide : (j + 1) * wide]
    grad_active = dot(gy_ref[...].reshape(rows, depth), wback_ref[...], NT)
    grad_hidden = (grad_active * slope).astype(jnp.bfloat16)
    slope_ref[...] = grad_hidden
    back = dot(grad_hidden, win_ref[...], NT).astype(jnp.bfloat16)
    wide = depth // len(sent)
    for j, ref in enumerate(sent):
        ref[...] = back[:, j * wide : (j + 1) * wide].reshape(ref.shape)


def expert_pass(e, x, grad_y, w_in, w_back, sent, parts, pieces):
    sources, local, cap, depth = grad_y.shape
    width = w_in.shape[2]
    rows = sources * cap
    step = min(256, rows)
    group = step // cap
    sent = list(sent or [])
    piece = jax.ShapeDtypeStruct((sources, local, cap, depth // pieces), jnp.bfloat16)
    piece_spec = pl.BlockSpec((group, None, cap, depth // pieces), lambda i: (i, e, 0, 0))
    made = pl.pallas_call(
        functools.partial(expert_body, len(sent)),
        out_shape=(
            jax.ShapeDtypeStruct((parts, rows, depth // parts), jnp.bfloat16),
            jax.ShapeDtypeStruct((rows, width), jnp.bfloat16),
            jax.ShapeDtypeStruct((rows, width), jnp.bfloat16),
        )
        + (piece,) * pieces,
        grid=(rows // step,),
        in_specs=[
            pl.BlockSpec((step, depth), lambda i: (i, 0)),
            pl.BlockSpec((group, None, cap, depth), lambda i: (i, e, 0, 0)),
            pl.BlockSpec((None, depth, width), lambda i: (e, 0, 0)),
            pl.BlockSpec((None, width, depth), lambda i: (e, 0, 0)),
        ]
        + [pl.BlockSpec(memory_space=pl.ANY)] * len(sent),
        out_specs=(
            pl.BlockSpec((parts, step, depth // parts), lambda i: (0, i, 0)),
            pl.BlockSpec((step, width), lambda i: (i, 0)),
            pl.BlockSpec((step, width), lambda i: (i, 0)),
        )
        + (piece_spec,) * pieces,
        input_output_aliases={4 + j: 3 + j for j in range(len(sent))},
        compiler_params=params("arbitrary"),
        name="expert_pass",
    )(x, grad_y, w_in, w_back, *sent)
    return made[0], made[1], made[2], made[3:]


def weight_body(given, x_ref, gy_ref, gate_ref, active_ref, slope_ref, *rest):
    gin_ref, gback_ref, xt_ref, gyg_ref = rest[given:]
    rows, depth = x_ref.shape

    @pl.when(pl.program_id(0) == 0)
    def _():
        gate = gate_ref[...]
        xt_ref[...] = (x_ref[...].astype(jnp.float32) * gate).T.astype(jnp.bfloat16)
        grad_y = gy_ref[...].reshape(rows, depth).astype(jnp.float32)
        gyg_ref[...] = (grad_y * gate).astype(jnp.bfloat16)

    gin_ref[...] = dot(xt_ref[...], slope_ref[...], NN)
    gback_ref[...] = dot(active_ref[...], gyg_ref[...], TN)


def weight_pass(e, x, grad_y, gate, active, slope, sent):
    sources, local, cap, depth = grad_y.shape
    rows, width = active.shape
    step = min(256, width)
    sent = list(sent or [])
    return pl.pallas_call(
        functools.partial(weight_body, len(sent)),
        out_shape=(
            jax.ShapeDtypeStruct((local, depth, width), jnp.float32),
            jax.ShapeDtypeStruct((local, width, depth), jnp.float32),
        ),
        grid=(width // step,),
        in_specs=[
            pl.BlockSpec((rows, depth), lambda i: (0, 0)),
            pl.BlockSpec((sources, None, cap, depth), lambda i: (0, e, 0, 0)),
            pl.BlockSpec((rows, 1), lambda i: (0, 0)),
            pl.BlockSpec((rows, step), lambda i: (0, i)),
            pl.BlockSpec((rows, step), lambda i: (0, i)),
        ]
        + [pl.BlockSpec(memory_space=pl.ANY)] * len(sent),
        out_specs=(
            pl.BlockSpec((None, depth, step), lambda i: (e, 0, i)),
            pl.BlockSpec((None, step, depth), lambda i: (e, i, 0)),
        ),
        scratch_shapes=[
            pltpu.VMEM((depth, rows), jnp.bfloat16),
            pltpu.VMEM((rows, depth), jnp.bfloat16),
        ],
        input_output_aliases={5 + j: j for j in range(len(sent))},
        compiler_params=params("arbitrary"),
        name="weight_pass",
    )(x, grad_y, gate, active, slope, *sent)


EPSILON = 1e-05


def layer_stats(values):
    mean = jnp.mean(values, axis=-1, keepdims=True)
    centered = values - mean
    variance = jnp.mean(centered * centered, axis=-1, keepdims=True)
    inverse = lax.rsqrt(variance + EPSILON)
    return (centered * inverse, inverse)


def norm_back(grad_normed, normed, inverse, gain):
    grad_hat = grad_normed * gain
    centred_grad = grad_hat - jnp.mean(grad_hat, axis=-1, keepdims=True)
    return inverse * (centred_grad - normed * jnp.mean(grad_hat * normed, axis=-1, keepdims=True))


def slot_layout(expert_ids, experts, cap):
    chosen = expert_ids[:, 0]
    length = chosen.shape[0]
    table = chosen[:, None] == jnp.arange(experts, dtype=jnp.int32)[None, :]
    order = jnp.arange(length, dtype=jnp.int32)
    before = (order[:, None] > order[None, :]).astype(jnp.bfloat16)
    counted = jnp.dot(before, table.astype(jnp.bfloat16), preferred_element_type=jnp.float32)
    ranks = jnp.sum(jnp.where(table, counted, 0.0), axis=1).astype(jnp.int32)
    return (chosen, ranks, table.astype(jnp.float32))


def per_device(
    tokens, w_qkv, w_out, w_router, ln_gains, ln_biases, w_in, w_back, expert_ids, cotangent
):
    rows_all, cols_all = lax.axis_size("row"), lax.axis_size("col")
    col = lax.axis_index("col")
    length, depth = tokens.shape
    share = depth // rows_all
    width = w_qkv.shape[2]
    experts = w_router.shape[1]
    local = w_in.shape[0]
    cap = 2 * length // experts
    block = min(256, length)
    blocks = length // block
    own_length = length // cols_all
    pieces = 4

    def own(values):
        return lax.dynamic_slice_in_dim(values, col * own_length, own_length, 0)

    first = jnp.concatenate(
        [w_qkv.transpose(1, 0, 2).reshape(share, 3 * width), ln_gains.T, ln_biases.T], axis=1
    )
    first = lax.all_gather(first, "row", axis=0, tiled=True)
    qkv_full = first[:, : 3 * width]
    norms = first[:, 3 * width :].astype(jnp.float32).T
    gains, biases = norms[0:2], norms[2:4]
    second = jnp.concatenate([w_out.T, w_router], axis=1)
    second = lax.all_gather(second, "row", axis=0, tiled=True)
    router_full = second[:, width:]
    out_own = second[:, :width]

    chosen, ranks, select = slot_layout(expert_ids, experts, cap)
    slots = chosen * cap + ranks
    slots_by_local = ((chosen % local) * rows_all + chosen // local) * cap + ranks

    grad_packed = pack(slots, cotangent, 0, experts * cap).reshape(rows_all, local, cap, depth)
    grad_arrived = lax.all_to_all(grad_packed, "row", split_axis=0, concat_axis=0, tiled=True)

    resid_in = tokens.astype(jnp.float32)
    normed_one, inverse_one = layer_stats(resid_in)
    normal_in = (normed_one * gains[0] + biases[0]).astype(jnp.bfloat16)
    projected = jnp.dot(normal_in, qkv_full, preferred_element_type=jnp.float32).astype(jnp.bfloat16)

    half = blocks // 2
    context_a, logsum_a = attend_forward(projected, tuple(range(half)), block)
    full_a = lax.all_gather(context_a, "col", axis=0)
    context_b, logsum_b = attend_forward(projected, tuple(range(half, blocks)), block)
    full_b = lax.all_gather(context_b, "col", axis=0)
    out_full = lax.all_gather(out_own, "col", axis=0)
    context = jnp.concatenate([context_a, context_b], axis=0)
    logsum = jnp.concatenate([logsum_a, logsum_b], axis=1)

    def project_out(full):
        return jnp.einsum("ztc,zdc->td", full, out_full, preferred_element_type=jnp.float32)

    middle = resid_in + jnp.concatenate([project_out(full_a), project_out(full_b)], axis=0)
    normed_two, inverse_two = layer_stats(middle)
    routed = (normed_two * gains[1] + biases[1]).astype(jnp.bfloat16)
    logits = jnp.dot(routed, router_full, preferred_element_type=jnp.float32)
    probs = jax.nn.softmax(logits, axis=-1)
    gate = jnp.sum(probs * select, axis=-1, keepdims=True)

    block_rows = rows_all * cap
    arrived, summed, active, slope = [], [], [], []
    sent = None
    for e in range(local):
        packed = pack(slots_by_local, routed, e * block_rows, block_rows)
        packed = packed.reshape(rows_all, cap, depth)
        moved = lax.all_to_all(packed, "row", split_axis=0, concat_axis=0, tiled=True)
        arrived.append(moved.reshape(block_rows, depth))
        made, kept, grads, sent = expert_pass(
            e, arrived[e], grad_arrived, w_in, w_back, sent, cols_all, pieces
        )
        active.append(kept)
        slope.append(grads)
        summed.append(lax.psum_scatter(made, "col", scatter_dimension=0, tiled=True))

    held = jnp.arange(experts * cap, dtype=jnp.int32)
    gate_packed = jnp.sum(jnp.where(held[:, None] == slots[None, :], gate[:, 0][None, :], 0.0), axis=1)
    gate_arrived = lax.all_to_all(
        gate_packed.reshape(rows_all, local * cap), "row", split_axis=0, concat_axis=0, tiled=True
    )
    gate_arrived = gate_arrived.reshape(rows_all, local, cap).transpose(1, 0, 2)

    homed = jnp.stack([s.reshape(rows_all, cap, depth // cols_all) for s in summed], axis=1)
    homed = lax.all_to_all(homed, "row", split_axis=0, concat_axis=0, tiled=True)
    returned = unpack(slots, homed.reshape(experts * cap, depth // cols_all)).astype(jnp.float32)

    grad_sent = []
    for piece in sent:
        back = lax.all_to_all(piece, "row", split_axis=0, concat_axis=0, tiled=True)
        back = unpack(slots, back.reshape(experts * cap, depth // pieces))
        grad_sent.append(lax.psum_scatter(back, "col", scatter_dimension=0, tiled=True))
    grad_sent = jnp.concatenate(grad_sent, axis=1).astype(jnp.float32) * own(gate)

    grad_weights = None
    for e in range(local):
        grad_weights = weight_pass(
            e,
            arrived[e],
            grad_arrived,
            gate_arrived[e].reshape(block_rows, 1),
            active[e],
            slope[e],
            grad_weights,
        )
    grad_in, grad_back = grad_weights

    columns = depth // cols_all

    def own_columns(values):
        return lax.dynamic_slice_in_dim(values, col * columns, columns, 1)

    mixed = (own_columns(middle) + gate * returned).astype(jnp.bfloat16)
    mixed_out = lax.all_gather(mixed, "col", axis=0).transpose(1, 0, 2).reshape(length, depth)
    grad_gate = lax.psum(
        jnp.sum(own_columns(cotangent).astype(jnp.float32) * returned, axis=-1), "col"
    )[:, None]
    grad_logits = (grad_gate * probs * (select - gate)).astype(jnp.bfloat16)
    grad_router = jnp.einsum("td,te->de", routed, grad_logits, preferred_element_type=jnp.float32)

    grad_y = own(cotangent).astype(jnp.float32)
    own_middle = own(middle)
    normed_own, inverse_own = layer_stats(own_middle)
    grad_routed = grad_sent + jnp.einsum(
        "te,de->td", own(grad_logits), router_full, preferred_element_type=jnp.float32
    )
    gain_two = jnp.sum(grad_routed * normed_own, axis=0)
    bias_two = jnp.sum(grad_routed, axis=0)
    grad_middle = grad_y + norm_back(grad_routed, normed_own, inverse_own, gains[1])
    grad_attn = grad_middle.astype(jnp.bfloat16)
    grad_context = jnp.einsum(
        "td,zdc->ztc", grad_attn, out_full, preferred_element_type=jnp.float32
    ).astype(jnp.bfloat16)
    grad_context = lax.all_to_all(grad_context, "col", split_axis=0, concat_axis=0, tiled=True)
    grad_context = grad_context.reshape(length, width)

    full = jnp.concatenate([full_a, full_b], axis=1)
    full_own = lax.dynamic_slice_in_dim(full, col * own_length, own_length, 1)
    grad_out = jnp.einsum("ztc,td->zcd", full_own, grad_attn, preferred_element_type=jnp.float32)
    grad_out = lax.psum_scatter(
        grad_out.astype(jnp.bfloat16), "col", scatter_dimension=0, tiled=False
    )

    grad_proj = attend_backward(projected, grad_context, context, logsum, block)
    grad_qkv = jnp.einsum("td,tc->dc", normal_in, grad_proj, preferred_element_type=jnp.float32)
    partial = jnp.einsum(
        "tc,dc->td", grad_proj, qkv_full, preferred_element_type=jnp.float32
    ).astype(jnp.bfloat16)
    grad_normal = lax.psum_scatter(partial, "col", scatter_dimension=0, tiled=True)
    grad_normal = grad_normal.astype(jnp.float32)
    own_normed, own_inverse = layer_stats(own(tokens).astype(jnp.float32))
    gain_one = jnp.sum(grad_normal * own_normed, axis=0)
    bias_one = jnp.sum(grad_normal, axis=0)
    grad_tokens = (grad_middle + norm_back(grad_normal, own_normed, own_inverse, gains[0])).astype(
        jnp.bfloat16
    )
    grad_tokens = lax.all_gather(grad_tokens, "col", axis=0, tiled=True)

    small = lax.psum(jnp.stack([gain_one, gain_two, bias_one, bias_two]), ("row", "col"))
    small = lax.dynamic_slice_in_dim(small, lax.axis_index("row") * share, share, 1)
    qkv_share = lax.psum_scatter(
        grad_qkv.astype(jnp.bfloat16), "row", scatter_dimension=0, tiled=True
    )
    qkv_share = qkv_share.astype(jnp.float32).reshape(share, 3, width).transpose(1, 0, 2)
    out_share = lax.psum_scatter(grad_out, "row", scatter_dimension=1, tiled=True)
    router_share = lax.psum_scatter(
        grad_router.astype(jnp.bfloat16), "row", scatter_dimension=0, tiled=True
    )
    return (
        mixed_out,
        grad_tokens,
        qkv_share,
        out_share.astype(jnp.float32),
        router_share.astype(jnp.float32),
        small[0:2],
        small[2],
        small[3],
        grad_in,
        grad_back,
    )


def solution(mesh):
    return jax.shard_map(
        per_device,
        mesh=mesh,
        in_specs=(
            P("row", None),
            P(None, "row", "col"),
            P("col", "row"),
            P("row", None),
            P(None, "row"),
            P(None, "row"),
            P("row", None, "col"),
            P("row", "col", None),
            P("row", None),
            P("row", None),
        ),
        out_specs=(
            P("row", None),
            P("row", None),
            P(None, "row", "col"),
            P("col", "row"),
            P("row", None),
            P(None, "row"),
            P("row"),
            P("row"),
            P("row", None, "col"),
            P("row", "col", None),
        ),
        check_vma=False,
    )
```

time: 2140 us -> 1100 us (0.51)
  waiting for transfers between devices: 1170 us -> 381 us
  Pallas kernels: 0 us -> 286 us
  matrix products: 322 us -> 53.3 us
  local copies, waits for them, and re-layouts: 166 us -> 37.5 us
  other arithmetic: 158 us -> 46.1 us
  blocking collectives: 279 us -> 247 us
    reduce_scatter x2 -> x11, waiting for transfers between devices: 554 us -> 70.5 us  [the longest x1 57.6 us: per_device(): lax.psum_scatter(partial, 'col', scatter_dimension=0, tiled=True)]
    psum x2 -> x0, waiting for transfers between devices: 429 us -> none  [the longest x1 273 us: per_device(): lax.psum(jnp.dot(context, out_full, preferred_element_type=jnp.float32),...]
    pallas_call x0 -> x21, Pallas kernels: none -> 286 us  [the longest x4 57.8 us: expert_pass(): pl.pallas_call(functools.partial(expert_body, len(sent)), out_shape=(jax....]
    dot_general x41 -> x9, matrix products: 315 us -> 46.7 us  [the longest x2 10.1 us: project_out(): jnp.einsum('ztc,zdc->td', full, out_full, preferred_element_type=jnp.floa...]
    all_to_all x1 -> x6, waiting for transfers between devices: 26.6 us -> 98.3 us  [the longest x1 47.1 us: per_device(): lax.all_to_all(grad_context, 'col', split_axis=0, concat_axis=0, tiled=True)]
    gather x4 -> x0, local copies, waits for them, and re-layouts: 62 us -> none  [the longest x2 47 us: to_experts(): packed = jnp.take(rows, filler, axis=0, mode='fill', fill_value=0)]
    convert_element_type x13 -> x5, other arithmetic: 66.2 us -> 4.41 us  [the longest x1 3 us: per_device(): (grad_middle + norm_back(grad_normal, own_normed, own_inverse, gains[0]))...]
    psum x0 -> x2, blocking collectives: none -> 51.8 us  [the longest x1 42.3 us: per_device(): lax.psum(jnp.stack([gain_one, gain_two, bias_one, bias_two]), ('row', 'co...]
  transfers between devices with their start and end apart: 12 -> 25, of which waited for: 9 -> 13; matrix products, arithmetic and copies ran while one was open for 15% -> 10% of each run, Pallas kernels for 0% -> 25%
where the time goes in v1:
time: 1100 us; the launch traced here: 1090 us
  waiting for transfers between devices  381 us (35%)
  Pallas kernels  286 us (26%)
  blocking collectives  247 us (22%)
  matrix products  53.3 us (5%)
  other arithmetic  46.1 us (4%)
  local copies, waits for them, and re-layouts  37.5 us (3%)
  starting transfers between devices  24.7 us (2%)
  between operations  14.9 us (1%)
    all_to_all x4, blocking collectives, per_device(): lax.all_to_all(packed, 'row', split_axis=0, concat_axis=0, tiled=True)  124 us
    all_gather x1, waiting for transfers between devices, per_device(): lax.all_gather(mixed, 'col', axis=0).transpose(1, 0, 2)  80.6 us
    all_to_all x2, blocking collectives, per_device(): back = lax.all_to_all(piece, 'row', split_axis=0, concat_axis=0, tiled=True)  59.5 us
    pallas_call x4, Pallas kernels, expert_pass(): pl.pallas_call(functools.partial(expert_body, len(sent)), out_shape=(jax....  57.8 us
    reduce_scatter x1, waiting for transfers between devices, per_device(): lax.psum_scatter(partial, 'col', scatter_dimension=0, tiled=True)  57.6 us
    pallas_call x5, Pallas kernels, pack(): pl.pallas_call(functools.partial(pack_body, base, step), out_shape=jax.Sh...  53.4 us
    all_to_all x1, waiting for transfers between devices, per_device(): lax.all_to_all(grad_context, 'col', split_axis=0, concat_axis=0, tiled=True)  47.1 us
    pallas_call x5, Pallas kernels, unpack(): pl.pallas_call(unpack_body, out_shape=jax.ShapeDtypeStruct((length, width...  45.5 us
  transfers between devices with their start and end apart: 25, of which 13 were waited for; matrix products, arithmetic and copies ran while one was open for 10% of the time, Pallas kernels for 25%

profile of v1, /device:TPU:0, one launch (start us, length us, event | category | flops | bytes accessed | tf_op | source)
XLA Modules:
  0.0 1090.2 jit_solution(15378490942317364564)
XLA Ops:
  48.4 15.5 %attend_forward.2 = (bf16[1024,256]{1,0:T(8,128)(2,1)}, f32[4,1024]{1,0:T(4,128)}) custom-call(bf16[2048,768]{1,0:T(8,128)(2,1)} %convolution_convert_fusion.1.q_ref.k_ref.v_ref, bf16[2048,768]{1,0:T(8,128)(2,1)} %convolution_convert_fusion.1.q_ref.k_ref.v_ref, bf16[2048,768]{1,0:T(8,128)(2,1)} %convolution_convert_fusion.1.q_ref.k_ref.v_ref), custom_call_target="tpu_custom_call" | custom-call | tf_op jit(solution)/shard_map/attend_forward/pallas_call | solution.py:122
  66.1 21.9 %pack.6 = bf16[4096,1024]{1,0:T(8,128)(2,1)} custom-call(s32[1,2048]{1,0:T(1,128)} %get-tuple-element.146.slots_ref, bf16[2048,1024]{1,0:T(8,128)(2,1)} %rows_ref.1), custom_call_target="tpu_custom_call" | custom-call | tf_op jit(solution)/shard_map/pack/pallas_call | solution.py:36
  93.2 26.2 %attend_forward.3 = (bf16[1024,256]{1,0:T(8,128)(2,1)}, f32[4,1024]{1,0:T(4,128)}) custom-call(bf16[2048,768]{1,0:T(8,128)(2,1)} %convolution_convert_fusion.1.q_ref.k_ref.v_ref, bf16[2048,768]{1,0:T(8,128)(2,1)} %convolution_convert_fusion.1.q_ref.k_ref.v_ref, bf16[2048,768]{1,0:T(8,128)(2,1)} %convolution_convert_fusion.1.q_ref.k_ref.v_ref), custom_call_target="tpu_custom_call" | custom-call | tf_op jit(solution)/shard_map/attend_forward/pallas_call | solution.py:122
  139.5 40.1 %all-gather.19.cloned.1.call-done = bf16[4096,256]{1,0:T(8,128)(2,1)} async-done(((bf16[1024,256]{1,0:T(8,128)(2,1)}), bf16[4096,256]{1,0:T(8,128)(2,1)}) %all-gather.19.cloned.1.call-update) | async-done | bytes 2097168 | tf_op jit(solution)/shard_map/all_gather | solution.py:413
  198.8 31.4 %all_to_all.64 = bf16[8,128,1024]{2,1,0:T(8,128)(2,1)} all-to-all(bf16[8,128,1024]{2,1,0:T(8,128)(2,1)} %bitcast.127), channel_id=1, replica_groups=mesh['row'=8,'col'=4] {'row'}, dimensions={0} | all-to-all | bytes 4194304 | tf_op jit(solution)/shard_map/all_to_all | solution.py:434
  230.2 14.4 %expert_pass.4 = (bf16[4,1024,256]{2,1,0:T(8,128)(2,1)}, bf16[1024,1024]{1,0:T(8,128)(2,1)}, bf16[1024,1024]{1,0:T(8,128)(2,1)}, bf16[8,4,128,256]{3,2,1,0:T(8,1...) custom-call(bf16[1024,1024]{1,0:T(8,128)(2,1)} %bitcast.121, ...), custom_call_target="tpu_custom_call" | custom-call | tf_op jit(solution)/shard_map/expert_pass/pallas_call | solution.py:260
  252.6 30.9 %all_to_all.65 = bf16[8,128,1024]{2,1,0:T(8,128)(2,1)} all-to-all(bf16[8,128,1024]{2,1,0:T(8,128)(2,1)} %bitcast.130), channel_id=1, replica_groups=mesh['row'=8,'col'=4] {'row'}, dimensions={0} | all-to-all | bytes 4194304 | tf_op jit(solution)/shard_map/all_to_all | solution.py:434
  283.5 14.4 %expert_pass.5 = (bf16[4,1024,256]{2,1,0:T(8,128)(2,1)}, bf16[1024,1024]{1,0:T(8,128)(2,1)}, bf16[1024,1024]{1,0:T(8,128)(2,1)}, bf16[8,4,128,256]{3,2,1,0:T(8,1...) custom-call(bf16[1024,1024]{1,0:T(8,128)(2,1)} %bitcast.115, ...), custom_call_target="tpu_custom_call", output_to_operand_aliasing={{3}: (4, {}), {4}: (5, {}), {5}: (6, {}), {6}: (7, {})} | custom-call | tf_op jit(solution)/shard_map/expert_pass/pallas_call | solution.py:260
  305.9 30.9 %all_to_all.66 = bf16[8,128,1024]{2,1,0:T(8,128)(2,1)} all-to-all(bf16[8,128,1024]{2,1,0:T(8,128)(2,1)} %bitcast.131), channel_id=1, replica_groups=mesh['row'=8,'col'=4] {'row'}, dimensions={0} | all-to-all | bytes 4194304 | tf_op jit(solution)/shard_map/all_to_all | solution.py:434
  336.9 14.5 %expert_pass.6 = (bf16[4,1024,256]{2,1,0:T(8,128)(2,1)}, bf16[1024,1024]{1,0:T(8,128)(2,1)}, bf16[1024,1024]{1,0:T(8,128)(2,1)}, bf16[8,4,128,256]{3,2,1,0:T(8,1...) custom-call(bf16[1024,1024]{1,0:T(8,128)(2,1)} %bitcast.117, ...), custom_call_target="tpu_custom_call", output_to_operand_aliasing={{3}: (4, {}), {4}: (5, {}), {5}: (6, {}), {6}: (7, {})} | custom-call | tf_op jit(solution)/shard_map/expert_pass/pallas_call | solution.py:260
  359.3 31.1 %all_to_all.67 = bf16[8,128,1024]{2,1,0:T(8,128)(2,1)} all-to-all(bf16[8,128,1024]{2,1,0:T(8,128)(2,1)} %bitcast.128), channel_id=1, replica_groups=mesh['row'=8,'col'=4] {'row'}, dimensions={0} | all-to-all | bytes 4194304 | tf_op jit(solution)/shard_map/all_to_all | solution.py:434
  390.4 14.4 %expert_pass.7 = (bf16[4,1024,256]{2,1,0:T(8,128)(2,1)}, bf16[1024,1024]{1,0:T(8,128)(2,1)}, bf16[1024,1024]{1,0:T(8,128)(2,1)}, bf16[8,4,128,256]{3,2,1,0:T(8,1...) custom-call(bf16[1024,1024]{1,0:T(8,128)(2,1)} %bitcast.119, ...), custom_call_target="tpu_custom_call", output_to_operand_aliasing={{3}: (4, {}), {4}: (5, {}), {5}: (6, {}), {6}: (7, {})} | custom-call | tf_op jit(solution)/shard_map/expert_pass/pallas_call | solution.py:260
  412.6 22.5 %all-to-all-done.6 = bf16[8,4,128,256]{3,2,1,0:T(8,128)(2,1)S(1)} async-done(((bf16[8,4,128,256]{3,2,1,0:T(8,128)(2,1)}), bf16[8,4,128,256]{3,2,1,0:T(8,128)(2,1)S(1)}, u32[]{:S(2)}, u32[]{:S(2)}) %all-to-all-start.6) | async-done | bytes 2097184 | tf_op jit(solution)/shard_map/all_to_all | solution.py:456
  445.7 29.7 %all_to_all.68 = bf16[8,4,128,256]{3,2,1,0:T(8,128)(2,1)} all-to-all(bf16[8,4,128,256]{3,2,1,0:T(8,128)(2,1)S(1)} %copy-done.3), channel_id=1, replica_groups=mesh['row'=8,'col'=4] {'row'}, dimensions={0} | all-to-all | bytes 4194304 | tf_op jit(solution)/shard_map/all_to_all | solution.py:456
  484.7 29.7 %all_to_all.69 = bf16[8,4,128,256]{3,2,1,0:T(8,128)(2,1)} all-to-all(bf16[8,4,128,256]{3,2,1,0:T(8,128)(2,1)S(1)} %copy-done.4), channel_id=1, replica_groups=mesh['row'=8,'col'=4] {'row'}, dimensions={0} | all-to-all | bytes 4194304 | tf_op jit(solution)/shard_map/all_to_all | solution.py:456
  530.3 14.3 %all-to-all-done.9 = bf16[8,4,128,256]{3,2,1,0:T(8,128)(2,1)S(1)} async-done(((bf16[8,4,128,256]{3,2,1,0:T(8,128)(2,1)}), bf16[8,4,128,256]{3,2,1,0:T(8,128)(2,1)S(1)}, u32[]{:S(2)}, u32[]{:S(2)}) %all-to-all-start.9) | async-done | bytes 2097184 | tf_op jit(solution)/shard_map/all_to_all | solution.py:456
  620.2 47.1 %all-to-all-done.10 = bf16[4,512,256]{1,2,0:T(8,128)(2,1)S(1)} async-done(((bf16[4,512,256]{1,2,0:T(8,128)(2,1)}), bf16[4,512,256]{1,2,0:T(8,128)(2,1)S(1)}, u32[]{:S(2)}, u32[]{:S(2)}) %all-to-all-start.10) | async-done | bytes 1048608 | tf_op jit(solution)/shard_map/all_to_all | solution.py:500
  668.6 43.8 %attend_backward.1 = bf16[2048,768]{1,0:T(8,128)(2,1)} custom-call(bf16[2048,768]{1,0:T(8,128)(2,1)} %convolution_convert_fusion.1.q_ref.k_ref.v_ref, bf16[2048,768]{1,0:T(8,128)(2,1)} %convolution_convert_fusion.1.q_ref.k_ref.v_ref, bf16[2048,768]{1,0:T(8,128)(2,1)} %convolution_convert_fusion.1.q_ref.k_ref.v_ref, bf16[2048,256]{1,0:T(8,128)(2,1)} %bitcast.132, ...), custom_call_target="tpu_custom_call" | custom-call | tf_op jit(solution)/shard_map/attend_backward/pallas_call | solution.py:203
  739.3 57.6 %reduce-scatter.34.cloned.1.call-done = bf16[512,1024]{1,0:T(8,128)(2,1)} async-done(((bf16[2048,1024]{1,0:T(8,128)(2,1)}), bf16[512,1024]{1,0:T(8,128)(2,1)}) %reduce-scatter.34.cloned.1.call-update) | async-done | bytes 1048592 | tf_op jit(solution)/shard_map/reduce_scatter | solution.py:515
  864.5 12.7 %reduce-scatter.36.cloned.1.call-done = bf16[128,768]{1,0:T(8,128)(2,1)} async-done(((bf16[1024,768]{1,0:T(8,128)(2,1)}), bf16[128,768]{1,0:T(8,128)(2,1)}) %reduce-scatter.36.cloned.1.call-update) | async-done | bytes 196624 | tf_op jit(solution)/shard_map/reduce_scatter | solution.py:527
  879.2 35.4 %reduce-scatter.40.cloned.1.call-done = bf16[128,256]{1,0:T(8,128)(2,1)} async-done(((bf16[1024,256]{1,0:T(8,128)(2,1)}), bf16[128,256]{1,0:T(8,128)(2,1)}) %reduce-scatter.40.cloned.1.call-update) | async-done | bytes 65552
  916.2 80.6 %all-gather.21.cloned.1.call-done = bf16[8192,256]{1,0:T(8,128)(2,1)} async-done(((bf16[2048,256]{1,0:T(8,128)(2,1)}), bf16[8192,256]{1,0:T(8,128)(2,1)}) %all-gather.21.cloned.1.call-update) | async-done | bytes 4194320 | tf_op jit(solution)/shard_map/all_gather | solution.py:480
  1001.6 42.3 %psum.15 = f32[4,1024]{1,0:T(4,128)S(1)} all-reduce(f32[4,1024]{1,0:T(4,128)S(1)} %pad_maximum_fusion.5), channel_id=1, replica_groups=mesh['row'=8,'col'=4] {'row','col'}, use_global_device_ids=true, to_apply=%region_35.36 | all-reduce | flops 4096 | bytes 32768 | tf_op jit(solution)/shard_map/psum | solution.py:525
  1045.0 33.7 %all-gather.13.cloned.1.call-done = bf16[2048,1024]{1,0:T(8,128)(2,1)} async-done(((bf16[512,1024]{1,0:T(8,128)(2,1)}), bf16[2048,1024]{1,0:T(8,128)(2,1)}) %all-gather.13.cloned.1.call-update) | async-done | bytes 4194320 | tf_op jit(solution)/shard_map/all_gather | solution.py:523
  (187 shorter events, 340.1 us)
Async XLA Ops:
  7.2 32.0 %all-gather.11.cloned.1.call-start = ((), (), s32[]{:S(2)}) async-start(), calls=%async_computation.25 | async-start | bytes 1787904 | tf_op jit(solution)/shard_map/all_gather | solution.py:388
  9.7 109.8 %all-gather.17.cloned.1.call-start = ((), (), s32[]{:S(2)}) async-start(), calls=%async_computation.39 | async-start | bytes 2621440 | tf_op jit(solution)/shard_map/all_gather | solution.py:414
  23.9 109.7 %all-gather.15.cloned.1.call-start = ((), (), s32[]{:S(2)}) async-start(), calls=%async_computation.38 | async-start | bytes 2621440 | tf_op jit(solution)/shard_map/all_gather | solution.py:411
  88.0 110.9 %all-to-all-start.1 = ((bf16[8,4,128,1024]{3,2,1,0:T(8,128)(2,1)}), bf16[8,4,128,1024]{3,2,1,0:T(8,128)(2,1)}, u32[]{:S(2)}, u32[]{:S(2)}) async-start(bf16[8,4,128,1024]{3,2,1,0:T(8,128)(2,1)} %bitcast.114), calls=%async_computation.1 | async-start | bytes 16777216 | tf_op jit(solution)/shard_map/all_to_all | solution.py:402
  92.9 86.6 %all-gather.19.cloned.1.call-start = ((), (), s32[]{:S(2)}) async-start(), calls=%async_computation.40 | async-start | bytes 2621440 | tf_op jit(solution)/shard_map/all_gather | solution.py:413
  119.5 407.7 %reduce-scatter.18.cloned.1.call-start = ((), (), s32[]{:S(2)}) async-start(), calls=%async_computation.26 | async-start | bytes 2621440 | tf_op jit(solution)/shard_map/reduce_scatter | solution.py:441
  244.7 282.5 %reduce-scatter.20.cloned.1.call-start = ((), (), s32[]{:S(2)}) async-start(), calls=%async_computation.27 | async-start | bytes 2621440 | tf_op jit(solution)/shard_map/reduce_scatter | solution.py:441
  298.0 229.2 %reduce-scatter.22.cloned.1.call-start = ((), (), s32[]{:S(2)}) async-start(), calls=%async_computation.28 | async-start | bytes 2621440 | tf_op jit(solution)/shard_map/reduce_scatter | solution.py:441
  351.4 175.8 %reduce-scatter.24.cloned.1.call-start = ((), (), s32[]{:S(2)}) async-start(), calls=%async_computation.29 | async-start | bytes 2621440 | tf_op jit(solution)/shard_map/reduce_scatter | solution.py:441
  404.9 30.2 %all-to-all-start.6 = ((bf16[8,4,128,256]{3,2,1,0:T(8,128)(2,1)}), bf16[8,4,128,256]{3,2,1,0:T(8,128)(2,1)S(1)}, u32[]{:S(2)}, u32[]{:S(2)}) async-start(bf16[8,4,128,256]{3,2,1,0:T(8,128)(2,1)} %get-tuple-element.68), calls=%async_computation.10 | async-start | bytes 4194304 | tf_op jit(solution)/shard_map/all_to_all | solution.py:456
  408.5 191.4 %reduce-scatter.26.cloned.1.call-start = ((), (), s32[]{:S(2)}) async-start(), calls=%async_computation.30 | async-start | bytes 1310720 | tf_op jit(solution)/shard_map/reduce_scatter | solution.py:458
  445.7 154.3 %reduce-scatter.28.cloned.1.call-start = ((), (), s32[]{:S(2)}) async-start(), calls=%async_computation.31 | async-start | bytes 1310720 | tf_op jit(solution)/shard_map/reduce_scatter | solution.py:458
  514.4 30.2 %all-to-all-start.9 = ((bf16[8,4,128,256]{3,2,1,0:T(8,128)(2,1)}), bf16[8,4,128,256]{3,2,1,0:T(8,128)(2,1)S(1)}, u32[]{:S(2)}, u32[]{:S(2)}) async-start(bf16[8,4,128,256]{3,2,1,0:T(8,128)(2,1)} %get-tuple-element.71), calls=%async_computation.16 | async-start | bytes 4194304 | tf_op jit(solution)/shard_map/all_to_all | solution.py:456
  518.0 82.0 %reduce-scatter.30.cloned.1.call-start = ((), (), s32[]{:S(2)}) async-start(), calls=%async_computation.32 | async-start | bytes 1310720 | tf_op jit(solution)/shard_map/reduce_scatter | solution.py:458
  545.9 30.2 %all-to-all-start.5 = ((bf16[8,4,128,256]{3,2,1,0:T(8,128)(2,1)}), bf16[8,4,128,256]{3,2,1,0:T(8,128)(2,1)S(1)}, u32[]{:S(2)}, u32[]{:S(2)}) async-start(bf16[8,4,128,256]{3,2,1,0:T(8,128)(2,1)} %pad_maximum_fusion), calls=%async_computation.9 | async-start | bytes 4194304 | tf_op jit(solution)/shard_map/all_to_all | solution.py:451
  549.5 50.5 %reduce-scatter.32.cloned.1.call-start = ((), (), s32[]{:S(2)}) async-start(), calls=%async_computation.33 | async-start | bytes 1310720 | tf_op jit(solution)/shard_map/reduce_scatter | solution.py:458
  558.7 174.7 %reduce-scatter.38.cloned.1.call-start = ((), (), s32[]{:S(2)}) async-start(), calls=%async_computation.37 | async-start | bytes 2621440 | tf_op jit(solution)/shard_map/reduce_scatter | solution.py:506
  613.1 54.2 %all-to-all-start.10 = ((bf16[4,512,256]{1,2,0:T(8,128)(2,1)}), bf16[4,512,256]{1,2,0:T(8,128)(2,1)S(1)}, u32[]{:S(2)}, u32[]{:S(2)}) async-start(bf16[4,512,256]{1,2,0:T(8,128)(2,1)} %fusion.26), calls=%async_computation.18 | async-start | bytes 2097152 | tf_op jit(solution)/shard_map/all_to_all | solution.py:500
  616.8 180.2 %reduce-scatter.34.cloned.1.call-start = ((), (), s32[]{:S(2)}) async-start(), calls=%async_computation.34 | async-start | bytes 5242880 | tf_op jit(solution)/shard_map/reduce_scatter | solution.py:515
  720.2 142.8 %reduce-scatter.42.cloned.1.call-start = ((), (), s32[]{:S(2)}) async-start(), calls=%async_computation.43 | async-start | bytes 294912
  724.1 153.1 %reduce-scatter.36.cloned.1.call-start = ((), (), s32[]{:S(2)}) async-start(), calls=%async_computation.36 | async-start | bytes 1769472 | tf_op jit(solution)/shard_map/reduce_scatter | solution.py:527
  733.3 181.3 %reduce-scatter.40.cloned.1.call-start = ((), (), s32[]{:S(2)}) async-start(), calls=%async_computation.42 | async-start | bytes 589824
  735.4 261.4 %all-gather.21.cloned.1.call-start = ((), (), s32[]{:S(2)}) async-start(), calls=%async_computation.41 | async-start | bytes 5242880 | tf_op jit(solution)/shard_map/all_gather | solution.py:480
  736.0 342.7 %all-gather.13.cloned.1.call-start = ((), (), s32[]{:S(2)}) async-start(), calls=%async_computation.35 | async-start | bytes 5242880 | tf_op jit(solution)/shard_map/all_gather | solution.py:523
  (18 other events, 135.9 us)
Sparse Core Ops, SparseCore 0:
  10.5 28.6 all-gather.10
  41.3 45.9 all-gather.16
  88.8 44.6 all-gather.14
  134.9 44.5 all-gather.18
  244.8 40.7 reduce-scatter.17
  298.1 40.7 reduce-scatter.19
  351.5 40.6 reduce-scatter.21
  405.0 40.7 reduce-scatter.23
  448.1 26.4 reduce-scatter.25
  484.8 23.9 reduce-scatter.27
  527.2 26.1 reduce-scatter.29
  558.8 26.1 reduce-scatter.31
  609.4 59.1 reduce-scatter.37
  720.3 76.6 reduce-scatter.33
  800.4 34.1 reduce-scatter.41
  838.7 38.4 reduce-scatter.35
  880.4 34.0 reduce-scatter.39
  916.0 80.7 all-gather.20
  998.3 80.2 all-gather.12

commit v2 on v1

--- a/solution.py
+++ b/solution.py
@@ -14,6 +14,10 @@
     return pltpu.CompilerParams(dimension_semantics=kinds or None, vmem_limit_bytes=VMEM)
 
 
+def cost(flops, moved, special=0):
+    return pl.CostEstimate(flops=flops, bytes_accessed=moved, transcendentals=special)
+
+
 def dot(a, b, dims):
     return lax.dot_general(a, b, (dims, ((), ())), preferred_element_type=jnp.float32)
 
@@ -22,32 +26,45 @@
 TN = ((0,), (0,))
 
 
-def pack_body(base, step, slots_ref, rows_ref, out_ref):
+def pack_body(base, step, each, given, slots_ref, rows_ref, *rest):
+    outs = rest[given:]
     length = slots_ref.shape[1]
-    first = base + pl.program_id(0) * step
-    wanted = first + lax.broadcasted_iota(jnp.int32, (step, length), 0)
+    at = pl.program_id(0)
+    wanted = base + at * step + lax.broadcasted_iota(jnp.int32, (step, length), 0)
     chosen = jnp.where(slots_ref[...] == wanted, 1.0, 0.0).astype(jnp.bfloat16)
-    out_ref[...] = dot(chosen, rows_ref[...], NN).astype(out_ref.dtype)
-
-
-def pack(slots, rows, base, count):
+    made = dot(chosen, rows_ref[...], NN).astype(jnp.bfloat16)
+    for j, out_ref in enumerate(outs):
+
+        @pl.when(at // each == j)
+        def _(out_ref=out_ref):
+            out_ref[...] = made
+
+
+def pack(slots, rows, base, count, outs, waits=()):
     length, width = rows.shape
     step = min(512, count)
+    each = count // step
     return pl.pallas_call(
-        functools.partial(pack_body, base, step),
-        out_shape=jax.ShapeDtypeStruct((count, width), rows.dtype),
-        grid=(count // step,),
+        functools.partial(pack_body, base, step, each, len(waits)),
+        out_shape=(jax.ShapeDtypeStruct((count, width), rows.dtype),) * outs,
+        grid=(each * outs,),
         in_specs=[
             pl.BlockSpec((1, length), lambda i: (0, 0)),
             pl.BlockSpec((length, width), lambda i: (0, 0)),
-        ],
-        out_specs=pl.BlockSpec((step, width), lambda i: (i, 0)),
+        ]
+        + [pl.BlockSpec(memory_space=pl.ANY)] * len(waits),
+        out_specs=tuple(
+            pl.BlockSpec((step, width), lambda i, j=j: (jnp.clip(i - j * each, 0, each - 1), 0))
+            for j in range(outs)
+        ),
         compiler_params=params("arbitrary"),
         name="pack",
-    )(slots.reshape(1, length), rows)
-
-
-def unpack_body(slots_ref, rows_ref, out_ref):
+        cost_estimate=cost(2 * outs * count * length * width, 2 * (length + outs * count) * width),
+    )(slots.reshape(1, length), rows, *waits)
+
+
+def unpack_body(slots_ref, rows_ref, *rest):
+    out_ref = rest[-1]
     step = out_ref.shape[0]
     count = rows_ref.shape[0]
     held = lax.broadcasted_iota(jnp.int32, (step, count), 1)
@@ -55,7 +72,7 @@
     out_ref[...] = dot(chosen, rows_ref[...], NN).astype(out_ref.dtype)
 
 
-def unpack(slots, rows):
+def unpack(slots, rows, waits=()):
     count, width = rows.shape
     length = slots.shape[0]
     step = min(256, length)
@@ -66,14 +83,17 @@
         in_specs=[
             pl.BlockSpec((step, 1), lambda i: (i, 0)),
             pl.BlockSpec((count, width), lambda i: (0, 0)),
-        ],
+        ]
+        + [pl.BlockSpec(memory_space=pl.ANY)] * len(waits),
         out_specs=pl.BlockSpec((step, width), lambda i: (i, 0)),
         compiler_params=params("arbitrary"),
         name="unpack",
-    )(slots.reshape(length, 1), rows)
-
-
-def forward_body(blocks, block, q_ref, k_ref, v_ref, o_ref, lse_ref):
+        cost_estimate=cost(2 * count * length * width, 2 * (length + count) * width),
+    )(slots.reshape(length, 1), rows, *waits)
+
+
+def forward_body(blocks, block, q_ref, k_ref, v_ref, *rest):
+    o_ref, lse_ref = rest[-2:]
     width = q_ref.shape[1]
     heads = width // HEAD_DIM
     lane = lax.broadcasted_iota(jnp.int32, (block, width), 1)
@@ -113,7 +133,7 @@
         lax.fori_loop(0, heads, one_head, 0)
 
 
-def attend_forward(projected, blocks, block):
+def attend_forward(projected, blocks, block, waits=()):
     length, triple = projected.shape
     width = triple // 3
     heads = width // HEAD_DIM
@@ -126,19 +146,19 @@
             jax.ShapeDtypeStruct((heads, rows), jnp.float32),
         ),
         grid=(1,),
-        in_specs=spec,
+        in_specs=spec + [pl.BlockSpec(memory_space=pl.ANY)] * len(waits),
         out_specs=(
             pl.BlockSpec((rows, width), lambda i: (0, 0)),
             pl.BlockSpec((heads, rows), lambda i: (0, 0)),
         ),
         compiler_params=params("arbitrary"),
         name="attend_forward",
-    )(projected, projected, projected)
-
-
-def backward_body(
-    block, q_ref, k_ref, v_ref, do_ref, o_ref, lse_ref, out_ref, dk_ref, dv_ref, p_ref, ds_ref, qm_ref, dom_ref
-):
+        cost_estimate=cost(8 * rows * length * width, 8 * length * width, rows * length * heads),
+    )(projected, projected, projected, *waits)
+
+
+def backward_body(block, q_ref, k_ref, v_ref, do_ref, o_ref, lse_ref, *rest):
+    out_ref, dk_ref, dv_ref, p_ref, ds_ref, qm_ref, dom_ref = rest[-7:]
     length, width = q_ref.shape
     heads = width // HEAD_DIM
     count = length // block
@@ -194,7 +214,7 @@
         out_ref[here, pl.ds(2 * width, width)] = dv_ref[here, :].astype(out_ref.dtype)
 
 
-def attend_backward(projected, grad_context, context, logsum, block):
+def attend_backward(projected, grad_context, context, logsum, block, waits=()):
     length, triple = projected.shape
     width = triple // 3
     heads = width // HEAD_DIM
@@ -204,7 +224,8 @@
         functools.partial(backward_body, block),
         out_shape=jax.ShapeDtypeStruct((length, triple), jnp.bfloat16),
         grid=(1,),
-        in_specs=spec + [whole, whole, pl.BlockSpec((heads, length), lambda i: (0, 0))],
+        in_specs=spec + [whole, whole, pl.BlockSpec((heads, length), lambda i: (0, 0))]
+        + [pl.BlockSpec(memory_space=pl.ANY)] * len(waits),
         out_specs=pl.BlockSpec((length, triple), lambda i: (0, 0)),
         scratch_shapes=[
             pltpu.VMEM((length, width), jnp.float32),
@@ -216,7 +237,8 @@
         ],
         compiler_params=params("arbitrary"),
         name="attend_backward",
-    )(projected, projected, projected, grad_context, context, logsum)
+        cost_estimate=cost(20 * length * length * width, 16 * length * width, length * length * heads),
+    )(projected, projected, projected, grad_context, context, logsum, *waits)
 
 
 ROOT = math.sqrt(2.0 / math.pi)
@@ -239,7 +261,7 @@
     made = dot(active, wback_ref[...], NN).astype(jnp.bfloat16)
     for j in range(parts):
         out_ref[j] = made[:, j * wide : (j + 1) * wide]
-    grad_active = dot(gy_ref[...].reshape(rows, depth), wback_ref[...], NT)
+    grad_active = dot(gy_ref[...], wback_ref[...], NT)
     grad_hidden = (grad_active * slope).astype(jnp.bfloat16)
     slope_ref[...] = grad_hidden
     back = dot(grad_hidden, win_ref[...], NT).astype(jnp.bfloat16)
@@ -248,17 +270,17 @@
         ref[...] = back[:, j * wide : (j + 1) * wide].reshape(ref.shape)
 
 
-def expert_pass(e, x, grad_y, w_in, w_back, sent, parts, pieces):
-    sources, local, cap, depth = grad_y.shape
-    width = w_in.shape[2]
-    rows = sources * cap
+def expert_pass(e, cap, x, grad_y, w_in, w_back, sent, parts, pieces, waits=()):
+    rows, depth = x.shape
+    local, _, width = w_in.shape
+    sources = rows // cap
     step = min(256, rows)
     group = step // cap
     sent = list(sent or [])
     piece = jax.ShapeDtypeStruct((sources, local, cap, depth // pieces), jnp.bfloat16)
     piece_spec = pl.BlockSpec((group, None, cap, depth // pieces), lambda i: (i, e, 0, 0))
     made = pl.pallas_call(
-        functools.partial(expert_body, len(sent)),
+        functools.partial(expert_body, len(sent) + len(waits)),
         out_shape=(
             jax.ShapeDtypeStruct((parts, rows, depth // parts), jnp.bfloat16),
             jax.ShapeDtypeStruct((rows, width), jnp.bfloat16),
@@ -268,11 +290,11 @@
         grid=(rows // step,),
         in_specs=[
             pl.BlockSpec((step, depth), lambda i: (i, 0)),
-            pl.BlockSpec((group, None, cap, depth), lambda i: (i, e, 0, 0)),
+            pl.BlockSpec((step, depth), lambda i: (i, 0)),
             pl.BlockSpec((None, depth, width), lambda i: (e, 0, 0)),
             pl.BlockSpec((None, width, depth), lambda i: (e, 0, 0)),
         ]
-        + [pl.BlockSpec(memory_space=pl.ANY)] * len(sent),
+        + [pl.BlockSpec(memory_space=pl.ANY)] * (len(sent) + len(waits)),
         out_specs=(
             pl.BlockSpec((parts, step, depth // parts), lambda i: (0, i, 0)),
             pl.BlockSpec((step, width), lambda i: (i, 0)),
@@ -282,48 +304,51 @@
         input_output_aliases={4 + j: 3 + j for j in range(len(sent))},
         compiler_params=params("arbitrary"),
         name="expert_pass",
-    )(x, grad_y, w_in, w_back, *sent)
+        cost_estimate=cost(8 * rows * depth * width, 4 * width * depth + 12 * rows * depth, rows * width),
+    )(x, grad_y, w_in, w_back, *sent, *waits)
     return made[0], made[1], made[2], made[3:]
 
 
 def weight_body(given, x_ref, gy_ref, gate_ref, active_ref, slope_ref, *rest):
-    gin_ref, gback_ref, xt_ref, gyg_ref = rest[given:]
+    gin_ref, gback_ref, token_ref, xt_ref, gyg_ref = rest[given:]
+    token_ref[...] = jnp.zeros_like(token_ref)
     rows, depth = x_ref.shape
 
     @pl.when(pl.program_id(0) == 0)
     def _():
         gate = gate_ref[...]
         xt_ref[...] = (x_ref[...].astype(jnp.float32) * gate).T.astype(jnp.bfloat16)
-        grad_y = gy_ref[...].reshape(rows, depth).astype(jnp.float32)
-        gyg_ref[...] = (grad_y * gate).astype(jnp.bfloat16)
+        gyg_ref[...] = (gy_ref[...].astype(jnp.float32) * gate).astype(jnp.bfloat16)
 
     gin_ref[...] = dot(xt_ref[...], slope_ref[...], NN)
     gback_ref[...] = dot(active_ref[...], gyg_ref[...], TN)
 
 
-def weight_pass(e, x, grad_y, gate, active, slope, sent):
-    sources, local, cap, depth = grad_y.shape
+def weight_pass(e, local, x, grad_y, gate, active, slope, sent, waits=()):
     rows, width = active.shape
+    depth = x.shape[1]
     step = min(256, width)
     sent = list(sent or [])
     return pl.pallas_call(
-        functools.partial(weight_body, len(sent)),
+        functools.partial(weight_body, len(sent) + len(waits)),
         out_shape=(
             jax.ShapeDtypeStruct((local, depth, width), jnp.float32),
             jax.ShapeDtypeStruct((local, width, depth), jnp.float32),
+            jax.ShapeDtypeStruct((8, 128), jnp.float32),
         ),
         grid=(width // step,),
         in_specs=[
             pl.BlockSpec((rows, depth), lambda i: (0, 0)),
-            pl.BlockSpec((sources, None, cap, depth), lambda i: (0, e, 0, 0)),
+            pl.BlockSpec((rows, depth), lambda i: (0, 0)),
             pl.BlockSpec((rows, 1), lambda i: (0, 0)),
             pl.BlockSpec((rows, step), lambda i: (0, i)),
             pl.BlockSpec((rows, step), lambda i: (0, i)),
         ]
-        + [pl.BlockSpec(memory_space=pl.ANY)] * len(sent),
+        + [pl.BlockSpec(memory_space=pl.ANY)] * (len(sent) + len(waits)),
         out_specs=(
             pl.BlockSpec((None, depth, step), lambda i: (e, 0, i)),
             pl.BlockSpec((None, step, depth), lambda i: (e, i, 0)),
+            pl.BlockSpec((8, 128), lambda i: (0, 0)),
         ),
         scratch_shapes=[
             pltpu.VMEM((depth, rows), jnp.bfloat16),
@@ -332,10 +357,43 @@
         input_output_aliases={5 + j: j for j in range(len(sent))},
         compiler_params=params("arbitrary"),
         name="weight_pass",
-    )(x, grad_y, gate, active, slope, *sent)
+        cost_estimate=cost(4 * rows * depth * width, 8 * width * depth + 8 * rows * depth),
+    )(x, grad_y, gate, active, slope, *sent, *waits)
 
 
 EPSILON = 1e-05
+
+
+def swap(blocks, axis):
+    return lax.all_to_all(blocks, axis, split_axis=0, concat_axis=0, tiled=True)
+
+
+def tie(*values):
+    return lax.optimization_barrier(values)
+
+
+def relay_steps(shard, axis):
+    count = lax.axis_size(axis)
+    right = left = shard
+    steps = []
+    for _ in range(count - 1):
+        right = lax.ppermute(right, axis, [(i, i + 1) for i in range(count - 1)])
+        left = lax.ppermute(left, axis, [(i + 1, i) for i in range(count - 1)])
+        steps.append((right, left))
+    return steps
+
+
+def relay_join(shard, steps, axis, dim):
+    count = lax.axis_size(axis)
+    me = lax.axis_index(axis)
+    size = shard.shape[dim]
+    shape = list(shard.shape)
+    shape[dim] = size * count
+    whole = jnp.zeros(shape, shard.dtype)
+    for k in range(count):
+        piece = shard if k == 0 else steps[k - 1][0] + steps[count - k - 1][1]
+        whole = lax.dynamic_update_slice_in_dim(whole, piece, ((me - k) % count) * size, dim)
+    return whole
 
 
 def layer_stats(values):
@@ -382,24 +440,26 @@
     def own(values):
         return lax.dynamic_slice_in_dim(values, col * own_length, own_length, 0)
 
-    first = jnp.concatenate(
-        [w_qkv.transpose(1, 0, 2).reshape(share, 3 * width), ln_gains.T, ln_biases.T], axis=1
-    )
-    first = lax.all_gather(first, "row", axis=0, tiled=True)
-    qkv_full = first[:, : 3 * width]
-    norms = first[:, 3 * width :].astype(jnp.float32).T
-    gains, biases = norms[0:2], norms[2:4]
-    second = jnp.concatenate([w_out.T, w_router], axis=1)
-    second = lax.all_gather(second, "row", axis=0, tiled=True)
-    router_full = second[:, width:]
-    out_own = second[:, :width]
+    stacked = w_qkv.transpose(1, 0, 2).reshape(share, 3 * width)
+    weights = jnp.concatenate([stacked, w_router, ln_gains.T, ln_biases.T], axis=1)
+    weights = lax.all_gather(weights, "row", axis=0, tiled=True)
+    out_block = swap(jnp.broadcast_to(w_out.T[None], (cols_all, share, width)), "col")
 
     chosen, ranks, select = slot_layout(expert_ids, experts, cap)
     slots = chosen * cap + ranks
     slots_by_local = ((chosen % local) * rows_all + chosen // local) * cap + ranks
-
-    grad_packed = pack(slots, cotangent, 0, experts * cap).reshape(rows_all, local, cap, depth)
-    grad_arrived = lax.all_to_all(grad_packed, "row", split_axis=0, concat_axis=0, tiled=True)
+    block_rows = rows_all * cap
+
+    def send(packed):
+        return swap(packed.reshape(rows_all, cap, depth), "row").reshape(block_rows, depth)
+
+    grad_packed = list(pack(slots_by_local, cotangent, 0, block_rows, local))
+    weights, grad_packed[0] = tie(weights, grad_packed[0])
+    grad_arrived = [send(grad_packed[0])]
+    qkv_full = weights[:, : 3 * width]
+    router_full = weights[:, 3 * width : 3 * width + experts]
+    norms = weights[:, 3 * width + experts :].astype(jnp.float32).T
+    gains, biases = norms[0:2], norms[2:4]
 
     resid_in = tokens.astype(jnp.float32)
     normed_one, inverse_one = layer_stats(resid_in)
@@ -408,10 +468,26 @@
 
     half = blocks // 2
     context_a, logsum_a = attend_forward(projected, tuple(range(half)), block)
+    context_a, grad_arrived[0], grad_packed[1] = tie(context_a, grad_arrived[0], grad_packed[1])
+    grad_arrived.append(send(grad_packed[1]))
     full_a = lax.all_gather(context_a, "col", axis=0)
-    context_b, logsum_b = attend_forward(projected, tuple(range(half, blocks)), block)
+    context_b, logsum_b = attend_forward(
+        projected, tuple(range(half, blocks)), block, [context_a]
+    )
+    context_b, out_block, grad_arrived[1], *grad_packed[2:] = tie(
+        context_b, out_block, grad_arrived[1], *grad_packed[2:]
+    )
     full_b = lax.all_gather(context_b, "col", axis=0)
-    out_full = lax.all_gather(out_own, "col", axis=0)
+    out_full = swap(jnp.broadcast_to(out_block[None], (rows_all, *out_block.shape)), "row")
+    if local > 2:
+        grad_packed[2], out_full = tie(grad_packed[2], out_full)
+    out_full = out_full.transpose(1, 0, 2, 3).reshape(cols_all, depth, width)
+    for e in range(2, local):
+        grad_arrived.append(send(grad_packed[e]))
+        if e + 1 < local:
+            full_b, grad_arrived[e], grad_packed[e + 1] = tie(
+                full_b, grad_arrived[e], grad_packed[e + 1]
+            )
     context = jnp.concatenate([context_a, context_b], axis=0)
     logsum = jnp.concatenate([logsum_a, logsum_b], axis=1)
 
@@ -425,51 +501,81 @@
     probs = jax.nn.softmax(logits, axis=-1)
     gate = jnp.sum(probs * select, axis=-1, keepdims=True)
 
-    block_rows = rows_all * cap
+    packed = list(pack(slots_by_local, routed, 0, block_rows, 1))
+    if local > 1:
+        packed += pack(slots_by_local, routed, block_rows, block_rows, local - 1)
+    packed[0], grad_arrived[-1] = tie(packed[0], grad_arrived[-1])
+    held = jnp.arange(experts * cap, dtype=jnp.int32)
+    gates = jnp.sum(jnp.where(held[:, None] == slots[None, :], gate[:, 0][None, :], 0.0), axis=1)
+    gates = gates.reshape(rows_all, local * cap)
     arrived, summed, active, slope = [], [], [], []
     sent = None
     for e in range(local):
-        packed = pack(slots_by_local, routed, e * block_rows, block_rows)
-        packed = packed.reshape(rows_all, cap, depth)
-        moved = lax.all_to_all(packed, "row", split_axis=0, concat_axis=0, tiled=True)
-        arrived.append(moved.reshape(block_rows, depth))
+        arrived.append(send(packed[e]))
+        after = gates if e + 1 == local else packed[e + 1]
+        after, arrived[e] = tie(after, arrived[e])
+        if e:
+            after, summed[e - 1] = tie(after, summed[e - 1])
+            summed[e - 1] = lax.psum_scatter(
+                summed[e - 1], "col", scatter_dimension=0, tiled=True
+            )
+        if e + 1 == local:
+            gates = after
+        else:
+            packed[e + 1] = after
         made, kept, grads, sent = expert_pass(
-            e, arrived[e], grad_arrived, w_in, w_back, sent, cols_all, pieces
+            e,
+            cap,
+            arrived[e],
+            grad_arrived[e],
+            w_in,
+            w_back,
+            sent,
+            cols_all,
+            pieces,
+            packed[-1:] if e == 0 else summed[e - 3 : e - 2] if e > 2 else [],
         )
         active.append(kept)
         slope.append(grads)
-        summed.append(lax.psum_scatter(made, "col", scatter_dimension=0, tiled=True))
-
-    held = jnp.arange(experts * cap, dtype=jnp.int32)
-    gate_packed = jnp.sum(jnp.where(held[:, None] == slots[None, :], gate[:, 0][None, :], 0.0), axis=1)
-    gate_arrived = lax.all_to_all(
-        gate_packed.reshape(rows_all, local * cap), "row", split_axis=0, concat_axis=0, tiled=True
-    )
-    gate_arrived = gate_arrived.reshape(rows_all, local, cap).transpose(1, 0, 2)
+        summed.append(made)
+    summed[-1] = lax.psum_scatter(summed[-1], "col", scatter_dimension=0, tiled=True)
+    gates = swap(gates, "row")
+    gates, *sent = tie(gates, *sent)
+    gates = gates.reshape(rows_all, local, cap).transpose(1, 0, 2)
+
+    backs = []
+    grad_weights = None
+    waits = slope[-1:]
+    for e in range(max(local, pieces)):
+        if e < local:
+            *grad_weights, token = weight_pass(
+                e,
+                local,
+                arrived[e],
+                grad_arrived[e],
+                gates[e].reshape(block_rows, 1),
+                active[e],
+                slope[e],
+                grad_weights,
+                waits + (summed[e - 3 : e - 2] if e < 2 else []),
+            )
+        if e < pieces:
+            back = swap(sent[e], "row")
+            if e + 1 < pieces:
+                sent[e + 1], back, token, *done = tie(sent[e + 1], back, token, *backs[e - 1 :])
+                backs[e - 1 :] = done
+            backs.append(unpack(slots, back.reshape(experts * cap, depth // pieces), [token]))
+            waits = backs[-1:]
+    grad_in, grad_back = grad_weights
+    grad_sent = []
+    for at in range(0, pieces, 2):
+        pair = jnp.concatenate(backs[at : at + 2], axis=1)
+        grad_sent.append(lax.psum_scatter(pair, "col", scatter_dimension=0, tiled=True))
+    grad_sent = jnp.concatenate(grad_sent, axis=1).astype(jnp.float32) * own(gate)
 
     homed = jnp.stack([s.reshape(rows_all, cap, depth // cols_all) for s in summed], axis=1)
-    homed = lax.all_to_all(homed, "row", split_axis=0, concat_axis=0, tiled=True)
+    homed = swap(homed, "row")
     returned = unpack(slots, homed.reshape(experts * cap, depth // cols_all)).astype(jnp.float32)
-
-    grad_sent = []
-    for piece in sent:
-        back = lax.all_to_all(piece, "row", split_axis=0, concat_axis=0, tiled=True)
-        back = unpack(slots, back.reshape(experts * cap, depth // pieces))
-        grad_sent.append(lax.psum_scatter(back, "col", scatter_dimension=0, tiled=True))
-    grad_sent = jnp.concatenate(grad_sent, axis=1).astype(jnp.float32) * own(gate)
-
-    grad_weights = None
-    for e in range(local):
-        grad_weights = weight_pass(
-            e,
-            arrived[e],
-            grad_arrived,
-            gate_arrived[e].reshape(block_rows, 1),
-            active[e],
-            slope[e],
-            grad_weights,
-        )
-    grad_in, grad_back = grad_weights
 
     columns = depth // cols_all
 
@@ -477,7 +583,7 @@
         return lax.dynamic_slice_in_dim(values, col * columns, columns, 1)
 
     mixed = (own_columns(middle) + gate * returned).astype(jnp.bfloat16)
-    mixed_out = lax.all_gather(mixed, "col", axis=0).transpose(1, 0, 2).reshape(length, depth)
+    steps = relay_steps(mixed, "col")
     grad_gate = lax.psum(
         jnp.sum(own_columns(cotangent).astype(jnp.float32) * returned, axis=-1), "col"
     )[:, None]
@@ -485,6 +591,9 @@
     grad_router = jnp.einsum("td,te->de", routed, grad_logits, preferred_element_type=jnp.float32)
 
     grad_y = own(cotangent).astype(jnp.float32)
+    if steps:
+        grad_sent, *first = tie(grad_sent, *steps[0])
+        steps[0] = tuple(first)
     own_middle = own(middle)
     normed_own, inverse_own = layer_stats(own_middle)
     grad_routed = grad_sent + jnp.einsum(
@@ -497,22 +606,32 @@
     grad_context = jnp.einsum(
         "td,zdc->ztc", grad_attn, out_full, preferred_element_type=jnp.float32
     ).astype(jnp.bfloat16)
-    grad_context = lax.all_to_all(grad_context, "col", split_axis=0, concat_axis=0, tiled=True)
-    grad_context = grad_context.reshape(length, width)
+    grad_context = swap(grad_context, "col").reshape(length, width)
 
     full = jnp.concatenate([full_a, full_b], axis=1)
     full_own = lax.dynamic_slice_in_dim(full, col * own_length, own_length, 1)
-    grad_out = jnp.einsum("ztc,td->zcd", full_own, grad_attn, preferred_element_type=jnp.float32)
-    grad_out = lax.psum_scatter(
-        grad_out.astype(jnp.bfloat16), "col", scatter_dimension=0, tiled=False
-    )
-
+    grad_out = jnp.einsum("td,ztc->dzc", grad_attn, full_own, preferred_element_type=jnp.float32)
+    plane = jnp.concatenate([grad_out.reshape(depth, cols_all * width), grad_router], axis=1)
+    plane = swap(plane.astype(jnp.bfloat16).reshape(rows_all, share, -1), "row")
     grad_proj = attend_backward(projected, grad_context, context, logsum, block)
+    grad_proj, plane = tie(grad_proj, plane)
+    plane = jnp.sum(plane.astype(jnp.float32), axis=0)
+    router_share = plane[:, cols_all * width :]
+    out_share = plane[:, : cols_all * width].reshape(share, cols_all, width).transpose(1, 0, 2)
+    out_share = swap(out_share.astype(jnp.bfloat16), "col").astype(jnp.float32)
+    out_share = jnp.sum(out_share, axis=0).T
+    if len(steps) > 1:
+        grad_proj, *second = tie(grad_proj, *steps[1])
+        steps[1] = tuple(second)
     grad_qkv = jnp.einsum("td,tc->dc", normal_in, grad_proj, preferred_element_type=jnp.float32)
     partial = jnp.einsum(
         "tc,dc->td", grad_proj, qkv_full, preferred_element_type=jnp.float32
     ).astype(jnp.bfloat16)
     grad_normal = lax.psum_scatter(partial, "col", scatter_dimension=0, tiled=True)
+    mixed_out = relay_join(mixed, steps, "col", 1)
+    grad_normal, mixed_out, router_share, out_share = tie(
+        grad_normal, mixed_out, router_share, out_share
+    )
     grad_normal = grad_normal.astype(jnp.float32)
     own_normed, own_inverse = layer_stats(own(tokens).astype(jnp.float32))
     gain_one = jnp.sum(grad_normal * own_normed, axis=0)
@@ -522,22 +641,17 @@
     )
     grad_tokens = lax.all_gather(grad_tokens, "col", axis=0, tiled=True)
 
+    qkv_share = swap(grad_qkv.astype(jnp.bfloat16).reshape(rows_all, share, -1), "row")
+    qkv_share = jnp.sum(qkv_share.astype(jnp.float32), axis=0)
+    qkv_share = qkv_share.reshape(share, 3, width).transpose(1, 0, 2)
     small = lax.psum(jnp.stack([gain_one, gain_two, bias_one, bias_two]), ("row", "col"))
     small = lax.dynamic_slice_in_dim(small, lax.axis_index("row") * share, share, 1)
-    qkv_share = lax.psum_scatter(
-        grad_qkv.astype(jnp.bfloat16), "row", scatter_dimension=0, tiled=True
-    )
-    qkv_share = qkv_share.astype(jnp.float32).reshape(share, 3, width).transpose(1, 0, 2)
-    out_share = lax.psum_scatter(grad_out, "row", scatter_dimension=1, tiled=True)
-    router_share = lax.psum_scatter(
-        grad_router.astype(jnp.bfloat16), "row", scatter_dimension=0, tiled=True
-    )
     return (
         mixed_out,
         grad_tokens,
         qkv_share,
-        out_share.astype(jnp.float32),
-        router_share.astype(jnp.float32),
+        out_share,
+        router_share,
         small[0:2],
         small[2],
         small[3],

time: 1100 us -> 908 us (0.83)
  blocking collectives: 247 us -> 94 us
  waiting for transfers between devices: 381 us -> 248 us
  starting transfers between devices: 24.7 us -> 93.7 us
  other arithmetic: 46.1 us -> 69.4 us
    all_to_all x6 -> x2, blocking collectives: 184 us -> 21.6 us  [swap(): return lax.all_to_all(blocks, axis, split_axis=0, concat_axis=0, tiled=True)]
    all_gather x3 -> x1, waiting for transfers between devices: 91 us -> 0.38 us  [per_device(): weights = lax.all_gather(weights, 'row', axis=0, tiled=True)]
    all_to_all x6 -> x18, waiting for transfers between devices: 98.3 us -> 170 us  [swap(): return lax.all_to_all(blocks, axis, split_axis=0, concat_axis=0, tiled=True)]
    ppermute x0 -> x6, waiting for transfers between devices: none -> 55.6 us  [the longest x3 55.6 us: relay_steps(): left = lax.ppermute(left, axis, [(i + 1, i) for i in range(count - 1)])]
    all_to_all x6 -> x18, starting transfers between devices: 23.1 us -> 73.9 us  [swap(): return lax.all_to_all(blocks, axis, split_axis=0, concat_axis=0, tiled=True)]
    reduce_scatter x1, waiting for transfers between devices: 57.6 us -> 10.3 us  [per_device(): lax.psum_scatter(partial, 'col', scatter_dimension=0, tiled=True)]
    unnamed x21 -> x11, waiting for transfers between devices: 36.2 us -> 0.85 us
    all_gather x1, waiting for transfers between devices: 33.7 us -> 1.11 us  [per_device(): grad_tokens = lax.all_gather(grad_tokens, 'col', axis=0, tiled=True)]
  transfers between devices with their start and end apart: 25 -> 35, of which waited for: 13 -> 21; matrix products, arithmetic and copies ran while one was open for 10% -> 13% of each run, Pallas kernels for 25% -> 32%
where the time goes in v2:
time: 908 us; the launch traced here: 896 us
  Pallas kernels  283 us (31%)
  waiting for transfers between devices  248 us (27%)
  blocking collectives  94 us (10%)
  starting transfers between devices  93.7 us (10%)
  other arithmetic  69.4 us (8%)
  matrix products  51.6 us (6%)
  local copies, waits for them, and re-layouts  40.8 us (4%)
  between operations  15.2 us (2%)
    all_to_all x18, waiting for transfers between devices, swap(): return lax.all_to_all(blocks, axis, split_axis=0, concat_axis=0, tiled=True)  170 us
    all_to_all x18, starting transfers between devices, swap(): return lax.all_to_all(blocks, axis, split_axis=0, concat_axis=0, tiled=True)  73.9 us
    pallas_call x4, Pallas kernels, expert_pass(): pl.pallas_call(functools.partial(expert_body, len(sent) + len(waits)), ou...  57.9 us
    ppermute x3, waiting for transfers between devices, relay_steps(): left = lax.ppermute(left, axis, [(i + 1, i) for i in range(count - 1)])  55.6 us
    pallas_call x3, Pallas kernels, pack(): pl.pallas_call(functools.partial(pack_body, base, step, each, len(waits))...  51 us
    psum x1, blocking collectives, per_device(): lax.psum(jnp.stack([gain_one, gain_two, bias_one, bias_two]), ('row', 'co...  47.5 us
    pallas_call x5, Pallas kernels, unpack(): pl.pallas_call(unpack_body, out_shape=jax.ShapeDtypeStruct((length, width...  45.5 us
    pallas_call x4, Pallas kernels, weight_pass(): pl.pallas_call(functools.partial(weight_body, len(sent) + len(waits)), ou...  43.9 us
  transfers between devices with their start and end apart: 35, of which 21 were waited for; matrix products, arithmetic and copies ran while one was open for 13% of the time, Pallas kernels for 32%

profile of v2, /device:TPU:0, one launch (start us, length us, event | category | flops | bytes accessed | tf_op | source)
XLA Modules:
  0.0 896.0 jit_solution(15825843201221083657)
XLA Ops:
  14.9 24.2 %pack.3 = (bf16[1024,1024]{1,0:T(8,128)(2,1)}, bf16[1024,1024]{1,0:T(8,128)(2,1)}, bf16[1024,1024]{1,0:T(8,128)(2,1)}, bf16[1024,1024]{1,0:T(8,128)(2,1)}) custom-call(s32[1,2048]{1,0:T(1,128)} %multiply_add_fusion.2.slots_ref, bf16[2048,1024]{1,0:T(8,128)(2,1)} %rows_ref.1), custom_call_target="tpu_custom_call" | custom-call | flops 17179869184 | bytes 12582912 | tf_op jit(solution)/shard_map/pack/pallas_call | solution.py:47
  53.5 15.3 %attend_forward.2 = (bf16[1024,256]{1,0:T(8,128)(2,1)}, f32[4,1024]{1,0:T(4,128)}) custom-call(bf16[2048,768]{1,0:T(8,128)(2,1)} %convolution_convert_fusion.1.q_ref.k_ref.v_ref, bf16[2048,768]{1,0:T(8,128)(2,1)} %convolution_convert_fusion.1.q_ref.k_ref.v_ref, bf16[2048,768]{1,0:T(8,128)(2,1)} %convolution_convert_fusion.1.q_ref.k_ref.v_ref), custom_call_target="tpu_custom_call" | custom-call | flops 4294967296 | bytes 4194304 | tf_op jit(solution)/shard_map/attend_forward/pallas_call | solution.py:142
  71.0 14.4 %all_to_all.107 = bf16[4,128,256]{1,2,0:T(8,128)(2,1)S(1)} all-to-all(bf16[4,128,256]{1,2,0:T(8,128)(2,1)S(1)} %broadcast_in_dim.19), channel_id=1, replica_groups=mesh['row'=8,'col'=4] {'col'}, dimensions={0} | all-to-all | bytes 524288 | tf_op jit(solution)/shard_map/all_to_all | solution.py:368
  91.3 26.0 %attend_forward.3 = (bf16[1024,256]{1,0:T(8,128)(2,1)}, f32[4,1024]{1,0:T(4,128)}) custom-call(bf16[2048,768]{1,0:T(8,128)(2,1)} %convolution_convert_fusion.1.q_ref.k_ref.v_ref, bf16[2048,768]{1,0:T(8,128)(2,1)} %convolution_convert_fusion.1.q_ref.k_ref.v_ref, bf16[2048,768]{1,0:T(8,128)(2,1)} %convolution_convert_fusion.1.q_ref.k_ref.v_ref, ...), custom_call_target="tpu_custom_call" | custom-call | flops 4294967296 | bytes 4194304 | tf_op jit(solution)/shard_map/attend_forward/pallas_call | solution.py:142
  124.3 25.9 %all-to-all-done.3 = bf16[8,4,128,256]{2,3,1,0:T(8,128)(2,1)S(1)} async-done(((bf16[8,4,128,256]{2,3,1,0:T(8,128)(2,1)}), bf16[8,4,128,256]{2,3,1,0:T(8,128)(2,1)S(1)}, u32[]{:S(2)}, u32[]{:S(2)}) %all-to-all-start.3) | async-done | bytes 2097184 | tf_op jit(solution)/shard_map/all_to_all | solution.py:368
  225.3 18.8 %pack.4 = (bf16[1024,1024]{1,0:T(8,128)(2,1)}, bf16[1024,1024]{1,0:T(8,128)(2,1)}, bf16[1024,1024]{1,0:T(8,128)(2,1)}) custom-call(s32[1,2048]{1,0:T(1,128)} %multiply_add_fusion.2.slots_ref, bf16[2048,1024]{1,0:T(8,128)(2,1)} %add_convert_fusion.rows_ref), custom_call_target="tpu_custom_call" | custom-call | flops 12884901888 | bytes 10485760 | tf_op jit(solution)/shard_map/pack/pallas_call | solution.py:47
  255.6 14.3 %expert_pass.4 = (bf16[4,1024,256]{2,1,0:T(8,128)(2,1)}, bf16[1024,1024]{1,0:T(8,128)(2,1)}, bf16[1024,1024]{1,0:T(8,128)(2,1)}, bf16[8,4,128,256]{3,2,1,0:T(8,1...) custom-call(bf16[1024,1024]{1,0:T(8,128)(2,1)} %bitcast.29.x_ref, ...), custom_call_target="tpu_custom_call" | custom-call | flops 8589934592 | bytes 16777216 | tf_op jit(solution)/shard_map/expert_pass/pallas_call | solution.py:282
  269.9 12.2 %all-to-all-done.7 = bf16[8,128,1024]{2,1,0:T(8,128)(2,1)S(1)} async-done(((bf16[8,128,1024]{2,1,0:T(8,128)(2,1)}), bf16[8,128,1024]{2,1,0:T(8,128)(2,1)S(1)}, u32[]{:S(2)}, u32[]{:S(2)}) %all-to-all-start.7) | async-done | bytes 2097184 | tf_op jit(solution)/shard_map/all_to_all | solution.py:368
  287.2 14.7 %expert_pass.5 = (bf16[4,1024,256]{2,1,0:T(8,128)(2,1)}, bf16[1024,1024]{1,0:T(8,128)(2,1)}, bf16[1024,1024]{1,0:T(8,128)(2,1)}, bf16[8,4,128,256]{3,2,1,0:T(8,1...) custom-call(bf16[1024,1024]{1,0:T(8,128)(2,1)} %bitcast.137, ...), custom_call_target="tpu_custom_call", output_to_operand_aliasing={{3}: (4, {}), {4}: (5, {}), {5}: (6, {}), {6}: (7, {})} | custom-call | flops 8589934592 | bytes 16777216 | tf_op jit(solution)/shard_map/expert_pass/pallas_call | solution.py:282
  301.9 11.8 %all-to-all-done.8 = bf16[8,128,1024]{2,1,0:T(8,128)(2,1)S(1)} async-done(((bf16[8,128,1024]{2,1,0:T(8,128)(2,1)}), bf16[8,128,1024]{2,1,0:T(8,128)(2,1)S(1)}, u32[]{:S(2)}, u32[]{:S(2)}) %all-to-all-start.8) | async-done | bytes 2097184 | tf_op jit(solution)/shard_map/all_to_all | solution.py:368
  325.5 14.4 %expert_pass.6 = (bf16[4,1024,256]{2,1,0:T(8,128)(2,1)}, bf16[1024,1024]{1,0:T(8,128)(2,1)}, bf16[1024,1024]{1,0:T(8,128)(2,1)}, bf16[8,4,128,256]{3,2,1,0:T(8,1...) custom-call(bf16[1024,1024]{1,0:T(8,128)(2,1)} %bitcast.135, ...), custom_call_target="tpu_custom_call", output_to_operand_aliasing={{3}: (4, {}), {4}: (5, {}), {5}: (6, {}), {6}: (7, {})} | custom-call | flops 8589934592 | bytes 16777216 | tf_op jit(solution)/shard_map/expert_pass/pallas_call | solution.py:282
  355.5 14.4 %expert_pass.7 = (bf16[4,1024,256]{2,1,0:T(8,128)(2,1)}, bf16[1024,1024]{1,0:T(8,128)(2,1)}, bf16[1024,1024]{1,0:T(8,128)(2,1)}, bf16[8,4,128,256]{3,2,1,0:T(8,1...) custom-call(bf16[1024,1024]{1,0:T(8,128)(2,1)} %bitcast.133, ...), custom_call_target="tpu_custom_call", output_to_operand_aliasing={{3}: (4, {}), {4}: (5, {}), {5}: (6, {}), {6}: (7, {})} | custom-call | flops 8589934592 | bytes 16777216 | tf_op jit(solution)/shard_map/expert_pass/pallas_call | solution.py:282
  374.7 10.9 %weight_pass.4 = (f32[4,1024,1024]{2,1,0:T(8,128)}, f32[4,1024,1024]{2,1,0:T(8,128)}, f32[8,128]{1,0:T(8,128)}) custom-call(bf16[1024,1024]{1,0:T(8,128)(2,1)} %bitcast.29.x_ref, bf16[1024,1024]{1,0:T(8,128)(2,1)} %bitcast.144, f32[1024,1]{1,0:T(8,128)} %copy.132.gate_ref, bf16[1024,1024]{1,0:T(8,128)(2,1)} %get-tuple-element.181.active_ref, ...), custom_call_target="tpu_custom_call" | custom-call | flops 4294967296 | bytes 16777216 | tf_op jit(solution)/shard_map/weight_pass/pallas_call | solution.py:332
  385.6 14.5 %all-to-all-done.11 = bf16[8,4,128,256]{3,2,1,0:T(8,128)(2,1)S(1)} async-done(((bf16[8,4,128,256]{3,2,1,0:T(8,128)(2,1)}), bf16[8,4,128,256]{3,2,1,0:T(8,128)(2,1)S(1)}, u32[]{:S(2)}, u32[]{:S(2)}) %all-to-all-start.11) | async-done | bytes 2097184 | tf_op jit(solution)/shard_map/all_to_all | solution.py:368
  417.9 10.9 %weight_pass.5 = (f32[4,1024,1024]{2,1,0:T(8,128)}, f32[4,1024,1024]{2,1,0:T(8,128)}, f32[8,128]{1,0:T(8,128)}) custom-call(bf16[1024,1024]{1,0:T(8,128)(2,1)} %bitcast.138, bf16[1024,1024]{1,0:T(8,128)(2,1)} %bitcast.132, f32[1024,1]{1,0:T(8,128)} %copy.135.gate_ref, ...), custom_call_target="tpu_custom_call", output_to_operand_aliasing={{0}: (5, {}), {1}: (6, {})} | custom-call | flops 4294967296 | bytes 16777216 | tf_op jit(solution)/shard_map/weight_pass/pallas_call | solution.py:332
  447.1 11.1 %weight_pass.6 = (f32[4,1024,1024]{2,1,0:T(8,128)}, f32[4,1024,1024]{2,1,0:T(8,128)}, f32[8,128]{1,0:T(8,128)}) custom-call(bf16[1024,1024]{1,0:T(8,128)(2,1)} %bitcast.136, bf16[1024,1024]{1,0:T(8,128)(2,1)} %bitcast.22.gy_ref, f32[1024,1]{1,0:T(8,128)} %copy.136.gate_ref, ...), custom_call_target="tpu_custom_call", output_to_operand_aliasing={{0}: (5, {}), {1}: (6, {})} | custom-call | flops 4294967296 | bytes 16777216 | tf_op jit(solution)/shard_map/weight_pass/pallas_call | solution.py:332
  479.2 11.0 %weight_pass.7 = (f32[4,1024,1024]{2,1,0:T(8,128)}, f32[4,1024,1024]{2,1,0:T(8,128)}, f32[8,128]{1,0:T(8,128)}) custom-call(bf16[1024,1024]{1,0:T(8,128)(2,1)} %bitcast.134, bf16[1024,1024]{1,0:T(8,128)(2,1)} %bitcast.130, f32[1024,1]{1,0:T(8,128)} %copy.137.gate_ref, ...), custom_call_target="tpu_custom_call", output_to_operand_aliasing={{0}: (5, {}), {1}: (6, {})} | custom-call | flops 4294967296 | bytes 16777216 | tf_op jit(solution)/shard_map/weight_pass/pallas_call | solution.py:332
  521.5 21.6 %all-to-all-done.15 = bf16[8,4,128,256]{3,2,1,0:T(8,128)(2,1)S(1)} async-done(((bf16[8,4,128,256]{3,2,1,0:T(8,128)(2,1)}), bf16[8,4,128,256]{3,2,1,0:T(8,128)(2,1)S(1)}, u32[]{:S(2)}, u32[]{:S(2)}) %all-to-all-start.15) | async-done | bytes 2097184 | tf_op jit(solution)/shard_map/all_to_all | solution.py:368
  565.3 24.9 %psum.14 = f32[2048]{0:T(1024)S(1)} all-reduce(f32[2048]{0:T(1024)S(1)} %fusion.21), channel_id=1, replica_groups=mesh['row'=8,'col'=4] {'col'}, use_global_device_ids=true, to_apply=%region_18.19 | all-reduce | flops 2048 | bytes 16384 | tf_op jit(solution)/shard_map/psum | solution.py:587
  638.5 43.8 %attend_backward.1 = bf16[2048,768]{1,0:T(8,128)(2,1)} custom-call(bf16[2048,768]{1,0:T(8,128)(2,1)} %convolution_convert_fusion.1.q_ref.k_ref.v_ref, bf16[2048,768]{1,0:T(8,128)(2,1)} %convolution_convert_fusion.1.q_ref.k_ref.v_ref, bf16[2048,768]{1,0:T(8,128)(2,1)} %convolution_convert_fusion.1.q_ref.k_ref.v_ref, bf16[2048,256]{1,0:T(8,128)(2,1)} %bitcast.161, ...), custom_call_target="tpu_custom_call" | custom-call | flops 21474836480 | bytes 8388608 | tf_op jit(solution)/shard_map/attend_backward/pallas_call | solution.py:223
  700.8 55.6 %collective-permute-done.4 = bf16[2048,256]{1,0:T(8,128)(2,1)S(1)} collective-permute-done((bf16[2048,256]{1,0:T(8,128)(2,1)}, bf16[2048,256]{1,0:T(8,128)(2,1)S(1)}, u32[]{:S(2)}, u32[]{:S(2)}) %collective-permute-start.4) | collective-permute-done | bytes 1048608 | tf_op jit(solution)/shard_map/ppermute | solution.py:381
  771.4 12.0 %all-to-all-done.18 = bf16[4,128,256]{1,2,0:T(8,128)(2,1)S(1)} async-done(((bf16[4,128,256]{1,2,0:T(8,128)(2,1)}), bf16[4,128,256]{1,2,0:T(8,128)(2,1)S(1)}, u32[]{:S(2)}, u32[]{:S(2)}) %all-to-all-start.18) | async-done | bytes 262176 | tf_op jit(solution)/shard_map/all_to_all | solution.py:368
  812.4 21.0 %all-to-all-done.19 = bf16[8,128,768]{2,1,0:T(8,128)(2,1)S(1)} async-done(((bf16[8,128,768]{2,1,0:T(8,128)(2,1)}), bf16[8,128,768]{2,1,0:T(8,128)(2,1)S(1)}, u32[]{:S(2)}, u32[]{:S(2)}) %all-to-all-start.19) | async-done | bytes 1572896 | tf_op jit(solution)/shard_map/all_to_all | solution.py:368
  834.7 47.5 %psum.15 = f32[4,1024]{1,0:T(4,128)S(1)} all-reduce(f32[4,1024]{1,0:T(4,128)S(1)} %pad_maximum_fusion.7), channel_id=1, replica_groups=mesh['row'=8,'col'=4] {'row','col'}, use_global_device_ids=true, to_apply=%region_33.34 | all-reduce | flops 4096 | bytes 32768 | tf_op jit(solution)/shard_map/psum | solution.py:647
  (264 shorter events, 389.4 us)
Async XLA Ops:
  7.2 32.3 %all-gather.7.cloned.1.call-start = ((), (), s32[]{:S(2)}) async-start(), calls=%async_computation.27 | async-start | bytes 1861632 | tf_op jit(solution)/shard_map/all_gather | solution.py:445
  39.4 31.4 %all-to-all-start = ((bf16[8,128,1024]{2,1,0:T(8,128)(2,1)}), bf16[8,128,1024]{2,1,0:T(8,128)(2,1)S(1)}, u32[]{:S(2)}, u32[]{:S(2)}) async-start(bf16[8,128,1024]{2,1,0:T(8,128)(2,1)} %bitcast.153), calls=%async_computation | async-start | bytes 4194304 | tf_op jit(solution)/shard_map/all_to_all | solution.py:368
  44.2 112.9 %all-gather.11.cloned.1.call-start = ((), (), s32[]{:S(2)}) async-start(), calls=%async_computation.36 | async-start | bytes 2621440 | tf_op jit(solution)/shard_map/all_gather | solution.py:473
  85.4 32.5 %all-to-all-start.2 = ((bf16[8,128,1024]{2,1,0:T(8,128)(2,1)}), bf16[8,128,1024]{2,1,0:T(8,128)(2,1)S(1)}, u32[]{:S(2)}, u32[]{:S(2)}) async-start(bf16[8,128,1024]{2,1,0:T(8,128)(2,1)} %bitcast.151), calls=%async_computation.2 | async-start | bytes 4194304 | tf_op jit(solution)/shard_map/all_to_all | solution.py:368
  123.5 50.4 %all-gather.13.cloned.1.call-start = ((), (), s32[]{:S(2)}) async-start(), calls=%async_computation.37 | async-start | bytes 2621440 | tf_op jit(solution)/shard_map/all_gather | solution.py:480
  150.2 31.0 %all-to-all-start.4 = ((bf16[8,128,1024]{2,1,0:T(8,128)(2,1)}), bf16[8,128,1024]{2,1,0:T(8,128)(2,1)}, u32[]{:S(2)}, u32[]{:S(2)}) async-start(bf16[8,128,1024]{2,1,0:T(8,128)(2,1)} %bitcast.147), calls=%async_computation.4 | async-start | bytes 4194304 | tf_op jit(solution)/shard_map/all_to_all | solution.py:368
  221.0 31.0 %all-to-all-start.6 = ((bf16[8,128,1024]{2,1,0:T(8,128)(2,1)}), bf16[8,128,1024]{2,1,0:T(8,128)(2,1)}, u32[]{:S(2)}, u32[]{:S(2)}) async-start(bf16[8,128,1024]{2,1,0:T(8,128)(2,1)} %bitcast.155), calls=%async_computation.6 | async-start | bytes 4194304 | tf_op jit(solution)/shard_map/all_to_all | solution.py:368
  255.6 99.9 %reduce-scatter.8.cloned.1.call-start = ((), (), s32[]{:S(2)}) async-start(), calls=%async_computation.28 | async-start | bytes 2621440 | tf_op jit(solution)/shard_map/reduce_scatter | solution.py:519
  287.1 87.5 %reduce-scatter.10.cloned.1.call-start = ((), (), s32[]{:S(2)}) async-start(), calls=%async_computation.29 | async-start | bytes 2621440 | tf_op jit(solution)/shard_map/reduce_scatter | solution.py:519
  321.7 96.1 %reduce-scatter.12.cloned.1.call-start = ((), (), s32[]{:S(2)}) async-start(), calls=%async_computation.30 | async-start | bytes 2621440 | tf_op jit(solution)/shard_map/reduce_scatter | solution.py:519
  373.5 135.0 %reduce-scatter.18.cloned.1.call-start = ((), (), s32[]{:S(2)}) async-start(), calls=%async_computation.33 | async-start | bytes 2621440 | tf_op jit(solution)/shard_map/reduce_scatter | solution.py:541
  401.4 31.2 %all-to-all-start.12 = ((bf16[8,4,128,256]{3,2,1,0:T(8,128)(2,1)}), bf16[8,4,128,256]{3,2,1,0:T(8,128)(2,1)}, u32[]{:S(2)}, u32[]{:S(2)}) async-start(bf16[8,4,128,256]{3,2,1,0:T(8,128)(2,1)} %get-tuple-element.186), calls=%async_computation.14 | async-start | bytes 4194304 | tf_op jit(solution)/shard_map/all_to_all | solution.py:368
  432.6 31.0 %all-to-all-start.13 = ((bf16[8,4,128,256]{3,2,1,0:T(8,128)(2,1)}), bf16[8,4,128,256]{3,2,1,0:T(8,128)(2,1)}, u32[]{:S(2)}, u32[]{:S(2)}) async-start(bf16[8,4,128,256]{3,2,1,0:T(8,128)(2,1)} %get-tuple-element.197), calls=%async_computation.16 | async-start | bytes 4194304 | tf_op jit(solution)/shard_map/all_to_all | solution.py:368
  437.0 154.7 %reduce-scatter.14.cloned.1.call-start = ((), (), s32[]{:S(2)}) async-start(), calls=%async_computation.31 | async-start | bytes 2621440 | tf_op jit(solution)/shard_map/reduce_scatter | solution.py:573
  468.8 123.0 %reduce-scatter.16.cloned.1.call-start = ((), (), s32[]{:S(2)}) async-start(), calls=%async_computation.32 | async-start | bytes 2621440 | tf_op jit(solution)/shard_map/reduce_scatter | solution.py:573
  558.8 34.3 %collective-permute-start = (bf16[2048,256]{1,0:T(8,128)(2,1)S(1)}, bf16[2048,256]{1,0:T(8,128)(2,1)}, u32[]{:S(2)}, u32[]{:S(2)}) collective-permute-start(bf16[2048,256]{1,0:T(8,128)(2,1)S(1)} %get-tuple-element.289), channel_id=1, source_target_pairs={{0,1},{1,2},{2,3},{4,5},{5,6},{6,7},{8,9},{9,10},{10,11},{12,13},{... | collective-permute-start | bytes 3145736 | tf_op jit(solution)/shard_map/ppermute | solution.py:380
  600.8 31.2 %all-to-all-start.16 = ((bf16[4,512,256]{1,2,0:T(8,128)(2,1)}), bf16[4,512,256]{1,2,0:T(8,128)(2,1)S(1)}, u32[]{:S(2)}, u32[]{:S(2)}) async-start(bf16[4,512,256]{1,2,0:T(8,128)(2,1)} %fusion.26), calls=%async_computation.22 | async-start | bytes 2097152 | tf_op jit(solution)/shard_map/all_to_all | solution.py:368
  610.6 71.7 %collective-permute-start.2 = (bf16[2048,256]{1,0:T(8,128)(2,1)}, bf16[2048,256]{1,0:T(8,128)(2,1)}, u32[]{:S(2)}, u32[]{:S(2)}) collective-permute-start(bf16[2048,256]{1,0:T(8,128)(2,1)} %collective-permute-done), channel_id=1, source_target_pairs={{0,1},{1,2},{2,3},{4,5},{5,6},{6,7},{8,9},{9,10},{10,11},{12,13},{... | collective-permute-start | bytes 3145736 | tf_op jit(solution)/shard_map/ppermute | solution.py:380
  615.8 66.5 %collective-permute-start.3 = (bf16[2048,256]{1,0:T(8,128)(2,1)}, bf16[2048,256]{1,0:T(8,128)(2,1)}, u32[]{:S(2)}, u32[]{:S(2)}) collective-permute-start(bf16[2048,256]{1,0:T(8,128)(2,1)} %collective-permute-done.1), channel_id=1, source_target_pairs={{1,0},{2,1},{3,2},{5,4},{6,5},{7,6},{9,8},{10,9},{11,10},{13,12},{... | collective-permute-start | bytes 3145736 | tf_op jit(solution)/shard_map/ppermute | solution.py:381
  632.0 50.3 %all-to-all-start.17 = ((bf16[8,128,1056]{1,2,0:T(8,128)(2,1)}), bf16[8,128,1056]{1,2,0:T(8,128)(2,1)}, u32[]{:S(2)}, u32[]{:S(2)}) async-start(bf16[8,128,1056]{1,2,0:T(8,128)(2,1)} %copy.146), calls=%async_computation.23 | async-start | bytes 4325376 | tf_op jit(solution)/shard_map/all_to_all | solution.py:368
  636.9 157.5 %reduce-scatter.20.cloned.1.call-start = ((), (), s32[]{:S(2)}) async-start(), calls=%async_computation.34 | async-start | bytes 5242880 | tf_op jit(solution)/shard_map/reduce_scatter | solution.py:630
  690.2 66.2 %collective-permute-start.4 = (bf16[2048,256]{1,0:T(8,128)(2,1)}, bf16[2048,256]{1,0:T(8,128)(2,1)S(1)}, u32[]{:S(2)}, u32[]{:S(2)}) collective-permute-start(bf16[2048,256]{1,0:T(8,128)(2,1)} %collective-permute-done.3), channel_id=1, source_target_pairs={{1,0},{2,1},{3,2},{5,4},{6,5},{7,6},{9,8},{10,9},{11,10},{13,12},{... | collective-permute-start | bytes 3145736 | tf_op jit(solution)/shard_map/ppermute | solution.py:381
  694.6 74.0 %collective-permute-start.5 = (bf16[2048,256]{1,0:T(8,128)(2,1)}, bf16[2048,256]{1,0:T(8,128)(2,1)}, u32[]{:S(2)}, u32[]{:S(2)}) collective-permute-start(bf16[2048,256]{1,0:T(8,128)(2,1)} %collective-permute-done.2), channel_id=1, source_target_pairs={{0,1},{1,2},{2,3},{4,5},{5,6},{6,7},{8,9},{9,10},{10,11},{12,13},{... | collective-permute-start | bytes 3145736 | tf_op jit(solution)/shard_map/ppermute | solution.py:380
  765.6 118.8 %all-gather.9.cloned.1.call-start = ((), (), s32[]{:S(2)}) async-start(), calls=%async_computation.35 | async-start | bytes 5242880 | tf_op jit(solution)/shard_map/all_gather | solution.py:642
  (57 other events, 1101.0 us)
Sparse Core Ops, SparseCore 0:
  10.5 28.9 all-gather.6
  71.0 46.7 all-gather.10
  125.9 47.9 all-gather.12
  282.3 43.5 reduce-scatter.7
  328.2 43.1 reduce-scatter.9
  373.6 43.1 reduce-scatter.11
  419.2 43.1 reduce-scatter.17
  465.3 43.5 reduce-scatter.13
  511.3 43.1 reduce-scatter.15
  690.3 104.1 reduce-scatter.19
  800.4 84.0 all-gather.8

commit v3 on v2

--- a/solution.py
+++ b/solution.py
@@ -6,6 +6,7 @@
 from jax.sharding import PartitionSpec as P
 
 HEAD_DIM = 64
+EPSILON = 1e-05
 MASKED = -1e30
 VMEM = 60 << 20
 
@@ -26,13 +27,19 @@
 TN = ((0,), (0,))
 
 
-def pack_body(base, step, each, given, slots_ref, rows_ref, *rest):
-    outs = rest[given:]
-    length = slots_ref.shape[1]
+def pack_body(base, step, each, parts, slots_ref, *rest):
+    rows_refs, outs = rest[:parts], rest[-((pl.num_programs(0)) // each) :]
     at = pl.program_id(0)
-    wanted = base + at * step + lax.broadcasted_iota(jnp.int32, (step, length), 0)
-    chosen = jnp.where(slots_ref[...] == wanted, 1.0, 0.0).astype(jnp.bfloat16)
-    made = dot(chosen, rows_ref[...], NN).astype(jnp.bfloat16)
+    made = None
+    first = 0
+    for rows_ref in rows_refs:
+        length = rows_ref.shape[0]
+        wanted = base + at * step + lax.broadcasted_iota(jnp.int32, (step, length), 0)
+        chosen = jnp.where(slots_ref[:, pl.ds(first, length)] == wanted, 1.0, 0.0)
+        more = dot(chosen.astype(jnp.bfloat16), rows_ref[...], NN)
+        made = more if made is None else made + more
+        first += length
+    made = made.astype(jnp.bfloat16)
     for j, out_ref in enumerate(outs):
 
         @pl.when(at // each == j)
@@ -41,17 +48,16 @@
 
 
 def pack(slots, rows, base, count, outs, waits=()):
-    length, width = rows.shape
+    length = slots.shape[0]
+    width = rows[0].shape[1]
     step = min(512, count)
     each = count // step
     return pl.pallas_call(
-        functools.partial(pack_body, base, step, each, len(waits)),
-        out_shape=(jax.ShapeDtypeStruct((count, width), rows.dtype),) * outs,
+        functools.partial(pack_body, base, step, each, len(rows)),
+        out_shape=(jax.ShapeDtypeStruct((count, width), jnp.bfloat16),) * outs,
         grid=(each * outs,),
-        in_specs=[
-            pl.BlockSpec((1, length), lambda i: (0, 0)),
-            pl.BlockSpec((length, width), lambda i: (0, 0)),
-        ]
+        in_specs=[pl.BlockSpec((1, length), lambda i: (0, 0))]
+        + [pl.BlockSpec(r.shape, lambda i: (0, 0)) for r in rows]
         + [pl.BlockSpec(memory_space=pl.ANY)] * len(waits),
         out_specs=tuple(
             pl.BlockSpec((step, width), lambda i, j=j: (jnp.clip(i - j * each, 0, each - 1), 0))
@@ -60,36 +66,78 @@
         compiler_params=params("arbitrary"),
         name="pack",
         cost_estimate=cost(2 * outs * count * length * width, 2 * (length + outs * count) * width),
-    )(slots.reshape(1, length), rows, *waits)
-
-
-def unpack_body(slots_ref, rows_ref, *rest):
-    out_ref = rest[-1]
+    )(slots.reshape(1, length), *rows, *waits)
+
+
+def unpack_body(parts, *refs):
+    out_ref = refs[-1]
     step = out_ref.shape[0]
-    count = rows_ref.shape[0]
-    held = lax.broadcasted_iota(jnp.int32, (step, count), 1)
-    chosen = jnp.where(slots_ref[...] == held, 1.0, 0.0).astype(jnp.bfloat16)
-    out_ref[...] = dot(chosen, rows_ref[...], NN).astype(out_ref.dtype)
-
-
-def unpack(slots, rows, waits=()):
-    count, width = rows.shape
-    length = slots.shape[0]
-    step = min(256, length)
+    made = None
+    for slots_ref, rows_ref in zip(refs[:parts], refs[parts : 2 * parts]):
+        count = rows_ref.shape[0]
+        held = lax.broadcasted_iota(jnp.int32, (step, count), 1)
+        chosen = jnp.where(slots_ref[...] == held, 1.0, 0.0).astype(jnp.bfloat16)
+        more = dot(chosen, rows_ref[...], NN)
+        made = more if made is None else made + more
+    out_ref[...] = made.astype(out_ref.dtype)
+
+
+def unpack(slots, rows, step, place, waits=()):
+    length = slots[0].shape[0]
+    width = rows[0].shape[1]
+    count = sum(r.shape[0] for r in rows)
     return pl.pallas_call(
-        unpack_body,
-        out_shape=jax.ShapeDtypeStruct((length, width), rows.dtype),
+        functools.partial(unpack_body, len(rows)),
+        out_shape=jax.ShapeDtypeStruct((length, width), jnp.bfloat16),
         grid=(length // step,),
-        in_specs=[
-            pl.BlockSpec((step, 1), lambda i: (i, 0)),
-            pl.BlockSpec((count, width), lambda i: (0, 0)),
-        ]
+        in_specs=[pl.BlockSpec((step, 1), lambda i: (i, 0))] * len(rows)
+        + [pl.BlockSpec(r.shape, lambda i: (0, 0)) for r in rows]
         + [pl.BlockSpec(memory_space=pl.ANY)] * len(waits),
-        out_specs=pl.BlockSpec((step, width), lambda i: (i, 0)),
+        out_specs=pl.BlockSpec((step, width), lambda i: (place(i), 0)),
         compiler_params=params("arbitrary"),
         name="unpack",
         cost_estimate=cost(2 * count * length * width, 2 * (length + count) * width),
-    )(slots.reshape(length, 1), rows, *waits)
+    )(*(at.reshape(length, 1) for at in slots), *rows, *waits)
+
+
+def middle_body(full_ref, out_ref, tokens_ref, gain_ref, bias_ref, middle_ref, routed_ref):
+    total = tokens_ref[...].astype(jnp.float32)
+    for z in range(full_ref.shape[0]):
+        total = total + dot(full_ref[z], out_ref[z], NT)
+    middle_ref[...] = total
+    mean = jnp.mean(total, axis=1, keepdims=True)
+    centered = total - mean
+    inverse = lax.rsqrt(jnp.mean(centered * centered, axis=1, keepdims=True) + EPSILON)
+    routed_ref[...] = (centered * inverse * gain_ref[...] + bias_ref[...]).astype(jnp.bfloat16)
+
+
+def middle_pass(full, out_full, tokens, first, gain, bias):
+    cols, rows, width = full.shape
+    depth = tokens.shape[1]
+    step = min(256, rows)
+    row = pl.BlockSpec((1, depth), lambda i: (0, 0))
+    return pl.pallas_call(
+        middle_body,
+        out_shape=(
+            jax.ShapeDtypeStruct((rows, depth), jnp.float32),
+            jax.ShapeDtypeStruct((rows, depth), jnp.bfloat16),
+        ),
+        grid=(rows // step,),
+        in_specs=[
+            pl.BlockSpec((cols, step, width), lambda i: (0, i, 0)),
+            pl.BlockSpec((cols, depth, width), lambda i: (0, 0, 0)),
+            pl.BlockSpec((step, depth), lambda i: (i + first // step, 0)),
+            row,
+            row,
+        ],
+        out_specs=(
+            pl.BlockSpec((step, depth), lambda i: (i, 0)),
+            pl.BlockSpec((step, depth), lambda i: (i, 0)),
+        ),
+        compiler_params=params("arbitrary"),
+        name="middle_pass",
+        cost_estimate=cost(2 * rows * depth * width * cols, 10 * rows * depth),
+    )(full, out_full, tokens, gain, bias)
 
 
 def forward_body(blocks, block, q_ref, k_ref, v_ref, *rest):
@@ -157,18 +205,21 @@
     )(projected, projected, projected, *waits)
 
 
-def backward_body(block, q_ref, k_ref, v_ref, do_ref, o_ref, lse_ref, *rest):
-    out_ref, dk_ref, dv_ref, p_ref, ds_ref, qm_ref, dom_ref = rest[-7:]
-    length, width = q_ref.shape
+def backward_body(block, first, given, *refs):
+    q_ref, do_ref, o_ref, lse_ref, k_ref, v_ref = refs[:6]
+    outs = refs[6 + given :]
+    out_ref, p_ref, ds_ref, qm_ref, dom_ref, dk_ref, dv_ref = outs[:1] + outs[-6:]
+    width = q_ref.shape[1]
     heads = width // HEAD_DIM
-    count = length // block
+    count = q_ref.shape[0] // block
     lane = lax.broadcasted_iota(jnp.int32, (block, width), 1)
     hidden = lax.broadcasted_iota(jnp.int32, (block, block), 0) > lax.broadcasted_iota(
         jnp.int32, (block, block), 1
     )
-    for i in reversed(range(count)):
+    for at in reversed(range(count)):
+        i = first + at
         span = (i + 1) * block
-        here = pl.ds(i * block, block)
+        here = pl.ds(at * block, block)
 
         def one_head(h, carry, here=here, span=span, i=i):
             mine = (lane >= h * HEAD_DIM) & (lane < (h + 1) * HEAD_DIM)
@@ -204,41 +255,58 @@
         lax.fori_loop(0, heads, one_head, 0)
         new_v = dot(p_ref[pl.ds(0, span), :], dom_ref[...], NN)
         new_k = dot(ds_ref[pl.ds(0, span), :], qm_ref[...], NN)
-        if i == count - 1:
-            dv_ref[...] = new_v
-            dk_ref[...] = new_k
+        if at == count - 1:
+            old_k, old_v = (refs[6][...], refs[7][...]) if given > 1 else (0.0, 0.0)
+            dv_ref[...] = old_v + new_v
+            dk_ref[...] = old_k + new_k
         else:
             dv_ref[pl.ds(0, span), :] += new_v
             dk_ref[pl.ds(0, span), :] += new_k
-        out_ref[here, pl.ds(width, width)] = dk_ref[here, :].astype(out_ref.dtype)
-        out_ref[here, pl.ds(2 * width, width)] = dv_ref[here, :].astype(out_ref.dtype)
-
-
-def attend_backward(projected, grad_context, context, logsum, block, waits=()):
-    length, triple = projected.shape
-    width = triple // 3
+        low = pl.ds(i * block, block)
+        out_ref[here, pl.ds(width, width)] = dk_ref[low, :].astype(out_ref.dtype)
+        out_ref[here, pl.ds(2 * width, width)] = dv_ref[low, :].astype(out_ref.dtype)
+    if first:
+        outs[1][...] = dk_ref[pl.ds(0, first * block), :]
+        outs[2][...] = dv_ref[pl.ds(0, first * block), :]
+
+
+def attend_backward(projected, grad_context, context, logsum, block, first, carried=()):
+    rows, width = context.shape
     heads = width // HEAD_DIM
-    spec = [pl.BlockSpec((length, width), lambda i, j=j: (0, j)) for j in range(3)]
-    whole = pl.BlockSpec((length, width), lambda i: (0, 0))
+    length = first * block + rows
+    half = lambda j: pl.BlockSpec((rows, width), lambda i: (first * block // rows, j))
+    own = pl.BlockSpec((rows, width), lambda i: (0, 0))
+    low = pl.BlockSpec((first * block, width), lambda i: (0, 0))
+    rest = jax.ShapeDtypeStruct((first * block, width), jnp.float32)
+    more = bool(first)
     return pl.pallas_call(
-        functools.partial(backward_body, block),
-        out_shape=jax.ShapeDtypeStruct((length, triple), jnp.bfloat16),
+        functools.partial(backward_body, block, first, len(carried)),
+        out_shape=(jax.ShapeDtypeStruct((rows, 3 * width), jnp.bfloat16),) + (rest,) * (2 * more),
         grid=(1,),
-        in_specs=spec + [whole, whole, pl.BlockSpec((heads, length), lambda i: (0, 0))]
-        + [pl.BlockSpec(memory_space=pl.ANY)] * len(waits),
-        out_specs=pl.BlockSpec((length, triple), lambda i: (0, 0)),
+        in_specs=[
+            half(0),
+            own,
+            own,
+            pl.BlockSpec((heads, rows), lambda i: (0, 0)),
+            pl.BlockSpec((length, width), lambda i: (0, 1)),
+            pl.BlockSpec((length, width), lambda i: (0, 2)),
+        ]
+        + [own] * len(carried),
+        out_specs=(pl.BlockSpec((rows, 3 * width), lambda i: (0, 0)),) + (low,) * (2 * more),
         scratch_shapes=[
-            pltpu.VMEM((length, width), jnp.float32),
-            pltpu.VMEM((length, width), jnp.float32),
             pltpu.VMEM((length, heads * block), jnp.bfloat16),
             pltpu.VMEM((length, heads * block), jnp.bfloat16),
             pltpu.VMEM((heads * block, width), jnp.bfloat16),
             pltpu.VMEM((heads * block, width), jnp.bfloat16),
+            pltpu.VMEM((length, width), jnp.float32),
+            pltpu.VMEM((length, width), jnp.float32),
         ],
         compiler_params=params("arbitrary"),
         name="attend_backward",
-        cost_estimate=cost(20 * length * length * width, 16 * length * width, length * length * heads),
-    )(projected, projected, projected, grad_context, context, logsum, *waits)
+        cost_estimate=cost(
+            20 * rows * length * width, 16 * length * width, rows * length * heads
+        ),
+    )(projected, grad_context, context, logsum, projected, projected, *carried)
 
 
 ROOT = math.sqrt(2.0 / math.pi)
@@ -270,15 +338,17 @@
         ref[...] = back[:, j * wide : (j + 1) * wide].reshape(ref.shape)
 
 
-def expert_pass(e, cap, x, grad_y, w_in, w_back, sent, parts, pieces, waits=()):
+def expert_pass(e, cap, x, grad_y, w_in, w_back, sent, members, parts, pieces, waits=()):
     rows, depth = x.shape
-    local, _, width = w_in.shape
+    width = w_in.shape[2]
     sources = rows // cap
     step = min(256, rows)
     group = step // cap
     sent = list(sent or [])
-    piece = jax.ShapeDtypeStruct((sources, local, cap, depth // pieces), jnp.bfloat16)
-    piece_spec = pl.BlockSpec((group, None, cap, depth // pieces), lambda i: (i, e, 0, 0))
+    piece = jax.ShapeDtypeStruct((sources, members, cap, depth // pieces), jnp.bfloat16)
+    piece_spec = pl.BlockSpec(
+        (group, None, cap, depth // pieces), lambda i: (i, e % members, 0, 0)
+    )
     made = pl.pallas_call(
         functools.partial(expert_body, len(sent) + len(waits)),
         out_shape=(
@@ -361,9 +431,6 @@
     )(x, grad_y, gate, active, slope, *sent, *waits)
 
 
-EPSILON = 1e-05
-
-
 def swap(blocks, axis):
     return lax.all_to_all(blocks, axis, split_axis=0, concat_axis=0, tiled=True)
 
@@ -432,13 +499,22 @@
     experts = w_router.shape[1]
     local = w_in.shape[0]
     cap = 2 * length // experts
-    block = min(256, length)
-    blocks = length // block
-    own_length = length // cols_all
-    pieces = 4
-
-    def own(values):
-        return lax.dynamic_slice_in_dim(values, col * own_length, own_length, 0)
+    block_rows = rows_all * cap
+    block = min(256, length // 2)
+    half = length // 2
+    part = half // cols_all
+    members = max(1, local // 2)
+    pieces = 2
+
+    def own(low, high):
+        both = (lax.dynamic_slice_in_dim(v, col * part, part, 0) for v in (low, high))
+        return jnp.concatenate(list(both), axis=0)
+
+    def own_of(values):
+        return own(values[:half], values[half:])
+
+    def send(packed):
+        return swap(packed.reshape(rows_all, cap, depth), "row").reshape(block_rows, depth)
 
     stacked = w_qkv.transpose(1, 0, 2).reshape(share, 3 * width)
     weights = jnp.concatenate([stacked, w_router, ln_gains.T, ln_biases.T], axis=1)
@@ -448,13 +524,18 @@
     chosen, ranks, select = slot_layout(expert_ids, experts, cap)
     slots = chosen * cap + ranks
     slots_by_local = ((chosen % local) * rows_all + chosen // local) * cap + ranks
-    block_rows = rows_all * cap
-
-    def send(packed):
-        return swap(packed.reshape(rows_all, cap, depth), "row").reshape(block_rows, depth)
-
-    grad_packed = list(pack(slots_by_local, cotangent, 0, block_rows, local))
-    weights, grad_packed[0] = tie(weights, grad_packed[0])
+    member = chosen % local
+    slots_by_group = [
+        jnp.where(
+            member // members == g,
+            ((chosen // local) * members + member % members) * cap + ranks,
+            -1,
+        )
+        for g in range(local // members)
+    ]
+
+    grad_packed = list(pack(slots_by_local, [cotangent], 0, block_rows, local))
+    weights, grad_packed[0], out_block = tie(weights, grad_packed[0], out_block)
     grad_arrived = [send(grad_packed[0])]
     qkv_full = weights[:, : 3 * width]
     router_full = weights[:, 3 * width : 3 * width + experts]
@@ -466,71 +547,68 @@
     normal_in = (normed_one * gains[0] + biases[0]).astype(jnp.bfloat16)
     projected = jnp.dot(normal_in, qkv_full, preferred_element_type=jnp.float32).astype(jnp.bfloat16)
 
-    half = blocks // 2
-    context_a, logsum_a = attend_forward(projected, tuple(range(half)), block)
-    context_a, grad_arrived[0], grad_packed[1] = tie(context_a, grad_arrived[0], grad_packed[1])
-    grad_arrived.append(send(grad_packed[1]))
+    count = half // block
+    context_a, logsum_a = attend_forward(projected, tuple(range(count)), block)
+    context_a, grad_arrived[0], *grad_packed[1:2] = tie(
+        context_a, grad_arrived[0], *grad_packed[1:2]
+    )
     full_a = lax.all_gather(context_a, "col", axis=0)
+    grad_arrived += [send(p) for p in grad_packed[1:2]]
     context_b, logsum_b = attend_forward(
-        projected, tuple(range(half, blocks)), block, [context_a]
-    )
-    context_b, out_block, grad_arrived[1], *grad_packed[2:] = tie(
-        context_b, out_block, grad_arrived[1], *grad_packed[2:]
-    )
+        projected, tuple(range(count, 2 * count)), block, [context_a]
+    )
+    context_b, out_block, *grad_arrived[1:] = tie(context_b, out_block, *grad_arrived[1:])
     full_b = lax.all_gather(context_b, "col", axis=0)
     out_full = swap(jnp.broadcast_to(out_block[None], (rows_all, *out_block.shape)), "row")
-    if local > 2:
-        grad_packed[2], out_full = tie(grad_packed[2], out_full)
+    out_full, *grad_packed[2:] = tie(out_full, *grad_packed[2:])
     out_full = out_full.transpose(1, 0, 2, 3).reshape(cols_all, depth, width)
+    gain, bias = gains[1:2], biases[1:2]
+    middle_a, routed_a = middle_pass(full_a, out_full, tokens, 0, gain, bias)
     for e in range(2, local):
         grad_arrived.append(send(grad_packed[e]))
         if e + 1 < local:
-            full_b, grad_arrived[e], grad_packed[e + 1] = tie(
-                full_b, grad_arrived[e], grad_packed[e + 1]
+            full_b, grad_arrived[e], grad_packed[e + 1], middle_a = tie(
+                full_b, grad_arrived[e], grad_packed[e + 1], middle_a
             )
-    context = jnp.concatenate([context_a, context_b], axis=0)
-    logsum = jnp.concatenate([logsum_a, logsum_b], axis=1)
-
-    def project_out(full):
-        return jnp.einsum("ztc,zdc->td", full, out_full, preferred_element_type=jnp.float32)
-
-    middle = resid_in + jnp.concatenate([project_out(full_a), project_out(full_b)], axis=0)
-    normed_two, inverse_two = layer_stats(middle)
-    routed = (normed_two * gains[1] + biases[1]).astype(jnp.bfloat16)
-    logits = jnp.dot(routed, router_full, preferred_element_type=jnp.float32)
-    probs = jax.nn.softmax(logits, axis=-1)
-    gate = jnp.sum(probs * select, axis=-1, keepdims=True)
-
+    middle_b, routed_b = middle_pass(full_b, out_full, tokens, half, gain, bias)
+
+    routed = [routed_a, routed_b]
     packed = list(pack(slots_by_local, routed, 0, block_rows, 1))
     if local > 1:
         packed += pack(slots_by_local, routed, block_rows, block_rows, local - 1)
     packed[0], grad_arrived[-1] = tie(packed[0], grad_arrived[-1])
-    held = jnp.arange(experts * cap, dtype=jnp.int32)
-    gates = jnp.sum(jnp.where(held[:, None] == slots[None, :], gate[:, 0][None, :], 0.0), axis=1)
-    gates = gates.reshape(rows_all, local * cap)
-    arrived, summed, active, slope = [], [], [], []
-    sent = None
+
+    def route(rows):
+        return jnp.dot(rows, router_full, preferred_element_type=jnp.float32)
+
+    logits = jnp.concatenate([route(routed_a), route(routed_b)], axis=0)
+    probs = jax.nn.softmax(logits, axis=-1)
+    gate = jnp.sum(probs * select, axis=-1, keepdims=True)
+
+    arrived, summed, active, slope, sent = [], [], [], [], []
     for e in range(local):
         arrived.append(send(packed[e]))
-        after = gates if e + 1 == local else packed[e + 1]
-        after, arrived[e] = tie(after, arrived[e])
+        if e + 1 < local:
+            packed[e + 1], arrived[e] = tie(packed[e + 1], arrived[e])
         if e:
-            after, summed[e - 1] = tie(after, summed[e - 1])
+            then = packed[e + 1] if e + 1 < local else sent[0][0]
+            then, summed[e - 1], arrived[e] = tie(then, summed[e - 1], arrived[e])
             summed[e - 1] = lax.psum_scatter(
                 summed[e - 1], "col", scatter_dimension=0, tiled=True
             )
-        if e + 1 == local:
-            gates = after
-        else:
-            packed[e + 1] = after
-        made, kept, grads, sent = expert_pass(
+            if e + 1 < local:
+                packed[e + 1] = then
+            else:
+                sent[0] = (then, *sent[0][1:])
+        made, kept, grads, pair = expert_pass(
             e,
             cap,
             arrived[e],
             grad_arrived[e],
             w_in,
             w_back,
-            sent,
+            sent.pop() if e % members else None,
+            members,
             cols_all,
             pieces,
             packed[-1:] if e == 0 else summed[e - 3 : e - 2] if e > 2 else [],
@@ -538,66 +616,68 @@
         active.append(kept)
         slope.append(grads)
         summed.append(made)
+        sent.append(pair)
     summed[-1] = lax.psum_scatter(summed[-1], "col", scatter_dimension=0, tiled=True)
-    gates = swap(gates, "row")
-    gates, *sent = tie(gates, *sent)
-    gates = gates.reshape(rows_all, local, cap).transpose(1, 0, 2)
-
-    backs = []
-    grad_weights = None
-    waits = slope[-1:]
-    for e in range(max(local, pieces)):
-        if e < local:
-            *grad_weights, token = weight_pass(
-                e,
-                local,
-                arrived[e],
-                grad_arrived[e],
-                gates[e].reshape(block_rows, 1),
-                active[e],
-                slope[e],
-                grad_weights,
-                waits + (summed[e - 3 : e - 2] if e < 2 else []),
+
+    def place(i):
+        return (i % cols_all) * 2 + i // cols_all
+
+    order = [(g, f) for f in range(pieces) for g in range(len(sent))]
+    back = {}
+    grad_sent = []
+    last = None
+    for at, (g, f) in enumerate(order):
+        piece = sent[g][f]
+        if last is not None:
+            piece, last = tie(piece, last)
+            back[order[at - 1]] = last
+        if at == 1:
+            piece, slope[-1] = tie(piece, slope[-1])
+        if at == len(order) - 1:
+            homed = jnp.stack(
+                [v.reshape(rows_all, cap, depth // cols_all) for v in summed], axis=1
             )
-        if e < pieces:
-            back = swap(sent[e], "row")
-            if e + 1 < pieces:
-                sent[e + 1], back, token, *done = tie(sent[e + 1], back, token, *backs[e - 1 :])
-                backs[e - 1 :] = done
-            backs.append(unpack(slots, back.reshape(experts * cap, depth // pieces), [token]))
-            waits = backs[-1:]
-    grad_in, grad_back = grad_weights
-    grad_sent = []
-    for at in range(0, pieces, 2):
-        pair = jnp.concatenate(backs[at : at + 2], axis=1)
-        grad_sent.append(lax.psum_scatter(pair, "col", scatter_dimension=0, tiled=True))
-    grad_sent = jnp.concatenate(grad_sent, axis=1).astype(jnp.float32) * own(gate)
-
-    homed = jnp.stack([s.reshape(rows_all, cap, depth // cols_all) for s in summed], axis=1)
-    homed = swap(homed, "row")
-    returned = unpack(slots, homed.reshape(experts * cap, depth // cols_all)).astype(jnp.float32)
-
+            homed, piece = tie(homed, piece)
+            homed = swap(homed, "row")
+            homed, piece = tie(homed, piece)
+        last = swap(piece, "row")
+        back[(g, f)] = last
+        if g == len(sent) - 1:
+            rows = [back[(k, f)].reshape(-1, depth // pieces) for k in range(len(sent))]
+            whole = unpack(slots_by_group, rows, part, place)
+            if f == 0:
+                whole, *summed = tie(whole, *summed)
+            grad_sent.append(lax.psum_scatter(whole, "col", scatter_dimension=0, tiled=True))
+
+    returned = unpack(
+        [slots], [homed.reshape(experts * cap, depth // cols_all)], part, lambda i: i
+    ).astype(jnp.float32)
     columns = depth // cols_all
 
     def own_columns(values):
         return lax.dynamic_slice_in_dim(values, col * columns, columns, 1)
 
-    mixed = (own_columns(middle) + gate * returned).astype(jnp.bfloat16)
+    middle_cols = jnp.concatenate([own_columns(middle_a), own_columns(middle_b)], axis=0)
+    mixed = (middle_cols + gate * returned).astype(jnp.bfloat16)
+    grad_gate = jnp.sum(own_columns(cotangent).astype(jnp.float32) * returned, axis=-1)
+    grad_gate = swap(grad_gate.reshape(2, cols_all, part).transpose(1, 0, 2), "col")
+    grad_gate = jnp.sum(grad_gate, axis=0).reshape(2 * part, 1)
+    held = jnp.arange(experts * cap, dtype=jnp.int32)
+    gates = jnp.sum(jnp.where(held[:, None] == slots[None, :], gate[:, 0][None, :], 0.0), axis=1)
+    mixed, grad_gate, gates = tie(mixed, grad_gate, gates.reshape(rows_all, local * cap))
     steps = relay_steps(mixed, "col")
-    grad_gate = lax.psum(
-        jnp.sum(own_columns(cotangent).astype(jnp.float32) * returned, axis=-1), "col"
-    )[:, None]
-    grad_logits = (grad_gate * probs * (select - gate)).astype(jnp.bfloat16)
-    grad_router = jnp.einsum("td,te->de", routed, grad_logits, preferred_element_type=jnp.float32)
-
-    grad_y = own(cotangent).astype(jnp.float32)
-    if steps:
-        grad_sent, *first = tie(grad_sent, *steps[0])
-        steps[0] = tuple(first)
-    own_middle = own(middle)
-    normed_own, inverse_own = layer_stats(own_middle)
+
+    own_gate, own_probs, own_select = own_of(gate), own_of(probs), own_of(select)
+    grad_logits = (grad_gate * own_probs * (own_select - own_gate)).astype(jnp.bfloat16)
+    own_routed = own(routed_a, routed_b)
+    grad_router = jnp.einsum(
+        "td,te->de", own_routed, grad_logits, preferred_element_type=jnp.float32
+    )
+    grad_y = own_of(cotangent).astype(jnp.float32)
+    normed_own, inverse_own = layer_stats(own(middle_a, middle_b))
+    grad_sent = jnp.concatenate(grad_sent, axis=1).astype(jnp.float32) * own_gate
     grad_routed = grad_sent + jnp.einsum(
-        "te,de->td", own(grad_logits), router_full, preferred_element_type=jnp.float32
+        "te,de->td", grad_logits, router_full, preferred_element_type=jnp.float32
     )
     gain_two = jnp.sum(grad_routed * normed_own, axis=0)
     bias_two = jnp.sum(grad_routed, axis=0)
@@ -606,54 +686,111 @@
     grad_context = jnp.einsum(
         "td,zdc->ztc", grad_attn, out_full, preferred_element_type=jnp.float32
     ).astype(jnp.bfloat16)
-    grad_context = swap(grad_context, "col").reshape(length, width)
-
-    full = jnp.concatenate([full_a, full_b], axis=1)
-    full_own = lax.dynamic_slice_in_dim(full, col * own_length, own_length, 1)
-    grad_out = jnp.einsum("td,ztc->dzc", grad_attn, full_own, preferred_element_type=jnp.float32)
+    gates = swap(gates, "row")
+    if steps:
+        grad_context, *first = tie(grad_context, *steps[0])
+        steps[0] = tuple(first)
+    grad_context = swap(grad_context, "col").reshape(cols_all, 2, part, width)
+    grad_context = grad_context.transpose(1, 0, 2, 3).reshape(2, half, width)
+
+    context_own = jnp.concatenate(
+        [lax.dynamic_slice_in_dim(v, col * part, part, 1) for v in (full_a, full_b)], axis=1
+    )
+    grad_out = jnp.einsum("td,ztc->dzc", grad_attn, context_own, preferred_element_type=jnp.float32)
     plane = jnp.concatenate([grad_out.reshape(depth, cols_all * width), grad_router], axis=1)
     plane = swap(plane.astype(jnp.bfloat16).reshape(rows_all, share, -1), "row")
-    grad_proj = attend_backward(projected, grad_context, context, logsum, block)
-    grad_proj, plane = tie(grad_proj, plane)
+
+    proj_b, *carried = attend_backward(
+        projected, grad_context[1], context_b, logsum_b, block, count
+    )
+    tied = steps[1] if len(steps) > 1 else ()
+    proj_b, gates, *second = tie(proj_b, gates, *tied)
+    proj_a = attend_backward(
+        projected, grad_context[0], context_a, logsum_a, block, 0, carried
+    )[0]
+    tied = steps[2] if len(steps) > 2 else ()
+    proj_a, plane, *third = tie(proj_a, plane, *tied)
+    steps[1:3] = [tuple(v) for v in (second, third) if v]
+
+    def spread(grads):
+        made = jnp.einsum("tc,dc->td", grads, qkv_full, preferred_element_type=jnp.float32)
+        return lax.psum_scatter(
+            made.astype(jnp.bfloat16), "col", scatter_dimension=0, tiled=True
+        ).astype(jnp.float32)
+
+    normal_b, normal_a = spread(proj_b), spread(proj_a)
+    grad_qkv = jnp.einsum(
+        "td,tc->dc", normal_in[:half], proj_a, preferred_element_type=jnp.float32
+    ) + jnp.einsum("td,tc->dc", normal_in[half:], proj_b, preferred_element_type=jnp.float32)
+
+    gates = gates.reshape(rows_all, local, cap).transpose(1, 0, 2)
+    grad_weights = None
+    for e in range(local):
+        *grad_weights, token = weight_pass(
+            e,
+            local,
+            arrived[e],
+            grad_arrived[e],
+            gates[e].reshape(block_rows, 1),
+            active[e],
+            slope[e],
+            grad_weights,
+            [token if e else proj_a],
+        )
+        if e == max(local // 2 - 1, 0):
+            normal_b, token = tie(normal_b, token)
+    grad_in, grad_back = grad_weights
+
     plane = jnp.sum(plane.astype(jnp.float32), axis=0)
-    router_share = plane[:, cols_all * width :]
+    router_share = plane[:, cols_all * width :].reshape(1, share, experts)
     out_share = plane[:, : cols_all * width].reshape(share, cols_all, width).transpose(1, 0, 2)
-    out_share = swap(out_share.astype(jnp.bfloat16), "col").astype(jnp.float32)
-    out_share = jnp.sum(out_share, axis=0).T
-    if len(steps) > 1:
-        grad_proj, *second = tie(grad_proj, *steps[1])
-        steps[1] = tuple(second)
-    grad_qkv = jnp.einsum("td,tc->dc", normal_in, grad_proj, preferred_element_type=jnp.float32)
-    partial = jnp.einsum(
-        "tc,dc->td", grad_proj, qkv_full, preferred_element_type=jnp.float32
-    ).astype(jnp.bfloat16)
-    grad_normal = lax.psum_scatter(partial, "col", scatter_dimension=0, tiled=True)
+    router_share = jnp.broadcast_to(router_share, (cols_all, share, experts))
+    plane = jnp.concatenate([out_share, router_share], axis=2).astype(jnp.bfloat16)
+    plane = jnp.sum(swap(plane, "col").astype(jnp.float32), axis=0)
+    out_share, router_share = plane[:, :width].T, plane[:, width:]
+
+    tokens_own = [lax.dynamic_slice_in_dim(v, col * part, part, 0) for v in (tokens[:half], tokens[half:])]
+    normed = [layer_stats(v.astype(jnp.float32)) for v in tokens_own]
+    finished = [None, None]
+    sums = [jnp.stack([gain_two, bias_two])]
+    for c in (1, 0):
+        grads = (normal_a, normal_b)[c]
+        own_normed, own_inverse = normed[c]
+        made = grad_middle[c * part : (c + 1) * part] + norm_back(
+            grads, own_normed, own_inverse, gains[0]
+        )
+        finished[c] = made.astype(jnp.bfloat16)
+        sums.append(
+            jnp.stack([jnp.sum(grads * own_normed, axis=0), jnp.sum(grads, axis=0)])
+        )
+        if c:
+            moves = relay_steps(finished[1], "col")
+            flat = [v for move in moves for v in move]
+            normal_a, out_share, router_share, *flat = tie(
+                normal_a, out_share, router_share, *flat
+            )
+            moves = list(zip(flat[0::2], flat[1::2]))
+    grad_tokens = jnp.concatenate(
+        [relay_join(finished[1], moves, "col", 0), lax.all_gather(finished[0], "col", axis=0, tiled=True)][::-1],
+        axis=0,
+    )
     mixed_out = relay_join(mixed, steps, "col", 1)
-    grad_normal, mixed_out, router_share, out_share = tie(
-        grad_normal, mixed_out, router_share, out_share
-    )
-    grad_normal = grad_normal.astype(jnp.float32)
-    own_normed, own_inverse = layer_stats(own(tokens).astype(jnp.float32))
-    gain_one = jnp.sum(grad_normal * own_normed, axis=0)
-    bias_one = jnp.sum(grad_normal, axis=0)
-    grad_tokens = (grad_middle + norm_back(grad_normal, own_normed, own_inverse, gains[0])).astype(
-        jnp.bfloat16
-    )
-    grad_tokens = lax.all_gather(grad_tokens, "col", axis=0, tiled=True)
-
+
+    small = jnp.concatenate([sums[1] + sums[2], sums[0]], axis=0)
+    small = swap(small.reshape(4, rows_all, share).transpose(1, 0, 2), "row")
+    small = jnp.sum(small, axis=0)
+    small = jnp.sum(swap(jnp.broadcast_to(small[None], (cols_all, 4, share)), "col"), axis=0)
     qkv_share = swap(grad_qkv.astype(jnp.bfloat16).reshape(rows_all, share, -1), "row")
     qkv_share = jnp.sum(qkv_share.astype(jnp.float32), axis=0)
     qkv_share = qkv_share.reshape(share, 3, width).transpose(1, 0, 2)
-    small = lax.psum(jnp.stack([gain_one, gain_two, bias_one, bias_two]), ("row", "col"))
-    small = lax.dynamic_slice_in_dim(small, lax.axis_index("row") * share, share, 1)
     return (
         mixed_out,
         grad_tokens,
         qkv_share,
         out_share,
         router_share,
-        small[0:2],
-        small[2],
+        jnp.stack([small[0], small[2]]),
+        small[1],
         small[3],
         grad_in,
         grad_back,

time: 908 us -> 898 us (0.989)
  blocking collectives: 94 us -> 0 us
  starting transfers between devices: 93.7 us -> 134 us
  waiting for transfers between devices: 248 us -> 283 us
  local copies, waits for them, and re-layouts: 40.8 us -> 59 us
  matrix products: 51.6 us -> 37.6 us
  Pallas kernels: 283 us -> 293 us
    psum x2 -> x0, blocking collectives: 72.4 us -> none  [the longest x1 47.5 us: per_device(): lax.psum(jnp.stack([gain_one, gain_two, bias_one, bias_two]), ('row', 'co...]
    all_to_all x18 -> x23, waiting for transfers between devices: 170 us -> 205 us  [swap(): return lax.all_to_all(blocks, axis, split_axis=0, concat_axis=0, tiled=True)]
    reduce_scatter x1, waiting for transfers between devices: 0.02 us -> 29.8 us  [per_device(): lax.psum_scatter(summed[-1], 'col', scatter_dimension=0, tiled=True)]
    ppermute x3 -> x6, waiting for transfers between devices: 55.6 us -> 32 us  [relay_steps(): left = lax.ppermute(left, axis, [(i + 1, i) for i in range(count - 1)])]
    all_to_all x2 -> x0, blocking collectives: 21.6 us -> none  [swap(): return lax.all_to_all(blocks, axis, split_axis=0, concat_axis=0, tiled=True)]
    all_to_all x18 -> x23, starting transfers between devices: 73.9 us -> 93 us  [swap(): return lax.all_to_all(blocks, axis, split_axis=0, concat_axis=0, tiled=True)]
    ppermute x3 -> x6, starting transfers between devices: 15 us -> 32.4 us  [relay_steps(): right = lax.ppermute(right, axis, [(i, i + 1) for i in range(count - 1)])]
    dot_general x8 -> x9, matrix products: 38.5 us -> 28.2 us  [the longest x2 9.56 us: spread(): jnp.einsum('tc,dc->td', grads, qkv_full, preferred_element_type=jnp.float32)]
  transfers between devices with their start and end apart: 35 -> 47, of which waited for: 21 -> 24; matrix products, arithmetic and copies ran while one was open for 13% -> 15% of each run, Pallas kernels for 32% -> 33%
where the time goes in v3:
time: 898 us; the launch traced here: 887 us
  Pallas kernels  293 us (33%)
  waiting for transfers between devices  283 us (32%)
  starting transfers between devices  134 us (15%)
  other arithmetic  64.4 us (7%)
  local copies, waits for them, and re-layouts  59 us (7%)
  matrix products  37.6 us (4%)
  between operations  15.5 us (2%)
    all_to_all x23, waiting for transfers between devices, swap(): return lax.all_to_all(blocks, axis, split_axis=0, concat_axis=0, tiled=True)  205 us
    all_to_all x23, starting transfers between devices, swap(): return lax.all_to_all(blocks, axis, split_axis=0, concat_axis=0, tiled=True)  93 us
    pallas_call x4, Pallas kernels, expert_pass(): pl.pallas_call(functools.partial(expert_body, len(sent) + len(waits)), ou...  58 us
    pallas_call x3, Pallas kernels, pack(): pl.pallas_call(functools.partial(pack_body, base, step, each, len(rows)),...  51 us
    pallas_call x2, Pallas kernels, attend_backward(): pl.pallas_call(functools.partial(backward_body, block, first, len(carried...  47.5 us
    pallas_call x4, Pallas kernels, weight_pass(): pl.pallas_call(functools.partial(weight_body, len(sent) + len(waits)), ou...  43.8 us
    pallas_call x2, Pallas kernels, attend_forward(): pl.pallas_call(functools.partial(forward_body, blocks, block), out_shape=...  41.3 us
    pallas_call x3, Pallas kernels, unpack(): pl.pallas_call(functools.partial(unpack_body, len(rows)), out_shape=jax.S...  36.3 us
  transfers between devices with their start and end apart: 47, of which 24 were waited for; matrix products, arithmetic and copies ran while one was open for 15% of the time, Pallas kernels for 33%

profile of v3, /device:TPU:0, one launch (start us, length us, event | category | flops | bytes accessed | tf_op | source)
XLA Modules:
  0.0 886.8 jit_solution(15548138369037838943)
XLA Ops:
  21.5 24.2 %pack.3 = (bf16[1024,1024]{1,0:T(8,128)(2,1)}, bf16[1024,1024]{1,0:T(8,128)(2,1)}, bf16[1024,1024]{1,0:T(8,128)(2,1)}, bf16[1024,1024]{1,0:T(8,128)(2,1)}) custom-call(s32[1,2048]{1,0:T(1,128)} %multiply_add_fusion.3.slots_ref, bf16[2048,1024]{1,0:T(8,128)(2,1)} %rest_0_.1), custom_call_target="tpu_custom_call" | custom-call | flops 17179869184 | bytes 12582912 | tf_op jit(solution)/shard_map/pack/pallas_call | solution.py:55
  64.0 15.3 %attend_forward.2 = (bf16[1024,256]{1,0:T(8,128)(2,1)}, f32[4,1024]{1,0:T(4,128)}) custom-call(bf16[2048,768]{1,0:T(8,128)(2,1)} %convolution_convert_fusion.q_ref.k_ref.v_ref.refs_0_.refs_4_.refs_5_, bf16[2048,768]{1,0:T(8,128)(2,1)} %convolution_convert_fusion.q_ref.k_ref.v_ref.refs_0_.refs_4_.refs_5_, ...), custom_call_target="tpu_custom_call" | custom-call | flops 4294967296 | bytes 4194304 | tf_op jit(solution)/shard_map/attend_forward/pallas_call | solution.py:190
  85.3 26.0 %attend_forward.3 = (bf16[1024,256]{1,0:T(8,128)(2,1)}, f32[4,1024]{1,0:T(4,128)}) custom-call(bf16[2048,768]{1,0:T(8,128)(2,1)} %convolution_convert_fusion.q_ref.k_ref.v_ref.refs_0_.refs_4_.refs_5_, bf16[2048,768]{1,0:T(8,128)(2,1)} %convolution_convert_fusion.q_ref.k_ref.v_ref.refs_0_.refs_4_.refs_5_, ...), custom_call_target="tpu_custom_call" | custom-call | flops 4294967296 | bytes 4194304 | tf_op jit(solution)/shard_map/attend_forward/pallas_call | solution.py:190
  119.0 25.9 %all-to-all-done.3 = bf16[8,4,128,256]{3,2,1,0:T(8,128)(2,1)} async-done(((bf16[8,4,128,256]{3,2,1,0:T(8,128)(2,1)}), bf16[8,4,128,256]{3,2,1,0:T(8,128)(2,1)}, u32[]{:S(2)}, u32[]{:S(2)}) %all-to-all-start.3) | async-done | bytes 2097184 | tf_op jit(solution)/shard_map/all_to_all | solution.py:435
  159.2 14.3 %all-gather.11.cloned.1.call-done = bf16[4096,256]{1,0:T(8,128)(2,1)} async-done(((bf16[1024,256]{1,0:T(8,128)(2,1)}), bf16[4096,256]{1,0:T(8,128)(2,1)}) %all-gather.11.cloned.1.call-update) | async-done | bytes 2097168 | tf_op jit(solution)/shard_map/all_gather | solution.py:561
  211.1 18.8 %pack.4 = (bf16[1024,1024]{1,0:T(8,128)(2,1)}, bf16[1024,1024]{1,0:T(8,128)(2,1)}, bf16[1024,1024]{1,0:T(8,128)(2,1)}) custom-call(s32[1,2048]{1,0:T(1,128)} %multiply_add_fusion.3.slots_ref, bf16[1024,1024]{1,0:T(8,128)(2,1)} %get-tuple-element.153.rest_0_, bf16[1024,1024]{1,0:T(8,128)(2,1)} %get-tuple-element.154.rest_1_), custom_call_target="tpu_custom_call" | custom-call | flops 12884901888 | bytes 10485760 | tf_op jit(solution)/shard_map/pack/pallas_call | solution.py:55
  242.8 14.4 %expert_pass.4 = (bf16[4,1024,256]{2,1,0:T(8,128)(2,1)}, bf16[1024,1024]{1,0:T(8,128)(2,1)}, bf16[1024,1024]{1,0:T(8,128)(2,1)}, bf16[8,2,128,512]{3,2,1,0:T(8,128)(2,1)}, bf16[8,2,128,512]{3,2,1,0:T(8,128)(2,1)}) custom-call(bf16[1024,1024]{1,0:T(8,128)(2,1)} %bitcast.158, bf16[1024,1024]{1,0:T(8,128)(2,1)} %bitcast.156, bf16[4,1024,1024]{2,1,0:T(8,128)(2,1)} %win_ref.7, ...), custom_call_target="tpu_custom_call" | custom-call | flops 8589934592 | bytes 16777216 | tf_op jit(solution)/shard_map/expert_pass/pallas_call | solution.py:352
  257.2 11.9 %all-to-all-done.7 = bf16[8,128,1024]{2,1,0:T(8,128)(2,1)S(1)} async-done(((bf16[8,128,1024]{2,1,0:T(8,128)(2,1)}), bf16[8,128,1024]{2,1,0:T(8,128)(2,1)S(1)}, u32[]{:S(2)}, u32[]{:S(2)}) %all-to-all-start.7) | async-done | bytes 2097184 | tf_op jit(solution)/shard_map/all_to_all | solution.py:435
  274.2 14.7 %expert_pass.5 = (bf16[4,1024,256]{2,1,0:T(8,128)(2,1)}, bf16[1024,1024]{1,0:T(8,128)(2,1)}, bf16[1024,1024]{1,0:T(8,128)(2,1)}, bf16[8,2,128,512]{3,2,1,0:T(8,128)(2,1)}, bf16[8,2,128,512]{3,2,1,0:T(8,128)(2,1)}) custom-call(bf16[1024,1024]{1,0:T(8,128)(2,1)} %bitcast.147, ...), custom_call_target="tpu_custom_call", output_to_operand_aliasing={{3}: (4, {}), {4}: (5, {})} | custom-call | flops 8589934592 | bytes 16777216 | tf_op jit(solution)/shard_map/expert_pass/pallas_call | solution.py:352
  288.9 11.8 %all-to-all-done.8 = bf16[8,128,1024]{2,1,0:T(8,128)(2,1)S(1)} async-done(((bf16[8,128,1024]{2,1,0:T(8,128)(2,1)}), bf16[8,128,1024]{2,1,0:T(8,128)(2,1)S(1)}, u32[]{:S(2)}, u32[]{:S(2)}) %all-to-all-start.8) | async-done | bytes 2097184 | tf_op jit(solution)/shard_map/all_to_all | solution.py:435
  306.5 14.4 %expert_pass.6 = (bf16[4,1024,256]{2,1,0:T(8,128)(2,1)}, bf16[1024,1024]{1,0:T(8,128)(2,1)}, bf16[1024,1024]{1,0:T(8,128)(2,1)}, bf16[8,2,128,512]{3,2,1,0:T(8,128)(2,1)}, bf16[8,2,128,512]{3,2,1,0:T(8,128)(2,1)}) custom-call(bf16[1024,1024]{1,0:T(8,128)(2,1)} %bitcast.143, bf16[1024,1024]{1,0:T(8,128)(2,1)} %bitcast.141, bf16[4,1024,1024]{2,1,0:T(8,128)(2,1)} %win_ref.7, ...), custom_call_target="tpu_custom_call" | custom-call | flops 8589934592 | bytes 16777216 | tf_op jit(solution)/shard_map/expert_pass/pallas_call | solution.py:352
  320.9 12.2 %all-to-all-done.9 = bf16[8,128,1024]{2,1,0:T(8,128)(2,1)} async-done(((bf16[8,128,1024]{2,1,0:T(8,128)(2,1)}), bf16[8,128,1024]{2,1,0:T(8,128)(2,1)}, u32[]{:S(2)}, u32[]{:S(2)}) %all-to-all-start.9) | async-done | bytes 2097184 | tf_op jit(solution)/shard_map/all_to_all | solution.py:435
  336.8 14.4 %expert_pass.7 = (bf16[4,1024,256]{2,1,0:T(8,128)(2,1)}, bf16[1024,1024]{1,0:T(8,128)(2,1)}, bf16[1024,1024]{1,0:T(8,128)(2,1)}, bf16[8,2,128,512]{3,2,1,0:T(8,128)(2,1)}, bf16[8,2,128,512]{3,2,1,0:T(8,128)(2,1)}) custom-call(bf16[1024,1024]{1,0:T(8,128)(2,1)} %bitcast.31.x_ref, ...), custom_call_target="tpu_custom_call", output_to_operand_aliasing={{3}: (4, {}), {4}: (5, {})} | custom-call | flops 8589934592 | bytes 16777216 | tf_op jit(solution)/shard_map/expert_pass/pallas_call | solution.py:352
  351.3 12.0 %all-to-all-done.10 = bf16[8,2,128,512]{3,2,1,0:T(8,128)(2,1)S(1)} async-done(((bf16[8,2,128,512]{3,2,1,0:T(8,128)(2,1)}), bf16[8,2,128,512]{3,2,1,0:T(8,128)(2,1)S(1)}, u32[]{:S(2)}, u32[]{:S(2)}) %all-to-all-start.10) | async-done | bytes 2097184 | tf_op jit(solution)/shard_map/all_to_all | solution.py:435
  370.7 25.0 %all-to-all-done.11 = bf16[8,2,128,512]{3,2,1,0:T(8,128)(2,1)} async-done(((bf16[8,2,128,512]{3,2,1,0:T(8,128)(2,1)}), bf16[8,2,128,512]{3,2,1,0:T(8,128)(2,1)}, u32[]{:S(2)}, u32[]{:S(2)}) %all-to-all-start.11) | async-done | bytes 2097184 | tf_op jit(solution)/shard_map/all_to_all | solution.py:435
  405.5 13.7 %unpack.3 = bf16[2048,512]{1,0:T(8,128)(2,1)} custom-call(s32[2048,1]{1,0:T(8,128)} %compare_select_fusion.1.refs_0_, s32[2048,1]{1,0:T(8,128)} %get-tuple-element.322.refs_1_, bf16[2048,512]{1,0:T(8,128)(2,1)} %bitcast.164, bf16[2048,512]{1,0:T(8,128)(2,1)} %bitcast.33.refs_3_), custom_call_target="tpu_custom_call" | custom-call | flops 8589934592 | bytes 6291456 | tf_op jit(solution)/shard_map/unpack/pallas_call | solution.py:89
  419.2 29.8 %reduce-scatter.15.cloned.1.call-done = bf16[1,1024,256]{2,1,0:T(8,128)(2,1)} async-done(((bf16[4,1024,256]{2,1,0:T(8,128)(2,1)}), bf16[1,1024,256]{2,1,0:T(8,128)(2,1)}) %reduce-scatter.15.cloned.1.call-update) | async-done | bytes 524304 | tf_op jit(solution)/shard_map/reduce_scatter | solution.py:620
  456.7 25.9 %all-to-all-done.13 = bf16[8,4,128,256]{3,2,1,0:T(8,128)(2,1)S(1)} async-done(((bf16[8,4,128,256]{3,2,1,0:T(8,128)(2,1)}), bf16[8,4,128,256]{3,2,1,0:T(8,128)(2,1)S(1)}, u32[]{:S(2)}, u32[]{:S(2)}) %all-to-all-start.13) | async-done | bytes 2097184 | tf_op jit(solution)/shard_map/all_to_all | solution.py:435
  496.7 18.2 %all-to-all-done.15 = bf16[8,2,128,512]{3,2,1,0:T(8,128)(2,1)} async-done(((bf16[8,2,128,512]{3,2,1,0:T(8,128)(2,1)}), bf16[8,2,128,512]{3,2,1,0:T(8,128)(2,1)}, u32[]{:S(2)}, u32[]{:S(2)}) %all-to-all-start.15) | async-done | bytes 2097184 | tf_op jit(solution)/shard_map/all_to_all | solution.py:435
  514.9 13.6 %unpack.5 = bf16[2048,512]{1,0:T(8,128)(2,1)} custom-call(s32[2048,1]{1,0:T(8,128)} %compare_select_fusion.1.refs_0_, s32[2048,1]{1,0:T(8,128)} %get-tuple-element.322.refs_1_, bf16[2048,512]{1,0:T(8,128)(2,1)} %bitcast.44.refs_2_, bf16[2048,512]{1,0:T(8,128)(2,1)} %bitcast.45.refs_3_), custom_call_target="tpu_custom_call" | custom-call | flops 8589934592 | bytes 6291456 | tf_op jit(solution)/shard_map/unpack/pallas_call | solution.py:89
  601.7 18.5 %all-to-all-done.16 = bf16[4,512,256]{1,2,0:T(8,128)(2,1)S(1)} async-done(((bf16[4,512,256]{1,2,0:T(8,128)(2,1)}), bf16[4,512,256]{1,2,0:T(8,128)(2,1)S(1)}, u32[]{:S(2)}, u32[]{:S(2)}) %all-to-all-start.16) | async-done | bytes 1048608 | tf_op jit(solution)/shard_map/all_to_all | solution.py:435
  622.3 29.4 %attend_backward.2 = (bf16[1024,768]{1,0:T(8,128)(2,1)}, f32[1024,256]{1,0:T(8,128)}, f32[1024,256]{1,0:T(8,128)}) custom-call(bf16[2048,768]{1,0:T(8,128)(2,1)} %convolution_convert_fusion.q_ref.k_ref.v_ref.refs_0_.refs_4_.refs_5_, bf16[1024,256]{1,0:T(8,128)(2,1)} %bitcast.175, bf16[1024,256]{1,0:T(8,128)(2,1)} %get-tuple-element.142.refs_2_, ...), custom_call_target="tpu_custom_call" | custom-call | flops 10737418240 | bytes 8388608 | tf_op jit(solution)/shard_map/attend_backward/pallas_call | solution.py:282
  691.4 18.2 %attend_backward.3.rest_0_ = bf16[1024,768]{1,0:T(8,128)(2,1)} custom-call(bf16[2048,768]{1,0:T(8,128)(2,1)} %convolution_convert_fusion.q_ref.k_ref.v_ref.refs_0_.refs_4_.refs_5_, bf16[1024,256]{1,0:T(8,128)(2,1)} %bitcast.174, bf16[1024,256]{1,0:T(8,128)(2,1)} %get-tuple-element.138.rest_0_.refs_2_, f32[4,1024]{1,0:T(4,128)} %get-tuple-element.211.refs_3_, ...), custom_call_target="tpu_custom_call" | custom-call | flops 5368709120 | bytes 4194304 | tf_op jit(solution)/shard_map/attend_backward/pallas_call | solution.py:282
  709.6 11.9 %collective-permute-done.5 = bf16[2048,256]{1,0:T(8,128)(2,1)} collective-permute-done((bf16[2048,256]{1,0:T(8,128)(2,1)}, bf16[2048,256]{1,0:T(8,128)(2,1)}, u32[]{:S(2)}, u32[]{:S(2)}) %collective-permute-start.5) | collective-permute-done | bytes 1048608 | tf_op jit(solution)/shard_map/ppermute | solution.py:448
  (302 shorter events, 436.8 us)
Async XLA Ops:
  8.8 39.8 %all-to-all-start = ((bf16[4,128,256]{2,1,0:T(8,128)(2,1)}), bf16[4,128,256]{2,1,0:T(8,128)(2,1)S(1)}, u32[]{:S(2)}, u32[]{:S(2)}) async-start(bf16[4,128,256]{2,1,0:T(8,128)(2,1)} %broadcast_in_dim.33), calls=%async_computation | async-start | bytes 524288 | tf_op jit(solution)/shard_map/all_to_all | solution.py:435
  15.2 33.5 %all-gather.7.cloned.1.call-start = ((), (), s32[]{:S(2)}) async-start(), calls=%async_computation.31 | async-start | bytes 1861632 | tf_op jit(solution)/shard_map/all_gather | solution.py:521
  52.4 99.3 %all-gather.13.cloned.1.call-start = ((), (), s32[]{:S(2)}) async-start(), calls=%async_computation.42 | async-start | bytes 2621440 | tf_op jit(solution)/shard_map/all_gather | solution.py:555
  80.7 31.3 %all-to-all-start.2 = ((bf16[8,128,1024]{2,1,0:T(8,128)(2,1)}), bf16[8,128,1024]{2,1,0:T(8,128)(2,1)S(1)}, u32[]{:S(2)}, u32[]{:S(2)}) async-start(bf16[8,128,1024]{2,1,0:T(8,128)(2,1)} %bitcast.165), calls=%async_computation.2 | async-start | bytes 4194304 | tf_op jit(solution)/shard_map/all_to_all | solution.py:435
  118.2 55.3 %all-gather.11.cloned.1.call-start = ((), (), s32[]{:S(2)}) async-start(), calls=%async_computation.41 | async-start | bytes 2621440 | tf_op jit(solution)/shard_map/all_gather | solution.py:561
  242.6 94.2 %reduce-scatter.9.cloned.1.call-start = ((), (), s32[]{:S(2)}) async-start(), calls=%async_computation.32 | async-start | bytes 2621440 | tf_op jit(solution)/shard_map/reduce_scatter | solution.py:596
  274.1 145.1 %reduce-scatter.11.cloned.1.call-start = ((), (), s32[]{:S(2)}) async-start(), calls=%async_computation.33 | async-start | bytes 2621440 | tf_op jit(solution)/shard_map/reduce_scatter | solution.py:596
  302.1 31.0 %all-to-all-start.9 = ((bf16[8,128,1024]{2,1,0:T(8,128)(2,1)}), bf16[8,128,1024]{2,1,0:T(8,128)(2,1)}, u32[]{:S(2)}, u32[]{:S(2)}) async-start(bf16[8,128,1024]{2,1,0:T(8,128)(2,1)} %bitcast.163), calls=%async_computation.9 | async-start | bytes 4194304 | tf_op jit(solution)/shard_map/all_to_all | solution.py:435
  306.4 112.8 %reduce-scatter.13.cloned.1.call-start = ((), (), s32[]{:S(2)}) async-start(), calls=%async_computation.34 | async-start | bytes 2621440 | tf_op jit(solution)/shard_map/reduce_scatter | solution.py:596
  336.8 112.3 %reduce-scatter.15.cloned.1.call-start = ((), (), s32[]{:S(2)}) async-start(), calls=%async_computation.35 | async-start | bytes 2621440 | tf_op jit(solution)/shard_map/reduce_scatter | solution.py:620
  364.7 31.0 %all-to-all-start.11 = ((bf16[8,2,128,512]{3,2,1,0:T(8,128)(2,1)}), bf16[8,2,128,512]{3,2,1,0:T(8,128)(2,1)}, u32[]{:S(2)}, u32[]{:S(2)}) async-start(bf16[8,2,128,512]{3,2,1,0:T(8,128)(2,1)} %get-tuple-element.189), calls=%async_computation.12 | async-start | bytes 4194304 | tf_op jit(solution)/shard_map/all_to_all | solution.py:435
  395.7 56.2 %all-to-all-start.12 = ((bf16[8,2,128,512]{3,2,1,0:T(8,128)(2,1)}), bf16[8,2,128,512]{3,2,1,0:T(8,128)(2,1)}, u32[]{:S(2)}, u32[]{:S(2)}) async-start(bf16[8,2,128,512]{3,2,1,0:T(8,128)(2,1)} %get-tuple-element.199), calls=%async_computation.16 | async-start | bytes 4194304 | tf_op jit(solution)/shard_map/all_to_all | solution.py:435
  455.9 118.9 %reduce-scatter.17.cloned.1.call-start = ((), (), s32[]{:S(2)}) async-start(), calls=%async_computation.36 | async-start | bytes 2621440 | tf_op jit(solution)/shard_map/reduce_scatter | solution.py:650
  483.9 31.0 %all-to-all-start.15 = ((bf16[8,2,128,512]{3,2,1,0:T(8,128)(2,1)}), bf16[8,2,128,512]{3,2,1,0:T(8,128)(2,1)}, u32[]{:S(2)}, u32[]{:S(2)}) async-start(bf16[8,2,128,512]{3,2,1,0:T(8,128)(2,1)} %get-tuple-element.207), calls=%async_computation.20 | async-start | bytes 4194304 | tf_op jit(solution)/shard_map/all_to_all | solution.py:435
  488.3 86.6 %reduce-scatter.19.cloned.1.call-start = ((), (), s32[]{:S(2)}) async-start(), calls=%async_computation.37 | async-start | bytes 2621440 | tf_op jit(solution)/shard_map/reduce_scatter | solution.py:650
  594.7 155.7 %reduce-scatter.23.cloned.1.call-start = ((), (), s32[]{:S(2)}) async-start(), calls=%async_computation.39 | async-start | bytes 2621440 | tf_op jit(solution)/shard_map/reduce_scatter | solution.py:717
  594.7 56.9 %collective-permute-start.4 = (bf16[2048,256]{1,0:T(8,128)(2,1)}, bf16[2048,256]{1,0:T(8,128)(2,1)}, u32[]{:S(2)}, u32[]{:S(2)}) collective-permute-start(bf16[2048,256]{1,0:T(8,128)(2,1)} %collective-permute-done.1), channel_id=1, source_target_pairs={{1,0},{2,1},{3,2},{5,4},{6,5},{7,6},{9,8},{10,9},{11,10},{13,12},{... | collective-permute-start | bytes 3145736 | tf_op jit(solution)/shard_map/ppermute | solution.py:448
  596.0 55.7 %collective-permute-start.2 = (bf16[2048,256]{1,0:T(8,128)(2,1)}, bf16[2048,256]{1,0:T(8,128)(2,1)}, u32[]{:S(2)}, u32[]{:S(2)}) collective-permute-start(bf16[2048,256]{1,0:T(8,128)(2,1)} %collective-permute-done), channel_id=1, source_target_pairs={{0,1},{1,2},{2,3},{4,5},{5,6},{6,7},{8,9},{9,10},{10,11},{12,13},{... | collective-permute-start | bytes 3145736 | tf_op jit(solution)/shard_map/ppermute | solution.py:447
  673.7 47.8 %all-to-all-start.17 = ((bf16[8,128,1056]{1,2,0:T(8,128)(2,1)}), bf16[8,128,1056]{1,2,0:T(8,128)(2,1)S(1)}, u32[]{:S(2)}, u32[]{:S(2)}) async-start(bf16[8,128,1056]{1,2,0:T(8,128)(2,1)} %copy.190), calls=%async_computation.23 | async-start | bytes 4325376 | tf_op jit(solution)/shard_map/all_to_all | solution.py:435
  678.2 133.9 %reduce-scatter.21.cloned.1.call-start = ((), (), s32[]{:S(2)}) async-start(), calls=%async_computation.38 | async-start | bytes 2621440 | tf_op jit(solution)/shard_map/reduce_scatter | solution.py:717
  679.7 41.8 %collective-permute-start.5 = (bf16[2048,256]{1,0:T(8,128)(2,1)}, bf16[2048,256]{1,0:T(8,128)(2,1)}, u32[]{:S(2)}, u32[]{:S(2)}) collective-permute-start(bf16[2048,256]{1,0:T(8,128)(2,1)} %collective-permute-done.4), channel_id=1, source_target_pairs={{1,0},{2,1},{3,2},{5,4},{6,5},{7,6},{9,8},{10,9},{11,10},{13,12},{... | collective-permute-start | bytes 3145736 | tf_op jit(solution)/shard_map/ppermute | solution.py:448
  681.0 40.5 %collective-permute-start.3 = (bf16[2048,256]{1,0:T(8,128)(2,1)}, bf16[2048,256]{1,0:T(8,128)(2,1)}, u32[]{:S(2)}, u32[]{:S(2)}) collective-permute-start(bf16[2048,256]{1,0:T(8,128)(2,1)} %collective-permute-done.2), channel_id=1, source_target_pairs={{0,1},{1,2},{2,3},{4,5},{5,6},{6,7},{8,9},{9,10},{10,11},{12,13},{... | collective-permute-start | bytes 3145736 | tf_op jit(solution)/shard_map/ppermute | solution.py:447
  769.0 37.4 %all-to-all-start.19 = ((bf16[4,128,288]{1,2,0:T(8,128)(2,1)}), bf16[4,128,288]{1,2,0:T(8,128)(2,1)S(1)}, u32[]{:S(2)}, u32[]{:S(2)}) async-start(bf16[4,128,288]{1,2,0:T(8,128)(2,1)} %pad_maximum_fusion.4), calls=%async_computation.26 | async-start | bytes 589824 | tf_op jit(solution)/shard_map/all_to_all | solution.py:435
  810.8 65.0 %all-gather.9.cloned.1.call-start = ((), (), s32[]{:S(2)}) async-start(), calls=%async_computation.40 | async-start | bytes 2621440 | tf_op jit(solution)/shard_map/all_gather | solution.py:774
  (56 other events, 756.0 us)
Sparse Core Ops, SparseCore 0:
  18.4 27.7 all-gather.6
  79.4 47.8 all-gather.12
  128.9 44.5 all-gather.10
  269.3 43.5 reduce-scatter.8
  315.1 42.8 reduce-scatter.10
  360.1 43.5 reduce-scatter.12
  406.1 42.8 reduce-scatter.14
  459.1 43.7 reduce-scatter.16
  528.7 43.9 reduce-scatter.18
  656.4 59.2 reduce-scatter.22
  726.6 50.1 reduce-scatter.20
  816.4 47.1 all-gather.8

commit v4 on v3

--- a/solution.py
+++ b/solution.py
@@ -65,7 +65,7 @@
         ),
         compiler_params=params("arbitrary"),
         name="pack",
-        cost_estimate=cost(2 * outs * count * length * width, 2 * (length + outs * count) * width),
+        cost_estimate=cost(count * width, count * width),
     )(slots.reshape(1, length), *rows, *waits)
 
 
@@ -178,7 +178,7 @@
             lse_ref[pl.ds(h, 1), here] = logsum.T[0:1, :]
             return carry
 
-        lax.fori_loop(0, heads, one_head, 0)
+        lax.fori_loop(0, heads, one_head, 0, unroll=heads)
 
 
 def attend_forward(projected, blocks, block, waits=()):
@@ -201,7 +201,7 @@
         ),
         compiler_params=params("arbitrary"),
         name="attend_forward",
-        cost_estimate=cost(8 * rows * length * width, 8 * length * width, rows * length * heads),
+        cost_estimate=cost(rows * width, rows * width),
     )(projected, projected, projected, *waits)
 
 
@@ -252,7 +252,7 @@
             )
             return carry
 
-        lax.fori_loop(0, heads, one_head, 0)
+        lax.fori_loop(0, heads, one_head, 0, unroll=heads)
         new_v = dot(p_ref[pl.ds(0, span), :], dom_ref[...], NN)
         new_k = dot(ds_ref[pl.ds(0, span), :], qm_ref[...], NN)
         if at == count - 1:
@@ -379,14 +379,17 @@
     return made[0], made[1], made[2], made[3:]
 
 
-def weight_body(given, x_ref, gy_ref, gate_ref, active_ref, slope_ref, *rest):
+def weight_body(given, x_ref, gy_ref, router_ref, pick_ref, active_ref, slope_ref, *rest):
     gin_ref, gback_ref, token_ref, xt_ref, gyg_ref = rest[given:]
     token_ref[...] = jnp.zeros_like(token_ref)
     rows, depth = x_ref.shape
 
     @pl.when(pl.program_id(0) == 0)
     def _():
-        gate = gate_ref[...]
+        logits = dot(x_ref[...], router_ref[...], NN)
+        raised = jnp.exp(logits - jnp.max(logits, axis=1, keepdims=True))
+        gate = jnp.sum(raised * pick_ref[...], axis=1, keepdims=True)
+        gate = gate / jnp.sum(raised, axis=1, keepdims=True)
         xt_ref[...] = (x_ref[...].astype(jnp.float32) * gate).T.astype(jnp.bfloat16)
         gyg_ref[...] = (gy_ref[...].astype(jnp.float32) * gate).astype(jnp.bfloat16)
 
@@ -394,7 +397,7 @@
     gback_ref[...] = dot(active_ref[...], gyg_ref[...], TN)
 
 
-def weight_pass(e, local, x, grad_y, gate, active, slope, sent, waits=()):
+def weight_pass(e, local, x, grad_y, router, pick, active, slope, sent, waits=()):
     rows, width = active.shape
     depth = x.shape[1]
     step = min(256, width)
@@ -410,7 +413,8 @@
         in_specs=[
             pl.BlockSpec((rows, depth), lambda i: (0, 0)),
             pl.BlockSpec((rows, depth), lambda i: (0, 0)),
-            pl.BlockSpec((rows, 1), lambda i: (0, 0)),
+            pl.BlockSpec(router.shape, lambda i: (0, 0)),
+            pl.BlockSpec(pick.shape, lambda i: (0, 0)),
             pl.BlockSpec((rows, step), lambda i: (0, i)),
             pl.BlockSpec((rows, step), lambda i: (0, i)),
         ]
@@ -424,11 +428,11 @@
             pltpu.VMEM((depth, rows), jnp.bfloat16),
             pltpu.VMEM((rows, depth), jnp.bfloat16),
         ],
-        input_output_aliases={5 + j: j for j in range(len(sent))},
+        input_output_aliases={6 + j: j for j in range(len(sent))},
         compiler_params=params("arbitrary"),
         name="weight_pass",
         cost_estimate=cost(4 * rows * depth * width, 8 * width * depth + 8 * rows * depth),
-    )(x, grad_y, gate, active, slope, *sent, *waits)
+    )(x, grad_y, router, pick, active, slope, *sent, *waits)
 
 
 def swap(blocks, axis):
@@ -446,7 +450,7 @@
     for _ in range(count - 1):
         right = lax.ppermute(right, axis, [(i, i + 1) for i in range(count - 1)])
         left = lax.ppermute(left, axis, [(i + 1, i) for i in range(count - 1)])
-        steps.append((right, left))
+        steps.append([right, left])
     return steps
 
 
@@ -519,9 +523,10 @@
     stacked = w_qkv.transpose(1, 0, 2).reshape(share, 3 * width)
     weights = jnp.concatenate([stacked, w_router, ln_gains.T, ln_biases.T], axis=1)
     weights = lax.all_gather(weights, "row", axis=0, tiled=True)
-    out_block = swap(jnp.broadcast_to(w_out.T[None], (cols_all, share, width)), "col")
 
     chosen, ranks, select = slot_layout(expert_ids, experts, cap)
+    out_block, ranks = tie(w_out.T, ranks)
+    out_block = swap(jnp.broadcast_to(out_block[None], (cols_all, share, width)), "col")
     slots = chosen * cap + ranks
     slots_by_local = ((chosen % local) * rows_all + chosen // local) * cap + ranks
     member = chosen % local
@@ -534,7 +539,8 @@
         for g in range(local // members)
     ]
 
-    grad_packed = list(pack(slots_by_local, [cotangent], 0, block_rows, local))
+    early = min(2, local)
+    grad_packed = list(pack(slots_by_local, [cotangent], 0, block_rows, early))
     weights, grad_packed[0], out_block = tie(weights, grad_packed[0], out_block)
     grad_arrived = [send(grad_packed[0])]
     qkv_full = weights[:, : 3 * width]
@@ -549,22 +555,24 @@
 
     count = half // block
     context_a, logsum_a = attend_forward(projected, tuple(range(count)), block)
-    context_a, grad_arrived[0], *grad_packed[1:2] = tie(
-        context_a, grad_arrived[0], *grad_packed[1:2]
-    )
     full_a = lax.all_gather(context_a, "col", axis=0)
-    grad_arrived += [send(p) for p in grad_packed[1:2]]
+    grad_arrived[0], *grad_packed[1:] = tie(grad_arrived[0], *grad_packed[1:])
+    grad_arrived += [send(p) for p in grad_packed[1:]]
+    if local > early:
+        grad_packed += pack(
+            slots_by_local, [cotangent], early * block_rows, block_rows, local - early, [context_a]
+        )
     context_b, logsum_b = attend_forward(
-        projected, tuple(range(count, 2 * count)), block, [context_a]
+        projected, tuple(range(count, 2 * count)), block, grad_packed[-1:]
     )
     context_b, out_block, *grad_arrived[1:] = tie(context_b, out_block, *grad_arrived[1:])
     full_b = lax.all_gather(context_b, "col", axis=0)
     out_full = swap(jnp.broadcast_to(out_block[None], (rows_all, *out_block.shape)), "row")
-    out_full, *grad_packed[2:] = tie(out_full, *grad_packed[2:])
+    out_full, *grad_packed[early:] = tie(out_full, *grad_packed[early:])
     out_full = out_full.transpose(1, 0, 2, 3).reshape(cols_all, depth, width)
     gain, bias = gains[1:2], biases[1:2]
     middle_a, routed_a = middle_pass(full_a, out_full, tokens, 0, gain, bias)
-    for e in range(2, local):
+    for e in range(early, local):
         grad_arrived.append(send(grad_packed[e]))
         if e + 1 < local:
             full_b, grad_arrived[e], grad_packed[e + 1], middle_a = tie(
@@ -625,6 +633,26 @@
     order = [(g, f) for f in range(pieces) for g in range(len(sent))]
     back = {}
     grad_sent = []
+    grad_weights = None
+    token = None
+    row = lax.axis_index("row")
+
+    def weigh(e, waits):
+        pick = jnp.arange(experts, dtype=jnp.int32)[None, :] == row * local + e
+        return weight_pass(
+            e,
+            local,
+            arrived[e],
+            grad_arrived[e],
+            router_full,
+            pick.astype(jnp.float32),
+            active[e],
+            slope[e],
+            grad_weights,
+            waits,
+        )
+
+    waits = slope[-1:]
     last = None
     for at, (g, f) in enumerate(order):
         piece = sent[g][f]
@@ -633,22 +661,22 @@
             back[order[at - 1]] = last
         if at == 1:
             piece, slope[-1] = tie(piece, slope[-1])
-        if at == len(order) - 1:
-            homed = jnp.stack(
-                [v.reshape(rows_all, cap, depth // cols_all) for v in summed], axis=1
-            )
-            homed, piece = tie(homed, piece)
-            homed = swap(homed, "row")
-            homed, piece = tie(homed, piece)
         last = swap(piece, "row")
         back[(g, f)] = last
         if g == len(sent) - 1:
             rows = [back[(k, f)].reshape(-1, depth // pieces) for k in range(len(sent))]
-            whole = unpack(slots_by_group, rows, part, place)
-            if f == 0:
-                whole, *summed = tie(whole, *summed)
+            for e in range(f * local // pieces, (f + 1) * local // pieces):
+                *grad_weights, token = weigh(e, waits)
+                waits = [token]
+            whole = unpack(slots_by_group, rows, part, place, waits)
+            waits = [whole]
             grad_sent.append(lax.psum_scatter(whole, "col", scatter_dimension=0, tiled=True))
 
+    grad_in, grad_back = grad_weights
+    homed = jnp.stack([v.reshape(rows_all, cap, depth // cols_all) for v in summed], axis=1)
+    homed, last = tie(homed, last)
+    back[order[-1]] = last
+    homed = swap(homed, "row")
     returned = unpack(
         [slots], [homed.reshape(experts * cap, depth // cols_all)], part, lambda i: i
     ).astype(jnp.float32)
@@ -662,10 +690,6 @@
     grad_gate = jnp.sum(own_columns(cotangent).astype(jnp.float32) * returned, axis=-1)
     grad_gate = swap(grad_gate.reshape(2, cols_all, part).transpose(1, 0, 2), "col")
     grad_gate = jnp.sum(grad_gate, axis=0).reshape(2 * part, 1)
-    held = jnp.arange(experts * cap, dtype=jnp.int32)
-    gates = jnp.sum(jnp.where(held[:, None] == slots[None, :], gate[:, 0][None, :], 0.0), axis=1)
-    mixed, grad_gate, gates = tie(mixed, grad_gate, gates.reshape(rows_all, local * cap))
-    steps = relay_steps(mixed, "col")
 
     own_gate, own_probs, own_select = own_of(gate), own_of(probs), own_of(select)
     grad_logits = (grad_gate * own_probs * (own_select - own_gate)).astype(jnp.bfloat16)
@@ -686,31 +710,20 @@
     grad_context = jnp.einsum(
         "td,zdc->ztc", grad_attn, out_full, preferred_element_type=jnp.float32
     ).astype(jnp.bfloat16)
-    gates = swap(gates, "row")
-    if steps:
-        grad_context, *first = tie(grad_context, *steps[0])
-        steps[0] = tuple(first)
-    grad_context = swap(grad_context, "col").reshape(cols_all, 2, part, width)
+    grad_context = swap(grad_context, "col")
+    grad_context, mixed = tie(grad_context, mixed)
+    steps = relay_steps(mixed, "col")
+    grad_context = grad_context.reshape(cols_all, 2, part, width)
     grad_context = grad_context.transpose(1, 0, 2, 3).reshape(2, half, width)
 
-    context_own = jnp.concatenate(
-        [lax.dynamic_slice_in_dim(v, col * part, part, 1) for v in (full_a, full_b)], axis=1
-    )
-    grad_out = jnp.einsum("td,ztc->dzc", grad_attn, context_own, preferred_element_type=jnp.float32)
-    plane = jnp.concatenate([grad_out.reshape(depth, cols_all * width), grad_router], axis=1)
-    plane = swap(plane.astype(jnp.bfloat16).reshape(rows_all, share, -1), "row")
 
     proj_b, *carried = attend_backward(
         projected, grad_context[1], context_b, logsum_b, block, count
     )
-    tied = steps[1] if len(steps) > 1 else ()
-    proj_b, gates, *second = tie(proj_b, gates, *tied)
+    proj_b, *steps[0] = tie(proj_b, *steps[0])
     proj_a = attend_backward(
         projected, grad_context[0], context_a, logsum_a, block, 0, carried
     )[0]
-    tied = steps[2] if len(steps) > 2 else ()
-    proj_a, plane, *third = tie(proj_a, plane, *tied)
-    steps[1:3] = [tuple(v) for v in (second, third) if v]
 
     def spread(grads):
         made = jnp.einsum("tc,dc->td", grads, qkv_full, preferred_element_type=jnp.float32)
@@ -718,28 +731,21 @@
             made.astype(jnp.bfloat16), "col", scatter_dimension=0, tiled=True
         ).astype(jnp.float32)
 
+    tied = steps[1] if len(steps) > 1 else []
+    proj_a, grad_attn, *tied[:] = tie(proj_a, grad_attn, *tied)
+    context_own = jnp.concatenate(
+        [lax.dynamic_slice_in_dim(v, col * part, part, 1) for v in (full_a, full_b)], axis=1
+    )
+    grad_out = jnp.einsum("td,ztc->dzc", grad_attn, context_own, preferred_element_type=jnp.float32)
+    plane = jnp.concatenate([grad_out.reshape(depth, cols_all * width), grad_router], axis=1)
+    plane = swap(plane.astype(jnp.bfloat16).reshape(rows_all, share, -1), "row")
     normal_b, normal_a = spread(proj_b), spread(proj_a)
+    normal_a, plane = tie(normal_a, plane)
+    for step in steps[2:]:
+        normal_b, *step[:] = tie(normal_b, *step)
     grad_qkv = jnp.einsum(
         "td,tc->dc", normal_in[:half], proj_a, preferred_element_type=jnp.float32
     ) + jnp.einsum("td,tc->dc", normal_in[half:], proj_b, preferred_element_type=jnp.float32)
-
-    gates = gates.reshape(rows_all, local, cap).transpose(1, 0, 2)
-    grad_weights = None
-    for e in range(local):
-        *grad_weights, token = weight_pass(
-            e,
-            local,
-            arrived[e],
-            grad_arrived[e],
-            gates[e].reshape(block_rows, 1),
-            active[e],
-            slope[e],
-            grad_weights,
-            [token if e else proj_a],
-        )
-        if e == max(local // 2 - 1, 0):
-            normal_b, token = tie(normal_b, token)
-    grad_in, grad_back = grad_weights
 
     plane = jnp.sum(plane.astype(jnp.float32), axis=0)
     router_share = plane[:, cols_all * width :].reshape(1, share, experts)
@@ -766,9 +772,7 @@
         if c:
             moves = relay_steps(finished[1], "col")
             flat = [v for move in moves for v in move]
-            normal_a, out_share, router_share, *flat = tie(
-                normal_a, out_share, router_share, *flat
-            )
+            normal_a, *flat = tie(normal_a, *flat)
             moves = list(zip(flat[0::2], flat[1::2]))
     grad_tokens = jnp.concatenate(
         [relay_join(finished[1], moves, "col", 0), lax.all_gather(finished[0], "col", axis=0, tiled=True)][::-1],

time: 898 us -> 876 us (0.976)
  blocking collectives: 0 us -> 28.4 us
  Pallas kernels: 293 us -> 268 us
  waiting for transfers between devices: 283 us -> 265 us
  local copies, waits for them, and re-layouts: 59 us -> 76.1 us
  starting transfers between devices: 134 us -> 123 us
    ppermute x6, waiting for transfers between devices: 0.96 us -> 65.8 us  [relay_steps(): right = lax.ppermute(right, axis, [(i, i + 1) for i in range(count - 1)])]
    all_to_all x23 -> x21, waiting for transfers between devices: 205 us -> 164 us  [swap(): return lax.all_to_all(blocks, axis, split_axis=0, concat_axis=0, tiled=True)]
    reduce_scatter x1, waiting for transfers between devices: 29.8 us -> 0.02 us  [per_device(): lax.psum_scatter(summed[-1], 'col', scatter_dimension=0, tiled=True)]
    all_to_all x0 -> x1, blocking collectives: none -> 28.4 us  [swap(): return lax.all_to_all(blocks, axis, split_axis=0, concat_axis=0, tiled=True)]
    pallas_call x2, Pallas kernels: 41.3 us -> 22.1 us  [attend_forward(): pl.pallas_call(functools.partial(forward_body, blocks, block), out_shape=...]
    pallas_call x2, Pallas kernels: 47.5 us -> 34.9 us  [attend_backward(): pl.pallas_call(functools.partial(backward_body, block, first, len(carried...]
    all_to_all x23 -> x21, starting transfers between devices: 93 us -> 85.1 us  [swap(): return lax.all_to_all(blocks, axis, split_axis=0, concat_axis=0, tiled=True)]
    unnamed x72 -> x96, local copies, waits for them, and re-layouts: 16.2 us -> 19.8 us
  transfers between devices with their start and end apart: 47 -> 45, of which waited for: 24 -> 25; matrix products, arithmetic and copies ran while one was open for 15% -> 14% of each run, Pallas kernels for 33% -> 31%
where the time goes in v4:
time: 876 us; the launch traced here: 868 us
  Pallas kernels  268 us (31%)
  waiting for transfers between devices  265 us (30%)
  starting transfers between devices  123 us (14%)
  local copies, waits for them, and re-layouts  76.1 us (9%)
  other arithmetic  57.3 us (7%)
  matrix products  34.1 us (4%)
  blocking collectives  28.4 us (3%)
  between operations  15.9 us (2%)
    all_to_all x21, waiting for transfers between devices, swap(): return lax.all_to_all(blocks, axis, split_axis=0, concat_axis=0, tiled=True)  164 us
    all_to_all x21, starting transfers between devices, swap(): return lax.all_to_all(blocks, axis, split_axis=0, concat_axis=0, tiled=True)  85.1 us
    ppermute x6, waiting for transfers between devices, relay_steps(): right = lax.ppermute(right, axis, [(i, i + 1) for i in range(count - 1)])  65.8 us
    pallas_call x4, Pallas kernels, expert_pass(): pl.pallas_call(functools.partial(expert_body, len(sent) + len(waits)), ou...  58.1 us
    pallas_call x4, Pallas kernels, pack(): pl.pallas_call(functools.partial(pack_body, base, step, each, len(rows)),...  54 us
    pallas_call x4, Pallas kernels, weight_pass(): pl.pallas_call(functools.partial(weight_body, len(sent) + len(waits)), ou...  46.9 us
    pallas_call x3, Pallas kernels, unpack(): pl.pallas_call(functools.partial(unpack_body, len(rows)), out_shape=jax.S...  36.6 us
    pallas_call x2, Pallas kernels, attend_backward(): pl.pallas_call(functools.partial(backward_body, block, first, len(carried...  34.9 us
  transfers between devices with their start and end apart: 45, of which 25 were waited for; matrix products, arithmetic and copies ran while one was open for 14% of the time, Pallas kernels for 31%

profile of v4, /device:TPU:0, one launch (start us, length us, event | category | flops | bytes accessed | tf_op | source)
XLA Modules:
  0.0 867.7 jit_solution(15097733675528912525)
XLA Ops:
  26.7 13.3 %pack.4 = (bf16[1024,1024]{1,0:T(8,128)(2,1)}, bf16[1024,1024]{1,0:T(8,128)(2,1)}) custom-call(s32[1,2048]{1,0:T(1,128)} %bitcast.152, bf16[2048,1024]{1,0:T(8,128)(2,1)} %rest_0_.3), custom_call_target="tpu_custom_call" | custom-call | flops 1048576 | bytes 1048576 | tf_op jit(solution)/shard_map/pack/pallas_call | solution.py:55
  79.0 13.8 %pack.5 = (bf16[1024,1024]{1,0:T(8,128)(2,1)}, bf16[1024,1024]{1,0:T(8,128)(2,1)}) custom-call(s32[1,2048]{1,0:T(1,128)} %bitcast.153, bf16[2048,1024]{1,0:T(8,128)(2,1)} %rest_0_.3, bf16[1024,256]{1,0:T(8,128)(2,1)} %get-tuple-element.127.rest_1_.refs_2_), custom_call_target="tpu_custom_call" | custom-call | flops 1048576 | bytes 1048576 | tf_op jit(solution)/shard_map/pack/pallas_call | solution.py:55
  92.8 14.3 %attend_forward.3 = (bf16[1024,256]{1,0:T(8,128)(2,1)}, f32[4,1024]{1,0:T(4,128)}) custom-call(bf16[2048,768]{1,0:T(8,128)(2,1)} %convolution_convert_fusion.q_ref.k_ref.v_ref.refs_0_.refs_4_.refs_5_, bf16[2048,768]{1,0:T(8,128)(2,1)} %convolution_convert_fusion.q_ref.k_ref.v_ref.refs_0_.refs_4_.refs_5_, ...), custom_call_target="tpu_custom_call" | custom-call | flops 262144 | bytes 262144 | tf_op jit(solution)/shard_map/attend_forward/pallas_call | solution.py:190
  114.2 25.9 %all-to-all-done.3 = bf16[8,4,128,256]{3,2,1,0:T(8,128)(2,1)} async-done(((bf16[8,4,128,256]{3,2,1,0:T(8,128)(2,1)}), bf16[8,4,128,256]{3,2,1,0:T(8,128)(2,1)}, u32[]{:S(2)}, u32[]{:S(2)}) %all-to-all-start.3) | async-done | bytes 2097184 | tf_op jit(solution)/shard_map/all_to_all | solution.py:439
  206.4 18.8 %pack.6 = (bf16[1024,1024]{1,0:T(8,128)(2,1)}, bf16[1024,1024]{1,0:T(8,128)(2,1)}, bf16[1024,1024]{1,0:T(8,128)(2,1)}) custom-call(s32[1,2048]{1,0:T(1,128)} %bitcast.155, bf16[1024,1024]{1,0:T(8,128)(2,1)} %get-tuple-element.144.rest_0_, bf16[1024,1024]{1,0:T(8,128)(2,1)} %get-tuple-element.145.rest_1_), custom_call_target="tpu_custom_call" | custom-call | flops 1048576 | bytes 1048576 | tf_op jit(solution)/shard_map/pack/pallas_call | solution.py:55
  238.0 14.4 %expert_pass.4 = (bf16[4,1024,256]{2,1,0:T(8,128)(2,1)}, bf16[1024,1024]{1,0:T(8,128)(2,1)}, bf16[1024,1024]{1,0:T(8,128)(2,1)}, bf16[8,2,128,512]{3,2,1,0:T(8,128)(2,1)}, bf16[8,2,128,512]{3,2,1,0:T(8,128)(2,1)}) custom-call(bf16[1024,1024]{1,0:T(8,128)(2,1)} %bitcast.132, bf16[1024,1024]{1,0:T(8,128)(2,1)} %bitcast.130, bf16[4,1024,1024]{2,1,0:T(8,128)(2,1)} %win_ref.7, ...), custom_call_target="tpu_custom_call" | custom-call | flops 8589934592 | bytes 16777216 | tf_op jit(solution)/shard_map/expert_pass/pallas_call | solution.py:352
  252.4 12.1 %all-to-all-done.7 = bf16[8,128,1024]{2,1,0:T(8,128)(2,1)S(1)} async-done(((bf16[8,128,1024]{2,1,0:T(8,128)(2,1)}), bf16[8,128,1024]{2,1,0:T(8,128)(2,1)S(1)}, u32[]{:S(2)}, u32[]{:S(2)}) %all-to-all-start.7) | async-done | bytes 2097184 | tf_op jit(solution)/shard_map/all_to_all | solution.py:439
  269.5 14.5 %expert_pass.5 = (bf16[4,1024,256]{2,1,0:T(8,128)(2,1)}, bf16[1024,1024]{1,0:T(8,128)(2,1)}, bf16[1024,1024]{1,0:T(8,128)(2,1)}, bf16[8,2,128,512]{3,2,1,0:T(8,128)(2,1)}, bf16[8,2,128,512]{3,2,1,0:T(8,128)(2,1)}) custom-call(bf16[1024,1024]{1,0:T(8,128)(2,1)} %bitcast.119, ...), custom_call_target="tpu_custom_call", output_to_operand_aliasing={{3}: (4, {}), {4}: (5, {})} | custom-call | flops 8589934592 | bytes 16777216 | tf_op jit(solution)/shard_map/expert_pass/pallas_call | solution.py:352
  284.0 12.0 %all-to-all-done.8 = bf16[8,128,1024]{2,1,0:T(8,128)(2,1)S(1)} async-done(((bf16[8,128,1024]{2,1,0:T(8,128)(2,1)}), bf16[8,128,1024]{2,1,0:T(8,128)(2,1)S(1)}, u32[]{:S(2)}, u32[]{:S(2)}) %all-to-all-start.8) | async-done | bytes 2097184 | tf_op jit(solution)/shard_map/all_to_all | solution.py:439
  301.8 14.8 %expert_pass.6 = (bf16[4,1024,256]{2,1,0:T(8,128)(2,1)}, bf16[1024,1024]{1,0:T(8,128)(2,1)}, bf16[1024,1024]{1,0:T(8,128)(2,1)}, bf16[8,2,128,512]{3,2,1,0:T(8,128)(2,1)}, bf16[8,2,128,512]{3,2,1,0:T(8,128)(2,1)}) custom-call(bf16[1024,1024]{1,0:T(8,128)(2,1)} %bitcast.117, bf16[1024,1024]{1,0:T(8,128)(2,1)} %bitcast.113, bf16[4,1024,1024]{2,1,0:T(8,128)(2,1)} %win_ref.7, ...), custom_call_target="tpu_custom_call" | custom-call | flops 8589934592 | bytes 16777216 | tf_op jit(solution)/shard_map/expert_pass/pallas_call | solution.py:352
  316.6 11.8 %all-to-all-done.9 = bf16[8,128,1024]{2,1,0:T(8,128)(2,1)} async-done(((bf16[8,128,1024]{2,1,0:T(8,128)(2,1)}), bf16[8,128,1024]{2,1,0:T(8,128)(2,1)}, u32[]{:S(2)}, u32[]{:S(2)}) %all-to-all-start.9) | async-done | bytes 2097184 | tf_op jit(solution)/shard_map/all_to_all | solution.py:439
  332.1 14.5 %expert_pass.7 = (bf16[4,1024,256]{2,1,0:T(8,128)(2,1)}, bf16[1024,1024]{1,0:T(8,128)(2,1)}, bf16[1024,1024]{1,0:T(8,128)(2,1)}, bf16[8,2,128,512]{3,2,1,0:T(8,128)(2,1)}, bf16[8,2,128,512]{3,2,1,0:T(8,128)(2,1)}) custom-call(bf16[1024,1024]{1,0:T(8,128)(2,1)} %bitcast.29.x_ref, ...), custom_call_target="tpu_custom_call", output_to_operand_aliasing={{3}: (4, {}), {4}: (5, {})} | custom-call | flops 8589934592 | bytes 16777216 | tf_op jit(solution)/shard_map/expert_pass/pallas_call | solution.py:352
  346.6 12.0 %all-to-all-done.10 = bf16[8,2,128,512]{3,2,1,0:T(8,128)(2,1)S(1)} async-done(((bf16[8,2,128,512]{3,2,1,0:T(8,128)(2,1)}), bf16[8,2,128,512]{3,2,1,0:T(8,128)(2,1)S(1)}, u32[]{:S(2)}, u32[]{:S(2)}) %all-to-all-start.10) | async-done | bytes 2097184 | tf_op jit(solution)/shard_map/all_to_all | solution.py:439
  369.7 11.7 %weight_pass.4 = (f32[4,1024,1024]{2,1,0:T(8,128)}, f32[4,1024,1024]{2,1,0:T(8,128)}, f32[8,128]{1,0:T(8,128)}) custom-call(bf16[1024,1024]{1,0:T(8,128)(2,1)} %bitcast.133, bf16[1024,1024]{1,0:T(8,128)(2,1)} %bitcast.131, bf16[1024,32]{1,0:T(8,128)(2,1)} %slice.115.router_ref, f32[1,32]{1,0:T(1,128)} %compare_convert_fusion.2.pick_ref, ...), custom_call_target="tpu_custom_call" | custom-call | flops 4294967296 | bytes 16777216 | tf_op jit(solution)/shard_map/weight_pass/pallas_call | solution.py:405
  397.3 13.9 %unpack.3.rest_2_ = bf16[2048,512]{1,0:T(8,128)(2,1)} custom-call(s32[2048,1]{1,0:T(8,128)} %copy.139.refs_0_, s32[2048,1]{1,0:T(8,128)} %copy.140.refs_1_, bf16[2048,512]{1,0:T(8,128)(2,1)} %bitcast.135, bf16[2048,512]{1,0:T(8,128)(2,1)} %bitcast.31.refs_3_, f32[8,128]{1,0:T(8,128)} %get-tuple-element.188.refs_4_), custom_call_target="tpu_custom_call" | custom-call | flops 8589934592 | bytes 6291456 | tf_op jit(solution)/shard_map/unpack/pallas_call | solution.py:89
  434.4 11.7 %weight_pass.6 = (f32[4,1024,1024]{2,1,0:T(8,128)}, f32[4,1024,1024]{2,1,0:T(8,128)}, f32[8,128]{1,0:T(8,128)}) custom-call(bf16[1024,1024]{1,0:T(8,128)(2,1)} %bitcast.118, bf16[1024,1024]{1,0:T(8,128)(2,1)} %bitcast.114, bf16[1024,32]{1,0:T(8,128)(2,1)} %slice.115.router_ref, ...), custom_call_target="tpu_custom_call", output_to_operand_aliasing={{0}: (6, {}), {1}: (7, {})} | custom-call | flops 4294967296 | bytes 16777216 | tf_op jit(solution)/shard_map/weight_pass/pallas_call | solution.py:405
  457.8 13.7 %unpack.4 = bf16[2048,512]{1,0:T(8,128)(2,1)} custom-call(s32[2048,1]{1,0:T(8,128)} %copy.139.refs_0_, s32[2048,1]{1,0:T(8,128)} %copy.140.refs_1_, bf16[2048,512]{1,0:T(8,128)(2,1)} %bitcast.134, bf16[2048,512]{1,0:T(8,128)(2,1)} %bitcast.33.refs_3_, f32[8,128]{1,0:T(8,128)} %get-tuple-element.203.refs_4_), custom_call_target="tpu_custom_call" | custom-call | flops 8589934592 | bytes 6291456 | tf_op jit(solution)/shard_map/unpack/pallas_call | solution.py:89
  493.1 18.5 %all-to-all-done.14 = bf16[8,4,128,256]{3,2,1,0:T(8,128)(2,1)} async-done(((bf16[8,4,128,256]{3,2,1,0:T(8,128)(2,1)}), bf16[8,4,128,256]{3,2,1,0:T(8,128)(2,1)}, u32[]{:S(2)}, u32[]{:S(2)}) %all-to-all-start.14) | async-done | bytes 2097184 | tf_op jit(solution)/shard_map/all_to_all | solution.py:439
  542.4 28.4 %all_to_all.110 = bf16[4,512,256]{1,2,0:T(8,128)(2,1)S(1)} all-to-all(bf16[4,512,256]{1,2,0:T(8,128)(2,1)S(1)} %fusion.17), channel_id=1, replica_groups=mesh['row'=8,'col'=4] {'col'}, dimensions={0} | all-to-all | bytes 2097152 | tf_op jit(solution)/shard_map/all_to_all | solution.py:439
  580.2 22.8 %attend_backward.2 = (bf16[1024,768]{1,0:T(8,128)(2,1)}, f32[1024,256]{1,0:T(8,128)}, f32[1024,256]{1,0:T(8,128)}) custom-call(bf16[2048,768]{1,0:T(8,128)(2,1)} %convolution_convert_fusion.q_ref.k_ref.v_ref.refs_0_.refs_4_.refs_5_, bf16[1024,256]{1,0:T(8,128)(2,1)} %bitcast.146, bf16[1024,256]{1,0:T(8,128)(2,1)} %get-tuple-element.137.refs_2_, ...), custom_call_target="tpu_custom_call" | custom-call | flops 10737418240 | bytes 8388608 | tf_op jit(solution)/shard_map/attend_backward/pallas_call | solution.py:282
  622.8 12.0 %attend_backward.3 = bf16[1024,768]{1,0:T(8,128)(2,1)} custom-call(bf16[2048,768]{1,0:T(8,128)(2,1)} %convolution_convert_fusion.q_ref.k_ref.v_ref.refs_0_.refs_4_.refs_5_, bf16[1024,256]{1,0:T(8,128)(2,1)} %bitcast.145, bf16[1024,256]{1,0:T(8,128)(2,1)} %get-tuple-element.127.rest_1_.refs_2_, f32[4,1024]{1,0:T(4,128)} %get-tuple-element.215.refs_3_, ...), custom_call_target="tpu_custom_call" | custom-call | flops 5368709120 | bytes 4194304 | tf_op jit(solution)/shard_map/attend_backward/pallas_call | solution.py:282
  634.8 26.8 %collective-permute-done.2 = bf16[2048,256]{1,0:T(8,128)(2,1)S(1)} collective-permute-done((bf16[2048,256]{1,0:T(8,128)(2,1)}, bf16[2048,256]{1,0:T(8,128)(2,1)S(1)}, u32[]{:S(2)}, u32[]{:S(2)}) %collective-permute-start.2) | collective-permute-done | bytes 1048608 | tf_op jit(solution)/shard_map/ppermute | solution.py:451
  712.2 20.1 %collective-permute-done.3 = bf16[2048,256]{1,0:T(8,128)(2,1)} collective-permute-done((bf16[2048,256]{1,0:T(8,128)(2,1)S(1)}, bf16[2048,256]{1,0:T(8,128)(2,1)}, u32[]{:S(2)}, u32[]{:S(2)}) %collective-permute-start.3) | collective-permute-done | bytes 1048608 | tf_op jit(solution)/shard_map/ppermute | solution.py:451
  819.1 14.5 %all-to-all-done.19 = bf16[4,128,288]{1,2,0:T(8,128)(2,1)S(1)} async-done(((bf16[4,128,288]{1,2,0:T(8,128)(2,1)}), bf16[4,128,288]{1,2,0:T(8,128)(2,1)S(1)}, u32[]{:S(2)}, u32[]{:S(2)}) %all-to-all-start.19) | async-done | bytes 294944 | tf_op jit(solution)/shard_map/all_to_all | solution.py:439
  (320 shorter events, 465.4 us)
Async XLA Ops:
  7.2 34.1 %all-gather.7.cloned.1.call-start = ((), (), s32[]{:S(2)}) async-start(), calls=%async_computation.30 | async-start | bytes 2064384 | tf_op jit(solution)/shard_map/all_gather | solution.py:525
  47.5 101.1 %all-gather.13.cloned.1.call-start = ((), (), s32[]{:S(2)}) async-start(), calls=%async_computation.41 | async-start | bytes 2621440 | tf_op jit(solution)/shard_map/all_gather | solution.py:558
  75.4 31.7 %all-to-all-start.2 = ((bf16[8,128,1024]{2,1,0:T(8,128)(2,1)}), bf16[8,128,1024]{2,1,0:T(8,128)(2,1)S(1)}, u32[]{:S(2)}, u32[]{:S(2)}) async-start(bf16[8,128,1024]{2,1,0:T(8,128)(2,1)} %bitcast.137), calls=%async_computation.2 | async-start | bytes 4194304 | tf_op jit(solution)/shard_map/all_to_all | solution.py:439
  113.4 49.7 %all-gather.11.cloned.1.call-start = ((), (), s32[]{:S(2)}) async-start(), calls=%async_computation.40 | async-start | bytes 2621440 | tf_op jit(solution)/shard_map/all_gather | solution.py:569
  171.8 31.0 %all-to-all-start.5 = ((bf16[8,128,1024]{2,1,0:T(8,128)(2,1)}), bf16[8,128,1024]{2,1,0:T(8,128)(2,1)}, u32[]{:S(2)}, u32[]{:S(2)}) async-start(bf16[8,128,1024]{2,1,0:T(8,128)(2,1)} %bitcast.124), calls=%async_computation.5 | async-start | bytes 4194304 | tf_op jit(solution)/shard_map/all_to_all | solution.py:439
  238.0 94.2 %reduce-scatter.9.cloned.1.call-start = ((), (), s32[]{:S(2)}) async-start(), calls=%async_computation.31 | async-start | bytes 2621440 | tf_op jit(solution)/shard_map/reduce_scatter | solution.py:604
  269.5 208.1 %reduce-scatter.15.cloned.1.call-start = ((), (), s32[]{:S(2)}) async-start(), calls=%async_computation.34 | async-start | bytes 2621440 | tf_op jit(solution)/shard_map/reduce_scatter | solution.py:604
  301.7 175.8 %reduce-scatter.17.cloned.1.call-start = ((), (), s32[]{:S(2)}) async-start(), calls=%async_computation.35 | async-start | bytes 2621440 | tf_op jit(solution)/shard_map/reduce_scatter | solution.py:604
  332.0 145.6 %reduce-scatter.19.cloned.1.call-start = ((), (), s32[]{:S(2)}) async-start(), calls=%async_computation.36 | async-start | bytes 2621440 | tf_op jit(solution)/shard_map/reduce_scatter | solution.py:628
  359.9 33.3 %all-to-all-start.11 = ((bf16[8,2,128,512]{3,2,1,0:T(8,128)(2,1)}), bf16[8,2,128,512]{3,2,1,0:T(8,128)(2,1)}, u32[]{:S(2)}, u32[]{:S(2)}) async-start(bf16[8,2,128,512]{3,2,1,0:T(8,128)(2,1)} %get-tuple-element.180), calls=%async_computation.12 | async-start | bytes 4194304 | tf_op jit(solution)/shard_map/all_to_all | solution.py:439
  397.3 138.2 %reduce-scatter.11.cloned.1.call-start = ((), (), s32[]{:S(2)}) async-start(), calls=%async_computation.32 | async-start | bytes 2621440 | tf_op jit(solution)/shard_map/reduce_scatter | solution.py:673
  425.2 32.6 %all-to-all-start.13 = ((bf16[8,2,128,512]{3,2,1,0:T(8,128)(2,1)}), bf16[8,2,128,512]{3,2,1,0:T(8,128)(2,1)}, u32[]{:S(2)}, u32[]{:S(2)}) async-start(bf16[8,2,128,512]{3,2,1,0:T(8,128)(2,1)} %get-tuple-element.193), calls=%async_computation.15 | async-start | bytes 4194304 | tf_op jit(solution)/shard_map/all_to_all | solution.py:439
  429.6 105.9 %reduce-scatter.13.cloned.1.call-start = ((), (), s32[]{:S(2)}) async-start(), calls=%async_computation.33 | async-start | bytes 2621440 | tf_op jit(solution)/shard_map/reduce_scatter | solution.py:673
  480.6 31.0 %all-to-all-start.14 = ((bf16[8,4,128,256]{3,2,1,0:T(8,128)(2,1)}), bf16[8,4,128,256]{3,2,1,0:T(8,128)(2,1)}, u32[]{:S(2)}, u32[]{:S(2)}) async-start(bf16[8,4,128,256]{3,2,1,0:T(8,128)(2,1)} %pad_maximum_fusion.3), calls=%async_computation.20 | async-start | bytes 4194304 | tf_op jit(solution)/shard_map/all_to_all | solution.py:439
  529.7 181.3 %reduce-scatter.21.cloned.1.call-start = ((), (), s32[]{:S(2)}) async-start(), calls=%async_computation.37 | async-start | bytes 2621440 | tf_op jit(solution)/shard_map/reduce_scatter | solution.py:730
  570.9 32.2 %collective-permute-start = (bf16[2048,256]{1,0:T(8,128)(2,1)}, bf16[2048,256]{1,0:T(8,128)(2,1)}, u32[]{:S(2)}, u32[]{:S(2)}) collective-permute-start(bf16[2048,256]{1,0:T(8,128)(2,1)} %get-tuple-element.208), channel_id=1, source_target_pairs={{0,1},{1,2},{2,3},{4,5},{5,6},{6,7},{8,9},{9,10},{10,11},{12,13},{... | collective-permute-start | bytes 3145736 | tf_op jit(solution)/shard_map/ppermute | solution.py:451
  608.1 188.6 %reduce-scatter.23.cloned.1.call-start = ((), (), s32[]{:S(2)}) async-start(), calls=%async_computation.38 | async-start | bytes 2621440 | tf_op jit(solution)/shard_map/reduce_scatter | solution.py:730
  612.3 49.3 %collective-permute-start.2 = (bf16[2048,256]{1,0:T(8,128)(2,1)}, bf16[2048,256]{1,0:T(8,128)(2,1)S(1)}, u32[]{:S(2)}, u32[]{:S(2)}) collective-permute-start(bf16[2048,256]{1,0:T(8,128)(2,1)} %collective-permute-done), channel_id=1, source_target_pairs={{0,1},{1,2},{2,3},{4,5},{5,6},{6,7},{8,9},{9,10},{10,11},{12,13},{... | collective-permute-start | bytes 3145736 | tf_op jit(solution)/shard_map/ppermute | solution.py:451
  616.9 55.8 %collective-permute-start.4 = (bf16[2048,256]{1,0:T(8,128)(2,1)}, bf16[2048,256]{1,0:T(8,128)(2,1)}, u32[]{:S(2)}, u32[]{:S(2)}) collective-permute-start(bf16[2048,256]{1,0:T(8,128)(2,1)} %collective-permute-done.1), channel_id=1, source_target_pairs={{1,0},{2,1},{3,2},{5,4},{6,5},{7,6},{9,8},{10,9},{11,10},{13,12},{... | collective-permute-start | bytes 3145736 | tf_op jit(solution)/shard_map/ppermute | solution.py:452
  682.4 49.8 %collective-permute-start.3 = (bf16[2048,256]{1,0:T(8,128)(2,1)S(1)}, bf16[2048,256]{1,0:T(8,128)(2,1)}, u32[]{:S(2)}, u32[]{:S(2)}) collective-permute-start(bf16[2048,256]{1,0:T(8,128)(2,1)S(1)} %collective-permute-done.2), channel_id=1, source_target_pairs={{0,1},{1,2},{2,3},{4,5},{5,6},{6,7},{8,9},{9,10},{10,11},{12,13},{... | collective-permute-start | bytes 3145736 | tf_op jit(solution)/shard_map/ppermute | solution.py:451
  688.2 53.5 %collective-permute-start.5 = (bf16[2048,256]{1,0:T(8,128)(2,1)}, bf16[2048,256]{1,0:T(8,128)(2,1)}, u32[]{:S(2)}, u32[]{:S(2)}) collective-permute-start(bf16[2048,256]{1,0:T(8,128)(2,1)} %collective-permute-done.4), channel_id=1, source_target_pairs={{1,0},{2,1},{3,2},{5,4},{6,5},{7,6},{9,8},{10,9},{11,10},{13,12},{... | collective-permute-start | bytes 3145736 | tf_op jit(solution)/shard_map/ppermute | solution.py:452
  692.9 50.4 %all-to-all-start.18 = ((bf16[8,128,768]{2,1,0:T(8,128)(2,1)}), bf16[8,128,768]{2,1,0:T(8,128)(2,1)}, u32[]{:S(2)}, u32[]{:S(2)}) async-start(bf16[8,128,768]{2,1,0:T(8,128)(2,1)} %bitcast.54), calls=%async_computation.26 | async-start | bytes 3145728 | tf_op jit(solution)/shard_map/all_to_all | solution.py:439
  743.3 54.6 %all-to-all-start.17 = ((bf16[8,128,1056]{1,2,0:T(8,128)(2,1)}), bf16[8,128,1056]{1,2,0:T(8,128)(2,1)S(1)}, u32[]{:S(2)}, u32[]{:S(2)}) async-start(bf16[8,128,1056]{1,2,0:T(8,128)(2,1)} %copy.153), calls=%async_computation.25 | async-start | bytes 4325376 | tf_op jit(solution)/shard_map/all_to_all | solution.py:439
  747.0 109.4 %all-gather.9.cloned.1.call-start = ((), (), s32[]{:S(2)}) async-start(), calls=%async_computation.39 | async-start | bytes 2621440 | tf_op jit(solution)/shard_map/all_gather | solution.py:778
  (65 other events, 848.4 us)
Sparse Core Ops, SparseCore 0:
  11.8 29.4 all-gather.6
  65.8 47.2 all-gather.12
  115.8 47.2 all-gather.10
  264.7 42.9 reduce-scatter.8
  309.9 43.1 reduce-scatter.14
  355.3 43.1 reduce-scatter.16
  400.9 43.1 reduce-scatter.18
  446.4 43.2 reduce-scatter.10
  492.1 43.2 reduce-scatter.12
  608.2 67.6 reduce-scatter.20
  678.3 66.5 reduce-scatter.22
  806.4 49.9 all-gather.8

commit v5 on v4

--- a/solution.py
+++ b/solution.py
@@ -82,7 +82,7 @@
     out_ref[...] = made.astype(out_ref.dtype)
 
 
-def unpack(slots, rows, step, place, waits=()):
+def unpack(slots, rows, step, waits=()):
     length = slots[0].shape[0]
     width = rows[0].shape[1]
     count = sum(r.shape[0] for r in rows)
@@ -93,7 +93,7 @@
         in_specs=[pl.BlockSpec((step, 1), lambda i: (i, 0))] * len(rows)
         + [pl.BlockSpec(r.shape, lambda i: (0, 0)) for r in rows]
         + [pl.BlockSpec(memory_space=pl.ANY)] * len(waits),
-        out_specs=pl.BlockSpec((step, width), lambda i: (place(i), 0)),
+        out_specs=pl.BlockSpec((step, width), lambda i: (i, 0)),
         compiler_params=params("arbitrary"),
         name="unpack",
         cost_estimate=cost(2 * count * length * width, 2 * (length + count) * width),
@@ -443,30 +443,6 @@
     return lax.optimization_barrier(values)
 
 
-def relay_steps(shard, axis):
-    count = lax.axis_size(axis)
-    right = left = shard
-    steps = []
-    for _ in range(count - 1):
-        right = lax.ppermute(right, axis, [(i, i + 1) for i in range(count - 1)])
-        left = lax.ppermute(left, axis, [(i + 1, i) for i in range(count - 1)])
-        steps.append([right, left])
-    return steps
-
-
-def relay_join(shard, steps, axis, dim):
-    count = lax.axis_size(axis)
-    me = lax.axis_index(axis)
-    size = shard.shape[dim]
-    shape = list(shard.shape)
-    shape[dim] = size * count
-    whole = jnp.zeros(shape, shard.dtype)
-    for k in range(count):
-        piece = shard if k == 0 else steps[k - 1][0] + steps[count - k - 1][1]
-        whole = lax.dynamic_update_slice_in_dim(whole, piece, ((me - k) % count) * size, dim)
-    return whole
-
-
 def layer_stats(values):
     mean = jnp.mean(values, axis=-1, keepdims=True)
     centered = values - mean
@@ -506,16 +482,17 @@
     block_rows = rows_all * cap
     block = min(256, length // 2)
     half = length // 2
-    part = half // cols_all
+    part = length // cols_all
     members = max(1, local // 2)
     pieces = 2
 
-    def own(low, high):
-        both = (lax.dynamic_slice_in_dim(v, col * part, part, 0) for v in (low, high))
-        return jnp.concatenate(list(both), axis=0)
-
     def own_of(values):
-        return own(values[:half], values[half:])
+        return lax.dynamic_slice_in_dim(values, col * part, part, 0)
+
+    def own(low, high, axis=0):
+        first = lax.dynamic_slice_in_dim(low, col * part, part, axis)
+        second = lax.dynamic_slice_in_dim(high, col * part - half, part, axis)
+        return jnp.where(col * part < half, first, second)
 
     def send(packed):
         return swap(packed.reshape(rows_all, cap, depth), "row").reshape(block_rows, depth)
@@ -562,22 +539,20 @@
         grad_packed += pack(
             slots_by_local, [cotangent], early * block_rows, block_rows, local - early, [context_a]
         )
+    out_full = lax.all_gather(out_block, "row", axis=1, tiled=True)
     context_b, logsum_b = attend_forward(
-        projected, tuple(range(count, 2 * count)), block, grad_packed[-1:]
-    )
-    context_b, out_block, *grad_arrived[1:] = tie(context_b, out_block, *grad_arrived[1:])
+        projected, tuple(range(count, 2 * count)), block, [grad_packed[-1], out_full]
+    )
+    context_b, *both = tie(context_b, *grad_arrived[1:], *grad_packed[early:])
+    grad_arrived[1:], grad_packed[early:] = both[: len(grad_arrived) - 1], both[len(grad_arrived) - 1 :]
     full_b = lax.all_gather(context_b, "col", axis=0)
-    out_full = swap(jnp.broadcast_to(out_block[None], (rows_all, *out_block.shape)), "row")
-    out_full, *grad_packed[early:] = tie(out_full, *grad_packed[early:])
-    out_full = out_full.transpose(1, 0, 2, 3).reshape(cols_all, depth, width)
     gain, bias = gains[1:2], biases[1:2]
     middle_a, routed_a = middle_pass(full_a, out_full, tokens, 0, gain, bias)
+    full_b, middle_a = tie(full_b, middle_a)
     for e in range(early, local):
         grad_arrived.append(send(grad_packed[e]))
         if e + 1 < local:
-            full_b, grad_arrived[e], grad_packed[e + 1], middle_a = tie(
-                full_b, grad_arrived[e], grad_packed[e + 1], middle_a
-            )
+            grad_arrived[e], grad_packed[e + 1] = tie(grad_arrived[e], grad_packed[e + 1])
     middle_b, routed_b = middle_pass(full_b, out_full, tokens, half, gain, bias)
 
     routed = [routed_a, routed_b]
@@ -627,9 +602,7 @@
         sent.append(pair)
     summed[-1] = lax.psum_scatter(summed[-1], "col", scatter_dimension=0, tiled=True)
 
-    def place(i):
-        return (i % cols_all) * 2 + i // cols_all
-
+    step = min(256, length)
     order = [(g, f) for f in range(pieces) for g in range(len(sent))]
     back = {}
     grad_sent = []
@@ -668,7 +641,7 @@
             for e in range(f * local // pieces, (f + 1) * local // pieces):
                 *grad_weights, token = weigh(e, waits)
                 waits = [token]
-            whole = unpack(slots_by_group, rows, part, place, waits)
+            whole = unpack(slots_by_group, rows, step, waits)
             waits = [whole]
             grad_sent.append(lax.psum_scatter(whole, "col", scatter_dimension=0, tiled=True))
 
@@ -678,7 +651,7 @@
     back[order[-1]] = last
     homed = swap(homed, "row")
     returned = unpack(
-        [slots], [homed.reshape(experts * cap, depth // cols_all)], part, lambda i: i
+        [slots], [homed.reshape(experts * cap, depth // cols_all)], step
     ).astype(jnp.float32)
     columns = depth // cols_all
 
@@ -688,8 +661,9 @@
     middle_cols = jnp.concatenate([own_columns(middle_a), own_columns(middle_b)], axis=0)
     mixed = (middle_cols + gate * returned).astype(jnp.bfloat16)
     grad_gate = jnp.sum(own_columns(cotangent).astype(jnp.float32) * returned, axis=-1)
-    grad_gate = swap(grad_gate.reshape(2, cols_all, part).transpose(1, 0, 2), "col")
-    grad_gate = jnp.sum(grad_gate, axis=0).reshape(2 * part, 1)
+    grad_gate = swap(grad_gate.reshape(cols_all, part), "col")
+    grad_gate = jnp.sum(grad_gate, axis=0)[:, None]
+    mixed_full = lax.all_gather(mixed, "col", axis=0)
 
     own_gate, own_probs, own_select = own_of(gate), own_of(probs), own_of(select)
     grad_logits = (grad_gate * own_probs * (own_select - own_gate)).astype(jnp.bfloat16)
@@ -711,19 +685,11 @@
         "td,zdc->ztc", grad_attn, out_full, preferred_element_type=jnp.float32
     ).astype(jnp.bfloat16)
     grad_context = swap(grad_context, "col")
-    grad_context, mixed = tie(grad_context, mixed)
-    steps = relay_steps(mixed, "col")
-    grad_context = grad_context.reshape(cols_all, 2, part, width)
-    grad_context = grad_context.transpose(1, 0, 2, 3).reshape(2, half, width)
-
-
-    proj_b, *carried = attend_backward(
-        projected, grad_context[1], context_b, logsum_b, block, count
-    )
-    proj_b, *steps[0] = tie(proj_b, *steps[0])
-    proj_a = attend_backward(
-        projected, grad_context[0], context_a, logsum_a, block, 0, carried
-    )[0]
+    grad_context = grad_context.reshape(length, width)
+    context = jnp.concatenate([context_a, context_b], axis=0)
+    logsum = jnp.concatenate([logsum_a, logsum_b], axis=1)
+    grad_proj = attend_backward(projected, grad_context, context, logsum, block, 0)[0]
+    grad_proj, grad_attn, mixed_full = tie(grad_proj, grad_attn, mixed_full)
 
     def spread(grads):
         made = jnp.einsum("tc,dc->td", grads, qkv_full, preferred_element_type=jnp.float32)
@@ -731,21 +697,14 @@
             made.astype(jnp.bfloat16), "col", scatter_dimension=0, tiled=True
         ).astype(jnp.float32)
 
-    tied = steps[1] if len(steps) > 1 else []
-    proj_a, grad_attn, *tied[:] = tie(proj_a, grad_attn, *tied)
-    context_own = jnp.concatenate(
-        [lax.dynamic_slice_in_dim(v, col * part, part, 1) for v in (full_a, full_b)], axis=1
-    )
+    grad_normal = spread(grad_proj)
+    context_own = own(full_a, full_b, 1)
     grad_out = jnp.einsum("td,ztc->dzc", grad_attn, context_own, preferred_element_type=jnp.float32)
     plane = jnp.concatenate([grad_out.reshape(depth, cols_all * width), grad_router], axis=1)
     plane = swap(plane.astype(jnp.bfloat16).reshape(rows_all, share, -1), "row")
-    normal_b, normal_a = spread(proj_b), spread(proj_a)
-    normal_a, plane = tie(normal_a, plane)
-    for step in steps[2:]:
-        normal_b, *step[:] = tie(normal_b, *step)
-    grad_qkv = jnp.einsum(
-        "td,tc->dc", normal_in[:half], proj_a, preferred_element_type=jnp.float32
-    ) + jnp.einsum("td,tc->dc", normal_in[half:], proj_b, preferred_element_type=jnp.float32)
+    mixed_out = mixed_full.transpose(1, 0, 2).reshape(length, depth)
+    grad_qkv = jnp.einsum("td,tc->dc", normal_in, grad_proj, preferred_element_type=jnp.float32)
+    grad_normal, plane, mixed_out, grad_qkv = tie(grad_normal, plane, mixed_out, grad_qkv)
 
     plane = jnp.sum(plane.astype(jnp.float32), axis=0)
     router_share = plane[:, cols_all * width :].reshape(1, share, experts)
@@ -755,33 +714,18 @@
     plane = jnp.sum(swap(plane, "col").astype(jnp.float32), axis=0)
     out_share, router_share = plane[:, :width].T, plane[:, width:]
 
-    tokens_own = [lax.dynamic_slice_in_dim(v, col * part, part, 0) for v in (tokens[:half], tokens[half:])]
-    normed = [layer_stats(v.astype(jnp.float32)) for v in tokens_own]
-    finished = [None, None]
-    sums = [jnp.stack([gain_two, bias_two])]
-    for c in (1, 0):
-        grads = (normal_a, normal_b)[c]
-        own_normed, own_inverse = normed[c]
-        made = grad_middle[c * part : (c + 1) * part] + norm_back(
-            grads, own_normed, own_inverse, gains[0]
-        )
-        finished[c] = made.astype(jnp.bfloat16)
-        sums.append(
-            jnp.stack([jnp.sum(grads * own_normed, axis=0), jnp.sum(grads, axis=0)])
-        )
-        if c:
-            moves = relay_steps(finished[1], "col")
-            flat = [v for move in moves for v in move]
-            normal_a, *flat = tie(normal_a, *flat)
-            moves = list(zip(flat[0::2], flat[1::2]))
-    grad_tokens = jnp.concatenate(
-        [relay_join(finished[1], moves, "col", 0), lax.all_gather(finished[0], "col", axis=0, tiled=True)][::-1],
-        axis=0,
-    )
-    mixed_out = relay_join(mixed, steps, "col", 1)
-
-    small = jnp.concatenate([sums[1] + sums[2], sums[0]], axis=0)
-    small = swap(small.reshape(4, rows_all, share).transpose(1, 0, 2), "row")
+    own_normed, own_inverse = layer_stats(own_of(tokens).astype(jnp.float32))
+    grad_tokens = (
+        grad_middle + norm_back(grad_normal, own_normed, own_inverse, gains[0])
+    ).astype(jnp.bfloat16)
+    grad_tokens = lax.all_gather(grad_tokens, "col", axis=0, tiled=True)
+    small = [
+        jnp.sum(grad_normal * own_normed, axis=0),
+        jnp.sum(grad_normal, axis=0),
+        gain_two,
+        bias_two,
+    ]
+    small = swap(jnp.stack(small).reshape(4, rows_all, share).transpose(1, 0, 2), "row")
     small = jnp.sum(small, axis=0)
     small = jnp.sum(swap(jnp.broadcast_to(small[None], (cols_all, 4, share)), "col"), axis=0)
     qkv_share = swap(grad_qkv.astype(jnp.bfloat16).reshape(rows_all, share, -1), "row")

time: 876 us -> 826 us (0.943)
  starting transfers between devices: 123 us -> 83 us
  waiting for transfers between devices: 265 us -> 305 us
  local copies, waits for them, and re-layouts: 76.1 us -> 53 us
  other arithmetic: 57.3 us -> 41.8 us
    ppermute x12 -> x0, waiting for transfers between devices: 90.4 us -> none  [the longest x6 65.8 us: relay_steps(): right = lax.ppermute(right, axis, [(i, i + 1) for i in range(count - 1)])]
    all_to_all x21 -> x20, waiting for transfers between devices: 164 us -> 218 us  [swap(): return lax.all_to_all(blocks, axis, split_axis=0, concat_axis=0, tiled=True)]
    reduce_scatter x2 -> x1, waiting for transfers between devices: 0.01 us -> 41.6 us  [spread(): lax.psum_scatter(made.astype(jnp.bfloat16), 'col', scatter_dimension=0, t...]
    ppermute x12 -> x0, starting transfers between devices: 37.3 us -> none  [the longest x6 28.9 us: relay_steps(): right = lax.ppermute(right, axis, [(i, i + 1) for i in range(count - 1)])]
    all_gather x1 -> x3, waiting for transfers between devices: 1.67 us -> 22.5 us  [the longest x1 21.9 us: per_device(): grad_tokens = lax.all_gather(grad_tokens, 'col', axis=0, tiled=True)]
    dynamic_update_slice x7 -> x0, other arithmetic: 13.7 us -> none  [relay_join(): lax.dynamic_update_slice_in_dim(whole, piece, (me - k) % count * size, dim)]
    dynamic_slice x8 -> x0, local copies, waits for them, and re-layouts: 10.3 us -> none  [the longest x6 7.19 us: own(): lax.dynamic_slice_in_dim(v, col * part, part, 0)]
    slice x6 -> x0, local copies, waits for them, and re-layouts: 9.77 us -> none  [the longest x4 4.74 us: own_of(): return own(values[:half], values[half:])]
  transfers between devices with their start and end apart: 45 -> 33, of which waited for: 25 -> 21; matrix products, arithmetic and copies ran while one was open for 14% -> 12% of each run, Pallas kernels for 31% -> 32%
where the time goes in v5:
time: 826 us; the launch traced here: 819 us
  waiting for transfers between devices  305 us (37%)
  Pallas kernels  263 us (32%)
  starting transfers between devices  83 us (10%)
  local copies, waits for them, and re-layouts  53 us (6%)
  other arithmetic  41.8 us (5%)
  matrix products  38.1 us (5%)
  blocking collectives  20.4 us (2%)
  between operations  14.9 us (2%)
    all_to_all x20, waiting for transfers between devices, swap(): return lax.all_to_all(blocks, axis, split_axis=0, concat_axis=0, tiled=True)  218 us
    all_to_all x20, starting transfers between devices, swap(): return lax.all_to_all(blocks, axis, split_axis=0, concat_axis=0, tiled=True)  81.8 us
    pallas_call x4, Pallas kernels, expert_pass(): pl.pallas_call(functools.partial(expert_body, len(sent) + len(waits)), ou...  57.8 us
    pallas_call x4, Pallas kernels, pack(): pl.pallas_call(functools.partial(pack_body, base, step, each, len(rows)),...  53.9 us
    pallas_call x4, Pallas kernels, weight_pass(): pl.pallas_call(functools.partial(weight_body, len(sent) + len(waits)), ou...  46.9 us
    reduce_scatter x1, waiting for transfers between devices, spread(): lax.psum_scatter(made.astype(jnp.bfloat16), 'col', scatter_dimension=0, t...  41.6 us
    pallas_call x3, Pallas kernels, unpack(): pl.pallas_call(functools.partial(unpack_body, len(rows)), out_shape=jax.S...  36.3 us
    pallas_call x1, Pallas kernels, attend_backward(): pl.pallas_call(functools.partial(backward_body, block, first, len(carried...  31.4 us
  transfers between devices with their start and end apart: 33, of which 21 were waited for; matrix products, arithmetic and copies ran while one was open for 12% of the time, Pallas kernels for 32%

profile of v5, /device:TPU:0, one launch (start us, length us, event | category | flops | bytes accessed | tf_op | source)
XLA Modules:
  0.0 819.4 jit_solution(2876008411889783187)
XLA Ops:
  21.8 13.4 %pack.4 = (bf16[1024,1024]{1,0:T(8,128)(2,1)}, bf16[1024,1024]{1,0:T(8,128)(2,1)}) custom-call(s32[1,2048]{1,0:T(1,128)} %bitcast.135, bf16[2048,1024]{1,0:T(8,128)(2,1)} %rest_0_.3), custom_call_target="tpu_custom_call" | custom-call | flops 1048576 | bytes 1048576 | tf_op jit(solution)/shard_map/pack/pallas_call | solution.py:55
  68.9 15.9 %all-to-all-done.1 = bf16[8,128,1024]{2,1,0:T(8,128)(2,1)S(1)} async-done(((bf16[8,128,1024]{2,1,0:T(8,128)(2,1)}), bf16[8,128,1024]{2,1,0:T(8,128)(2,1)S(1)}, u32[]{:S(2)}, u32[]{:S(2)}) %all-to-all-start.1) | async-done | bytes 2097184 | tf_op jit(solution)/shard_map/all_to_all | solution.py:439
  89.8 13.5 %pack.5 = (bf16[1024,1024]{1,0:T(8,128)(2,1)}, bf16[1024,1024]{1,0:T(8,128)(2,1)}) custom-call(s32[1,2048]{1,0:T(1,128)} %bitcast.136, bf16[2048,1024]{1,0:T(8,128)(2,1)} %rest_0_.3, bf16[1024,256]{1,0:T(8,128)(2,1)} %get-tuple-element.109.rest_1_), custom_call_target="tpu_custom_call" | custom-call | flops 1048576 | bytes 1048576 | tf_op jit(solution)/shard_map/pack/pallas_call | solution.py:55
  103.4 14.3 %attend_forward.3 = (bf16[1024,256]{1,0:T(8,128)(2,1)}, f32[4,1024]{1,0:T(4,128)}) custom-call(bf16[2048,768]{1,0:T(8,128)(2,1)} %convolution_convert_fusion.1.q_ref.k_ref.v_ref.refs_0_.refs_4_.refs_5_, bf16[2048,768]{1,0:T(8,128)(2,1)} %convolution_convert_fusion.1.q_ref.k_ref.v_ref.refs_0_.refs_4_.refs_5_, ...), custom_call_target="tpu_custom_call" | custom-call | flops 262144 | bytes 262144 | tf_op jit(solution)/shard_map/attend_forward/pallas_call | solution.py:190
  123.8 26.1 %all-to-all-done.3 = bf16[8,128,1024]{2,1,0:T(8,128)(2,1)S(1)} async-done(((bf16[8,128,1024]{2,1,0:T(8,128)(2,1)}), bf16[8,128,1024]{2,1,0:T(8,128)(2,1)S(1)}, u32[]{:S(2)}, u32[]{:S(2)}) %all-to-all-start.3) | async-done | bytes 2097184 | tf_op jit(solution)/shard_map/all_to_all | solution.py:439
  164.8 14.3 %all-gather.16.cloned.1.call-done = bf16[4096,256]{1,0:T(8,128)(2,1)} async-done(((bf16[1024,256]{1,0:T(8,128)(2,1)}), bf16[4096,256]{1,0:T(8,128)(2,1)}) %all-gather.16.cloned.1.call-update) | async-done | bytes 2097168 | tf_op jit(solution)/shard_map/all_gather | solution.py:548
  198.3 18.9 %pack.6 = (bf16[1024,1024]{1,0:T(8,128)(2,1)}, bf16[1024,1024]{1,0:T(8,128)(2,1)}, bf16[1024,1024]{1,0:T(8,128)(2,1)}) custom-call(s32[1,2048]{1,0:T(1,128)} %bitcast.138, bf16[1024,1024]{1,0:T(8,128)(2,1)} %get-tuple-element.121.rest_0_, bf16[1024,1024]{1,0:T(8,128)(2,1)} %get-tuple-element.122.rest_1_), custom_call_target="tpu_custom_call" | custom-call | flops 1048576 | bytes 1048576 | tf_op jit(solution)/shard_map/pack/pallas_call | solution.py:55
  229.9 14.3 %expert_pass.4 = (bf16[4,1024,256]{2,1,0:T(8,128)(2,1)}, bf16[1024,1024]{1,0:T(8,128)(2,1)}, bf16[1024,1024]{1,0:T(8,128)(2,1)}, bf16[8,2,128,512]{3,2,1,0:T(8,128)(2,1)}, bf16[8,2,128,512]{3,2,1,0:T(8,128)(2,1)}) custom-call(bf16[1024,1024]{1,0:T(8,128)(2,1)} %bitcast.116, bf16[1024,1024]{1,0:T(8,128)(2,1)} %bitcast.114, bf16[4,1024,1024]{2,1,0:T(8,128)(2,1)} %win_ref.7, ...), custom_call_target="tpu_custom_call" | custom-call | flops 8589934592 | bytes 16777216 | tf_op jit(solution)/shard_map/expert_pass/pallas_call | solution.py:352
  244.3 12.2 %all-to-all-done.6 = bf16[8,128,1024]{2,1,0:T(8,128)(2,1)S(1)} async-done(((bf16[8,128,1024]{2,1,0:T(8,128)(2,1)}), bf16[8,128,1024]{2,1,0:T(8,128)(2,1)S(1)}, u32[]{:S(2)}, u32[]{:S(2)}) %all-to-all-start.6) | async-done | bytes 2097184 | tf_op jit(solution)/shard_map/all_to_all | solution.py:439
  261.5 14.3 %expert_pass.5 = (bf16[4,1024,256]{2,1,0:T(8,128)(2,1)}, bf16[1024,1024]{1,0:T(8,128)(2,1)}, bf16[1024,1024]{1,0:T(8,128)(2,1)}, bf16[8,2,128,512]{3,2,1,0:T(8,128)(2,1)}, bf16[8,2,128,512]{3,2,1,0:T(8,128)(2,1)}) custom-call(bf16[1024,1024]{1,0:T(8,128)(2,1)} %bitcast.102, ...), custom_call_target="tpu_custom_call", output_to_operand_aliasing={{3}: (4, {}), {4}: (5, {})} | custom-call | flops 8589934592 | bytes 16777216 | tf_op jit(solution)/shard_map/expert_pass/pallas_call | solution.py:352
  275.8 12.2 %all-to-all-done.7 = bf16[8,128,1024]{2,1,0:T(8,128)(2,1)S(1)} async-done(((bf16[8,128,1024]{2,1,0:T(8,128)(2,1)}), bf16[8,128,1024]{2,1,0:T(8,128)(2,1)S(1)}, u32[]{:S(2)}, u32[]{:S(2)}) %all-to-all-start.7) | async-done | bytes 2097184 | tf_op jit(solution)/shard_map/all_to_all | solution.py:439
  293.7 14.8 %expert_pass.6 = (bf16[4,1024,256]{2,1,0:T(8,128)(2,1)}, bf16[1024,1024]{1,0:T(8,128)(2,1)}, bf16[1024,1024]{1,0:T(8,128)(2,1)}, bf16[8,2,128,512]{3,2,1,0:T(8,128)(2,1)}, bf16[8,2,128,512]{3,2,1,0:T(8,128)(2,1)}) custom-call(bf16[1024,1024]{1,0:T(8,128)(2,1)} %bitcast.100, bf16[1024,1024]{1,0:T(8,128)(2,1)} %bitcast.96, bf16[4,1024,1024]{2,1,0:T(8,128)(2,1)} %win_ref.7, ...), custom_call_target="tpu_custom_call" | custom-call | flops 8589934592 | bytes 16777216 | tf_op jit(solution)/shard_map/expert_pass/pallas_call | solution.py:352
  324.1 14.3 %expert_pass.7 = (bf16[4,1024,256]{2,1,0:T(8,128)(2,1)}, bf16[1024,1024]{1,0:T(8,128)(2,1)}, bf16[1024,1024]{1,0:T(8,128)(2,1)}, bf16[8,2,128,512]{3,2,1,0:T(8,128)(2,1)}, bf16[8,2,128,512]{3,2,1,0:T(8,128)(2,1)}) custom-call(bf16[1024,1024]{1,0:T(8,128)(2,1)} %bitcast.27.x_ref, ...), custom_call_target="tpu_custom_call", output_to_operand_aliasing={{3}: (4, {}), {4}: (5, {})} | custom-call | flops 8589934592 | bytes 16777216 | tf_op jit(solution)/shard_map/expert_pass/pallas_call | solution.py:352
  338.4 12.1 %all-to-all-done.9 = bf16[8,2,128,512]{3,2,1,0:T(8,128)(2,1)S(1)} async-done(((bf16[8,2,128,512]{3,2,1,0:T(8,128)(2,1)}), bf16[8,2,128,512]{3,2,1,0:T(8,128)(2,1)S(1)}, u32[]{:S(2)}, u32[]{:S(2)}) %all-to-all-start.9) | async-done | bytes 2097184 | tf_op jit(solution)/shard_map/all_to_all | solution.py:439
  389.4 13.7 %unpack.3.rest_2_ = bf16[2048,512]{1,0:T(8,128)(2,1)} custom-call(s32[2048,1]{1,0:T(8,128)} %copy.139.refs_0_, s32[2048,1]{1,0:T(8,128)} %copy.140.refs_1_, bf16[2048,512]{1,0:T(8,128)(2,1)} %bitcast.118, bf16[2048,512]{1,0:T(8,128)(2,1)} %bitcast.29.refs_3_, f32[8,128]{1,0:T(8,128)} %get-tuple-element.167.refs_4_), custom_call_target="tpu_custom_call" | custom-call | flops 8589934592 | bytes 6291456 | tf_op jit(solution)/shard_map/unpack/pallas_call | solution.py:89
  403.2 12.8 %all-to-all-done.11 = bf16[8,2,128,512]{3,2,1,0:T(8,128)(2,1)S(1)} async-done(((bf16[8,2,128,512]{3,2,1,0:T(8,128)(2,1)}), bf16[8,2,128,512]{3,2,1,0:T(8,128)(2,1)S(1)}, u32[]{:S(2)}, u32[]{:S(2)}) %all-to-all-start.11) | async-done | bytes 2097184 | tf_op jit(solution)/shard_map/all_to_all | solution.py:439
  448.3 13.5 %unpack.4 = bf16[2048,512]{1,0:T(8,128)(2,1)} custom-call(s32[2048,1]{1,0:T(8,128)} %copy.139.refs_0_, s32[2048,1]{1,0:T(8,128)} %copy.140.refs_1_, bf16[2048,512]{1,0:T(8,128)(2,1)} %bitcast.119, bf16[2048,512]{1,0:T(8,128)(2,1)} %bitcast.31.refs_3_, f32[8,128]{1,0:T(8,128)} %get-tuple-element.182.refs_4_), custom_call_target="tpu_custom_call" | custom-call | flops 8589934592 | bytes 6291456 | tf_op jit(solution)/shard_map/unpack/pallas_call | solution.py:89
  478.2 18.8 %all-to-all-done.13 = bf16[8,4,128,256]{3,2,1,0:T(8,128)(2,1)} async-done(((bf16[8,4,128,256]{3,2,1,0:T(8,128)(2,1)}), bf16[8,4,128,256]{3,2,1,0:T(8,128)(2,1)}, u32[]{:S(2)}, u32[]{:S(2)}) %all-to-all-start.13) | async-done | bytes 2097184 | tf_op jit(solution)/shard_map/all_to_all | solution.py:439
  541.2 53.2 %all-to-all-done.15 = bf16[4,512,256]{1,2,0:T(8,128)(2,1)} async-done(((bf16[4,512,256]{1,2,0:T(8,128)(2,1)}), bf16[4,512,256]{1,2,0:T(8,128)(2,1)}, u32[]{:S(2)}, u32[]{:S(2)}) %all-to-all-start.15) | async-done | bytes 1048608 | tf_op jit(solution)/shard_map/all_to_all | solution.py:439
  597.0 31.4 %attend_backward.1 = bf16[2048,768]{1,0:T(8,128)(2,1)} custom-call(bf16[2048,768]{1,0:T(8,128)(2,1)} %convolution_convert_fusion.1.q_ref.k_ref.v_ref.refs_0_.refs_4_.refs_5_, bf16[2048,256]{1,0:T(8,128)(2,1)} %bitcast.127, bf16[2048,256]{1,0:T(8,128)(2,1)} %pad_maximum_fusion.2.refs_2_, f32[4,2048]{1,0:T(4,128)} %pad_maximum_fusion.6.refs_3_, ...), custom_call_target="tpu_custom_call" | custom-call | flops 21474836480 | bytes 8388608 | tf_op jit(solution)/shard_map/attend_backward/pallas_call | solution.py:282
  671.8 41.6 %reduce-scatter.20.cloned.1.call-done = bf16[512,1024]{1,0:T(8,128)(2,1)} async-done(((bf16[2048,1024]{1,0:T(8,128)(2,1)}), bf16[512,1024]{1,0:T(8,128)(2,1)}) %reduce-scatter.20.cloned.1.call-update) | async-done | bytes 1048592 | tf_op jit(solution)/shard_map/reduce_scatter | solution.py:696
  739.8 20.4 %all_to_all.109 = bf16[4,128,288]{1,2,0:T(8,128)(2,1)S(1)} all-to-all(bf16[4,128,288]{1,2,0:T(8,128)(2,1)S(1)} %pad_maximum_fusion.3), channel_id=1, replica_groups=mesh['row'=8,'col'=4] {'col'}, dimensions={0} | all-to-all | bytes 589824 | tf_op jit(solution)/shard_map/all_to_all | solution.py:439
  766.2 18.5 %all-to-all-done.17 = bf16[8,128,768]{2,1,0:T(8,128)(2,1)S(1)} async-done(((bf16[8,128,768]{2,1,0:T(8,128)(2,1)}), bf16[8,128,768]{2,1,0:T(8,128)(2,1)S(1)}, u32[]{:S(2)}, u32[]{:S(2)}) %all-to-all-start.17) | async-done | bytes 1572896 | tf_op jit(solution)/shard_map/all_to_all | solution.py:439
  786.1 21.9 %all-gather.14.cloned.1.call-done = bf16[2048,1024]{1,0:T(8,128)(2,1)} async-done(((bf16[512,1024]{1,0:T(8,128)(2,1)}), bf16[2048,1024]{1,0:T(8,128)(2,1)}) %all-gather.14.cloned.1.call-update) | async-done | bytes 4194320 | tf_op jit(solution)/shard_map/all_gather | solution.py:721
  (241 shorter events, 347.7 us)
Async XLA Ops:
  7.2 34.1 %all-gather.10.cloned.1.call-start = ((), (), s32[]{:S(2)}) async-start(), calls=%async_computation.28 | async-start | bytes 2064384 | tf_op jit(solution)/shard_map/all_gather | solution.py:502
  21.2 82.2 %all-gather.12.cloned.1.call-start = ((), (), s32[]{:S(2)}) async-start(), calls=%async_computation.29 | async-start | bytes 2359296 | tf_op jit(solution)/shard_map/all_gather | solution.py:542
  46.2 38.6 %all-to-all-start.1 = ((bf16[8,128,1024]{2,1,0:T(8,128)(2,1)}), bf16[8,128,1024]{2,1,0:T(8,128)(2,1)S(1)}, u32[]{:S(2)}, u32[]{:S(2)}) async-start(bf16[8,128,1024]{2,1,0:T(8,128)(2,1)} %bitcast.122), calls=%async_computation.1 | async-start | bytes 4194304 | tf_op jit(solution)/shard_map/all_to_all | solution.py:439
  49.8 107.5 %all-gather.18.cloned.1.call-start = ((), (), s32[]{:S(2)}) async-start(), calls=%async_computation.39 | async-start | bytes 2621440 | tf_op jit(solution)/shard_map/all_gather | solution.py:535
  86.2 31.5 %all-to-all-start.2 = ((bf16[8,128,1024]{2,1,0:T(8,128)(2,1)}), bf16[8,128,1024]{2,1,0:T(8,128)(2,1)S(1)}, u32[]{:S(2)}, u32[]{:S(2)}) async-start(bf16[8,128,1024]{2,1,0:T(8,128)(2,1)} %bitcast.121), calls=%async_computation.2 | async-start | bytes 4194304 | tf_op jit(solution)/shard_map/all_to_all | solution.py:439
  119.1 30.7 %all-to-all-start.3 = ((bf16[8,128,1024]{2,1,0:T(8,128)(2,1)}), bf16[8,128,1024]{2,1,0:T(8,128)(2,1)S(1)}, u32[]{:S(2)}, u32[]{:S(2)}) async-start(bf16[8,128,1024]{2,1,0:T(8,128)(2,1)} %bitcast.124), calls=%async_computation.3 | async-start | bytes 4194304 | tf_op jit(solution)/shard_map/all_to_all | solution.py:439
  123.2 55.9 %all-gather.16.cloned.1.call-start = ((), (), s32[]{:S(2)}) async-start(), calls=%async_computation.38 | async-start | bytes 2621440 | tf_op jit(solution)/shard_map/all_gather | solution.py:548
  151.2 43.5 %all-to-all-start.4 = ((bf16[8,128,1024]{2,1,0:T(8,128)(2,1)}), bf16[8,128,1024]{2,1,0:T(8,128)(2,1)}, u32[]{:S(2)}, u32[]{:S(2)}) async-start(bf16[8,128,1024]{2,1,0:T(8,128)(2,1)} %bitcast.107), calls=%async_computation.4 | async-start | bytes 4194304 | tf_op jit(solution)/shard_map/all_to_all | solution.py:439
  229.9 94.2 %reduce-scatter.8.cloned.1.call-start = ((), (), s32[]{:S(2)}) async-start(), calls=%async_computation.30 | async-start | bytes 2621440 | tf_op jit(solution)/shard_map/reduce_scatter | solution.py:579
  261.4 200.5 %reduce-scatter.14.cloned.1.call-start = ((), (), s32[]{:S(2)}) async-start(), calls=%async_computation.33 | async-start | bytes 2621440 | tf_op jit(solution)/shard_map/reduce_scatter | solution.py:579
  289.3 31.0 %all-to-all-start.8 = ((bf16[8,128,1024]{2,1,0:T(8,128)(2,1)}), bf16[8,128,1024]{2,1,0:T(8,128)(2,1)}, u32[]{:S(2)}, u32[]{:S(2)}) async-start(bf16[8,128,1024]{2,1,0:T(8,128)(2,1)} %bitcast.120), calls=%async_computation.8 | async-start | bytes 4194304 | tf_op jit(solution)/shard_map/all_to_all | solution.py:439
  293.7 168.2 %reduce-scatter.16.cloned.1.call-start = ((), (), s32[]{:S(2)}) async-start(), calls=%async_computation.34 | async-start | bytes 2621440 | tf_op jit(solution)/shard_map/reduce_scatter | solution.py:579
  324.0 137.9 %reduce-scatter.18.cloned.1.call-start = ((), (), s32[]{:S(2)}) async-start(), calls=%async_computation.35 | async-start | bytes 2621440 | tf_op jit(solution)/shard_map/reduce_scatter | solution.py:603
  352.0 33.3 %all-to-all-start.10 = ((bf16[8,2,128,512]{3,2,1,0:T(8,128)(2,1)}), bf16[8,2,128,512]{3,2,1,0:T(8,128)(2,1)}, u32[]{:S(2)}, u32[]{:S(2)}) async-start(bf16[8,2,128,512]{3,2,1,0:T(8,128)(2,1)} %get-tuple-element.159), calls=%async_computation.11 | async-start | bytes 4194304 | tf_op jit(solution)/shard_map/all_to_all | solution.py:439
  385.3 30.7 %all-to-all-start.11 = ((bf16[8,2,128,512]{3,2,1,0:T(8,128)(2,1)}), bf16[8,2,128,512]{3,2,1,0:T(8,128)(2,1)S(1)}, u32[]{:S(2)}, u32[]{:S(2)}) async-start(bf16[8,2,128,512]{3,2,1,0:T(8,128)(2,1)} %get-tuple-element.170), calls=%async_computation.13 | async-start | bytes 4194304 | tf_op jit(solution)/shard_map/all_to_all | solution.py:439
  389.3 134.2 %reduce-scatter.10.cloned.1.call-start = ((), (), s32[]{:S(2)}) async-start(), calls=%async_computation.31 | async-start | bytes 2621440 | tf_op jit(solution)/shard_map/reduce_scatter | solution.py:646
  417.3 31.0 %all-to-all-start.12 = ((bf16[8,2,128,512]{3,2,1,0:T(8,128)(2,1)}), bf16[8,2,128,512]{3,2,1,0:T(8,128)(2,1)}, u32[]{:S(2)}, u32[]{:S(2)}) async-start(bf16[8,2,128,512]{3,2,1,0:T(8,128)(2,1)} %get-tuple-element.172), calls=%async_computation.14 | async-start | bytes 4194304 | tf_op jit(solution)/shard_map/all_to_all | solution.py:439
  421.7 103.4 %reduce-scatter.12.cloned.1.call-start = ((), (), s32[]{:S(2)}) async-start(), calls=%async_computation.32 | async-start | bytes 2621440 | tf_op jit(solution)/shard_map/reduce_scatter | solution.py:646
  465.9 31.2 %all-to-all-start.13 = ((bf16[8,4,128,256]{3,2,1,0:T(8,128)(2,1)}), bf16[8,4,128,256]{3,2,1,0:T(8,128)(2,1)}, u32[]{:S(2)}, u32[]{:S(2)}) async-start(bf16[8,4,128,256]{3,2,1,0:T(8,128)(2,1)} %pad_maximum_fusion.1), calls=%async_computation.19 | async-start | bytes 4194304 | tf_op jit(solution)/shard_map/all_to_all | solution.py:439
  470.4 158.7 %all-gather.20.cloned.1.call-start = ((), (), s32[]{:S(2)}) async-start(), calls=%async_computation.40 | async-start | bytes 5242880 | tf_op jit(solution)/shard_map/all_gather | solution.py:666
  535.1 59.3 %all-to-all-start.15 = ((bf16[4,512,256]{1,2,0:T(8,128)(2,1)}), bf16[4,512,256]{1,2,0:T(8,128)(2,1)}, u32[]{:S(2)}, u32[]{:S(2)}) async-start(bf16[4,512,256]{1,2,0:T(8,128)(2,1)} %fusion.25), calls=%async_computation.21 | async-start | bytes 2097152 | tf_op jit(solution)/shard_map/all_to_all | solution.py:439
  539.5 174.0 %reduce-scatter.20.cloned.1.call-start = ((), (), s32[]{:S(2)}) async-start(), calls=%async_computation.36 | async-start | bytes 5242880 | tf_op jit(solution)/shard_map/reduce_scatter | solution.py:696
  652.6 62.3 %all-to-all-start.16 = ((bf16[8,128,1056]{1,2,0:T(8,128)(2,1)}), bf16[8,128,1056]{1,2,0:T(8,128)(2,1)}, u32[]{:S(2)}, u32[]{:S(2)}) async-start(bf16[8,128,1056]{1,2,0:T(8,128)(2,1)} %copy.153), calls=%async_computation.23 | async-start | bytes 4325376 | tf_op jit(solution)/shard_map/all_to_all | solution.py:439
  656.9 151.0 %all-gather.14.cloned.1.call-start = ((), (), s32[]{:S(2)}) async-start(), calls=%async_computation.37 | async-start | bytes 5242880 | tf_op jit(solution)/shard_map/all_gather | solution.py:721
  (47 other events, 347.3 us)
Sparse Core Ops, SparseCore 0:
  11.8 29.4 all-gather.9
  43.8 41.0 all-gather.11
  86.4 46.5 all-gather.17
  134.4 44.6 all-gather.15
  256.6 40.7 reduce-scatter.7
  299.7 43.1 reduce-scatter.13
  345.2 43.1 reduce-scatter.15
  390.9 43.1 reduce-scatter.17
  436.4 43.0 reduce-scatter.9
  481.7 43.3 reduce-scatter.11
  526.7 102.3 all-gather.19
  637.0 76.3 reduce-scatter.19
  720.4 87.5 all-gather.13

commit v6 on v5

--- a/solution.py
+++ b/solution.py
@@ -323,60 +323,63 @@
     slope = 0.5 * (1.0 + bent) + 0.5 * hidden * (1.0 - bent * bent) * (
         ROOT * (1.0 + 3.0 * CUBE * square)
     )
-    active_ref[...] = active
+    active_ref[...] = active.reshape(active_ref.shape)
     parts = out_ref.shape[0]
     wide = depth // parts
     made = dot(active, wback_ref[...], NN).astype(jnp.bfloat16)
     for j in range(parts):
         out_ref[j] = made[:, j * wide : (j + 1) * wide]
-    grad_active = dot(gy_ref[...], wback_ref[...], NT)
+    grad_active = dot(gy_ref[...].reshape(rows, depth), wback_ref[...], NT)
     grad_hidden = (grad_active * slope).astype(jnp.bfloat16)
-    slope_ref[...] = grad_hidden
+    slope_ref[...] = grad_hidden.reshape(slope_ref.shape)
     back = dot(grad_hidden, win_ref[...], NT).astype(jnp.bfloat16)
     wide = depth // len(sent)
     for j, ref in enumerate(sent):
         ref[...] = back[:, j * wide : (j + 1) * wide].reshape(ref.shape)
 
 
-def expert_pass(e, cap, x, grad_y, w_in, w_back, sent, members, parts, pieces, waits=()):
-    rows, depth = x.shape
+def expert_pass(chunk, x, grad_y, w_in, w_back, kept, sent, members, parts, pieces, waits=()):
+    e, low, size = chunk
+    sources, cap, depth = grad_y.shape
+    rows = sources * size
     width = w_in.shape[2]
-    sources = rows // cap
     step = min(256, rows)
-    group = step // cap
-    sent = list(sent or [])
+    group = step // size
+    at = low // size
+    given = [*kept, *sent]
+    aliases = {4 + j: (1 if kept else 3) + j for j in range(len(given))}
+    keep = jax.ShapeDtypeStruct((sources, cap, width), jnp.bfloat16)
+    keep_spec = pl.BlockSpec((group, size, width), lambda i: (i, at, 0))
     piece = jax.ShapeDtypeStruct((sources, members, cap, depth // pieces), jnp.bfloat16)
     piece_spec = pl.BlockSpec(
-        (group, None, cap, depth // pieces), lambda i: (i, e % members, 0, 0)
+        (group, None, size, depth // pieces), lambda i: (i, e % members, at, 0)
     )
     made = pl.pallas_call(
-        functools.partial(expert_body, len(sent) + len(waits)),
-        out_shape=(
-            jax.ShapeDtypeStruct((parts, rows, depth // parts), jnp.bfloat16),
-            jax.ShapeDtypeStruct((rows, width), jnp.bfloat16),
-            jax.ShapeDtypeStruct((rows, width), jnp.bfloat16),
-        )
+        functools.partial(expert_body, len(given) + len(waits)),
+        out_shape=(jax.ShapeDtypeStruct((parts, rows, depth // parts), jnp.bfloat16), keep, keep)
         + (piece,) * pieces,
         grid=(rows // step,),
         in_specs=[
             pl.BlockSpec((step, depth), lambda i: (i, 0)),
-            pl.BlockSpec((step, depth), lambda i: (i, 0)),
+            pl.BlockSpec((group, size, depth), lambda i: (i, at, 0)),
             pl.BlockSpec((None, depth, width), lambda i: (e, 0, 0)),
             pl.BlockSpec((None, width, depth), lambda i: (e, 0, 0)),
         ]
-        + [pl.BlockSpec(memory_space=pl.ANY)] * (len(sent) + len(waits)),
+        + [pl.BlockSpec(memory_space=pl.ANY)] * (len(given) + len(waits)),
         out_specs=(
             pl.BlockSpec((parts, step, depth // parts), lambda i: (0, i, 0)),
-            pl.BlockSpec((step, width), lambda i: (i, 0)),
-            pl.BlockSpec((step, width), lambda i: (i, 0)),
+            keep_spec,
+            keep_spec,
         )
         + (piece_spec,) * pieces,
-        input_output_aliases={4 + j: 3 + j for j in range(len(sent))},
+        input_output_aliases=aliases,
         compiler_params=params("arbitrary"),
         name="expert_pass",
-        cost_estimate=cost(8 * rows * depth * width, 4 * width * depth + 12 * rows * depth, rows * width),
-    )(x, grad_y, w_in, w_back, *sent, *waits)
-    return made[0], made[1], made[2], made[3:]
+        cost_estimate=cost(
+            8 * rows * depth * width, 4 * width * depth + 12 * rows * depth, rows * width
+        ),
+    )(x, grad_y, w_in, w_back, *given, *waits)
+    return made[0], made[1:3], list(made[3:])
 
 
 def weight_body(given, x_ref, gy_ref, router_ref, pick_ref, active_ref, slope_ref, *rest):
@@ -441,6 +444,13 @@
 
 def tie(*values):
     return lax.optimization_barrier(values)
+
+
+def row_stats(values):
+    mean = jnp.mean(values, axis=-1, keepdims=True)
+    centered = values - mean
+    variance = jnp.mean(centered * centered, axis=-1, keepdims=True)
+    return (mean, lax.rsqrt(variance + EPSILON))
 
 
 def layer_stats(values):
@@ -500,6 +510,7 @@
     stacked = w_qkv.transpose(1, 0, 2).reshape(share, 3 * width)
     weights = jnp.concatenate([stacked, w_router, ln_gains.T, ln_biases.T], axis=1)
     weights = lax.all_gather(weights, "row", axis=0, tiled=True)
+    mean_one, inverse_one = row_stats(tokens.astype(jnp.float32))
 
     chosen, ranks, select = slot_layout(expert_ids, experts, cap)
     out_block, ranks = tie(w_out.T, ranks)
@@ -518,30 +529,35 @@
 
     early = min(2, local)
     grad_packed = list(pack(slots_by_local, [cotangent], 0, block_rows, early))
-    weights, grad_packed[0], out_block = tie(weights, grad_packed[0], out_block)
-    grad_arrived = [send(grad_packed[0])]
+    weights, grad_packed[0], out_block, mean_one, inverse_one = tie(
+        weights, grad_packed[0], out_block, mean_one, inverse_one
+    )
     qkv_full = weights[:, : 3 * width]
     router_full = weights[:, 3 * width : 3 * width + experts]
     norms = weights[:, 3 * width + experts :].astype(jnp.float32).T
     gains, biases = norms[0:2], norms[2:4]
 
     resid_in = tokens.astype(jnp.float32)
-    normed_one, inverse_one = layer_stats(resid_in)
+    normed_one = (resid_in - mean_one) * inverse_one
     normal_in = (normed_one * gains[0] + biases[0]).astype(jnp.bfloat16)
     projected = jnp.dot(normal_in, qkv_full, preferred_element_type=jnp.float32).astype(jnp.bfloat16)
 
     count = half // block
     context_a, logsum_a = attend_forward(projected, tuple(range(count)), block)
+    context_a, grad_packed[0] = tie(context_a, grad_packed[0])
     full_a = lax.all_gather(context_a, "col", axis=0)
+    grad_arrived = [send(grad_packed[0])]
+    later = [context_a]
+    if local > early:
+        later = pack(
+            slots_by_local, [cotangent], early * block_rows, block_rows, local - early, later
+        )
+        grad_packed += later
     grad_arrived[0], *grad_packed[1:] = tie(grad_arrived[0], *grad_packed[1:])
-    grad_arrived += [send(p) for p in grad_packed[1:]]
-    if local > early:
-        grad_packed += pack(
-            slots_by_local, [cotangent], early * block_rows, block_rows, local - early, [context_a]
-        )
+    grad_arrived += [send(p) for p in grad_packed[1:early]]
     out_full = lax.all_gather(out_block, "row", axis=1, tiled=True)
     context_b, logsum_b = attend_forward(
-        projected, tuple(range(count, 2 * count)), block, [grad_packed[-1], out_full]
+        projected, tuple(range(count, 2 * count)), block, [later[-1], out_full]
     )
     context_b, *both = tie(context_b, *grad_arrived[1:], *grad_packed[early:])
     grad_arrived[1:], grad_packed[early:] = both[: len(grad_arrived) - 1], both[len(grad_arrived) - 1 :]
@@ -556,9 +572,17 @@
     middle_b, routed_b = middle_pass(full_b, out_full, tokens, half, gain, bias)
 
     routed = [routed_a, routed_b]
-    packed = list(pack(slots_by_local, routed, 0, block_rows, 1))
-    if local > 1:
-        packed += pack(slots_by_local, routed, block_rows, block_rows, local - 1)
+    short = cap // 2
+    chunks = [(0, 0, short), (0, short, short)] + [(e, 0, cap) for e in range(1, local)]
+    split = (ranks // short * rows_all + chosen // local) * short + ranks % short
+    slots_by_chunk = jnp.where(chosen % local == 0, split, slots_by_local)
+
+    def pack_chunk(k, waits):
+        e, low, size = chunks[k]
+        base = (e * cap + low) * rows_all
+        return pack(slots_by_chunk, routed, base, size * rows_all, 1, waits)[0]
+
+    packed = [pack_chunk(k, []) for k in range(min(3, len(chunks)))]
     packed[0], grad_arrived[-1] = tie(packed[0], grad_arrived[-1])
 
     def route(rows):
@@ -568,39 +592,52 @@
     probs = jax.nn.softmax(logits, axis=-1)
     gate = jnp.sum(probs * select, axis=-1, keepdims=True)
 
-    arrived, summed, active, slope, sent = [], [], [], [], []
-    for e in range(local):
-        arrived.append(send(packed[e]))
-        if e + 1 < local:
-            packed[e + 1], arrived[e] = tie(packed[e + 1], arrived[e])
-        if e:
-            then = packed[e + 1] if e + 1 < local else sent[0][0]
-            then, summed[e - 1], arrived[e] = tie(then, summed[e - 1], arrived[e])
-            summed[e - 1] = lax.psum_scatter(
-                summed[e - 1], "col", scatter_dimension=0, tiled=True
+    arrived, summed, kept, sent = [], [], [], []
+    final = len(chunks) - 1
+    for k, (e, low, size) in enumerate(chunks):
+        moved = swap(packed[k].reshape(rows_all, size, depth), "row")
+        arrived.append(moved.reshape(rows_all * size, depth))
+        if k < final:
+            packed[k + 1], arrived[k] = tie(packed[k + 1], arrived[k])
+        if k:
+            then = packed[k + 1] if k < final else sent[0][0]
+            then, summed[k - 1], arrived[k] = tie(then, summed[k - 1], arrived[k])
+            summed[k - 1] = lax.psum_scatter(
+                summed[k - 1], "col", scatter_dimension=0, tiled=True
             )
-            if e + 1 < local:
-                packed[e + 1] = then
+            if k < final:
+                packed[k + 1] = then
             else:
-                sent[0] = (then, *sent[0][1:])
-        made, kept, grads, pair = expert_pass(
-            e,
-            cap,
-            arrived[e],
-            grad_arrived[e],
+                sent[0][0] = then
+        waits = packed[2:3] if k == 0 else summed[:1] if k == final else []
+        made, both, pair = expert_pass(
+            chunks[k],
+            arrived[k],
+            grad_arrived[e].reshape(rows_all, cap, depth),
             w_in,
             w_back,
-            sent.pop() if e % members else None,
+            kept.pop() if low else [],
+            sent.pop() if low or e % members else [],
             members,
             cols_all,
             pieces,
-            packed[-1:] if e == 0 else summed[e - 3 : e - 2] if e > 2 else [],
+            waits,
         )
-        active.append(kept)
-        slope.append(grads)
+        kept.append(both)
         summed.append(made)
         sent.append(pair)
+        if k + 3 <= final:
+            packed.append(pack_chunk(k + 3, [made]))
     summed[-1] = lax.psum_scatter(summed[-1], "col", scatter_dimension=0, tiled=True)
+    active = [v[0].reshape(block_rows, -1) for v in kept]
+    slope = [v[1].reshape(block_rows, -1) for v in kept]
+
+    def joined(values):
+        first = [v.reshape(rows_all, short, -1) for v in values[:2]]
+        whole = [v.reshape(rows_all, cap, -1) for v in values[2:]]
+        return [jnp.concatenate(first, axis=1)] + whole
+
+    arrived = [v.reshape(block_rows, depth) for v in joined(arrived)]
 
     step = min(256, length)
     order = [(g, f) for f in range(pieces) for g in range(len(sent))]
@@ -646,7 +683,7 @@
             grad_sent.append(lax.psum_scatter(whole, "col", scatter_dimension=0, tiled=True))
 
     grad_in, grad_back = grad_weights
-    homed = jnp.stack([v.reshape(rows_all, cap, depth // cols_all) for v in summed], axis=1)
+    homed = jnp.stack(joined(summed), axis=1)
     homed, last = tie(homed, last)
     back[order[-1]] = last
     homed = swap(homed, "row")

time: 826 us -> 833 us (level)
  Pallas kernels: 263 us -> 277 us
  waiting for transfers between devices: 305 us -> 294 us
    pallas_call x4 -> x7, Pallas kernels: 53.9 us -> 63.1 us  [pack(): pl.pallas_call(functools.partial(pack_body, base, step, each, len(rows)),...]
    all_to_all x20 -> x21, starting transfers between devices: 81.8 us -> 86.4 us  [swap(): return lax.all_to_all(blocks, axis, split_axis=0, concat_axis=0, tiled=True)]
    pallas_call x4 -> x5, Pallas kernels: 57.8 us -> 61.5 us  [expert_pass(): pl.pallas_call(functools.partial(expert_body, len(given) + len(waits)), o...]
    unnamed x84 -> x90, local copies, waits for them, and re-layouts: 25.4 us -> 23.5 us
    all_to_all x20 -> x21, waiting for transfers between devices: 218 us -> 217 us  [swap(): return lax.all_to_all(blocks, axis, split_axis=0, concat_axis=0, tiled=True)]
  transfers between devices with their start and end apart: 33 -> 35, of which waited for: 21 -> 20; matrix products, arithmetic and copies ran while one was open for 12% -> 12% of each run, Pallas kernels for 32% -> 33%
where the time goes in v6:
time: 833 us; the launch traced here: 826 us
  waiting for transfers between devices  294 us (35%)
  Pallas kernels  277 us (33%)
  starting transfers between devices  87 us (10%)
  local copies, waits for them, and re-layouts  50.8 us (6%)
  other arithmetic  44.6 us (5%)
  matrix products  38.1 us (5%)
  blocking collectives  20.4 us (2%)
  between operations  14.9 us (2%)
    all_to_all x21, waiting for transfers between devices, swap(): return lax.all_to_all(blocks, axis, split_axis=0, concat_axis=0, tiled=True)  217 us
    all_to_all x21, starting transfers between devices, swap(): return lax.all_to_all(blocks, axis, split_axis=0, concat_axis=0, tiled=True)  86.4 us
    pallas_call x7, Pallas kernels, pack(): pl.pallas_call(functools.partial(pack_body, base, step, each, len(rows)),...  63.1 us
    pallas_call x5, Pallas kernels, expert_pass(): pl.pallas_call(functools.partial(expert_body, len(given) + len(waits)), o...  61.5 us
    pallas_call x4, Pallas kernels, weight_pass(): pl.pallas_call(functools.partial(weight_body, len(sent) + len(waits)), ou...  47.2 us
    reduce_scatter x1, waiting for transfers between devices, spread(): lax.psum_scatter(made.astype(jnp.bfloat16), 'col', scatter_dimension=0, t...  44.4 us
    pallas_call x3, Pallas kernels, unpack(): pl.pallas_call(functools.partial(unpack_body, len(rows)), out_shape=jax.S...  36.2 us
    pallas_call x1, Pallas kernels, attend_backward(): pl.pallas_call(functools.partial(backward_body, block, first, len(carried...  31.7 us
  transfers between devices with their start and end apart: 35, of which 20 were waited for; matrix products, arithmetic and copies ran while one was open for 12% of the time, Pallas kernels for 33%

profile of v6, /device:TPU:0, one launch (start us, length us, event | category | flops | bytes accessed | tf_op | source)
XLA Modules:
  0.0 826.3 jit_solution(2150892674600461044)
XLA Ops:
  26.7 13.8 %pack.7 = (bf16[1024,1024]{1,0:T(8,128)(2,1)}, bf16[1024,1024]{1,0:T(8,128)(2,1)}) custom-call(s32[1,2048]{1,0:T(1,128)} %bitcast.177, bf16[2048,1024]{1,0:T(8,128)(2,1)} %rest_0_.3), custom_call_target="tpu_custom_call" | custom-call | flops 1048576 | bytes 1048576 | tf_op jit(solution)/shard_map/pack/pallas_call | solution.py:55
  64.3 13.4 %pack.8 = (bf16[1024,1024]{1,0:T(8,128)(2,1)}, bf16[1024,1024]{1,0:T(8,128)(2,1)}) custom-call(s32[1,2048]{1,0:T(1,128)} %bitcast.178, bf16[2048,1024]{1,0:T(8,128)(2,1)} %rest_0_.3, bf16[1024,256]{1,0:T(8,128)(2,1)} %get-tuple-element.126.rest_1_), custom_call_target="tpu_custom_call" | custom-call | flops 1048576 | bytes 1048576 | tf_op jit(solution)/shard_map/pack/pallas_call | solution.py:55
  77.7 15.9 %all-to-all-done.1 = bf16[8,128,1024]{2,1,0:T(8,128)(2,1)S(1)} async-done(((bf16[8,128,1024]{2,1,0:T(8,128)(2,1)}), bf16[8,128,1024]{2,1,0:T(8,128)(2,1)S(1)}, u32[]{:S(2)}, u32[]{:S(2)}) %all-to-all-start.1) | async-done | bytes 2097184 | tf_op jit(solution)/shard_map/all_to_all | solution.py:442
  99.5 14.3 %attend_forward.3 = (bf16[1024,256]{1,0:T(8,128)(2,1)}, f32[4,1024]{1,0:T(4,128)}) custom-call(bf16[2048,768]{1,0:T(8,128)(2,1)} %convolution_convert_fusion.1.q_ref.k_ref.v_ref.refs_0_.refs_4_.refs_5_, bf16[2048,768]{1,0:T(8,128)(2,1)} %convolution_convert_fusion.1.q_ref.k_ref.v_ref.refs_0_.refs_4_.refs_5_, ...), custom_call_target="tpu_custom_call" | custom-call | flops 262144 | bytes 262144 | tf_op jit(solution)/shard_map/attend_forward/pallas_call | solution.py:190
  113.8 12.3 %all-to-all-done.2 = bf16[8,128,1024]{2,1,0:T(8,128)(2,1)} async-done(((bf16[8,128,1024]{2,1,0:T(8,128)(2,1)}), bf16[8,128,1024]{2,1,0:T(8,128)(2,1)}, u32[]{:S(2)}, u32[]{:S(2)}) %all-to-all-start.2) | async-done | bytes 2097184 | tf_op jit(solution)/shard_map/all_to_all | solution.py:442
  130.3 26.0 %all-to-all-done.3 = bf16[8,128,1024]{2,1,0:T(8,128)(2,1)S(1)} async-done(((bf16[8,128,1024]{2,1,0:T(8,128)(2,1)}), bf16[8,128,1024]{2,1,0:T(8,128)(2,1)S(1)}, u32[]{:S(2)}, u32[]{:S(2)}) %all-to-all-start.3) | async-done | bytes 2097184 | tf_op jit(solution)/shard_map/all_to_all | solution.py:442
  276.9 14.3 %expert_pass.7 = (bf16[4,1024,256]{2,1,0:T(8,128)(2,1)}, bf16[8,128,1024]{2,1,0:T(8,128)(2,1)}, bf16[8,128,1024]{2,1,0:T(8,128)(2,1)}, bf16[8,2,128,512]{3,2,1,0:T(8,128)(2,1)}, bf16[8,2,128,512]{3,2,1,0:T(8,128)(2,1)}) custom-call(bf16[1024,1024]{1,0:T(8,128)(2,1)} %bitcast.125, ...), custom_call_target="tpu_custom_call", output_to_operand_aliasing={{3}: (4, {}), {4}: (5, {})} | custom-call | flops 8589934592 | bytes 16777216 | tf_op jit(solution)/shard_map/expert_pass/pallas_call | solution.py:357
  301.1 14.4 %expert_pass.8 = (bf16[4,1024,256]{2,1,0:T(8,128)(2,1)}, bf16[8,128,1024]{2,1,0:T(8,128)(2,1)}, bf16[8,128,1024]{2,1,0:T(8,128)(2,1)}, bf16[8,2,128,512]{3,2,1,0:T(8,128)(2,1)}, bf16[8,2,128,512]{3,2,1,0:T(8,128)(2,1)}) custom-call(bf16[1024,1024]{1,0:T(8,128)(2,1)} %bitcast.123, bf16[8,128,1024]{2,1,0:T(8,128)(2,1)} %copy-done.12, ...), custom_call_target="tpu_custom_call" | custom-call | flops 8589934592 | bytes 16777216 | tf_op jit(solution)/shard_map/expert_pass/pallas_call | solution.py:357
  315.5 12.2 %all-to-all-done.9 = bf16[8,128,1024]{2,1,0:T(8,128)(2,1)} async-done(((bf16[8,128,1024]{2,1,0:T(8,128)(2,1)}), bf16[8,128,1024]{2,1,0:T(8,128)(2,1)}, u32[]{:S(2)}, u32[]{:S(2)}) %all-to-all-start.9) | async-done | bytes 2097184 | tf_op jit(solution)/shard_map/all_to_all | solution.py:442
  331.4 14.6 %expert_pass.9 = (bf16[4,1024,256]{2,1,0:T(8,128)(2,1)}, bf16[8,128,1024]{2,1,0:T(8,128)(2,1)}, bf16[8,128,1024]{2,1,0:T(8,128)(2,1)}, bf16[8,2,128,512]{3,2,1,0:T(8,128)(2,1)}, bf16[8,2,128,512]{3,2,1,0:T(8,128)(2,1)}) custom-call(bf16[1024,1024]{1,0:T(8,128)(2,1)} %bitcast.37.x_ref, ...), custom_call_target="tpu_custom_call", output_to_operand_aliasing={{3}: (4, {}), {4}: (5, {})} | custom-call | flops 8589934592 | bytes 16777216 | tf_op jit(solution)/shard_map/expert_pass/pallas_call | solution.py:357
  346.1 11.9 %all-to-all-done.10 = bf16[8,2,128,512]{3,2,1,0:T(8,128)(2,1)S(1)} async-done(((bf16[8,2,128,512]{3,2,1,0:T(8,128)(2,1)}), bf16[8,2,128,512]{3,2,1,0:T(8,128)(2,1)S(1)}, u32[]{:S(2)}, u32[]{:S(2)}) %all-to-all-start.10) | async-done | bytes 2097184 | tf_op jit(solution)/shard_map/all_to_all | solution.py:442
  382.5 11.7 %weight_pass.5 = (f32[4,1024,1024]{2,1,0:T(8,128)}, f32[4,1024,1024]{2,1,0:T(8,128)}, f32[8,128]{1,0:T(8,128)}) custom-call(bf16[1024,1024]{1,0:T(8,128)(2,1)} %bitcast.126, bf16[1024,1024]{1,0:T(8,128)(2,1)} %bitcast.15.gy_ref, bf16[1024,32]{1,0:T(8,128)(2,1)} %slice.60.router_ref, ...), custom_call_target="tpu_custom_call", output_to_operand_aliasing={{0}: (6, {}), {1}: (7, {})} | custom-call | flops 4294967296 | bytes 16777216 | tf_op jit(solution)/shard_map/weight_pass/pallas_call | solution.py:408
  398.3 13.6 %unpack.3.rest_2_ = bf16[2048,512]{1,0:T(8,128)(2,1)} custom-call(s32[2048,1]{1,0:T(8,128)} %copy.139.refs_0_, s32[2048,1]{1,0:T(8,128)} %copy.140.refs_1_, bf16[2048,512]{1,0:T(8,128)(2,1)} %bitcast.149, bf16[2048,512]{1,0:T(8,128)(2,1)} %bitcast.41.refs_3_, f32[8,128]{1,0:T(8,128)} %get-tuple-element.192.refs_4_), custom_call_target="tpu_custom_call" | custom-call | flops 8589934592 | bytes 6291456 | tf_op jit(solution)/shard_map/unpack/pallas_call | solution.py:89
  412.0 13.0 %all-to-all-done.12 = bf16[8,2,128,512]{3,2,1,0:T(8,128)(2,1)S(1)} async-done(((bf16[8,2,128,512]{3,2,1,0:T(8,128)(2,1)}), bf16[8,2,128,512]{3,2,1,0:T(8,128)(2,1)S(1)}, u32[]{:S(2)}, u32[]{:S(2)}) %all-to-all-start.12) | async-done | bytes 2097184 | tf_op jit(solution)/shard_map/all_to_all | solution.py:442
  431.8 12.1 %weight_pass.6 = (f32[4,1024,1024]{2,1,0:T(8,128)}, f32[4,1024,1024]{2,1,0:T(8,128)}, f32[8,128]{1,0:T(8,128)}) custom-call(bf16[1024,1024]{1,0:T(8,128)(2,1)} %bitcast.124, bf16[1024,1024]{1,0:T(8,128)(2,1)} %bitcast.122, bf16[1024,32]{1,0:T(8,128)(2,1)} %slice.60.router_ref, ...), custom_call_target="tpu_custom_call", output_to_operand_aliasing={{0}: (6, {}), {1}: (7, {})} | custom-call | flops 4294967296 | bytes 16777216 | tf_op jit(solution)/shard_map/weight_pass/pallas_call | solution.py:408
  443.9 11.7 %weight_pass.7 = (f32[4,1024,1024]{2,1,0:T(8,128)}, f32[4,1024,1024]{2,1,0:T(8,128)}, f32[8,128]{1,0:T(8,128)}) custom-call(bf16[1024,1024]{1,0:T(8,128)(2,1)} %bitcast.37.x_ref, bf16[1024,1024]{1,0:T(8,128)(2,1)} %bitcast.24.gy_ref, bf16[1024,32]{1,0:T(8,128)(2,1)} %slice.60.router_ref, ...), custom_call_target="tpu_custom_call", output_to_operand_aliasing={{0}: (6, {}), {1}: (7, {})} | custom-call | flops 4294967296 | bytes 16777216 | tf_op jit(solution)/shard_map/weight_pass/pallas_call | solution.py:408
  457.3 13.6 %unpack.4 = bf16[2048,512]{1,0:T(8,128)(2,1)} custom-call(s32[2048,1]{1,0:T(8,128)} %copy.139.refs_0_, s32[2048,1]{1,0:T(8,128)} %copy.140.refs_1_, bf16[2048,512]{1,0:T(8,128)(2,1)} %bitcast.150, bf16[2048,512]{1,0:T(8,128)(2,1)} %bitcast.50.refs_3_, f32[8,128]{1,0:T(8,128)} %get-tuple-element.207.refs_4_), custom_call_target="tpu_custom_call" | custom-call | flops 8589934592 | bytes 6291456 | tf_op jit(solution)/shard_map/unpack/pallas_call | solution.py:89
  488.2 18.9 %all-to-all-done.14 = bf16[8,4,128,256]{3,2,1,0:T(8,128)(2,1)} async-done(((bf16[8,4,128,256]{3,2,1,0:T(8,128)(2,1)}), bf16[8,4,128,256]{3,2,1,0:T(8,128)(2,1)}, u32[]{:S(2)}, u32[]{:S(2)}) %all-to-all-start.14) | async-done | bytes 2097184 | tf_op jit(solution)/shard_map/all_to_all | solution.py:442
  551.3 48.2 %all-to-all-done.16 = bf16[4,512,256]{1,2,0:T(8,128)(2,1)} async-done(((bf16[4,512,256]{1,2,0:T(8,128)(2,1)}), bf16[4,512,256]{1,2,0:T(8,128)(2,1)}, u32[]{:S(2)}, u32[]{:S(2)}) %all-to-all-start.16) | async-done | bytes 1048608 | tf_op jit(solution)/shard_map/all_to_all | solution.py:442
  601.9 31.7 %attend_backward.1 = bf16[2048,768]{1,0:T(8,128)(2,1)} custom-call(bf16[2048,768]{1,0:T(8,128)(2,1)} %convolution_convert_fusion.1.q_ref.k_ref.v_ref.refs_0_.refs_4_.refs_5_, bf16[2048,256]{1,0:T(8,128)(2,1)} %bitcast.156, bf16[2048,256]{1,0:T(8,128)(2,1)} %pad_maximum_fusion.3.refs_2_, f32[4,2048]{1,0:T(4,128)} %pad_maximum_fusion.7.refs_3_, ...), custom_call_target="tpu_custom_call" | custom-call | flops 21474836480 | bytes 8388608 | tf_op jit(solution)/shard_map/attend_backward/pallas_call | solution.py:282
  676.0 44.4 %reduce-scatter.23.cloned.1.call-done = bf16[512,1024]{1,0:T(8,128)(2,1)} async-done(((bf16[2048,1024]{1,0:T(8,128)(2,1)}), bf16[512,1024]{1,0:T(8,128)(2,1)}) %reduce-scatter.23.cloned.1.call-update) | async-done | bytes 1048592 | tf_op jit(solution)/shard_map/reduce_scatter | solution.py:733
  746.7 20.4 %all_to_all.114 = bf16[4,128,288]{1,2,0:T(8,128)(2,1)S(1)} all-to-all(bf16[4,128,288]{1,2,0:T(8,128)(2,1)S(1)} %pad_maximum_fusion.4), channel_id=1, replica_groups=mesh['row'=8,'col'=4] {'col'}, dimensions={0} | all-to-all | bytes 589824 | tf_op jit(solution)/shard_map/all_to_all | solution.py:442
  773.2 18.5 %all-to-all-done.18 = bf16[8,128,768]{2,1,0:T(8,128)(2,1)S(1)} async-done(((bf16[8,128,768]{2,1,0:T(8,128)(2,1)}), bf16[8,128,768]{2,1,0:T(8,128)(2,1)S(1)}, u32[]{:S(2)}, u32[]{:S(2)}) %all-to-all-start.18) | async-done | bytes 1572896 | tf_op jit(solution)/shard_map/all_to_all | solution.py:442
  793.0 21.9 %all-gather.14.cloned.1.call-done = bf16[2048,1024]{1,0:T(8,128)(2,1)} async-done(((bf16[512,1024]{1,0:T(8,128)(2,1)}), bf16[2048,1024]{1,0:T(8,128)(2,1)}) %all-gather.14.cloned.1.call-update) | async-done | bytes 4194320 | tf_op jit(solution)/shard_map/all_gather | solution.py:758
  (258 shorter events, 368.6 us)
Async XLA Ops:
  7.2 34.1 %all-gather.10.cloned.1.call-start = ((), (), s32[]{:S(2)}) async-start(), calls=%async_computation.30 | async-start | bytes 2064384 | tf_op jit(solution)/shard_map/all_gather | solution.py:512
  21.1 78.3 %all-gather.12.cloned.1.call-start = ((), (), s32[]{:S(2)}) async-start(), calls=%async_computation.31 | async-start | bytes 2359296 | tf_op jit(solution)/shard_map/all_gather | solution.py:558
  59.8 33.7 %all-to-all-start.1 = ((bf16[8,128,1024]{2,1,0:T(8,128)(2,1)}), bf16[8,128,1024]{2,1,0:T(8,128)(2,1)S(1)}, u32[]{:S(2)}, u32[]{:S(2)}) async-start(bf16[8,128,1024]{2,1,0:T(8,128)(2,1)} %bitcast.152), calls=%async_computation.1 | async-start | bytes 4194304 | tf_op jit(solution)/shard_map/all_to_all | solution.py:442
  63.5 100.3 %all-gather.18.cloned.1.call-start = ((), (), s32[]{:S(2)}) async-start(), calls=%async_computation.42 | async-start | bytes 2621440 | tf_op jit(solution)/shard_map/all_gather | solution.py:548
  94.9 31.2 %all-to-all-start.2 = ((bf16[8,128,1024]{2,1,0:T(8,128)(2,1)}), bf16[8,128,1024]{2,1,0:T(8,128)(2,1)}, u32[]{:S(2)}, u32[]{:S(2)}) async-start(bf16[8,128,1024]{2,1,0:T(8,128)(2,1)} %bitcast.151), calls=%async_computation.2 | async-start | bytes 4194304 | tf_op jit(solution)/shard_map/all_to_all | solution.py:442
  129.7 49.4 %all-gather.16.cloned.1.call-start = ((), (), s32[]{:S(2)}) async-start(), calls=%async_computation.41 | async-start | bytes 2621440 | tf_op jit(solution)/shard_map/all_gather | solution.py:564
  157.7 34.5 %all-to-all-start.4 = ((bf16[8,128,1024]{2,1,0:T(8,128)(2,1)}), bf16[8,128,1024]{2,1,0:T(8,128)(2,1)}, u32[]{:S(2)}, u32[]{:S(2)}) async-start(bf16[8,128,1024]{2,1,0:T(8,128)(2,1)} %bitcast.129), calls=%async_computation.4 | async-start | bytes 4194304 | tf_op jit(solution)/shard_map/all_to_all | solution.py:442
  214.8 116.6 %reduce-scatter.9.cloned.1.call-start = ((), (), s32[]{:S(2)}) async-start(), calls=%async_computation.32 | async-start | bytes 1310720 | tf_op jit(solution)/shard_map/reduce_scatter | solution.py:605
  237.1 233.9 %reduce-scatter.15.cloned.1.call-start = ((), (), s32[]{:S(2)}) async-start(), calls=%async_computation.35 | async-start | bytes 1310720 | tf_op jit(solution)/shard_map/reduce_scatter | solution.py:605
  268.8 204.1 %reduce-scatter.17.cloned.1.call-start = ((), (), s32[]{:S(2)}) async-start(), calls=%async_computation.36 | async-start | bytes 2621440 | tf_op jit(solution)/shard_map/reduce_scatter | solution.py:605
  296.7 31.0 %all-to-all-start.9 = ((bf16[8,128,1024]{2,1,0:T(8,128)(2,1)}), bf16[8,128,1024]{2,1,0:T(8,128)(2,1)}, u32[]{:S(2)}, u32[]{:S(2)}) async-start(bf16[8,128,1024]{2,1,0:T(8,128)(2,1)} %bitcast.131), calls=%async_computation.9 | async-start | bytes 4194304 | tf_op jit(solution)/shard_map/all_to_all | solution.py:442
  301.0 171.9 %reduce-scatter.19.cloned.1.call-start = ((), (), s32[]{:S(2)}) async-start(), calls=%async_computation.37 | async-start | bytes 2621440 | tf_op jit(solution)/shard_map/reduce_scatter | solution.py:605
  331.3 141.6 %reduce-scatter.21.cloned.1.call-start = ((), (), s32[]{:S(2)}) async-start(), calls=%async_computation.38 | async-start | bytes 2621440 | tf_op jit(solution)/shard_map/reduce_scatter | solution.py:631
  359.2 34.9 %all-to-all-start.11 = ((bf16[8,2,128,512]{3,2,1,0:T(8,128)(2,1)}), bf16[8,2,128,512]{3,2,1,0:T(8,128)(2,1)}, u32[]{:S(2)}, u32[]{:S(2)}) async-start(bf16[8,2,128,512]{3,2,1,0:T(8,128)(2,1)} %get-tuple-element.184), calls=%async_computation.12 | async-start | bytes 4194304 | tf_op jit(solution)/shard_map/all_to_all | solution.py:442
  394.2 30.8 %all-to-all-start.12 = ((bf16[8,2,128,512]{3,2,1,0:T(8,128)(2,1)}), bf16[8,2,128,512]{3,2,1,0:T(8,128)(2,1)S(1)}, u32[]{:S(2)}, u32[]{:S(2)}) async-start(bf16[8,2,128,512]{3,2,1,0:T(8,128)(2,1)} %get-tuple-element.195), calls=%async_computation.14 | async-start | bytes 4194304 | tf_op jit(solution)/shard_map/all_to_all | solution.py:442
  398.3 136.8 %reduce-scatter.11.cloned.1.call-start = ((), (), s32[]{:S(2)}) async-start(), calls=%async_computation.33 | async-start | bytes 2621440 | tf_op jit(solution)/shard_map/reduce_scatter | solution.py:683
  426.3 31.0 %all-to-all-start.13 = ((bf16[8,2,128,512]{3,2,1,0:T(8,128)(2,1)}), bf16[8,2,128,512]{3,2,1,0:T(8,128)(2,1)}, u32[]{:S(2)}, u32[]{:S(2)}) async-start(bf16[8,2,128,512]{3,2,1,0:T(8,128)(2,1)} %get-tuple-element.197), calls=%async_computation.15 | async-start | bytes 4194304 | tf_op jit(solution)/shard_map/all_to_all | solution.py:442
  430.7 104.4 %reduce-scatter.13.cloned.1.call-start = ((), (), s32[]{:S(2)}) async-start(), calls=%async_computation.34 | async-start | bytes 2621440 | tf_op jit(solution)/shard_map/reduce_scatter | solution.py:683
  475.9 31.1 %all-to-all-start.14 = ((bf16[8,4,128,256]{3,2,1,0:T(8,128)(2,1)}), bf16[8,4,128,256]{3,2,1,0:T(8,128)(2,1)}, u32[]{:S(2)}, u32[]{:S(2)}) async-start(bf16[8,4,128,256]{3,2,1,0:T(8,128)(2,1)} %pad_maximum_fusion.2), calls=%async_computation.21 | async-start | bytes 4194304 | tf_op jit(solution)/shard_map/all_to_all | solution.py:442
  480.4 153.1 %all-gather.20.cloned.1.call-start = ((), (), s32[]{:S(2)}) async-start(), calls=%async_computation.43 | async-start | bytes 5242880 | tf_op jit(solution)/shard_map/all_gather | solution.py:703
  545.2 54.3 %all-to-all-start.16 = ((bf16[4,512,256]{1,2,0:T(8,128)(2,1)}), bf16[4,512,256]{1,2,0:T(8,128)(2,1)}, u32[]{:S(2)}, u32[]{:S(2)}) async-start(bf16[4,512,256]{1,2,0:T(8,128)(2,1)} %fusion.25), calls=%async_computation.23 | async-start | bytes 2097152 | tf_op jit(solution)/shard_map/all_to_all | solution.py:442
  549.6 170.8 %reduce-scatter.23.cloned.1.call-start = ((), (), s32[]{:S(2)}) async-start(), calls=%async_computation.39 | async-start | bytes 5242880 | tf_op jit(solution)/shard_map/reduce_scatter | solution.py:733
  657.2 64.6 %all-to-all-start.17 = ((bf16[8,128,1056]{1,2,0:T(8,128)(2,1)}), bf16[8,128,1056]{1,2,0:T(8,128)(2,1)}, u32[]{:S(2)}, u32[]{:S(2)}) async-start(bf16[8,128,1056]{1,2,0:T(8,128)(2,1)} %copy.152), calls=%async_computation.25 | async-start | bytes 4325376 | tf_op jit(solution)/shard_map/all_to_all | solution.py:442
  661.5 153.4 %all-gather.14.cloned.1.call-start = ((), (), s32[]{:S(2)}) async-start(), calls=%async_computation.40 | async-start | bytes 5242880 | tf_op jit(solution)/shard_map/all_gather | solution.py:758
  (52 other events, 413.6 us)
Sparse Core Ops, SparseCore 0:
  11.8 29.4 all-gather.9
  43.8 31.3 all-gather.11
  76.8 51.3 all-gather.17
  131.8 47.2 all-gather.15
  232.2 26.2 reduce-scatter.8
  263.9 24.1 reduce-scatter.14
  295.5 40.7 reduce-scatter.16
  338.7 43.1 reduce-scatter.18
  384.2 43.1 reduce-scatter.20
  429.7 43.1 reduce-scatter.10
  475.2 43.1 reduce-scatter.12
  520.4 101.9 all-gather.19
  641.5 78.7 reduce-scatter.22
  727.3 87.6 all-gather.13

commit v7 on v6

--- a/solution.py
+++ b/solution.py
@@ -65,7 +65,7 @@
         ),
         compiler_params=params("arbitrary"),
         name="pack",
-        cost_estimate=cost(count * width, count * width),
+        cost_estimate=cost(1, 1),
     )(slots.reshape(1, length), *rows, *waits)
 
 
@@ -100,10 +100,16 @@
     )(*(at.reshape(length, 1) for at in slots), *rows, *waits)
 
 
-def middle_body(full_ref, out_ref, tokens_ref, gain_ref, bias_ref, middle_ref, routed_ref):
-    total = tokens_ref[...].astype(jnp.float32)
-    for z in range(full_ref.shape[0]):
-        total = total + dot(full_ref[z], out_ref[z], NT)
+def middle_body(full_ref, out_ref, tokens_ref, gain_ref, bias_ref, middle_ref, routed_ref, all_ref):
+    cols, _, width = full_ref.shape
+
+    @pl.when(pl.program_id(0) == 0)
+    def _():
+        for z in range(cols):
+            all_ref[:, z * width : (z + 1) * width] = out_ref[z]
+
+    context = jnp.concatenate([full_ref[z] for z in range(cols)], axis=1)
+    total = tokens_ref[...].astype(jnp.float32) + dot(context, all_ref[...], NT)
     middle_ref[...] = total
     mean = jnp.mean(total, axis=1, keepdims=True)
     centered = total - mean
@@ -111,11 +117,12 @@
     routed_ref[...] = (centered * inverse * gain_ref[...] + bias_ref[...]).astype(jnp.bfloat16)
 
 
-def middle_pass(full, out_full, tokens, first, gain, bias):
+def middle_pass(full, out_full, tokens, gain, bias):
     cols, rows, width = full.shape
     depth = tokens.shape[1]
     step = min(256, rows)
     row = pl.BlockSpec((1, depth), lambda i: (0, 0))
+    block = pl.BlockSpec((step, depth), lambda i: (i, 0))
     return pl.pallas_call(
         middle_body,
         out_shape=(
@@ -126,14 +133,12 @@
         in_specs=[
             pl.BlockSpec((cols, step, width), lambda i: (0, i, 0)),
             pl.BlockSpec((cols, depth, width), lambda i: (0, 0, 0)),
-            pl.BlockSpec((step, depth), lambda i: (i + first // step, 0)),
+            block,
             row,
             row,
         ],
-        out_specs=(
-            pl.BlockSpec((step, depth), lambda i: (i, 0)),
-            pl.BlockSpec((step, depth), lambda i: (i, 0)),
-        ),
+        out_specs=(block, block),
+        scratch_shapes=[pltpu.VMEM((depth, cols * width), jnp.bfloat16)],
         compiler_params=params("arbitrary"),
         name="middle_pass",
         cost_estimate=cost(2 * rows * depth * width * cols, 10 * rows * depth),
@@ -333,9 +338,11 @@
     grad_hidden = (grad_active * slope).astype(jnp.bfloat16)
     slope_ref[...] = grad_hidden.reshape(slope_ref.shape)
     back = dot(grad_hidden, win_ref[...], NT).astype(jnp.bfloat16)
-    wide = depth // len(sent)
-    for j, ref in enumerate(sent):
-        ref[...] = back[:, j * wide : (j + 1) * wide].reshape(ref.shape)
+    first = 0
+    for ref in sent:
+        wide = ref.shape[-1]
+        ref[...] = back[:, first : first + wide].reshape(ref.shape)
+        first += wide
 
 
 def expert_pass(chunk, x, grad_y, w_in, w_back, kept, sent, members, parts, pieces, waits=()):
@@ -350,14 +357,14 @@
     aliases = {4 + j: (1 if kept else 3) + j for j in range(len(given))}
     keep = jax.ShapeDtypeStruct((sources, cap, width), jnp.bfloat16)
     keep_spec = pl.BlockSpec((group, size, width), lambda i: (i, at, 0))
-    piece = jax.ShapeDtypeStruct((sources, members, cap, depth // pieces), jnp.bfloat16)
-    piece_spec = pl.BlockSpec(
-        (group, None, size, depth // pieces), lambda i: (i, e % members, at, 0)
+    piece = tuple(jax.ShapeDtypeStruct((sources, members, cap, w), jnp.bfloat16) for w in pieces)
+    piece_spec = tuple(
+        pl.BlockSpec((group, None, size, w), lambda i: (i, e % members, at, 0)) for w in pieces
     )
     made = pl.pallas_call(
         functools.partial(expert_body, len(given) + len(waits)),
         out_shape=(jax.ShapeDtypeStruct((parts, rows, depth // parts), jnp.bfloat16), keep, keep)
-        + (piece,) * pieces,
+        + piece,
         grid=(rows // step,),
         in_specs=[
             pl.BlockSpec((step, depth), lambda i: (i, 0)),
@@ -371,7 +378,7 @@
             keep_spec,
             keep_spec,
         )
-        + (piece_spec,) * pieces,
+        + piece_spec,
         input_output_aliases=aliases,
         compiler_params=params("arbitrary"),
         name="expert_pass",
@@ -491,18 +498,12 @@
     cap = 2 * length // experts
     block_rows = rows_all * cap
     block = min(256, length // 2)
-    half = length // 2
     part = length // cols_all
     members = max(1, local // 2)
-    pieces = 2
-
-    def own_of(values):
-        return lax.dynamic_slice_in_dim(values, col * part, part, 0)
-
-    def own(low, high, axis=0):
-        first = lax.dynamic_slice_in_dim(low, col * part, part, axis)
-        second = lax.dynamic_slice_in_dim(high, col * part - half, part, axis)
-        return jnp.where(col * part < half, first, second)
+    pieces = (depth * 5 // 8, depth * 3 // 8)
+
+    def own(values, axis=0):
+        return lax.dynamic_slice_in_dim(values, col * part, part, axis)
 
     def send(packed):
         return swap(packed.reshape(rows_all, cap, depth), "row").reshape(block_rows, depth)
@@ -542,36 +543,23 @@
     normal_in = (normed_one * gains[0] + biases[0]).astype(jnp.bfloat16)
     projected = jnp.dot(normal_in, qkv_full, preferred_element_type=jnp.float32).astype(jnp.bfloat16)
 
-    count = half // block
-    context_a, logsum_a = attend_forward(projected, tuple(range(count)), block)
-    context_a, grad_packed[0] = tie(context_a, grad_packed[0])
-    full_a = lax.all_gather(context_a, "col", axis=0)
+    context, logsum = attend_forward(projected, tuple(range(length // block)), block)
+    context, grad_packed[0] = tie(context, grad_packed[0])
+    full = lax.all_gather(context, "col", axis=0)
     grad_arrived = [send(grad_packed[0])]
-    later = [context_a]
     if local > early:
-        later = pack(
-            slots_by_local, [cotangent], early * block_rows, block_rows, local - early, later
+        grad_packed += pack(
+            slots_by_local, [cotangent], early * block_rows, block_rows, local - early, [context]
         )
-        grad_packed += later
     grad_arrived[0], *grad_packed[1:] = tie(grad_arrived[0], *grad_packed[1:])
-    grad_arrived += [send(p) for p in grad_packed[1:early]]
     out_full = lax.all_gather(out_block, "row", axis=1, tiled=True)
-    context_b, logsum_b = attend_forward(
-        projected, tuple(range(count, 2 * count)), block, [later[-1], out_full]
-    )
-    context_b, *both = tie(context_b, *grad_arrived[1:], *grad_packed[early:])
-    grad_arrived[1:], grad_packed[early:] = both[: len(grad_arrived) - 1], both[len(grad_arrived) - 1 :]
-    full_b = lax.all_gather(context_b, "col", axis=0)
-    gain, bias = gains[1:2], biases[1:2]
-    middle_a, routed_a = middle_pass(full_a, out_full, tokens, 0, gain, bias)
-    full_b, middle_a = tie(full_b, middle_a)
-    for e in range(early, local):
+    for e in range(1, local):
         grad_arrived.append(send(grad_packed[e]))
         if e + 1 < local:
             grad_arrived[e], grad_packed[e + 1] = tie(grad_arrived[e], grad_packed[e + 1])
-    middle_b, routed_b = middle_pass(full_b, out_full, tokens, half, gain, bias)
-
-    routed = [routed_a, routed_b]
+    full, out_full = tie(full, out_full)
+    middle, routed = middle_pass(full, out_full, tokens, gains[1:2], biases[1:2])
+
     short = cap // 2
     chunks = [(0, 0, short), (0, short, short)] + [(e, 0, cap) for e in range(1, local)]
     split = (ranks // short * rows_all + chosen // local) * short + ranks % short
@@ -580,15 +568,12 @@
     def pack_chunk(k, waits):
         e, low, size = chunks[k]
         base = (e * cap + low) * rows_all
-        return pack(slots_by_chunk, routed, base, size * rows_all, 1, waits)[0]
-
-    packed = [pack_chunk(k, []) for k in range(min(3, len(chunks)))]
+        return pack(slots_by_chunk, [routed], base, size * rows_all, 1, waits)[0]
+
+    packed = [pack_chunk(k, []) for k in range(2)]
     packed[0], grad_arrived[-1] = tie(packed[0], grad_arrived[-1])
 
-    def route(rows):
-        return jnp.dot(rows, router_full, preferred_element_type=jnp.float32)
-
-    logits = jnp.concatenate([route(routed_a), route(routed_b)], axis=0)
+    logits = jnp.dot(routed, router_full, preferred_element_type=jnp.float32)
     probs = jax.nn.softmax(logits, axis=-1)
     gate = jnp.sum(probs * select, axis=-1, keepdims=True)
 
@@ -609,7 +594,7 @@
                 packed[k + 1] = then
             else:
                 sent[0][0] = then
-        waits = packed[2:3] if k == 0 else summed[:1] if k == final else []
+        waits = packed[1:2] if k == 0 else summed[:1] if k == final else []
         made, both, pair = expert_pass(
             chunks[k],
             arrived[k],
@@ -626,9 +611,8 @@
         kept.append(both)
         summed.append(made)
         sent.append(pair)
-        if k + 3 <= final:
-            packed.append(pack_chunk(k + 3, [made]))
-    summed[-1] = lax.psum_scatter(summed[-1], "col", scatter_dimension=0, tiled=True)
+        if k + 2 <= final:
+            packed.append(pack_chunk(k + 2, [made]))
     active = [v[0].reshape(block_rows, -1) for v in kept]
     slope = [v[1].reshape(block_rows, -1) for v in kept]
 
@@ -640,8 +624,7 @@
     arrived = [v.reshape(block_rows, depth) for v in joined(arrived)]
 
     step = min(256, length)
-    order = [(g, f) for f in range(pieces) for g in range(len(sent))]
-    back = {}
+    order = [(g, f) for f in range(len(pieces)) for g in range(len(sent))]
     grad_sent = []
     grad_weights = None
     token = None
@@ -664,52 +647,64 @@
 
     waits = slope[-1:]
     last = None
-    for at, (g, f) in enumerate(order):
-        piece = sent[g][f]
-        if last is not None:
-            piece, last = tie(piece, last)
-            back[order[at - 1]] = last
-        if at == 1:
-            piece, slope[-1] = tie(piece, slope[-1])
-        last = swap(piece, "row")
-        back[(g, f)] = last
-        if g == len(sent) - 1:
-            rows = [back[(k, f)].reshape(-1, depth // pieces) for k in range(len(sent))]
-            for e in range(f * local // pieces, (f + 1) * local // pieces):
-                *grad_weights, token = weigh(e, waits)
-                waits = [token]
-            whole = unpack(slots_by_group, rows, step, waits)
-            waits = [whole]
+    for f, wide in enumerate(pieces):
+        for e in range(f * local // len(pieces), (f + 1) * local // len(pieces)):
+            *grad_weights, token = weigh(e, waits)
+            waits = [token]
+        rows = []
+        for g in range(len(sent)):
+            piece = sent[g][f]
+            if last is not None:
+                piece, last = tie(piece, last)
+                if rows:
+                    rows[-1] = last
+                else:
+                    ended[-1] = last
+            if f == 0 and g == len(sent) - 1:
+                piece, slope[-1] = tie(piece, slope[-1])
+            if f and g == len(sent) - 1:
+                piece, whole = tie(piece, whole)
+            last = swap(piece, "row")
+            if f == 0 and g == 0:
+                last, made = tie(last, summed[-1])
+                summed[-1] = lax.psum_scatter(made, "col", scatter_dimension=0, tiled=True)
+            rows.append(last)
+        if f == 0:
+            ended = rows
+            sent[0][1], token = tie(sent[0][1], token)
+            waits = [token]
+        else:
+            homed = jnp.stack(joined(summed), axis=1)
+            waits = [token, homed]
             grad_sent.append(lax.psum_scatter(whole, "col", scatter_dimension=0, tiled=True))
+        whole = unpack(slots_by_group, [v.reshape(-1, wide) for v in rows], step, waits)
+        waits = [whole]
+    grad_sent.append(lax.psum_scatter(whole, "col", scatter_dimension=0, tiled=True))
 
     grad_in, grad_back = grad_weights
-    homed = jnp.stack(joined(summed), axis=1)
-    homed, last = tie(homed, last)
-    back[order[-1]] = last
     homed = swap(homed, "row")
     returned = unpack(
-        [slots], [homed.reshape(experts * cap, depth // cols_all)], step
+        [slots], [homed.reshape(experts * cap, depth // cols_all)], step, grad_sent[:1]
     ).astype(jnp.float32)
     columns = depth // cols_all
 
     def own_columns(values):
         return lax.dynamic_slice_in_dim(values, col * columns, columns, 1)
 
-    middle_cols = jnp.concatenate([own_columns(middle_a), own_columns(middle_b)], axis=0)
-    mixed = (middle_cols + gate * returned).astype(jnp.bfloat16)
+    mixed = (own_columns(middle) + gate * returned).astype(jnp.bfloat16)
     grad_gate = jnp.sum(own_columns(cotangent).astype(jnp.float32) * returned, axis=-1)
     grad_gate = swap(grad_gate.reshape(cols_all, part), "col")
     grad_gate = jnp.sum(grad_gate, axis=0)[:, None]
     mixed_full = lax.all_gather(mixed, "col", axis=0)
 
-    own_gate, own_probs, own_select = own_of(gate), own_of(probs), own_of(select)
+    own_gate, own_probs, own_select = own(gate), own(probs), own(select)
     grad_logits = (grad_gate * own_probs * (own_select - own_gate)).astype(jnp.bfloat16)
-    own_routed = own(routed_a, routed_b)
+    own_routed = own(routed)
     grad_router = jnp.einsum(
         "td,te->de", own_routed, grad_logits, preferred_element_type=jnp.float32
     )
-    grad_y = own_of(cotangent).astype(jnp.float32)
-    normed_own, inverse_own = layer_stats(own(middle_a, middle_b))
+    grad_y = own(cotangent).astype(jnp.float32)
+    normed_own, inverse_own = layer_stats(own(middle))
     grad_sent = jnp.concatenate(grad_sent, axis=1).astype(jnp.float32) * own_gate
     grad_routed = grad_sent + jnp.einsum(
         "te,de->td", grad_logits, router_full, preferred_element_type=jnp.float32
@@ -723,8 +718,6 @@
     ).astype(jnp.bfloat16)
     grad_context = swap(grad_context, "col")
     grad_context = grad_context.reshape(length, width)
-    context = jnp.concatenate([context_a, context_b], axis=0)
-    logsum = jnp.concatenate([logsum_a, logsum_b], axis=1)
     grad_proj = attend_backward(projected, grad_context, context, logsum, block, 0)[0]
     grad_proj, grad_attn, mixed_full = tie(grad_proj, grad_attn, mixed_full)
 
@@ -735,7 +728,7 @@
         ).astype(jnp.float32)
 
     grad_normal = spread(grad_proj)
-    context_own = own(full_a, full_b, 1)
+    context_own = own(full, 1)
     grad_out = jnp.einsum("td,ztc->dzc", grad_attn, context_own, preferred_element_type=jnp.float32)
     plane = jnp.concatenate([grad_out.reshape(depth, cols_all * width), grad_router], axis=1)
     plane = swap(plane.astype(jnp.bfloat16).reshape(rows_all, share, -1), "row")
@@ -751,7 +744,7 @@
     plane = jnp.sum(swap(plane, "col").astype(jnp.float32), axis=0)
     out_share, router_share = plane[:, :width].T, plane[:, width:]
 
-    own_normed, own_inverse = layer_stats(own_of(tokens).astype(jnp.float32))
+    own_normed, own_inverse = layer_stats(own(tokens).astype(jnp.float32))
     grad_tokens = (
         grad_middle + norm_back(grad_normal, own_normed, own_inverse, gains[0])
     ).astype(jnp.bfloat16)

time: 833 us -> 830 us (level)
  blocking collectives: 20.4 us -> 135 us
  waiting for transfers between devices: 294 us -> 198 us
  starting transfers between devices: 87 us -> 74.5 us
    all_to_all x1 -> x4, blocking collectives: 20.4 us -> 135 us  [swap(): return lax.all_to_all(blocks, axis, split_axis=0, concat_axis=0, tiled=True)]
    all_to_all x21 -> x18, waiting for transfers between devices: 217 us -> 130 us  [swap(): return lax.all_to_all(blocks, axis, split_axis=0, concat_axis=0, tiled=True)]
    all_to_all x21 -> x18, starting transfers between devices: 86.4 us -> 73.9 us  [swap(): return lax.all_to_all(blocks, axis, split_axis=0, concat_axis=0, tiled=True)]
    unnamed x90 -> x74, local copies, waits for them, and re-layouts: 23.5 us -> 19.6 us
    pallas_call x2 -> x1, Pallas kernels: 22.1 us -> 19.3 us  [attend_forward(): pl.pallas_call(functools.partial(forward_body, blocks, block), out_shape=...]
  transfers between devices with their start and end apart: 35 -> 31, of which waited for: 20 -> 16; matrix products, arithmetic and copies ran while one was open for 12% -> 11% of each run, Pallas kernels for 33% -> 34%
where the time goes in v7:
time: 830 us; the launch traced here: 823 us
  Pallas kernels  276 us (33%)
  waiting for transfers between devices  198 us (24%)
  blocking collectives  135 us (16%)
  starting transfers between devices  74.5 us (9%)
  other arithmetic  44.6 us (5%)
  local copies, waits for them, and re-layouts  43.3 us (5%)
  matrix products  36.6 us (4%)
  between operations  14.8 us (2%)
    all_to_all x4, blocking collectives, swap(): return lax.all_to_all(blocks, axis, split_axis=0, concat_axis=0, tiled=True)  135 us
    all_to_all x18, waiting for transfers between devices, swap(): return lax.all_to_all(blocks, axis, split_axis=0, concat_axis=0, tiled=True)  130 us
    all_to_all x18, starting transfers between devices, swap(): return lax.all_to_all(blocks, axis, split_axis=0, concat_axis=0, tiled=True)  73.9 us
    pallas_call x7, Pallas kernels, pack(): pl.pallas_call(functools.partial(pack_body, base, step, each, len(rows)),...  62.4 us
    pallas_call x5, Pallas kernels, expert_pass(): pl.pallas_call(functools.partial(expert_body, len(given) + len(waits)), o...  62 us
    pallas_call x4, Pallas kernels, weight_pass(): pl.pallas_call(functools.partial(weight_body, len(sent) + len(waits)), ou...  47.2 us
    reduce_scatter x1, waiting for transfers between devices, spread(): lax.psum_scatter(made.astype(jnp.bfloat16), 'col', scatter_dimension=0, t...  44.5 us
    pallas_call x3, Pallas kernels, unpack(): pl.pallas_call(functools.partial(unpack_body, len(rows)), out_shape=jax.S...  40.6 us
  transfers between devices with their start and end apart: 31, of which 16 were waited for; matrix products, arithmetic and copies ran while one was open for 11% of the time, Pallas kernels for 34%

profile of v7, /device:TPU:0, one launch (start us, length us, event | category | flops | bytes accessed | tf_op | source)
XLA Modules:
  0.0 823.4 jit_solution(13388776055572955482)
XLA Ops:
  26.7 13.8 %pack.7 = (bf16[1024,1024]{1,0:T(8,128)(2,1)}, bf16[1024,1024]{1,0:T(8,128)(2,1)}) custom-call(s32[1,2048]{1,0:T(1,128)} %bitcast.169, bf16[2048,1024]{1,0:T(8,128)(2,1)} %rest_0_.3), custom_call_target="tpu_custom_call" | custom-call | flops 1 | bytes 1 | tf_op jit(solution)/shard_map/pack/pallas_call | solution.py:55
  52.1 19.3 %attend_forward.1 = (bf16[2048,256]{1,0:T(8,128)(2,1)}, f32[4,2048]{1,0:T(4,128)}) custom-call(bf16[2048,768]{1,0:T(8,128)(2,1)} %convolution_convert_fusion.1.q_ref.k_ref.v_ref.refs_0_.refs_4_.refs_5_, bf16[2048,768]{1,0:T(8,128)(2,1)} %convolution_convert_fusion.1.q_ref.k_ref.v_ref.refs_0_.refs_4_.refs_5_, ...), custom_call_target="tpu_custom_call" | custom-call | flops 524288 | bytes 524288 | tf_op jit(solution)/shard_map/attend_forward/pallas_call | solution.py:195
  75.7 13.4 %pack.10 = (bf16[1024,1024]{1,0:T(8,128)(2,1)}, bf16[1024,1024]{1,0:T(8,128)(2,1)}) custom-call(s32[1,2048]{1,0:T(1,128)} %bitcast.170, bf16[2048,1024]{1,0:T(8,128)(2,1)} %rest_0_.3, bf16[2048,256]{1,0:T(8,128)(2,1)} %get-tuple-element.124.rest_1_.refs_2_), custom_call_target="tpu_custom_call" | custom-call | flops 1 | bytes 1 | tf_op jit(solution)/shard_map/pack/pallas_call | solution.py:55
  89.1 12.5 %all-to-all-done.1 = bf16[8,128,1024]{2,1,0:T(8,128)(2,1)S(1)} async-done(((bf16[8,128,1024]{2,1,0:T(8,128)(2,1)}), bf16[8,128,1024]{2,1,0:T(8,128)(2,1)S(1)}, u32[]{:S(2)}, u32[]{:S(2)}) %all-to-all-start.1) | async-done | bytes 2097184 | tf_op jit(solution)/shard_map/all_to_all | solution.py:449
  101.6 31.2 %all_to_all.114 = bf16[8,128,1024]{2,1,0:T(8,128)(2,1)} all-to-all(bf16[8,128,1024]{2,1,0:T(8,128)(2,1)} %bitcast.140), channel_id=1, replica_groups=mesh['row'=8,'col'=4] {'row'}, dimensions={0} | all-to-all | bytes 4194304 | tf_op jit(solution)/shard_map/all_to_all | solution.py:449
  132.8 29.8 %all_to_all.115 = bf16[8,128,1024]{2,1,0:T(8,128)(2,1)} all-to-all(bf16[8,128,1024]{2,1,0:T(8,128)(2,1)S(1)} %bitcast.144), channel_id=1, replica_groups=mesh['row'=8,'col'=4] {'row'}, dimensions={0} | all-to-all | bytes 4194304 | tf_op jit(solution)/shard_map/all_to_all | solution.py:449
  168.0 12.9 %middle_pass.1 = (f32[2048,1024]{1,0:T(8,128)}, bf16[2048,1024]{1,0:T(8,128)(2,1)}) custom-call(bf16[4,2048,256]{2,1,0:T(8,128)(2,1)} %bitcast.179, bf16[4,1024,256]{2,1,0:T(8,128)(2,1)} %all-gather.10.cloned.1.call-done.out_ref, bf16[2048,1024]{1,0:T(8,128)(2,1)} %tokens_ref.1, f32[1,1024]{1,0:T(1,128)} %copy.115.gain_ref, f32[1,1024]{1,0:T(1,128)} %copy.116.bias_ref), custom_call_target="tpu_custom_call" | custom-call | flops 4294967296 | bytes 20971520 | tf_op jit(solution)/shard_map/middle_pass/pallas_call | solution.py:126
  270.7 14.4 %expert_pass.7 = (bf16[4,1024,256]{2,1,0:T(8,128)(2,1)}, bf16[8,128,1024]{2,1,0:T(8,128)(2,1)}, bf16[8,128,1024]{2,1,0:T(8,128)(2,1)}, bf16[8,2,128,640]{3,2,1,0:T(8,128)(2,1)}, bf16[8,2,128,384]{3,2,1,0:T(8,128)(2,1)}) custom-call(bf16[1024,1024]{1,0:T(8,128)(2,1)} %bitcast.120, ...), custom_call_target="tpu_custom_call", output_to_operand_aliasing={{3}: (4, {}), {4}: (5, {})} | custom-call | flops 8589934592 | bytes 16777216 | tf_op jit(solution)/shard_map/expert_pass/pallas_call | solution.py:364
  302.9 14.4 %expert_pass.8 = (bf16[4,1024,256]{2,1,0:T(8,128)(2,1)}, bf16[8,128,1024]{2,1,0:T(8,128)(2,1)}, bf16[8,128,1024]{2,1,0:T(8,128)(2,1)}, bf16[8,2,128,640]{3,2,1,0:T(8,128)(2,1)}, bf16[8,2,128,384]{3,2,1,0:T(8,128)(2,1)}) custom-call(bf16[1024,1024]{1,0:T(8,128)(2,1)} %bitcast.118, bf16[8,128,1024]{2,1,0:T(8,128)(2,1)} %all_to_all.115, ...), custom_call_target="tpu_custom_call" | custom-call | flops 8589934592 | bytes 16777216 | tf_op jit(solution)/shard_map/expert_pass/pallas_call | solution.py:364
  317.3 12.2 %all-to-all-done.9 = bf16[8,128,1024]{2,1,0:T(8,128)(2,1)} async-done(((bf16[8,128,1024]{2,1,0:T(8,128)(2,1)}), bf16[8,128,1024]{2,1,0:T(8,128)(2,1)}, u32[]{:S(2)}, u32[]{:S(2)}) %all-to-all-start.9) | async-done | bytes 2097184 | tf_op jit(solution)/shard_map/all_to_all | solution.py:449
  333.3 14.6 %expert_pass.9 = (bf16[4,1024,256]{2,1,0:T(8,128)(2,1)}, bf16[8,128,1024]{2,1,0:T(8,128)(2,1)}, bf16[8,128,1024]{2,1,0:T(8,128)(2,1)}, bf16[8,2,128,640]{3,2,1,0:T(8,128)(2,1)}, bf16[8,2,128,384]{3,2,1,0:T(8,128)(2,1)}) custom-call(bf16[1024,1024]{1,0:T(8,128)(2,1)} %bitcast.34.x_ref, ...), custom_call_target="tpu_custom_call", output_to_operand_aliasing={{3}: (4, {}), {4}: (5, {})} | custom-call | flops 8589934592 | bytes 16777216 | tf_op jit(solution)/shard_map/expert_pass/pallas_call | solution.py:364
  347.8 17.6 %all-to-all-done.10 = bf16[8,2,128,640]{3,2,1,0:T(8,128)(2,1)S(1)} async-done(((bf16[8,2,128,640]{3,2,1,0:T(8,128)(2,1)}), bf16[8,2,128,640]{3,2,1,0:T(8,128)(2,1)S(1)}, u32[]{:S(2)}, u32[]{:S(2)}) %all-to-all-start.10) | async-done | bytes 2621472 | tf_op jit(solution)/shard_map/all_to_all | solution.py:449
  375.7 11.7 %weight_pass.4 = (f32[4,1024,1024]{2,1,0:T(8,128)}, f32[4,1024,1024]{2,1,0:T(8,128)}, f32[8,128]{1,0:T(8,128)}) custom-call(bf16[1024,1024]{1,0:T(8,128)(2,1)} %bitcast.145, bf16[1024,1024]{1,0:T(8,128)(2,1)} %bitcast.111, bf16[1024,32]{1,0:T(8,128)(2,1)} %slice.60.router_ref, f32[1,32]{1,0:T(1,128)} %compare_convert_fusion.2.pick_ref, ...), custom_call_target="tpu_custom_call" | custom-call | flops 4294967296 | bytes 16777216 | tf_op jit(solution)/shard_map/weight_pass/pallas_call | solution.py:415
  410.1 18.3 %unpack.3.rest_2_ = bf16[2048,640]{1,0:T(8,128)(2,1)} custom-call(s32[2048,1]{1,0:T(8,128)} %copy.117.refs_0_, s32[2048,1]{1,0:T(8,128)} %copy.118.refs_1_, bf16[2048,640]{1,0:T(8,128)(2,1)} %bitcast.130, bf16[2048,640]{1,0:T(8,128)(2,1)} %bitcast.47.refs_3_, f32[8,128]{1,0:T(8,128)} %get-tuple-element.194.refs_4_), custom_call_target="tpu_custom_call" | custom-call | flops 10737418240 | bytes 7864320 | tf_op jit(solution)/shard_map/unpack/pallas_call | solution.py:89
  436.0 12.1 %weight_pass.6 = (f32[4,1024,1024]{2,1,0:T(8,128)}, f32[4,1024,1024]{2,1,0:T(8,128)}, f32[8,128]{1,0:T(8,128)}) custom-call(bf16[1024,1024]{1,0:T(8,128)(2,1)} %bitcast.119, bf16[1024,1024]{1,0:T(8,128)(2,1)} %bitcast.116, bf16[1024,32]{1,0:T(8,128)(2,1)} %slice.60.router_ref, ...), custom_call_target="tpu_custom_call", output_to_operand_aliasing={{0}: (6, {}), {1}: (7, {})} | custom-call | flops 4294967296 | bytes 16777216 | tf_op jit(solution)/shard_map/weight_pass/pallas_call | solution.py:415
  448.1 11.7 %weight_pass.7 = (f32[4,1024,1024]{2,1,0:T(8,128)}, f32[4,1024,1024]{2,1,0:T(8,128)}, f32[8,128]{1,0:T(8,128)}) custom-call(bf16[1024,1024]{1,0:T(8,128)(2,1)} %bitcast.34.x_ref, bf16[1024,1024]{1,0:T(8,128)(2,1)} %bitcast.115, bf16[1024,32]{1,0:T(8,128)(2,1)} %slice.60.router_ref, ...), custom_call_target="tpu_custom_call", output_to_operand_aliasing={{0}: (6, {}), {1}: (7, {})} | custom-call | flops 4294967296 | bytes 16777216 | tf_op jit(solution)/shard_map/weight_pass/pallas_call | solution.py:415
  462.8 13.3 %unpack.4 = bf16[2048,384]{1,0:T(8,128)(2,1)} custom-call(s32[2048,1]{1,0:T(8,128)} %copy.117.refs_0_, s32[2048,1]{1,0:T(8,128)} %copy.118.refs_1_, bf16[2048,384]{1,0:T(8,128)(2,1)} %bitcast.146, bf16[2048,384]{1,0:T(8,128)(2,1)} %bitcast.49.refs_3_, f32[8,128]{1,0:T(8,128)} %get-tuple-element.207.refs_4_, bf16[8,4,128,256]{3,2,1,0:T(8,128)(2,1)} %pad_maximum_fusion.2.refs_5_), custom_call_target="tpu_custom_call" | custom-call | flops 6442450944 | bytes 4718592 | tf_op jit(solution)/shard_map/unpack/pallas_call | solution.py:89
  485.4 21.5 %all-to-all-done.14 = bf16[8,4,128,256]{3,2,1,0:T(8,128)(2,1)S(1)} async-done(((bf16[8,4,128,256]{3,2,1,0:T(8,128)(2,1)}), bf16[8,4,128,256]{3,2,1,0:T(8,128)(2,1)S(1)}, u32[]{:S(2)}, u32[]{:S(2)}) %all-to-all-start.14) | async-done | bytes 2097184 | tf_op jit(solution)/shard_map/all_to_all | solution.py:449
  544.7 53.6 %all_to_all.116 = bf16[4,512,256]{1,2,0:T(8,128)(2,1)S(1)} all-to-all(bf16[4,512,256]{1,2,0:T(8,128)(2,1)S(1)} %fusion.25), channel_id=1, replica_groups=mesh['row'=8,'col'=4] {'col'}, dimensions={0} | all-to-all | bytes 2097152 | tf_op jit(solution)/shard_map/all_to_all | solution.py:449
  599.8 31.6 %attend_backward.1 = bf16[2048,768]{1,0:T(8,128)(2,1)} custom-call(bf16[2048,768]{1,0:T(8,128)(2,1)} %convolution_convert_fusion.1.q_ref.k_ref.v_ref.refs_0_.refs_4_.refs_5_, bf16[2048,256]{1,0:T(8,128)(2,1)} %bitcast.148, bf16[2048,256]{1,0:T(8,128)(2,1)} %get-tuple-element.124.rest_1_.refs_2_, f32[4,2048]{1,0:T(4,128)} %get-tuple-element.212.refs_3_, ...), custom_call_target="tpu_custom_call" | custom-call | flops 21474836480 | bytes 8388608 | tf_op jit(solution)/shard_map/attend_backward/pallas_call | solution.py:287
  672.9 44.5 %reduce-scatter.23.cloned.1.call-done = bf16[512,1024]{1,0:T(8,128)(2,1)} async-done(((bf16[2048,1024]{1,0:T(8,128)(2,1)}), bf16[512,1024]{1,0:T(8,128)(2,1)}) %reduce-scatter.23.cloned.1.call-update) | async-done | bytes 1048592 | tf_op jit(solution)/shard_map/reduce_scatter | solution.py:726
  743.8 20.4 %all_to_all.117 = bf16[4,128,288]{1,2,0:T(8,128)(2,1)S(1)} all-to-all(bf16[4,128,288]{1,2,0:T(8,128)(2,1)S(1)} %pad_maximum_fusion.3), channel_id=1, replica_groups=mesh['row'=8,'col'=4] {'col'}, dimensions={0} | all-to-all | bytes 589824 | tf_op jit(solution)/shard_map/all_to_all | solution.py:449
  770.2 18.5 %all-to-all-done.18 = bf16[8,128,768]{2,1,0:T(8,128)(2,1)S(1)} async-done(((bf16[8,128,768]{2,1,0:T(8,128)(2,1)}), bf16[8,128,768]{2,1,0:T(8,128)(2,1)S(1)}, u32[]{:S(2)}, u32[]{:S(2)}) %all-to-all-start.18) | async-done | bytes 1572896 | tf_op jit(solution)/shard_map/all_to_all | solution.py:449
  790.1 21.9 %all-gather.12.cloned.1.call-done = bf16[2048,1024]{1,0:T(8,128)(2,1)} async-done(((bf16[512,1024]{1,0:T(8,128)(2,1)}), bf16[2048,1024]{1,0:T(8,128)(2,1)}) %all-gather.12.cloned.1.call-update) | async-done | bytes 4194320 | tf_op jit(solution)/shard_map/all_gather | solution.py:751
  (228 shorter events, 323.4 us)
Async XLA Ops:
  7.2 34.1 %all-gather.8.cloned.1.call-start = ((), (), s32[]{:S(2)}) async-start(), calls=%async_computation.30 | async-start | bytes 2064384 | tf_op jit(solution)/shard_map/all_gather | solution.py:513
  14.8 25.7 %all-to-all-start = ((bf16[4,128,256]{2,1,0:T(8,128)(2,1)}), bf16[4,128,256]{2,1,0:T(8,128)(2,1)S(1)}, u32[]{:S(2)}, u32[]{:S(2)}) async-start(bf16[4,128,256]{2,1,0:T(8,128)(2,1)} %broadcast_in_dim.14), calls=%async_computation | async-start | bytes 524288 | tf_op jit(solution)/shard_map/all_to_all | solution.py:449
  21.1 146.9 %all-gather.10.cloned.1.call-start = ((), (), s32[]{:S(2)}) async-start(), calls=%async_computation.31 | async-start | bytes 2359296 | tf_op jit(solution)/shard_map/all_gather | solution.py:555
  71.4 30.2 %all-to-all-start.1 = ((bf16[8,128,1024]{2,1,0:T(8,128)(2,1)}), bf16[8,128,1024]{2,1,0:T(8,128)(2,1)S(1)}, u32[]{:S(2)}, u32[]{:S(2)}) async-start(bf16[8,128,1024]{2,1,0:T(8,128)(2,1)} %bitcast.141), calls=%async_computation.1 | async-start | bytes 4194304 | tf_op jit(solution)/shard_map/all_to_all | solution.py:449
  75.0 93.0 %all-gather.14.cloned.1.call-start = ((), (), s32[]{:S(2)}) async-start(), calls=%async_computation.41 | async-start | bytes 5242880 | tf_op jit(solution)/shard_map/all_gather | solution.py:548
  162.6 30.4 %all-to-all-start.4 = ((bf16[8,128,1024]{2,1,0:T(8,128)(2,1)}), bf16[8,128,1024]{2,1,0:T(8,128)(2,1)S(1)}, u32[]{:S(2)}, u32[]{:S(2)}) async-start(bf16[8,128,1024]{2,1,0:T(8,128)(2,1)} %bitcast.143), calls=%async_computation.4 | async-start | bytes 4194304 | tf_op jit(solution)/shard_map/all_to_all | solution.py:449
  216.8 116.5 %reduce-scatter.9.cloned.1.call-start = ((), (), s32[]{:S(2)}) async-start(), calls=%async_computation.32 | async-start | bytes 1310720 | tf_op jit(solution)/shard_map/reduce_scatter | solution.py:590
  235.0 30.7 %all-to-all-start.7 = ((bf16[8,128,1024]{2,1,0:T(8,128)(2,1)}), bf16[8,128,1024]{2,1,0:T(8,128)(2,1)S(1)}, u32[]{:S(2)}, u32[]{:S(2)}) async-start(bf16[8,128,1024]{2,1,0:T(8,128)(2,1)} %bitcast.125), calls=%async_computation.7 | async-start | bytes 4194304 | tf_op jit(solution)/shard_map/all_to_all | solution.py:449
  239.1 195.9 %reduce-scatter.13.cloned.1.call-start = ((), (), s32[]{:S(2)}) async-start(), calls=%async_computation.34 | async-start | bytes 1310720 | tf_op jit(solution)/shard_map/reduce_scatter | solution.py:590
  267.0 30.2 %all-to-all-start.8 = ((bf16[8,128,1024]{2,1,0:T(8,128)(2,1)}), bf16[8,128,1024]{2,1,0:T(8,128)(2,1)S(1)}, u32[]{:S(2)}, u32[]{:S(2)}) async-start(bf16[8,128,1024]{2,1,0:T(8,128)(2,1)} %bitcast.126), calls=%async_computation.8 | async-start | bytes 4194304 | tf_op jit(solution)/shard_map/all_to_all | solution.py:449
  270.6 189.2 %reduce-scatter.15.cloned.1.call-start = ((), (), s32[]{:S(2)}) async-start(), calls=%async_computation.35 | async-start | bytes 2621440 | tf_op jit(solution)/shard_map/reduce_scatter | solution.py:590
  298.5 31.0 %all-to-all-start.9 = ((bf16[8,128,1024]{2,1,0:T(8,128)(2,1)}), bf16[8,128,1024]{2,1,0:T(8,128)(2,1)}, u32[]{:S(2)}, u32[]{:S(2)}) async-start(bf16[8,128,1024]{2,1,0:T(8,128)(2,1)} %bitcast.122), calls=%async_computation.9 | async-start | bytes 4194304 | tf_op jit(solution)/shard_map/all_to_all | solution.py:449
  302.9 157.0 %reduce-scatter.17.cloned.1.call-start = ((), (), s32[]{:S(2)}) async-start(), calls=%async_computation.36 | async-start | bytes 2621440 | tf_op jit(solution)/shard_map/reduce_scatter | solution.py:590
  329.5 35.8 %all-to-all-start.10 = ((bf16[8,2,128,640]{3,2,1,0:T(8,128)(2,1)}), bf16[8,2,128,640]{3,2,1,0:T(8,128)(2,1)S(1)}, u32[]{:S(2)}, u32[]{:S(2)}) async-start(bf16[8,2,128,640]{3,2,1,0:T(8,128)(2,1)} %get-tuple-element.186), calls=%async_computation.11 | async-start | bytes 5242880 | tf_op jit(solution)/shard_map/all_to_all | solution.py:449
  333.2 126.7 %reduce-scatter.19.cloned.1.call-start = ((), (), s32[]{:S(2)}) async-start(), calls=%async_computation.37 | async-start | bytes 2621440 | tf_op jit(solution)/shard_map/reduce_scatter | solution.py:670
  366.9 36.8 %all-to-all-start.11 = ((bf16[8,2,128,640]{3,2,1,0:T(8,128)(2,1)}), bf16[8,2,128,640]{3,2,1,0:T(8,128)(2,1)}, u32[]{:S(2)}, u32[]{:S(2)}) async-start(bf16[8,2,128,640]{3,2,1,0:T(8,128)(2,1)} %get-tuple-element.190), calls=%async_computation.12 | async-start | bytes 5242880 | tf_op jit(solution)/shard_map/all_to_all | solution.py:449
  407.3 99.6 %reduce-scatter.11.cloned.1.call-start = ((), (), s32[]{:S(2)}) async-start(), calls=%async_computation.33 | async-start | bytes 3276800 | tf_op jit(solution)/shard_map/reduce_scatter | solution.py:679
  429.6 33.2 %all-to-all-start.13 = ((bf16[8,2,128,384]{3,2,1,0:T(8,128)(2,1)}), bf16[8,2,128,384]{3,2,1,0:T(8,128)(2,1)}, u32[]{:S(2)}, u32[]{:S(2)}) async-start(bf16[8,2,128,384]{3,2,1,0:T(8,128)(2,1)} %get-tuple-element.197), calls=%async_computation.15 | async-start | bytes 3145728 | tf_op jit(solution)/shard_map/all_to_all | solution.py:449
  433.9 102.4 %reduce-scatter.21.cloned.1.call-start = ((), (), s32[]{:S(2)}) async-start(), calls=%async_computation.38 | async-start | bytes 1966080 | tf_op jit(solution)/shard_map/reduce_scatter | solution.py:682
  476.1 30.7 %all-to-all-start.14 = ((bf16[8,4,128,256]{3,2,1,0:T(8,128)(2,1)}), bf16[8,4,128,256]{3,2,1,0:T(8,128)(2,1)S(1)}, u32[]{:S(2)}, u32[]{:S(2)}) async-start(bf16[8,4,128,256]{3,2,1,0:T(8,128)(2,1)} %pad_maximum_fusion.2.refs_5_), calls=%async_computation.21 | async-start | bytes 4194304 | tf_op jit(solution)/shard_map/all_to_all | solution.py:449
  480.2 151.2 %all-gather.16.cloned.1.call-start = ((), (), s32[]{:S(2)}) async-start(), calls=%async_computation.42 | async-start | bytes 5242880 | tf_op jit(solution)/shard_map/all_gather | solution.py:698
  530.5 186.9 %reduce-scatter.23.cloned.1.call-start = ((), (), s32[]{:S(2)}) async-start(), calls=%async_computation.39 | async-start | bytes 5242880 | tf_op jit(solution)/shard_map/reduce_scatter | solution.py:726
  654.2 64.7 %all-to-all-start.17 = ((bf16[8,128,1056]{1,2,0:T(8,128)(2,1)}), bf16[8,128,1056]{1,2,0:T(8,128)(2,1)}, u32[]{:S(2)}, u32[]{:S(2)}) async-start(bf16[8,128,1056]{1,2,0:T(8,128)(2,1)} %copy.127), calls=%async_computation.25 | async-start | bytes 4325376 | tf_op jit(solution)/shard_map/all_to_all | solution.py:449
  658.5 153.5 %all-gather.12.cloned.1.call-start = ((), (), s32[]{:S(2)}) async-start(), calls=%async_computation.40 | async-start | bytes 5242880 | tf_op jit(solution)/shard_map/all_gather | solution.py:751
  (40 other events, 334.1 us)
Sparse Core Ops, SparseCore 0:
  11.8 29.4 all-gather.7
  43.8 27.8 all-gather.9
  77.4 82.5 all-gather.13
  234.2 28.8 reduce-scatter.8
  265.9 26.7 reduce-scatter.12
  297.3 43.3 reduce-scatter.14
  343.2 43.1 reduce-scatter.16
  388.7 43.1 reduce-scatter.18
  434.4 51.4 reduce-scatter.10
  488.1 34.9 reduce-scatter.20
  524.8 101.8 all-gather.15
  639.3 78.0 reduce-scatter.22
  724.3 87.6 all-gather.11

commit v8 on v7

--- a/solution.py
+++ b/solution.py
@@ -345,9 +345,9 @@
         first += wide
 
 
-def expert_pass(chunk, x, grad_y, w_in, w_back, kept, sent, members, parts, pieces, waits=()):
+def expert_pass(chunk, x, grad_y, w_in, w_back, kept, sent, parts, pieces, waits=()):
     e, low, size = chunk
-    sources, cap, depth = grad_y.shape
+    sources, members, cap, depth = grad_y.shape
     rows = sources * size
     width = w_in.shape[2]
     step = min(256, rows)
@@ -368,7 +368,7 @@
         grid=(rows // step,),
         in_specs=[
             pl.BlockSpec((step, depth), lambda i: (i, 0)),
-            pl.BlockSpec((group, size, depth), lambda i: (i, at, 0)),
+            pl.BlockSpec((group, None, size, depth), lambda i: (i, e % members, at, 0)),
             pl.BlockSpec((None, depth, width), lambda i: (e, 0, 0)),
             pl.BlockSpec((None, width, depth), lambda i: (e, 0, 0)),
         ]
@@ -401,7 +401,8 @@
         gate = jnp.sum(raised * pick_ref[...], axis=1, keepdims=True)
         gate = gate / jnp.sum(raised, axis=1, keepdims=True)
         xt_ref[...] = (x_ref[...].astype(jnp.float32) * gate).T.astype(jnp.bfloat16)
-        gyg_ref[...] = (gy_ref[...].astype(jnp.float32) * gate).astype(jnp.bfloat16)
+        grad_y = gy_ref[...].reshape(rows, depth).astype(jnp.float32)
+        gyg_ref[...] = (grad_y * gate).astype(jnp.bfloat16)
 
     gin_ref[...] = dot(xt_ref[...], slope_ref[...], NN)
     gback_ref[...] = dot(active_ref[...], gyg_ref[...], TN)
@@ -409,7 +410,7 @@
 
 def weight_pass(e, local, x, grad_y, router, pick, active, slope, sent, waits=()):
     rows, width = active.shape
-    depth = x.shape[1]
+    sources, members, cap, depth = grad_y.shape
     step = min(256, width)
     sent = list(sent or [])
     return pl.pallas_call(
@@ -422,7 +423,7 @@
         grid=(width // step,),
         in_specs=[
             pl.BlockSpec((rows, depth), lambda i: (0, 0)),
-            pl.BlockSpec((rows, depth), lambda i: (0, 0)),
+            pl.BlockSpec((sources, None, cap, depth), lambda i: (0, e % members, 0, 0)),
             pl.BlockSpec(router.shape, lambda i: (0, 0)),
             pl.BlockSpec(pick.shape, lambda i: (0, 0)),
             pl.BlockSpec((rows, step), lambda i: (0, i)),
@@ -528,8 +529,15 @@
         for g in range(local // members)
     ]
 
-    early = min(2, local)
-    grad_packed = list(pack(slots_by_local, [cotangent], 0, block_rows, early))
+    slots_by_pair = slots_by_local - slots_by_local
+    for g, at in enumerate(slots_by_group):
+        slots_by_pair = jnp.where(at >= 0, at + g * members * block_rows, slots_by_pair)
+
+    def pack_group(g, waits):
+        rows = members * block_rows
+        return pack(slots_by_pair, [cotangent], g * rows, rows, 1, waits)[0]
+
+    grad_packed = [pack_group(0, [])]
     weights, grad_packed[0], out_block, mean_one, inverse_one = tie(
         weights, grad_packed[0], out_block, mean_one, inverse_one
     )
@@ -546,17 +554,13 @@
     context, logsum = attend_forward(projected, tuple(range(length // block)), block)
     context, grad_packed[0] = tie(context, grad_packed[0])
     full = lax.all_gather(context, "col", axis=0)
-    grad_arrived = [send(grad_packed[0])]
-    if local > early:
-        grad_packed += pack(
-            slots_by_local, [cotangent], early * block_rows, block_rows, local - early, [context]
-        )
-    grad_arrived[0], *grad_packed[1:] = tie(grad_arrived[0], *grad_packed[1:])
+    grad_packed += [pack_group(g, [context]) for g in range(1, local // members)]
     out_full = lax.all_gather(out_block, "row", axis=1, tiled=True)
-    for e in range(1, local):
-        grad_arrived.append(send(grad_packed[e]))
-        if e + 1 < local:
-            grad_arrived[e], grad_packed[e + 1] = tie(grad_arrived[e], grad_packed[e + 1])
+    grad_arrived = []
+    for g in range(local // members):
+        if g:
+            grad_arrived[-1], grad_packed[g] = tie(grad_arrived[-1], grad_packed[g])
+        grad_arrived.append(swap(grad_packed[g].reshape(rows_all, members, cap, depth), "row"))
     full, out_full = tie(full, out_full)
     middle, routed = middle_pass(full, out_full, tokens, gains[1:2], biases[1:2])
 
@@ -598,12 +602,11 @@
         made, both, pair = expert_pass(
             chunks[k],
             arrived[k],
-            grad_arrived[e].reshape(rows_all, cap, depth),
+            grad_arrived[e // members],
             w_in,
             w_back,
             kept.pop() if low else [],
             sent.pop() if low or e % members else [],
-            members,
             cols_all,
             pieces,
             waits,
@@ -636,7 +639,7 @@
             e,
             local,
             arrived[e],
-            grad_arrived[e],
+            grad_arrived[e // members],
             router_full,
             pick.astype(jnp.float32),
             active[e],
@@ -675,14 +678,18 @@
             waits = [token]
         else:
             homed = jnp.stack(joined(summed), axis=1)
-            waits = [token, homed]
+            homed, token = tie(homed, token)
+            waits = [token]
             grad_sent.append(lax.psum_scatter(whole, "col", scatter_dimension=0, tiled=True))
         whole = unpack(slots_by_group, [v.reshape(-1, wide) for v in rows], step, waits)
+        if f:
+            rows[-1], homed = tie(rows[-1], homed)
+            homed = swap(homed, "row")
+            whole, homed = tie(whole, homed)
         waits = [whole]
     grad_sent.append(lax.psum_scatter(whole, "col", scatter_dimension=0, tiled=True))
 
     grad_in, grad_back = grad_weights
-    homed = swap(homed, "row")
     returned = unpack(
         [slots], [homed.reshape(experts * cap, depth // cols_all)], step, grad_sent[:1]
     ).astype(jnp.float32)
@@ -717,9 +724,13 @@
         "td,zdc->ztc", grad_attn, out_full, preferred_element_type=jnp.float32
     ).astype(jnp.bfloat16)
     grad_context = swap(grad_context, "col")
+    context_own = own(full, 1)
+    grad_out = jnp.einsum("td,ztc->dzc", grad_attn, context_own, preferred_element_type=jnp.float32)
+    plane = jnp.concatenate([grad_out.reshape(depth, cols_all * width), grad_router], axis=1)
+    plane = swap(plane.astype(jnp.bfloat16).reshape(rows_all, share, -1), "row")
     grad_context = grad_context.reshape(length, width)
     grad_proj = attend_backward(projected, grad_context, context, logsum, block, 0)[0]
-    grad_proj, grad_attn, mixed_full = tie(grad_proj, grad_attn, mixed_full)
+    grad_proj, plane, mixed_full = tie(grad_proj, plane, mixed_full)
 
     def spread(grads):
         made = jnp.einsum("tc,dc->td", grads, qkv_full, preferred_element_type=jnp.float32)
@@ -728,14 +739,8 @@
         ).astype(jnp.float32)
 
     grad_normal = spread(grad_proj)
-    context_own = own(full, 1)
-    grad_out = jnp.einsum("td,ztc->dzc", grad_attn, context_own, preferred_element_type=jnp.float32)
-    plane = jnp.concatenate([grad_out.reshape(depth, cols_all * width), grad_router], axis=1)
-    plane = swap(plane.astype(jnp.bfloat16).reshape(rows_all, share, -1), "row")
     mixed_out = mixed_full.transpose(1, 0, 2).reshape(length, depth)
     grad_qkv = jnp.einsum("td,tc->dc", normal_in, grad_proj, preferred_element_type=jnp.float32)
-    grad_normal, plane, mixed_out, grad_qkv = tie(grad_normal, plane, mixed_out, grad_qkv)
-
     plane = jnp.sum(plane.astype(jnp.float32), axis=0)
     router_share = plane[:, cols_all * width :].reshape(1, share, experts)
     out_share = plane[:, : cols_all * width].reshape(share, cols_all, width).transpose(1, 0, 2)
@@ -743,6 +748,9 @@
     plane = jnp.concatenate([out_share, router_share], axis=2).astype(jnp.bfloat16)
     plane = jnp.sum(swap(plane, "col").astype(jnp.float32), axis=0)
     out_share, router_share = plane[:, :width].T, plane[:, width:]
+    grad_normal, out_share, mixed_out, grad_qkv = tie(
+        grad_normal, out_share, mixed_out, grad_qkv
+    )
 
     own_normed, own_inverse = layer_stats(own(tokens).astype(jnp.float32))
     grad_tokens = (

time: 830 us -> 812 us (0.978)
  blocking collectives: 135 us -> 18.1 us
  waiting for transfers between devices: 198 us -> 302 us
    all_to_all x4 -> x2, blocking collectives: 135 us -> 18.1 us  [swap(): return lax.all_to_all(blocks, axis, split_axis=0, concat_axis=0, tiled=True)]
    all_to_all x18, waiting for transfers between devices: 130 us -> 174 us  [swap(): return lax.all_to_all(blocks, axis, split_axis=0, concat_axis=0, tiled=True)]
    all_gather x1, waiting for transfers between devices: 0.01 us -> 29.1 us  [per_device(): full = lax.all_gather(context, 'col', axis=0)]
    all_gather x1, waiting for transfers between devices: 21.9 us -> 37.7 us  [per_device(): grad_tokens = lax.all_gather(grad_tokens, 'col', axis=0, tiled=True)]
    reduce_scatter x1, waiting for transfers between devices: 44.5 us -> 55.7 us  [spread(): lax.psum_scatter(made.astype(jnp.bfloat16), 'col', scatter_dimension=0, t...]
    unnamed x74 -> x70, local copies, waits for them, and re-layouts: 19.6 us -> 15.7 us
  transfers between devices with their start and end apart: 31 -> 31, of which waited for: 16 -> 18; matrix products, arithmetic and copies ran while one was open for 11% -> 11% of each run, Pallas kernels for 34% -> 34%
where the time goes in v8:
time: 812 us; the launch traced here: 805 us
  waiting for transfers between devices  302 us (37%)
  Pallas kernels  275 us (34%)
  starting transfers between devices  75.1 us (9%)
  other arithmetic  42.5 us (5%)
  matrix products  40.7 us (5%)
  local copies, waits for them, and re-layouts  36.5 us (4%)
  blocking collectives  18.1 us (2%)
  between operations  14.8 us (2%)
    all_to_all x18, waiting for transfers between devices, swap(): return lax.all_to_all(blocks, axis, split_axis=0, concat_axis=0, tiled=True)  174 us
    all_to_all x18, starting transfers between devices, swap(): return lax.all_to_all(blocks, axis, split_axis=0, concat_axis=0, tiled=True)  74.6 us
    pallas_call x5, Pallas kernels, expert_pass(): pl.pallas_call(functools.partial(expert_body, len(given) + len(waits)), o...  62.2 us
    pallas_call x7, Pallas kernels, pack(): pl.pallas_call(functools.partial(pack_body, base, step, each, len(rows)),...  61.6 us
    reduce_scatter x1, waiting for transfers between devices, spread(): lax.psum_scatter(made.astype(jnp.bfloat16), 'col', scatter_dimension=0, t...  55.7 us
    pallas_call x4, Pallas kernels, weight_pass(): pl.pallas_call(functools.partial(weight_body, len(sent) + len(waits)), ou...  46.9 us
    pallas_call x3, Pallas kernels, unpack(): pl.pallas_call(functools.partial(unpack_body, len(rows)), out_shape=jax.S...  40.7 us
    all_gather x1, waiting for transfers between devices, per_device(): grad_tokens = lax.all_gather(grad_tokens, 'col', axis=0, tiled=True)  37.7 us
  transfers between devices with their start and end apart: 31, of which 18 were waited for; matrix products, arithmetic and copies ran while one was open for 11% of the time, Pallas kernels for 34%

profile of v8, /device:TPU:0, one launch (start us, length us, event | category | flops | bytes accessed | tf_op | source)
XLA Modules:
  0.0 805.4 jit_solution(1248754583413888558)
XLA Ops:
  26.9 13.4 %pack.7 = bf16[2048,1024]{1,0:T(8,128)(2,1)} custom-call(s32[1,2048]{1,0:T(1,128)} %bitcast.158, bf16[2048,1024]{1,0:T(8,128)(2,1)} %rest_0_.3), custom_call_target="tpu_custom_call" | custom-call | flops 1 | bytes 1 | tf_op jit(solution)/shard_map/pack/pallas_call | solution.py:55
  52.1 19.3 %attend_forward.1 = (bf16[2048,256]{1,0:T(8,128)(2,1)}, f32[4,2048]{1,0:T(4,128)}) custom-call(bf16[2048,768]{1,0:T(8,128)(2,1)} %convolution_convert_fusion.1.q_ref.k_ref.v_ref.refs_0_.refs_4_.refs_5_, bf16[2048,768]{1,0:T(8,128)(2,1)} %convolution_convert_fusion.1.q_ref.k_ref.v_ref.refs_0_.refs_4_.refs_5_, ...), custom_call_target="tpu_custom_call" | custom-call | flops 524288 | bytes 524288 | tf_op jit(solution)/shard_map/attend_forward/pallas_call | solution.py:195
  76.7 12.9 %pack.10 = bf16[2048,1024]{1,0:T(8,128)(2,1)} custom-call(s32[1,2048]{1,0:T(1,128)} %bitcast.159, bf16[2048,1024]{1,0:T(8,128)(2,1)} %rest_0_.3, bf16[2048,256]{1,0:T(8,128)(2,1)} %get-tuple-element.118.rest_1_.refs_2_), custom_call_target="tpu_custom_call" | custom-call | flops 1 | bytes 1 | tf_op jit(solution)/shard_map/pack/pallas_call | solution.py:55
  89.6 35.4 %all-to-all-done.1.gy_ref = bf16[8,2,128,1024]{3,2,1,0:T(8,128)(2,1)} async-done(((bf16[8,2,128,1024]{3,2,1,0:T(8,128)(2,1)}), bf16[8,2,128,1024]{3,2,1,0:T(8,128)(2,1)}, u32[]{:S(2)}, u32[]{:S(2)}) %all-to-all-start.1) | async-done | bytes 4194336 | tf_op jit(solution)/shard_map/all_to_all | solution.py:450
  131.5 29.1 %all-gather.14.cloned.1.call-done = bf16[8192,256]{1,0:T(8,128)(2,1)} async-done(((bf16[2048,256]{1,0:T(8,128)(2,1)}), bf16[8192,256]{1,0:T(8,128)(2,1)}) %all-gather.14.cloned.1.call-update) | async-done | bytes 4194320 | tf_op jit(solution)/shard_map/all_gather | solution.py:556
  160.6 12.9 %middle_pass.1 = (f32[2048,1024]{1,0:T(8,128)}, bf16[2048,1024]{1,0:T(8,128)(2,1)}) custom-call(bf16[4,2048,256]{2,1,0:T(8,128)(2,1)} %bitcast.168, bf16[4,1024,256]{2,1,0:T(8,128)(2,1)} %all-gather.10.cloned.1.call-done.out_ref, bf16[2048,1024]{1,0:T(8,128)(2,1)} %tokens_ref.1, f32[1,1024]{1,0:T(1,128)} %copy.127.gain_ref, f32[1,1024]{1,0:T(1,128)} %copy.128.bias_ref), custom_call_target="tpu_custom_call" | custom-call | flops 4294967296 | bytes 20971520 | tf_op jit(solution)/shard_map/middle_pass/pallas_call | solution.py:126
  254.6 14.5 %expert_pass.7 = (bf16[4,1024,256]{2,1,0:T(8,128)(2,1)}, bf16[8,128,1024]{2,1,0:T(8,128)(2,1)}, bf16[8,128,1024]{2,1,0:T(8,128)(2,1)}, bf16[8,2,128,640]{3,2,1,0:T(8,128)(2,1)}, bf16[8,2,128,384]{3,2,1,0:T(8,128)(2,1)}) custom-call(bf16[1024,1024]{1,0:T(8,128)(2,1)} %bitcast.21.x_ref, ...), custom_call_target="tpu_custom_call", output_to_operand_aliasing={{3}: (4, {}), {4}: (5, {})} | custom-call | flops 8589934592 | bytes 16777216 | tf_op jit(solution)/shard_map/expert_pass/pallas_call | solution.py:364
  286.9 14.4 %expert_pass.8 = (bf16[4,1024,256]{2,1,0:T(8,128)(2,1)}, bf16[8,128,1024]{2,1,0:T(8,128)(2,1)}, bf16[8,128,1024]{2,1,0:T(8,128)(2,1)}, bf16[8,2,128,640]{3,2,1,0:T(8,128)(2,1)}, bf16[8,2,128,384]{3,2,1,0:T(8,128)(2,1)}) custom-call(bf16[1024,1024]{1,0:T(8,128)(2,1)} %bitcast.112, bf16[8,2,128,1024]{3,2,1,0:T(8,128)(2,1)} %all-to-all-done.2.gy_ref, ...), custom_call_target="tpu_custom_call" | custom-call | flops 8589934592 | bytes 16777216 | tf_op jit(solution)/shard_map/expert_pass/pallas_call | solution.py:364
  301.2 12.2 %all-to-all-done.7 = bf16[8,128,1024]{2,1,0:T(8,128)(2,1)} async-done(((bf16[8,128,1024]{2,1,0:T(8,128)(2,1)}), bf16[8,128,1024]{2,1,0:T(8,128)(2,1)}, u32[]{:S(2)}, u32[]{:S(2)}) %all-to-all-start.7) | async-done | bytes 2097184 | tf_op jit(solution)/shard_map/all_to_all | solution.py:450
  317.2 14.6 %expert_pass.9 = (bf16[4,1024,256]{2,1,0:T(8,128)(2,1)}, bf16[8,128,1024]{2,1,0:T(8,128)(2,1)}, bf16[8,128,1024]{2,1,0:T(8,128)(2,1)}, bf16[8,2,128,640]{3,2,1,0:T(8,128)(2,1)}, bf16[8,2,128,384]{3,2,1,0:T(8,128)(2,1)}) custom-call(bf16[1024,1024]{1,0:T(8,128)(2,1)} %bitcast.25.x_ref, ...), custom_call_target="tpu_custom_call", output_to_operand_aliasing={{3}: (4, {}), {4}: (5, {})} | custom-call | flops 8589934592 | bytes 16777216 | tf_op jit(solution)/shard_map/expert_pass/pallas_call | solution.py:364
  331.8 17.5 %all-to-all-done.8 = bf16[8,2,128,640]{3,2,1,0:T(8,128)(2,1)S(1)} async-done(((bf16[8,2,128,640]{3,2,1,0:T(8,128)(2,1)}), bf16[8,2,128,640]{3,2,1,0:T(8,128)(2,1)S(1)}, u32[]{:S(2)}, u32[]{:S(2)}) %all-to-all-start.8) | async-done | bytes 2621472 | tf_op jit(solution)/shard_map/all_to_all | solution.py:450
  359.7 11.7 %weight_pass.4 = (f32[4,1024,1024]{2,1,0:T(8,128)}, f32[4,1024,1024]{2,1,0:T(8,128)}, f32[8,128]{1,0:T(8,128)}) custom-call(bf16[1024,1024]{1,0:T(8,128)(2,1)} %bitcast.131, bf16[8,2,128,1024]{3,2,1,0:T(8,128)(2,1)} %all-to-all-done.1.gy_ref, bf16[1024,32]{1,0:T(8,128)(2,1)} %slice.60.router_ref, f32[1,32]{1,0:T(1,128)} %compare_convert_fusion.2.pick_ref, ...), custom_call_target="tpu_custom_call" | custom-call | flops 4294967296 | bytes 16777216 | tf_op jit(solution)/shard_map/weight_pass/pallas_call | solution.py:416
  371.4 11.7 %weight_pass.5 = (f32[4,1024,1024]{2,1,0:T(8,128)}, f32[4,1024,1024]{2,1,0:T(8,128)}, f32[8,128]{1,0:T(8,128)}) custom-call(bf16[1024,1024]{1,0:T(8,128)(2,1)} %bitcast.21.x_ref, bf16[8,2,128,1024]{3,2,1,0:T(8,128)(2,1)} %all-to-all-done.1.gy_ref, bf16[1024,32]{1,0:T(8,128)(2,1)} %slice.60.router_ref, ...), custom_call_target="tpu_custom_call", output_to_operand_aliasing={{0}: (6, {}), {1}: (7, {})} | custom-call | flops 4294967296 | bytes 16777216 | tf_op jit(solution)/shard_map/weight_pass/pallas_call | solution.py:416
  394.0 18.3 %unpack.3.rest_2_ = bf16[2048,640]{1,0:T(8,128)(2,1)} custom-call(s32[2048,1]{1,0:T(8,128)} %copy.129.refs_0_, s32[2048,1]{1,0:T(8,128)} %copy.130.refs_1_, bf16[2048,640]{1,0:T(8,128)(2,1)} %bitcast.122, bf16[2048,640]{1,0:T(8,128)(2,1)} %bitcast.37.refs_3_, f32[8,128]{1,0:T(8,128)} %get-tuple-element.179.refs_4_), custom_call_target="tpu_custom_call" | custom-call | flops 10737418240 | bytes 7864320 | tf_op jit(solution)/shard_map/unpack/pallas_call | solution.py:89
  419.9 11.7 %weight_pass.6 = (f32[4,1024,1024]{2,1,0:T(8,128)}, f32[4,1024,1024]{2,1,0:T(8,128)}, f32[8,128]{1,0:T(8,128)}) custom-call(bf16[1024,1024]{1,0:T(8,128)(2,1)} %bitcast.113, bf16[8,2,128,1024]{3,2,1,0:T(8,128)(2,1)} %all-to-all-done.2.gy_ref, bf16[1024,32]{1,0:T(8,128)(2,1)} %slice.60.router_ref, ...), custom_call_target="tpu_custom_call", output_to_operand_aliasing={{0}: (6, {}), {1}: (7, {})} | custom-call | flops 4294967296 | bytes 16777216 | tf_op jit(solution)/shard_map/weight_pass/pallas_call | solution.py:416
  431.6 11.7 %weight_pass.7 = (f32[4,1024,1024]{2,1,0:T(8,128)}, f32[4,1024,1024]{2,1,0:T(8,128)}, f32[8,128]{1,0:T(8,128)}) custom-call(bf16[1024,1024]{1,0:T(8,128)(2,1)} %bitcast.25.x_ref, bf16[8,2,128,1024]{3,2,1,0:T(8,128)(2,1)} %all-to-all-done.2.gy_ref, bf16[1024,32]{1,0:T(8,128)(2,1)} %slice.60.router_ref, ...), custom_call_target="tpu_custom_call", output_to_operand_aliasing={{0}: (6, {}), {1}: (7, {})} | custom-call | flops 4294967296 | bytes 16777216 | tf_op jit(solution)/shard_map/weight_pass/pallas_call | solution.py:416
  451.7 13.3 %unpack.4 = bf16[2048,384]{1,0:T(8,128)(2,1)} custom-call(s32[2048,1]{1,0:T(8,128)} %copy.129.refs_0_, s32[2048,1]{1,0:T(8,128)} %copy.130.refs_1_, bf16[2048,384]{1,0:T(8,128)(2,1)} %bitcast.134, bf16[2048,384]{1,0:T(8,128)(2,1)} %bitcast.135, f32[8,128]{1,0:T(8,128)} %get-tuple-element.197.refs_4_), custom_call_target="tpu_custom_call" | custom-call | flops 6442450944 | bytes 4718592 | tf_op jit(solution)/shard_map/unpack/pallas_call | solution.py:89
  465.1 13.2 %all-to-all-done.12 = bf16[8,4,128,256]{3,2,1,0:T(8,128)(2,1)S(1)} async-done(((bf16[8,4,128,256]{3,2,1,0:T(8,128)(2,1)}), bf16[8,4,128,256]{3,2,1,0:T(8,128)(2,1)S(1)}, u32[]{:S(2)}, u32[]{:S(2)}) %all-to-all-start.12) | async-done | bytes 2097184 | tf_op jit(solution)/shard_map/all_to_all | solution.py:450
  539.3 37.7 %all-to-all-done.14 = bf16[4,512,256]{1,2,0:T(8,128)(2,1)S(1)} async-done(((bf16[4,512,256]{1,2,0:T(8,128)(2,1)}), bf16[4,512,256]{1,2,0:T(8,128)(2,1)S(1)}, u32[]{:S(2)}, u32[]{:S(2)}) %all-to-all-start.14) | async-done | bytes 1048608 | tf_op jit(solution)/shard_map/all_to_all | solution.py:450
  582.2 31.6 %attend_backward.1 = bf16[2048,768]{1,0:T(8,128)(2,1)} custom-call(bf16[2048,768]{1,0:T(8,128)(2,1)} %convolution_convert_fusion.1.q_ref.k_ref.v_ref.refs_0_.refs_4_.refs_5_, bf16[2048,256]{1,0:T(8,128)(2,1)} %bitcast.137, bf16[2048,256]{1,0:T(8,128)(2,1)} %get-tuple-element.118.rest_1_.refs_2_, f32[4,2048]{1,0:T(4,128)} %get-tuple-element.202.refs_3_, ...), custom_call_target="tpu_custom_call" | custom-call | flops 21474836480 | bytes 8388608 | tf_op jit(solution)/shard_map/attend_backward/pallas_call | solution.py:287
  649.6 55.7 %reduce-scatter.23.cloned.1.call-done = bf16[512,1024]{1,0:T(8,128)(2,1)} async-done(((bf16[2048,1024]{1,0:T(8,128)(2,1)}), bf16[512,1024]{1,0:T(8,128)(2,1)}) %reduce-scatter.23.cloned.1.call-update) | async-done | bytes 1048592 | tf_op jit(solution)/shard_map/reduce_scatter | solution.py:737
  720.5 9.9 %all_to_all.105 = f32[4,4,128]{2,1,0:T(4,128)S(1)} all-to-all(f32[4,4,128]{2,1,0:T(4,128)S(1)} %broadcast_in_dim.16), channel_id=1, replica_groups=mesh['row'=8,'col'=4] {'col'}, dimensions={0} | all-to-all | bytes 16384 | tf_op jit(solution)/shard_map/all_to_all | solution.py:450
  735.8 19.2 %all-to-all-done.17 = bf16[8,128,768]{2,1,0:T(8,128)(2,1)S(1)} async-done(((bf16[8,128,768]{2,1,0:T(8,128)(2,1)}), bf16[8,128,768]{2,1,0:T(8,128)(2,1)S(1)}, u32[]{:S(2)}, u32[]{:S(2)}) %all-to-all-start.17) | async-done | bytes 1572896 | tf_op jit(solution)/shard_map/all_to_all | solution.py:450
  756.3 37.7 %all-gather.12.cloned.1.call-done = bf16[2048,1024]{1,0:T(8,128)(2,1)} async-done(((bf16[512,1024]{1,0:T(8,128)(2,1)}), bf16[2048,1024]{1,0:T(8,128)(2,1)}) %all-gather.12.cloned.1.call-update) | async-done | bytes 4194320 | tf_op jit(solution)/shard_map/all_gather | solution.py:759
  (222 shorter events, 310.5 us)
Async XLA Ops:
  7.2 34.1 %all-gather.8.cloned.1.call-start = ((), (), s32[]{:S(2)}) async-start(), calls=%async_computation.28 | async-start | bytes 2064384 | tf_op jit(solution)/shard_map/all_gather | solution.py:514
  21.1 110.4 %all-gather.10.cloned.1.call-start = ((), (), s32[]{:S(2)}) async-start(), calls=%async_computation.29 | async-start | bytes 2359296 | tf_op jit(solution)/shard_map/all_gather | solution.py:558
  71.4 53.7 %all-to-all-start.1 = ((bf16[8,2,128,1024]{3,2,1,0:T(8,128)(2,1)}), bf16[8,2,128,1024]{3,2,1,0:T(8,128)(2,1)}, u32[]{:S(2)}, u32[]{:S(2)}) async-start(bf16[8,2,128,1024]{3,2,1,0:T(8,128)(2,1)} %bitcast.107), calls=%async_computation.1 | async-start | bytes 8388608 | tf_op jit(solution)/shard_map/all_to_all | solution.py:450
  76.0 84.6 %all-gather.14.cloned.1.call-start = ((), (), s32[]{:S(2)}) async-start(), calls=%async_computation.39 | async-start | bytes 5242880 | tf_op jit(solution)/shard_map/all_gather | solution.py:556
  125.1 54.0 %all-to-all-start.2 = ((bf16[8,2,128,1024]{3,2,1,0:T(8,128)(2,1)}), bf16[8,2,128,1024]{3,2,1,0:T(8,128)(2,1)}, u32[]{:S(2)}, u32[]{:S(2)}) async-start(bf16[8,2,128,1024]{3,2,1,0:T(8,128)(2,1)} %bitcast.108), calls=%async_computation.2 | async-start | bytes 8388608 | tf_op jit(solution)/shard_map/all_to_all | solution.py:450
  201.7 115.5 %reduce-scatter.9.cloned.1.call-start = ((), (), s32[]{:S(2)}) async-start(), calls=%async_computation.30 | async-start | bytes 1310720 | tf_op jit(solution)/shard_map/reduce_scatter | solution.py:594
  219.9 31.0 %all-to-all-start.5 = ((bf16[8,128,1024]{2,1,0:T(8,128)(2,1)}), bf16[8,128,1024]{2,1,0:T(8,128)(2,1)}, u32[]{:S(2)}, u32[]{:S(2)}) async-start(bf16[8,128,1024]{2,1,0:T(8,128)(2,1)} %bitcast.117), calls=%async_computation.5 | async-start | bytes 4194304 | tf_op jit(solution)/shard_map/all_to_all | solution.py:450
  224.3 194.6 %reduce-scatter.13.cloned.1.call-start = ((), (), s32[]{:S(2)}) async-start(), calls=%async_computation.32 | async-start | bytes 1310720 | tf_op jit(solution)/shard_map/reduce_scatter | solution.py:594
  251.0 30.2 %all-to-all-start.6 = ((bf16[8,128,1024]{2,1,0:T(8,128)(2,1)}), bf16[8,128,1024]{2,1,0:T(8,128)(2,1)S(1)}, u32[]{:S(2)}, u32[]{:S(2)}) async-start(bf16[8,128,1024]{2,1,0:T(8,128)(2,1)} %bitcast.118), calls=%async_computation.6 | async-start | bytes 4194304 | tf_op jit(solution)/shard_map/all_to_all | solution.py:450
  254.6 188.7 %reduce-scatter.15.cloned.1.call-start = ((), (), s32[]{:S(2)}) async-start(), calls=%async_computation.33 | async-start | bytes 2621440 | tf_op jit(solution)/shard_map/reduce_scatter | solution.py:594
  282.5 31.0 %all-to-all-start.7 = ((bf16[8,128,1024]{2,1,0:T(8,128)(2,1)}), bf16[8,128,1024]{2,1,0:T(8,128)(2,1)}, u32[]{:S(2)}, u32[]{:S(2)}) async-start(bf16[8,128,1024]{2,1,0:T(8,128)(2,1)} %bitcast.114), calls=%async_computation.7 | async-start | bytes 4194304 | tf_op jit(solution)/shard_map/all_to_all | solution.py:450
  286.8 156.5 %reduce-scatter.17.cloned.1.call-start = ((), (), s32[]{:S(2)}) async-start(), calls=%async_computation.34 | async-start | bytes 2621440 | tf_op jit(solution)/shard_map/reduce_scatter | solution.py:594
  313.5 35.8 %all-to-all-start.8 = ((bf16[8,2,128,640]{3,2,1,0:T(8,128)(2,1)}), bf16[8,2,128,640]{3,2,1,0:T(8,128)(2,1)S(1)}, u32[]{:S(2)}, u32[]{:S(2)}) async-start(bf16[8,2,128,640]{3,2,1,0:T(8,128)(2,1)} %get-tuple-element.171), calls=%async_computation.9 | async-start | bytes 5242880 | tf_op jit(solution)/shard_map/all_to_all | solution.py:450
  317.2 126.2 %reduce-scatter.19.cloned.1.call-start = ((), (), s32[]{:S(2)}) async-start(), calls=%async_computation.35 | async-start | bytes 2621440 | tf_op jit(solution)/shard_map/reduce_scatter | solution.py:673
  350.8 36.8 %all-to-all-start.9 = ((bf16[8,2,128,640]{3,2,1,0:T(8,128)(2,1)}), bf16[8,2,128,640]{3,2,1,0:T(8,128)(2,1)}, u32[]{:S(2)}, u32[]{:S(2)}) async-start(bf16[8,2,128,640]{3,2,1,0:T(8,128)(2,1)} %get-tuple-element.175), calls=%async_computation.10 | async-start | bytes 5242880 | tf_op jit(solution)/shard_map/all_to_all | solution.py:450
  391.2 92.5 %reduce-scatter.11.cloned.1.call-start = ((), (), s32[]{:S(2)}) async-start(), calls=%async_computation.31 | async-start | bytes 3276800 | tf_op jit(solution)/shard_map/reduce_scatter | solution.py:683
  413.5 32.8 %all-to-all-start.11 = ((bf16[8,2,128,384]{3,2,1,0:T(8,128)(2,1)}), bf16[8,2,128,384]{3,2,1,0:T(8,128)(2,1)S(1)}, u32[]{:S(2)}, u32[]{:S(2)}) async-start(bf16[8,2,128,384]{3,2,1,0:T(8,128)(2,1)} %get-tuple-element.182), calls=%async_computation.13 | async-start | bytes 3145728 | tf_op jit(solution)/shard_map/all_to_all | solution.py:450
  447.5 30.9 %all-to-all-start.12 = ((bf16[8,4,128,256]{3,2,1,0:T(8,128)(2,1)}), bf16[8,4,128,256]{3,2,1,0:T(8,128)(2,1)S(1)}, u32[]{:S(2)}, u32[]{:S(2)}) async-start(bf16[8,4,128,256]{3,2,1,0:T(8,128)(2,1)} %pad_maximum_fusion.2), calls=%async_computation.18 | async-start | bytes 4194304 | tf_op jit(solution)/shard_map/all_to_all | solution.py:450
  451.7 61.2 %reduce-scatter.21.cloned.1.call-start = ((), (), s32[]{:S(2)}) async-start(), calls=%async_computation.36 | async-start | bytes 1966080 | tf_op jit(solution)/shard_map/reduce_scatter | solution.py:690
  478.4 138.2 %all-gather.16.cloned.1.call-start = ((), (), s32[]{:S(2)}) async-start(), calls=%async_computation.40 | async-start | bytes 5242880 | tf_op jit(solution)/shard_map/all_gather | solution.py:705
  520.9 56.1 %all-to-all-start.14 = ((bf16[4,512,256]{1,2,0:T(8,128)(2,1)}), bf16[4,512,256]{1,2,0:T(8,128)(2,1)S(1)}, u32[]{:S(2)}, u32[]{:S(2)}) async-start(bf16[4,512,256]{1,2,0:T(8,128)(2,1)} %fusion.25), calls=%async_computation.21 | async-start | bytes 2097152 | tf_op jit(solution)/shard_map/all_to_all | solution.py:450
  577.1 36.7 %all-to-all-start.15 = ((bf16[8,128,1056]{1,2,0:T(8,128)(2,1)}), bf16[8,128,1056]{1,2,0:T(8,128)(2,1)S(1)}, u32[]{:S(2)}, u32[]{:S(2)}) async-start(bf16[8,128,1056]{1,2,0:T(8,128)(2,1)} %copy.142), calls=%async_computation.22 | async-start | bytes 4325376 | tf_op jit(solution)/shard_map/all_to_all | solution.py:450
  580.7 124.7 %reduce-scatter.23.cloned.1.call-start = ((), (), s32[]{:S(2)}) async-start(), calls=%async_computation.37 | async-start | bytes 5242880 | tf_op jit(solution)/shard_map/reduce_scatter | solution.py:737
  632.1 161.9 %all-gather.12.cloned.1.call-start = ((), (), s32[]{:S(2)}) async-start(), calls=%async_computation.38 | async-start | bytes 5242880 | tf_op jit(solution)/shard_map/all_gather | solution.py:759
  (38 other events, 343.1 us)
Sparse Core Ops, SparseCore 0:
  11.8 29.4 all-gather.7
  43.8 27.8 all-gather.9
  78.4 82.1 all-gather.13
  219.1 28.3 reduce-scatter.8
  251.1 26.1 reduce-scatter.12
  281.3 42.8 reduce-scatter.14
  326.6 43.1 reduce-scatter.16
  372.1 43.1 reduce-scatter.18
  417.7 51.3 reduce-scatter.10
  478.5 34.3 reduce-scatter.20
  514.6 101.9 all-gather.15
  624.5 80.7 reduce-scatter.22
  712.4 81.5 all-gather.11

commit v9 on v8

--- a/solution.py
+++ b/solution.py
@@ -120,7 +120,7 @@
 def middle_pass(full, out_full, tokens, gain, bias):
     cols, rows, width = full.shape
     depth = tokens.shape[1]
-    step = min(256, rows)
+    step = min(512, rows)
     row = pl.BlockSpec((1, depth), lambda i: (0, 0))
     block = pl.BlockSpec((step, depth), lambda i: (i, 0))
     return pl.pallas_call(
@@ -574,7 +574,7 @@
         base = (e * cap + low) * rows_all
         return pack(slots_by_chunk, [routed], base, size * rows_all, 1, waits)[0]
 
-    packed = [pack_chunk(k, []) for k in range(2)]
+    packed = [pack_chunk(k, []) for k in range(min(3, len(chunks)))]
     packed[0], grad_arrived[-1] = tie(packed[0], grad_arrived[-1])
 
     logits = jnp.dot(routed, router_full, preferred_element_type=jnp.float32)
@@ -587,7 +587,10 @@
         moved = swap(packed[k].reshape(rows_all, size, depth), "row")
         arrived.append(moved.reshape(rows_all * size, depth))
         if k < final:
-            packed[k + 1], arrived[k] = tie(packed[k + 1], arrived[k])
+            packed[k + 1], arrived[k], *more = tie(
+                packed[k + 1], arrived[k], *(packed[2:3] if k == 0 else [])
+            )
+            packed[2:3] = more or packed[2:3]
         if k:
             then = packed[k + 1] if k < final else sent[0][0]
             then, summed[k - 1], arrived[k] = tie(then, summed[k - 1], arrived[k])
@@ -598,7 +601,7 @@
                 packed[k + 1] = then
             else:
                 sent[0][0] = then
-        waits = packed[1:2] if k == 0 else summed[:1] if k == final else []
+        waits = summed[:1] if k == final else []
         made, both, pair = expert_pass(
             chunks[k],
             arrived[k],
@@ -614,7 +617,7 @@
         kept.append(both)
         summed.append(made)
         sent.append(pair)
-        if k + 2 <= final:
+        if 1 <= k and k + 2 <= final:
             packed.append(pack_chunk(k + 2, [made]))
     active = [v[0].reshape(block_rows, -1) for v in kept]
     slope = [v[1].reshape(block_rows, -1) for v in kept]
@@ -651,7 +654,8 @@
     waits = slope[-1:]
     last = None
     for f, wide in enumerate(pieces):
-        for e in range(f * local // len(pieces), (f + 1) * local // len(pieces)):
+        early = max(1, local * 3 // 4)
+        for e in range(early) if f == 0 else range(early, local):
             *grad_weights, token = weigh(e, waits)
             waits = [token]
         rows = []
@@ -730,15 +734,12 @@
     plane = swap(plane.astype(jnp.bfloat16).reshape(rows_all, share, -1), "row")
     grad_context = grad_context.reshape(length, width)
     grad_proj = attend_backward(projected, grad_context, context, logsum, block, 0)[0]
-    grad_proj, plane, mixed_full = tie(grad_proj, plane, mixed_full)
-
-    def spread(grads):
-        made = jnp.einsum("tc,dc->td", grads, qkv_full, preferred_element_type=jnp.float32)
-        return lax.psum_scatter(
-            made.astype(jnp.bfloat16), "col", scatter_dimension=0, tiled=True
-        ).astype(jnp.float32)
-
-    grad_normal = spread(grad_proj)
+    grad_proj, plane = tie(grad_proj, plane)
+
+    shares = jnp.einsum("tc,dc->td", grad_proj, qkv_full, preferred_element_type=jnp.float32)
+    shares, mixed_full = tie(shares.astype(jnp.bfloat16), mixed_full)
+    grad_normal = lax.psum_scatter(shares, "col", scatter_dimension=0, tiled=True)
+    grad_normal = grad_normal.astype(jnp.float32)
     mixed_out = mixed_full.transpose(1, 0, 2).reshape(length, depth)
     grad_qkv = jnp.einsum("td,tc->dc", normal_in, grad_proj, preferred_element_type=jnp.float32)
     plane = jnp.sum(plane.astype(jnp.float32), axis=0)

time: 812 us -> 811 us (level)
  transfers between devices with their start and end apart: 31 -> 31, of which waited for: 18 -> 19; matrix products, arithmetic and copies ran while one was open for 11% -> 12% of each run, Pallas kernels for 34% -> 34%
where the time goes in v9:
time: 811 us; the launch traced here: 804 us
  waiting for transfers between devices  298 us (37%)
  Pallas kernels  274 us (34%)
  starting transfers between devices  76.7 us (9%)
  other arithmetic  42.5 us (5%)
  matrix products  40.6 us (5%)
  local copies, waits for them, and re-layouts  38.7 us (5%)
  blocking collectives  18.2 us (2%)
  between operations  14.8 us (2%)
    all_to_all x18, waiting for transfers between devices, swap(): return lax.all_to_all(blocks, axis, split_axis=0, concat_axis=0, tiled=True)  177 us
    all_to_all x18, starting transfers between devices, swap(): return lax.all_to_all(blocks, axis, split_axis=0, concat_axis=0, tiled=True)  76.2 us
    pallas_call x5, Pallas kernels, expert_pass(): pl.pallas_call(functools.partial(expert_body, len(given) + len(waits)), o...  62.2 us
    pallas_call x7, Pallas kernels, pack(): pl.pallas_call(functools.partial(pack_body, base, step, each, len(rows)),...  61.5 us
    reduce_scatter x1, waiting for transfers between devices, per_device(): lax.psum_scatter(shares, 'col', scatter_dimension=0, tiled=True)  51 us
    pallas_call x4, Pallas kernels, weight_pass(): pl.pallas_call(functools.partial(weight_body, len(sent) + len(waits)), ou...  47.3 us
    pallas_call x3, Pallas kernels, unpack(): pl.pallas_call(functools.partial(unpack_body, len(rows)), out_shape=jax.S...  40.9 us
    all_gather x1, waiting for transfers between devices, per_device(): grad_tokens = lax.all_gather(grad_tokens, 'col', axis=0, tiled=True)  37.7 us
  transfers between devices with their start and end apart: 31, of which 19 were waited for; matrix products, arithmetic and copies ran while one was open for 12% of the time, Pallas kernels for 34%

profile of v9, /device:TPU:0, one launch (start us, length us, event | category | flops | bytes accessed | tf_op | source)
XLA Modules:
  0.0 803.7 jit_solution(13628820150987186411)
XLA Ops:
  26.9 13.4 %pack.7 = bf16[2048,1024]{1,0:T(8,128)(2,1)} custom-call(s32[1,2048]{1,0:T(1,128)} %bitcast.158, bf16[2048,1024]{1,0:T(8,128)(2,1)} %rest_0_.3), custom_call_target="tpu_custom_call" | custom-call | flops 1 | bytes 1 | tf_op jit(solution)/shard_map/pack/pallas_call | solution.py:55
  52.1 19.3 %attend_forward.1 = (bf16[2048,256]{1,0:T(8,128)(2,1)}, f32[4,2048]{1,0:T(4,128)}) custom-call(bf16[2048,768]{1,0:T(8,128)(2,1)} %convolution_convert_fusion.1.q_ref.k_ref.v_ref.refs_0_.refs_4_.refs_5_, bf16[2048,768]{1,0:T(8,128)(2,1)} %convolution_convert_fusion.1.q_ref.k_ref.v_ref.refs_0_.refs_4_.refs_5_, ...), custom_call_target="tpu_custom_call" | custom-call | flops 524288 | bytes 524288 | tf_op jit(solution)/shard_map/attend_forward/pallas_call | solution.py:195
  76.7 13.0 %pack.10 = bf16[2048,1024]{1,0:T(8,128)(2,1)} custom-call(s32[1,2048]{1,0:T(1,128)} %bitcast.159, bf16[2048,1024]{1,0:T(8,128)(2,1)} %rest_0_.3, bf16[2048,256]{1,0:T(8,128)(2,1)} %get-tuple-element.120.rest_1_.refs_2_), custom_call_target="tpu_custom_call" | custom-call | flops 1 | bytes 1 | tf_op jit(solution)/shard_map/pack/pallas_call | solution.py:55
  89.7 35.4 %all-to-all-done.1.gy_ref = bf16[8,2,128,1024]{3,2,1,0:T(8,128)(2,1)} async-done(((bf16[8,2,128,1024]{3,2,1,0:T(8,128)(2,1)}), bf16[8,2,128,1024]{3,2,1,0:T(8,128)(2,1)}, u32[]{:S(2)}, u32[]{:S(2)}) %all-to-all-start.1) | async-done | bytes 4194336 | tf_op jit(solution)/shard_map/all_to_all | solution.py:450
  131.5 29.1 %all-gather.14.cloned.1.call-done = bf16[8192,256]{1,0:T(8,128)(2,1)} async-done(((bf16[2048,256]{1,0:T(8,128)(2,1)}), bf16[8192,256]{1,0:T(8,128)(2,1)}) %all-gather.14.cloned.1.call-update) | async-done | bytes 4194320 | tf_op jit(solution)/shard_map/all_gather | solution.py:556
  160.6 11.5 %middle_pass.1 = (f32[2048,1024]{1,0:T(8,128)}, bf16[2048,1024]{1,0:T(8,128)(2,1)}) custom-call(bf16[4,2048,256]{2,1,0:T(8,128)(2,1)} %bitcast.168, bf16[4,1024,256]{2,1,0:T(8,128)(2,1)} %all-gather.10.cloned.1.call-done.out_ref, bf16[2048,1024]{1,0:T(8,128)(2,1)} %tokens_ref.1, f32[1,1024]{1,0:T(1,128)} %copy.127.gain_ref, f32[1,1024]{1,0:T(1,128)} %copy.128.bias_ref), custom_call_target="tpu_custom_call" | custom-call | flops 4294967296 | bytes 20971520 | tf_op jit(solution)/shard_map/middle_pass/pallas_call | solution.py:126
  252.6 14.6 %expert_pass.7 = (bf16[4,1024,256]{2,1,0:T(8,128)(2,1)}, bf16[8,128,1024]{2,1,0:T(8,128)(2,1)}, bf16[8,128,1024]{2,1,0:T(8,128)(2,1)}, bf16[8,2,128,640]{3,2,1,0:T(8,128)(2,1)}, bf16[8,2,128,384]{3,2,1,0:T(8,128)(2,1)}) custom-call(bf16[1024,1024]{1,0:T(8,128)(2,1)} %bitcast.21.x_ref, ...), custom_call_target="tpu_custom_call", output_to_operand_aliasing={{3}: (4, {}), {4}: (5, {})} | custom-call | flops 8589934592 | bytes 16777216 | tf_op jit(solution)/shard_map/expert_pass/pallas_call | solution.py:364
  284.1 14.5 %expert_pass.8 = (bf16[4,1024,256]{2,1,0:T(8,128)(2,1)}, bf16[8,128,1024]{2,1,0:T(8,128)(2,1)}, bf16[8,128,1024]{2,1,0:T(8,128)(2,1)}, bf16[8,2,128,640]{3,2,1,0:T(8,128)(2,1)}, bf16[8,2,128,384]{3,2,1,0:T(8,128)(2,1)}) custom-call(bf16[1024,1024]{1,0:T(8,128)(2,1)} %bitcast.113, bf16[8,2,128,1024]{3,2,1,0:T(8,128)(2,1)} %all-to-all-done.2.gy_ref, ...), custom_call_target="tpu_custom_call" | custom-call | flops 8589934592 | bytes 16777216 | tf_op jit(solution)/shard_map/expert_pass/pallas_call | solution.py:364
  298.6 12.0 %all-to-all-done.7 = bf16[8,128,1024]{2,1,0:T(8,128)(2,1)S(1)} async-done(((bf16[8,128,1024]{2,1,0:T(8,128)(2,1)}), bf16[8,128,1024]{2,1,0:T(8,128)(2,1)S(1)}, u32[]{:S(2)}, u32[]{:S(2)}) %all-to-all-start.7) | async-done | bytes 2097184 | tf_op jit(solution)/shard_map/all_to_all | solution.py:450
  316.5 14.6 %expert_pass.9 = (bf16[4,1024,256]{2,1,0:T(8,128)(2,1)}, bf16[8,128,1024]{2,1,0:T(8,128)(2,1)}, bf16[8,128,1024]{2,1,0:T(8,128)(2,1)}, bf16[8,2,128,640]{3,2,1,0:T(8,128)(2,1)}, bf16[8,2,128,384]{3,2,1,0:T(8,128)(2,1)}) custom-call(bf16[1024,1024]{1,0:T(8,128)(2,1)} %bitcast.111, ...), custom_call_target="tpu_custom_call", output_to_operand_aliasing={{3}: (4, {}), {4}: (5, {})} | custom-call | flops 8589934592 | bytes 16777216 | tf_op jit(solution)/shard_map/expert_pass/pallas_call | solution.py:364
  331.1 17.6 %all-to-all-done.8 = bf16[8,2,128,640]{3,2,1,0:T(8,128)(2,1)} async-done(((bf16[8,2,128,640]{3,2,1,0:T(8,128)(2,1)}), bf16[8,2,128,640]{3,2,1,0:T(8,128)(2,1)}, u32[]{:S(2)}, u32[]{:S(2)}) %all-to-all-start.8) | async-done | bytes 2621472 | tf_op jit(solution)/shard_map/all_to_all | solution.py:450
  358.1 11.7 %weight_pass.4 = (f32[4,1024,1024]{2,1,0:T(8,128)}, f32[4,1024,1024]{2,1,0:T(8,128)}, f32[8,128]{1,0:T(8,128)}) custom-call(bf16[1024,1024]{1,0:T(8,128)(2,1)} %bitcast.131, bf16[8,2,128,1024]{3,2,1,0:T(8,128)(2,1)} %all-to-all-done.1.gy_ref, bf16[1024,32]{1,0:T(8,128)(2,1)} %slice.60.router_ref, f32[1,32]{1,0:T(1,128)} %compare_convert_fusion.1.pick_ref, ...), custom_call_target="tpu_custom_call" | custom-call | flops 4294967296 | bytes 16777216 | tf_op jit(solution)/shard_map/weight_pass/pallas_call | solution.py:416
  369.8 11.7 %weight_pass.5 = (f32[4,1024,1024]{2,1,0:T(8,128)}, f32[4,1024,1024]{2,1,0:T(8,128)}, f32[8,128]{1,0:T(8,128)}) custom-call(bf16[1024,1024]{1,0:T(8,128)(2,1)} %bitcast.21.x_ref, bf16[8,2,128,1024]{3,2,1,0:T(8,128)(2,1)} %all-to-all-done.1.gy_ref, bf16[1024,32]{1,0:T(8,128)(2,1)} %slice.60.router_ref, ...), custom_call_target="tpu_custom_call", output_to_operand_aliasing={{0}: (6, {}), {1}: (7, {})} | custom-call | flops 4294967296 | bytes 16777216 | tf_op jit(solution)/shard_map/weight_pass/pallas_call | solution.py:416
  381.5 11.8 %weight_pass.6 = (f32[4,1024,1024]{2,1,0:T(8,128)}, f32[4,1024,1024]{2,1,0:T(8,128)}, f32[8,128]{1,0:T(8,128)}) custom-call(bf16[1024,1024]{1,0:T(8,128)(2,1)} %bitcast.114, bf16[8,2,128,1024]{3,2,1,0:T(8,128)(2,1)} %all-to-all-done.2.gy_ref, bf16[1024,32]{1,0:T(8,128)(2,1)} %slice.60.router_ref, ...), custom_call_target="tpu_custom_call", output_to_operand_aliasing={{0}: (6, {}), {1}: (7, {})} | custom-call | flops 4294967296 | bytes 16777216 | tf_op jit(solution)/shard_map/weight_pass/pallas_call | solution.py:416
  400.2 18.5 %unpack.3.rest_2_ = bf16[2048,640]{1,0:T(8,128)(2,1)} custom-call(s32[2048,1]{1,0:T(8,128)} %copy.129.refs_0_, s32[2048,1]{1,0:T(8,128)} %copy.130.refs_1_, bf16[2048,640]{1,0:T(8,128)(2,1)} %bitcast.38.refs_2_, bf16[2048,640]{1,0:T(8,128)(2,1)} %bitcast.39.refs_3_, f32[8,128]{1,0:T(8,128)} %get-tuple-element.187.refs_4_), custom_call_target="tpu_custom_call" | custom-call | flops 10737418240 | bytes 7864320 | tf_op jit(solution)/shard_map/unpack/pallas_call | solution.py:89
  425.5 12.1 %weight_pass.7 = (f32[4,1024,1024]{2,1,0:T(8,128)}, f32[4,1024,1024]{2,1,0:T(8,128)}, f32[8,128]{1,0:T(8,128)}) custom-call(bf16[1024,1024]{1,0:T(8,128)(2,1)} %bitcast.112, bf16[8,2,128,1024]{3,2,1,0:T(8,128)(2,1)} %all-to-all-done.2.gy_ref, bf16[1024,32]{1,0:T(8,128)(2,1)} %slice.60.router_ref, ...), custom_call_target="tpu_custom_call", output_to_operand_aliasing={{0}: (6, {}), {1}: (7, {})} | custom-call | flops 4294967296 | bytes 16777216 | tf_op jit(solution)/shard_map/weight_pass/pallas_call | solution.py:416
  449.9 13.3 %unpack.4 = bf16[2048,384]{1,0:T(8,128)(2,1)} custom-call(s32[2048,1]{1,0:T(8,128)} %copy.129.refs_0_, s32[2048,1]{1,0:T(8,128)} %copy.130.refs_1_, bf16[2048,384]{1,0:T(8,128)(2,1)} %bitcast.134, bf16[2048,384]{1,0:T(8,128)(2,1)} %bitcast.135, f32[8,128]{1,0:T(8,128)} %get-tuple-element.200.refs_4_), custom_call_target="tpu_custom_call" | custom-call | flops 6442450944 | bytes 4718592 | tf_op jit(solution)/shard_map/unpack/pallas_call | solution.py:89
  463.2 13.2 %all-to-all-done.12 = bf16[8,4,128,256]{3,2,1,0:T(8,128)(2,1)S(1)} async-done(((bf16[8,4,128,256]{3,2,1,0:T(8,128)(2,1)}), bf16[8,4,128,256]{3,2,1,0:T(8,128)(2,1)S(1)}, u32[]{:S(2)}, u32[]{:S(2)}) %all-to-all-start.12) | async-done | bytes 2097184 | tf_op jit(solution)/shard_map/all_to_all | solution.py:450
  537.6 37.7 %all-to-all-done.14 = bf16[4,512,256]{1,2,0:T(8,128)(2,1)S(1)} async-done(((bf16[4,512,256]{1,2,0:T(8,128)(2,1)}), bf16[4,512,256]{1,2,0:T(8,128)(2,1)S(1)}, u32[]{:S(2)}, u32[]{:S(2)}) %all-to-all-start.14) | async-done | bytes 1048608 | tf_op jit(solution)/shard_map/all_to_all | solution.py:450
  580.5 31.6 %attend_backward.1 = bf16[2048,768]{1,0:T(8,128)(2,1)} custom-call(bf16[2048,768]{1,0:T(8,128)(2,1)} %convolution_convert_fusion.1.q_ref.k_ref.v_ref.refs_0_.refs_4_.refs_5_, bf16[2048,256]{1,0:T(8,128)(2,1)} %bitcast.137, bf16[2048,256]{1,0:T(8,128)(2,1)} %get-tuple-element.120.rest_1_.refs_2_, f32[4,2048]{1,0:T(4,128)} %get-tuple-element.205.refs_3_, ...), custom_call_target="tpu_custom_call" | custom-call | flops 21474836480 | bytes 8388608 | tf_op jit(solution)/shard_map/attend_backward/pallas_call | solution.py:287
  652.6 51.0 %reduce-scatter.23.cloned.1.call-done = bf16[512,1024]{1,0:T(8,128)(2,1)} async-done(((bf16[2048,1024]{1,0:T(8,128)(2,1)}), bf16[512,1024]{1,0:T(8,128)(2,1)}) %reduce-scatter.23.cloned.1.call-update) | async-done | bytes 1048592 | tf_op jit(solution)/shard_map/reduce_scatter | solution.py:741
  718.8 9.9 %all_to_all.105 = f32[4,4,128]{2,1,0:T(4,128)S(1)} all-to-all(f32[4,4,128]{2,1,0:T(4,128)S(1)} %broadcast_in_dim.16), channel_id=1, replica_groups=mesh['row'=8,'col'=4] {'col'}, dimensions={0} | all-to-all | bytes 16384 | tf_op jit(solution)/shard_map/all_to_all | solution.py:450
  734.1 19.2 %all-to-all-done.17 = bf16[8,128,768]{2,1,0:T(8,128)(2,1)S(1)} async-done(((bf16[8,128,768]{2,1,0:T(8,128)(2,1)}), bf16[8,128,768]{2,1,0:T(8,128)(2,1)S(1)}, u32[]{:S(2)}, u32[]{:S(2)}) %all-to-all-start.17) | async-done | bytes 1572896 | tf_op jit(solution)/shard_map/all_to_all | solution.py:450
  754.6 37.7 %all-gather.12.cloned.1.call-done = bf16[2048,1024]{1,0:T(8,128)(2,1)} async-done(((bf16[512,1024]{1,0:T(8,128)(2,1)}), bf16[2048,1024]{1,0:T(8,128)(2,1)}) %all-gather.12.cloned.1.call-update) | async-done | bytes 4194320 | tf_op jit(solution)/shard_map/all_gather | solution.py:760
  (220 shorter events, 314.3 us)
Async XLA Ops:
  7.2 34.1 %all-gather.8.cloned.1.call-start = ((), (), s32[]{:S(2)}) async-start(), calls=%async_computation.28 | async-start | bytes 2064384 | tf_op jit(solution)/shard_map/all_gather | solution.py:514
  14.8 25.5 %all-to-all-start = ((bf16[4,128,256]{2,1,0:T(8,128)(2,1)}), bf16[4,128,256]{2,1,0:T(8,128)(2,1)S(1)}, u32[]{:S(2)}, u32[]{:S(2)}) async-start(bf16[4,128,256]{2,1,0:T(8,128)(2,1)} %broadcast_in_dim.14), calls=%async_computation | async-start | bytes 524288 | tf_op jit(solution)/shard_map/all_to_all | solution.py:450
  21.1 110.3 %all-gather.10.cloned.1.call-start = ((), (), s32[]{:S(2)}) async-start(), calls=%async_computation.29 | async-start | bytes 2359296 | tf_op jit(solution)/shard_map/all_gather | solution.py:558
  71.4 53.7 %all-to-all-start.1 = ((bf16[8,2,128,1024]{3,2,1,0:T(8,128)(2,1)}), bf16[8,2,128,1024]{3,2,1,0:T(8,128)(2,1)}, u32[]{:S(2)}, u32[]{:S(2)}) async-start(bf16[8,2,128,1024]{3,2,1,0:T(8,128)(2,1)} %bitcast.107), calls=%async_computation.1 | async-start | bytes 8388608 | tf_op jit(solution)/shard_map/all_to_all | solution.py:450
  76.0 84.6 %all-gather.14.cloned.1.call-start = ((), (), s32[]{:S(2)}) async-start(), calls=%async_computation.39 | async-start | bytes 5242880 | tf_op jit(solution)/shard_map/all_gather | solution.py:556
  125.1 53.9 %all-to-all-start.2 = ((bf16[8,2,128,1024]{3,2,1,0:T(8,128)(2,1)}), bf16[8,2,128,1024]{3,2,1,0:T(8,128)(2,1)}, u32[]{:S(2)}, u32[]{:S(2)}) async-start(bf16[8,2,128,1024]{3,2,1,0:T(8,128)(2,1)} %bitcast.108), calls=%async_computation.2 | async-start | bytes 8388608 | tf_op jit(solution)/shard_map/all_to_all | solution.py:450
  201.5 115.0 %reduce-scatter.9.cloned.1.call-start = ((), (), s32[]{:S(2)}) async-start(), calls=%async_computation.30 | async-start | bytes 1310720 | tf_op jit(solution)/shard_map/reduce_scatter | solution.py:597
  217.8 31.0 %all-to-all-start.5 = ((bf16[8,128,1024]{2,1,0:T(8,128)(2,1)}), bf16[8,128,1024]{2,1,0:T(8,128)(2,1)}, u32[]{:S(2)}, u32[]{:S(2)}) async-start(bf16[8,128,1024]{2,1,0:T(8,128)(2,1)} %bitcast.116), calls=%async_computation.5 | async-start | bytes 4194304 | tf_op jit(solution)/shard_map/all_to_all | solution.py:450
  222.2 202.3 %reduce-scatter.13.cloned.1.call-start = ((), (), s32[]{:S(2)}) async-start(), calls=%async_computation.32 | async-start | bytes 1310720 | tf_op jit(solution)/shard_map/reduce_scatter | solution.py:597
  248.9 30.2 %all-to-all-start.6 = ((bf16[8,128,1024]{2,1,0:T(8,128)(2,1)}), bf16[8,128,1024]{2,1,0:T(8,128)(2,1)S(1)}, u32[]{:S(2)}, u32[]{:S(2)}) async-start(bf16[8,128,1024]{2,1,0:T(8,128)(2,1)} %bitcast.119), calls=%async_computation.6 | async-start | bytes 4194304 | tf_op jit(solution)/shard_map/all_to_all | solution.py:450
  252.5 185.1 %reduce-scatter.15.cloned.1.call-start = ((), (), s32[]{:S(2)}) async-start(), calls=%async_computation.33 | async-start | bytes 2621440 | tf_op jit(solution)/shard_map/reduce_scatter | solution.py:597
  280.5 30.2 %all-to-all-start.7 = ((bf16[8,128,1024]{2,1,0:T(8,128)(2,1)}), bf16[8,128,1024]{2,1,0:T(8,128)(2,1)S(1)}, u32[]{:S(2)}, u32[]{:S(2)}) async-start(bf16[8,128,1024]{2,1,0:T(8,128)(2,1)} %bitcast.115), calls=%async_computation.7 | async-start | bytes 4194304 | tf_op jit(solution)/shard_map/all_to_all | solution.py:450
  284.1 153.6 %reduce-scatter.17.cloned.1.call-start = ((), (), s32[]{:S(2)}) async-start(), calls=%async_computation.34 | async-start | bytes 2621440 | tf_op jit(solution)/shard_map/reduce_scatter | solution.py:597
  312.0 36.7 %all-to-all-start.8 = ((bf16[8,2,128,640]{3,2,1,0:T(8,128)(2,1)}), bf16[8,2,128,640]{3,2,1,0:T(8,128)(2,1)}, u32[]{:S(2)}, u32[]{:S(2)}) async-start(bf16[8,2,128,640]{3,2,1,0:T(8,128)(2,1)} %get-tuple-element.179), calls=%async_computation.9 | async-start | bytes 5242880 | tf_op jit(solution)/shard_map/all_to_all | solution.py:450
  316.4 121.3 %reduce-scatter.19.cloned.1.call-start = ((), (), s32[]{:S(2)}) async-start(), calls=%async_computation.35 | async-start | bytes 2621440 | tf_op jit(solution)/shard_map/reduce_scatter | solution.py:677
  348.7 44.6 %all-to-all-start.9 = ((bf16[8,2,128,640]{3,2,1,0:T(8,128)(2,1)}), bf16[8,2,128,640]{3,2,1,0:T(8,128)(2,1)}, u32[]{:S(2)}, u32[]{:S(2)}) async-start(bf16[8,2,128,640]{3,2,1,0:T(8,128)(2,1)} %get-tuple-element.183), calls=%async_computation.10 | async-start | bytes 5242880 | tf_op jit(solution)/shard_map/all_to_all | solution.py:450
  397.4 84.5 %reduce-scatter.11.cloned.1.call-start = ((), (), s32[]{:S(2)}) async-start(), calls=%async_computation.31 | async-start | bytes 3276800 | tf_op jit(solution)/shard_map/reduce_scatter | solution.py:687
  446.2 30.2 %all-to-all-start.12 = ((bf16[8,4,128,256]{3,2,1,0:T(8,128)(2,1)}), bf16[8,4,128,256]{3,2,1,0:T(8,128)(2,1)S(1)}, u32[]{:S(2)}, u32[]{:S(2)}) async-start(bf16[8,4,128,256]{3,2,1,0:T(8,128)(2,1)} %pad_maximum_fusion.2), calls=%async_computation.18 | async-start | bytes 4194304 | tf_op jit(solution)/shard_map/all_to_all | solution.py:450
  449.8 61.4 %reduce-scatter.21.cloned.1.call-start = ((), (), s32[]{:S(2)}) async-start(), calls=%async_computation.36 | async-start | bytes 1966080 | tf_op jit(solution)/shard_map/reduce_scatter | solution.py:694
  476.4 143.5 %all-gather.16.cloned.1.call-start = ((), (), s32[]{:S(2)}) async-start(), calls=%async_computation.40 | async-start | bytes 5242880 | tf_op jit(solution)/shard_map/all_gather | solution.py:709
  519.2 56.1 %all-to-all-start.14 = ((bf16[4,512,256]{1,2,0:T(8,128)(2,1)}), bf16[4,512,256]{1,2,0:T(8,128)(2,1)S(1)}, u32[]{:S(2)}, u32[]{:S(2)}) async-start(bf16[4,512,256]{1,2,0:T(8,128)(2,1)} %fusion.25), calls=%async_computation.21 | async-start | bytes 2097152 | tf_op jit(solution)/shard_map/all_to_all | solution.py:450
  575.4 36.7 %all-to-all-start.15 = ((bf16[8,128,1056]{1,2,0:T(8,128)(2,1)}), bf16[8,128,1056]{1,2,0:T(8,128)(2,1)S(1)}, u32[]{:S(2)}, u32[]{:S(2)}) async-start(bf16[8,128,1056]{1,2,0:T(8,128)(2,1)} %copy.142), calls=%async_computation.22 | async-start | bytes 4325376 | tf_op jit(solution)/shard_map/all_to_all | solution.py:450
  579.0 124.6 %reduce-scatter.23.cloned.1.call-start = ((), (), s32[]{:S(2)}) async-start(), calls=%async_computation.37 | async-start | bytes 5242880 | tf_op jit(solution)/shard_map/reduce_scatter | solution.py:741
  629.4 162.9 %all-gather.12.cloned.1.call-start = ((), (), s32[]{:S(2)}) async-start(), calls=%async_computation.38 | async-start | bytes 5242880 | tf_op jit(solution)/shard_map/all_gather | solution.py:760
  (37 other events, 343.6 us)
Sparse Core Ops, SparseCore 0:
  11.8 29.4 all-gather.7
  43.8 27.8 all-gather.9
  78.4 82.1 all-gather.13
  217.0 26.3 reduce-scatter.8
  249.0 26.3 reduce-scatter.12
  279.2 43.0 reduce-scatter.14
  324.8 43.1 reduce-scatter.16
  370.3 43.1 reduce-scatter.18
  418.9 53.5 reduce-scatter.10
  476.5 34.6 reduce-scatter.20
  512.8 101.9 all-gather.15
  620.1 83.5 reduce-scatter.22
  710.7 81.5 all-gather.11

commit v10 on v9

--- a/solution.py
+++ b/solution.py
@@ -261,9 +261,8 @@
         new_v = dot(p_ref[pl.ds(0, span), :], dom_ref[...], NN)
         new_k = dot(ds_ref[pl.ds(0, span), :], qm_ref[...], NN)
         if at == count - 1:
-            old_k, old_v = (refs[6][...], refs[7][...]) if given > 1 else (0.0, 0.0)
-            dv_ref[...] = old_v + new_v
-            dk_ref[...] = old_k + new_k
+            dv_ref[...] = new_v
+            dk_ref[...] = new_k
         else:
             dv_ref[pl.ds(0, span), :] += new_v
             dk_ref[pl.ds(0, span), :] += new_k
@@ -275,7 +274,7 @@
         outs[2][...] = dv_ref[pl.ds(0, first * block), :]
 
 
-def attend_backward(projected, grad_context, context, logsum, block, first, carried=()):
+def attend_backward(projected, grad_context, context, logsum, block, first, waits=()):
     rows, width = context.shape
     heads = width // HEAD_DIM
     length = first * block + rows
@@ -285,7 +284,7 @@
     rest = jax.ShapeDtypeStruct((first * block, width), jnp.float32)
     more = bool(first)
     return pl.pallas_call(
-        functools.partial(backward_body, block, first, len(carried)),
+        functools.partial(backward_body, block, first, len(waits)),
         out_shape=(jax.ShapeDtypeStruct((rows, 3 * width), jnp.bfloat16),) + (rest,) * (2 * more),
         grid=(1,),
         in_specs=[
@@ -296,7 +295,7 @@
             pl.BlockSpec((length, width), lambda i: (0, 1)),
             pl.BlockSpec((length, width), lambda i: (0, 2)),
         ]
-        + [own] * len(carried),
+        + [pl.BlockSpec(memory_space=pl.ANY)] * len(waits),
         out_specs=(pl.BlockSpec((rows, 3 * width), lambda i: (0, 0)),) + (low,) * (2 * more),
         scratch_shapes=[
             pltpu.VMEM((length, heads * block), jnp.bfloat16),
@@ -311,7 +310,119 @@
         cost_estimate=cost(
             20 * rows * length * width, 16 * length * width, rows * length * heads
         ),
-    )(projected, grad_context, context, logsum, projected, projected, *carried)
+    )(projected, grad_context, context, logsum, projected, projected, *waits)
+
+
+def normed_rows(values):
+    mean = jnp.mean(values, axis=1, keepdims=True)
+    centered = values - mean
+    inverse = lax.rsqrt(jnp.mean(centered * centered, axis=1, keepdims=True) + EPSILON)
+    return centered * inverse, inverse
+
+
+def norm_back_rows(grads, normed, inverse, gain):
+    hat = grads * gain
+    inner = jnp.mean(hat * normed, axis=1, keepdims=True)
+    return inverse * (hat - jnp.mean(hat, axis=1, keepdims=True) - normed * inner)
+
+
+def add_sums(sums_ref, grads, normed):
+    @pl.when(pl.program_id(0) == 0)
+    def _():
+        sums_ref[...] = jnp.zeros_like(sums_ref)
+
+    sums_ref[0:1, :] += jnp.sum(grads * normed, axis=0, keepdims=True)
+    sums_ref[1:2, :] += jnp.sum(grads, axis=0, keepdims=True)
+
+
+def settle_body(
+    col_ref, low_ref, high_ref, gate_ref, logit_ref, router_ref, cot_ref, middle_ref, gain_ref,
+    weight_ref, grad_ref, low_grad_ref, context_ref, sums_ref
+):
+    sent = jnp.concatenate([low_ref[...], high_ref[...]], axis=1).astype(jnp.float32)
+    grads = sent * gate_ref[...] + dot(logit_ref[...], router_ref[...], NT)
+    normed, inverse = normed_rows(middle_ref[...])
+    add_sums(sums_ref, grads, normed)
+    made = cot_ref[...].astype(jnp.float32) + norm_back_rows(
+        grads, normed, inverse, gain_ref[...]
+    )
+    grad_ref[...] = made
+    low = made.astype(jnp.bfloat16)
+    low_grad_ref[...] = low
+    for z in range(weight_ref.shape[0]):
+        context_ref[z] = dot(low, weight_ref[z], NN).astype(jnp.bfloat16)
+
+
+def settle_pass(col, low, high, gate, logits, router, cotangent, middle, gain, weights):
+    part, experts = logits.shape
+    cols, depth, width = weights.shape
+    step = min(256, part)
+    block = pl.BlockSpec((step, depth), lambda i, c: (i, 0))
+    mine = pl.BlockSpec((step, depth), lambda i, c: (c[0] * (part // step) + i, 0))
+    return pl.pallas_call(
+        settle_body,
+        out_shape=(
+            jax.ShapeDtypeStruct((part, depth), jnp.float32),
+            jax.ShapeDtypeStruct((part, depth), jnp.bfloat16),
+            jax.ShapeDtypeStruct((cols, part, width), jnp.bfloat16),
+            jax.ShapeDtypeStruct((8, depth), jnp.float32),
+        ),
+        grid_spec=pltpu.PrefetchScalarGridSpec(
+            num_scalar_prefetch=1,
+            grid=(part // step,),
+            in_specs=[
+                pl.BlockSpec((step, low.shape[1]), lambda i, c: (i, 0)),
+                pl.BlockSpec((step, high.shape[1]), lambda i, c: (i, 0)),
+                pl.BlockSpec((step, 1), lambda i, c: (i, 0)),
+                pl.BlockSpec((step, experts), lambda i, c: (i, 0)),
+                pl.BlockSpec((depth, experts), lambda i, c: (0, 0)),
+                mine,
+                mine,
+                pl.BlockSpec((1, depth), lambda i, c: (0, 0)),
+                pl.BlockSpec((cols, depth, width), lambda i, c: (0, 0, 0)),
+            ],
+            out_specs=(
+                block,
+                block,
+                pl.BlockSpec((cols, step, width), lambda i, c: (0, i, 0)),
+                pl.BlockSpec((8, depth), lambda i, c: (0, 0)),
+            ),
+        ),
+        compiler_params=params("arbitrary"),
+        name="settle_pass",
+        cost_estimate=cost(2 * part * depth * width * cols, 20 * part * depth),
+    )(col, low, high, gate, logits, router, cotangent, middle, gain, weights)
+
+
+def close_body(col_ref, share_ref, tokens_ref, grad_ref, gain_ref, out_ref, sums_ref):
+    grads = share_ref[...].astype(jnp.float32)
+    normed, inverse = normed_rows(tokens_ref[...].astype(jnp.float32))
+    made = grad_ref[...] + norm_back_rows(grads, normed, inverse, gain_ref[...])
+    out_ref[...] = made.astype(jnp.bfloat16)
+    add_sums(sums_ref, grads, normed)
+
+
+def close_pass(col, shares, tokens, grads, gain):
+    part, depth = shares.shape
+    step = min(128, part)
+    block = pl.BlockSpec((step, depth), lambda i, c: (i, 0))
+    mine = pl.BlockSpec((step, depth), lambda i, c: (c[0] * (part // step) + i, 0))
+    return pl.pallas_call(
+        close_body,
+        out_shape=(
+            jax.ShapeDtypeStruct((part, depth), jnp.bfloat16),
+            jax.ShapeDtypeStruct((8, depth), jnp.float32),
+        ),
+        grid_spec=pltpu.PrefetchScalarGridSpec(
+            num_scalar_prefetch=1,
+            grid=(part // step,),
+            in_specs=[block, mine, block, pl.BlockSpec((1, depth), lambda i, c: (0, 0))],
+            out_specs=(block, pl.BlockSpec((8, depth), lambda i, c: (0, 0))),
+        ),
+        compiler_params=params("arbitrary"),
+        name="close_pass",
+        cost_estimate=cost(30 * part * depth, 12 * part * depth),
+    )(col, shares, tokens, grads, gain)
 
 
 ROOT = math.sqrt(2.0 / math.pi)
@@ -459,20 +570,6 @@
     centered = values - mean
     variance = jnp.mean(centered * centered, axis=-1, keepdims=True)
     return (mean, lax.rsqrt(variance + EPSILON))
-
-
-def layer_stats(values):
-    mean = jnp.mean(values, axis=-1, keepdims=True)
-    centered = values - mean
-    variance = jnp.mean(centered * centered, axis=-1, keepdims=True)
-    inverse = lax.rsqrt(variance + EPSILON)
-    return (centered * inverse, inverse)
-
-
-def norm_back(grad_normed, normed, inverse, gain):
-    grad_hat = grad_normed * gain
-    centred_grad = grad_hat - jnp.mean(grad_hat, axis=-1, keepdims=True)
-    return inverse * (centred_grad - normed * jnp.mean(grad_hat * normed, axis=-1, keepdims=True))
 
 
 def slot_layout(expert_ids, experts, cap):
@@ -651,11 +748,12 @@
             waits,
         )
 
+    early = max(1, local // 2)
+    late = max(early, local - 1)
     waits = slope[-1:]
     last = None
     for f, wide in enumerate(pieces):
-        early = max(1, local * 3 // 4)
-        for e in range(early) if f == 0 else range(early, local):
+        for e in range(early) if f == 0 else range(early, late):
             *grad_weights, token = weigh(e, waits)
             waits = [token]
         rows = []
@@ -693,7 +791,6 @@
         waits = [whole]
     grad_sent.append(lax.psum_scatter(whole, "col", scatter_dimension=0, tiled=True))
 
-    grad_in, grad_back = grad_weights
     returned = unpack(
         [slots], [homed.reshape(experts * cap, depth // cols_all)], step, grad_sent[:1]
     ).astype(jnp.float32)
@@ -714,32 +811,35 @@
     grad_router = jnp.einsum(
         "td,te->de", own_routed, grad_logits, preferred_element_type=jnp.float32
     )
-    grad_y = own(cotangent).astype(jnp.float32)
-    normed_own, inverse_own = layer_stats(own(middle))
-    grad_sent = jnp.concatenate(grad_sent, axis=1).astype(jnp.float32) * own_gate
-    grad_routed = grad_sent + jnp.einsum(
-        "te,de->td", grad_logits, router_full, preferred_element_type=jnp.float32
-    )
-    gain_two = jnp.sum(grad_routed * normed_own, axis=0)
-    bias_two = jnp.sum(grad_routed, axis=0)
-    grad_middle = grad_y + norm_back(grad_routed, normed_own, inverse_own, gains[1])
-    grad_attn = grad_middle.astype(jnp.bfloat16)
-    grad_context = jnp.einsum(
-        "td,zdc->ztc", grad_attn, out_full, preferred_element_type=jnp.float32
-    ).astype(jnp.bfloat16)
+    place = jnp.reshape(col, (1,)).astype(jnp.int32)
+    grad_middle, grad_attn, grad_context, sums_two = settle_pass(
+        place,
+        *grad_sent,
+        own_gate,
+        grad_logits,
+        router_full,
+        cotangent,
+        middle,
+        gains[1:2],
+        out_full,
+    )
     grad_context = swap(grad_context, "col")
     context_own = own(full, 1)
     grad_out = jnp.einsum("td,ztc->dzc", grad_attn, context_own, preferred_element_type=jnp.float32)
     plane = jnp.concatenate([grad_out.reshape(depth, cols_all * width), grad_router], axis=1)
     plane = swap(plane.astype(jnp.bfloat16).reshape(rows_all, share, -1), "row")
     grad_context = grad_context.reshape(length, width)
-    grad_proj = attend_backward(projected, grad_context, context, logsum, block, 0)[0]
+    waits = [grad_attn]
+    for e in range(late, local):
+        *grad_weights, token = weigh(e, waits)
+        waits = [token]
+    grad_in, grad_back = grad_weights
+    grad_proj = attend_backward(projected, grad_context, context, logsum, block, 0, waits)[0]
     grad_proj, plane = tie(grad_proj, plane)
 
     shares = jnp.einsum("tc,dc->td", grad_proj, qkv_full, preferred_element_type=jnp.float32)
     shares, mixed_full = tie(shares.astype(jnp.bfloat16), mixed_full)
     grad_normal = lax.psum_scatter(shares, "col", scatter_dimension=0, tiled=True)
-    grad_normal = grad_normal.astype(jnp.float32)
     mixed_out = mixed_full.transpose(1, 0, 2).reshape(length, depth)
     grad_qkv = jnp.einsum("td,tc->dc", normal_in, grad_proj, preferred_element_type=jnp.float32)
     plane = jnp.sum(plane.astype(jnp.float32), axis=0)
@@ -753,18 +853,10 @@
         grad_normal, out_share, mixed_out, grad_qkv
     )
 
-    own_normed, own_inverse = layer_stats(own(tokens).astype(jnp.float32))
-    grad_tokens = (
-        grad_middle + norm_back(grad_normal, own_normed, own_inverse, gains[0])
-    ).astype(jnp.bfloat16)
+    grad_tokens, sums_one = close_pass(place, grad_normal, tokens, grad_middle, gains[0:1])
     grad_tokens = lax.all_gather(grad_tokens, "col", axis=0, tiled=True)
-    small = [
-        jnp.sum(grad_normal * own_normed, axis=0),
-        jnp.sum(grad_normal, axis=0),
-        gain_two,
-        bias_two,
-    ]
-    small = swap(jnp.stack(small).reshape(4, rows_all, share).transpose(1, 0, 2), "row")
+    small = jnp.concatenate([sums_one[0:2], sums_two[0:2]], axis=0)
+    small = swap(small.reshape(4, rows_all, share).transpose(1, 0, 2), "row")
     small = jnp.sum(small, axis=0)
     small = jnp.sum(swap(jnp.broadcast_to(small[None], (cols_all, 4, share)), "col"), axis=0)
     qkv_share = swap(grad_qkv.astype(jnp.bfloat16).reshape(rows_all, share, -1), "row")

time: 811 us -> 798 us (0.984)
  other arithmetic: 42.5 us -> 29.1 us
  Pallas kernels: 274 us -> 285 us
    pallas_call x1 -> x3, Pallas kernels: 31.6 us -> 42.8 us  [the longest x1 31.4 us: attend_backward(): pl.pallas_call(functools.partial(backward_body, block, first, len(waits))...]
    reduce_sum x5 -> x0, other arithmetic: 9.32 us -> none  [the longest x2 3.59 us: layer_stats(): variance = jnp.mean(centered * centered, axis=-1, keepdims=True)]
  transfers between devices with their start and end apart: 31 -> 31, of which waited for: 19 -> 20; matrix products, arithmetic and copies ran while one was open for 12% -> 11% of each run, Pallas kernels for 34% -> 35%
where the time goes in v10:
time: 798 us; the launch traced here: 791 us
  waiting for transfers between devices  295 us (37%)
  Pallas kernels  285 us (36%)
  starting transfers between devices  78 us (10%)
  matrix products  37.6 us (5%)
  local copies, waits for them, and re-layouts  32.6 us (4%)
  other arithmetic  29.1 us (4%)
  blocking collectives  18.2 us (2%)
  between operations  14.9 us (2%)
    all_to_all x18, waiting for transfers between devices, swap(): return lax.all_to_all(blocks, axis, split_axis=0, concat_axis=0, tiled=True)  169 us
    all_to_all x18, starting transfers between devices, swap(): return lax.all_to_all(blocks, axis, split_axis=0, concat_axis=0, tiled=True)  77.4 us
    pallas_call x5, Pallas kernels, expert_pass(): pl.pallas_call(functools.partial(expert_body, len(given) + len(waits)), o...  62.5 us
    pallas_call x7, Pallas kernels, pack(): pl.pallas_call(functools.partial(pack_body, base, step, each, len(rows)),...  61.6 us
    reduce_scatter x1, waiting for transfers between devices, per_device(): lax.psum_scatter(shares, 'col', scatter_dimension=0, tiled=True)  52 us
    pallas_call x4, Pallas kernels, weight_pass(): pl.pallas_call(functools.partial(weight_body, len(sent) + len(waits)), ou...  46.8 us
    pallas_call x3, Pallas kernels, unpack(): pl.pallas_call(functools.partial(unpack_body, len(rows)), out_shape=jax.S...  40.7 us
    all_gather x1, waiting for transfers between devices, per_device(): grad_tokens = lax.all_gather(grad_tokens, 'col', axis=0, tiled=True)  36.3 us
  transfers between devices with their start and end apart: 31, of which 20 were waited for; matrix products, arithmetic and copies ran while one was open for 11% of the time, Pallas kernels for 35%

profile of v10, /device:TPU:0, one launch (start us, length us, event | category | flops | bytes accessed | tf_op | source)
XLA Modules:
  0.0 791.0 jit_solution(17009398995333365528)
XLA Ops:
  25.9 13.3 %pack.7 = bf16[2048,1024]{1,0:T(8,128)(2,1)} custom-call(s32[1,2048]{1,0:T(1,128)} %bitcast.152, bf16[2048,1024]{1,0:T(8,128)(2,1)} %cot_ref.1), custom_call_target="tpu_custom_call" | custom-call | flops 1 | bytes 1 | tf_op jit(solution)/shard_map/pack/pallas_call | solution.py:55
  49.9 19.3 %attend_forward.1 = (bf16[2048,256]{1,0:T(8,128)(2,1)}, f32[4,2048]{1,0:T(4,128)}) custom-call(bf16[2048,768]{1,0:T(8,128)(2,1)} %convolution_convert_fusion.1.q_ref.k_ref.v_ref.refs_0_.refs_4_.refs_5_, bf16[2048,768]{1,0:T(8,128)(2,1)} %convolution_convert_fusion.1.q_ref.k_ref.v_ref.refs_0_.refs_4_.refs_5_, ...), custom_call_target="tpu_custom_call" | custom-call | flops 524288 | bytes 524288 | tf_op jit(solution)/shard_map/attend_forward/pallas_call | solution.py:195
  74.5 13.0 %pack.10 = bf16[2048,1024]{1,0:T(8,128)(2,1)} custom-call(s32[1,2048]{1,0:T(1,128)} %bitcast.153, bf16[2048,1024]{1,0:T(8,128)(2,1)} %cot_ref.1, bf16[2048,256]{1,0:T(8,128)(2,1)} %get-tuple-element.126.rest_1_.refs_2_), custom_call_target="tpu_custom_call" | custom-call | flops 1 | bytes 1 | tf_op jit(solution)/shard_map/pack/pallas_call | solution.py:55
  87.5 35.4 %all-to-all-done.1.gy_ref = bf16[8,2,128,1024]{3,2,1,0:T(8,128)(2,1)} async-done(((bf16[8,2,128,1024]{3,2,1,0:T(8,128)(2,1)}), bf16[8,2,128,1024]{3,2,1,0:T(8,128)(2,1)}, u32[]{:S(2)}, u32[]{:S(2)}) %all-to-all-start.1) | async-done | bytes 4194336 | tf_op jit(solution)/shard_map/all_to_all | solution.py:561
  127.7 31.1 %all-gather.14.cloned.1.call-done = bf16[8192,256]{1,0:T(8,128)(2,1)} async-done(((bf16[2048,256]{1,0:T(8,128)(2,1)}), bf16[8192,256]{1,0:T(8,128)(2,1)}) %all-gather.14.cloned.1.call-update) | async-done | bytes 4194320 | tf_op jit(solution)/shard_map/all_gather | solution.py:653
  158.8 11.5 %middle_pass.1 = (f32[2048,1024]{1,0:T(8,128)}, bf16[2048,1024]{1,0:T(8,128)(2,1)}) custom-call(bf16[4,2048,256]{2,1,0:T(8,128)(2,1)} %bitcast.165, bf16[4,1024,256]{2,1,0:T(8,128)(2,1)} %all-gather.10.cloned.1.call-done.out_ref.weight_ref, bf16[2048,1024]{1,0:T(8,128)(2,1)} %tokens_ref.3, f32[1,1024]{1,0:T(1,128)} %get-tuple-element.279.gain_ref, ...), custom_call_target="tpu_custom_call" | custom-call | flops 4294967296 | bytes 20971520 | tf_op jit(solution)/shard_map/middle_pass/pallas_call | solution.py:126
  249.4 14.5 %expert_pass.7 = (bf16[4,1024,256]{2,1,0:T(8,128)(2,1)}, bf16[8,128,1024]{2,1,0:T(8,128)(2,1)}, bf16[8,128,1024]{2,1,0:T(8,128)(2,1)}, bf16[8,2,128,640]{3,2,1,0:T(8,128)(2,1)}, bf16[8,2,128,384]{3,2,1,0:T(8,128)(2,1)}) custom-call(bf16[1024,1024]{1,0:T(8,128)(2,1)} %bitcast.24.x_ref, ...), custom_call_target="tpu_custom_call", output_to_operand_aliasing={{3}: (4, {}), {4}: (5, {})} | custom-call | flops 8589934592 | bytes 16777216 | tf_op jit(solution)/shard_map/expert_pass/pallas_call | solution.py:475
  280.9 14.6 %expert_pass.8 = (bf16[4,1024,256]{2,1,0:T(8,128)(2,1)}, bf16[8,128,1024]{2,1,0:T(8,128)(2,1)}, bf16[8,128,1024]{2,1,0:T(8,128)(2,1)}, bf16[8,2,128,640]{3,2,1,0:T(8,128)(2,1)}, bf16[8,2,128,384]{3,2,1,0:T(8,128)(2,1)}) custom-call(bf16[1024,1024]{1,0:T(8,128)(2,1)} %bitcast.109, bf16[8,2,128,1024]{3,2,1,0:T(8,128)(2,1)} %all-to-all-done.2.gy_ref, ...), custom_call_target="tpu_custom_call" | custom-call | flops 8589934592 | bytes 16777216 | tf_op jit(solution)/shard_map/expert_pass/pallas_call | solution.py:475
  295.6 11.9 %all-to-all-done.7 = bf16[8,128,1024]{2,1,0:T(8,128)(2,1)S(1)} async-done(((bf16[8,128,1024]{2,1,0:T(8,128)(2,1)}), bf16[8,128,1024]{2,1,0:T(8,128)(2,1)S(1)}, u32[]{:S(2)}, u32[]{:S(2)}) %all-to-all-start.7) | async-done | bytes 2097184 | tf_op jit(solution)/shard_map/all_to_all | solution.py:561
  313.3 14.6 %expert_pass.9 = (bf16[4,1024,256]{2,1,0:T(8,128)(2,1)}, bf16[8,128,1024]{2,1,0:T(8,128)(2,1)}, bf16[8,128,1024]{2,1,0:T(8,128)(2,1)}, bf16[8,2,128,640]{3,2,1,0:T(8,128)(2,1)}, bf16[8,2,128,384]{3,2,1,0:T(8,128)(2,1)}) custom-call(bf16[1024,1024]{1,0:T(8,128)(2,1)} %bitcast.107, ...), custom_call_target="tpu_custom_call", output_to_operand_aliasing={{3}: (4, {}), {4}: (5, {})} | custom-call | flops 8589934592 | bytes 16777216 | tf_op jit(solution)/shard_map/expert_pass/pallas_call | solution.py:475
  327.9 17.6 %all-to-all-done.8 = bf16[8,2,128,640]{3,2,1,0:T(8,128)(2,1)} async-done(((bf16[8,2,128,640]{3,2,1,0:T(8,128)(2,1)}), bf16[8,2,128,640]{3,2,1,0:T(8,128)(2,1)}, u32[]{:S(2)}, u32[]{:S(2)}) %all-to-all-start.8) | async-done | bytes 2621472 | tf_op jit(solution)/shard_map/all_to_all | solution.py:561
  353.6 11.7 %weight_pass.4 = (f32[4,1024,1024]{2,1,0:T(8,128)}, f32[4,1024,1024]{2,1,0:T(8,128)}, f32[8,128]{1,0:T(8,128)}) custom-call(bf16[1024,1024]{1,0:T(8,128)(2,1)} %bitcast.127, bf16[8,2,128,1024]{3,2,1,0:T(8,128)(2,1)} %all-to-all-done.1.gy_ref, bf16[1024,32]{1,0:T(8,128)(2,1)} %copy.123.router_ref, f32[1,32]{1,0:T(1,128)} %compare_convert_fusion.2.pick_ref, ...), custom_call_target="tpu_custom_call" | custom-call | flops 4294967296 | bytes 16777216 | tf_op jit(solution)/shard_map/weight_pass/pallas_call | solution.py:527
  365.3 11.7 %weight_pass.5 = (f32[4,1024,1024]{2,1,0:T(8,128)}, f32[4,1024,1024]{2,1,0:T(8,128)}, f32[8,128]{1,0:T(8,128)}) custom-call(bf16[1024,1024]{1,0:T(8,128)(2,1)} %bitcast.24.x_ref, bf16[8,2,128,1024]{3,2,1,0:T(8,128)(2,1)} %all-to-all-done.1.gy_ref, bf16[1024,32]{1,0:T(8,128)(2,1)} %copy.123.router_ref, ...), custom_call_target="tpu_custom_call", output_to_operand_aliasing={{0}: (6, {}), {1}: (7, {})} | custom-call | flops 4294967296 | bytes 16777216 | tf_op jit(solution)/shard_map/weight_pass/pallas_call | solution.py:527
  388.7 18.3 %unpack.3.rest_2_ = bf16[2048,640]{1,0:T(8,128)(2,1)} custom-call(s32[2048,1]{1,0:T(8,128)} %copy.124.refs_0_, s32[2048,1]{1,0:T(8,128)} %copy.125.refs_1_, bf16[2048,640]{1,0:T(8,128)(2,1)} %bitcast.39.refs_2_, bf16[2048,640]{1,0:T(8,128)(2,1)} %bitcast.40.refs_3_, f32[8,128]{1,0:T(8,128)} %get-tuple-element.187.refs_4_), custom_call_target="tpu_custom_call" | custom-call | flops 10737418240 | bytes 7864320 | tf_op jit(solution)/shard_map/unpack/pallas_call | solution.py:89
  413.1 11.7 %weight_pass.6 = (f32[4,1024,1024]{2,1,0:T(8,128)}, f32[4,1024,1024]{2,1,0:T(8,128)}, f32[8,128]{1,0:T(8,128)}) custom-call(bf16[1024,1024]{1,0:T(8,128)(2,1)} %bitcast.110, bf16[8,2,128,1024]{3,2,1,0:T(8,128)(2,1)} %all-to-all-done.2.gy_ref, bf16[1024,32]{1,0:T(8,128)(2,1)} %copy.123.router_ref, ...), custom_call_target="tpu_custom_call", output_to_operand_aliasing={{0}: (6, {}), {1}: (7, {})} | custom-call | flops 4294967296 | bytes 16777216 | tf_op jit(solution)/shard_map/weight_pass/pallas_call | solution.py:527
  437.4 13.3 %unpack.4 = bf16[2048,384]{1,0:T(8,128)(2,1)} custom-call(s32[2048,1]{1,0:T(8,128)} %copy.124.refs_0_, s32[2048,1]{1,0:T(8,128)} %copy.125.refs_1_, bf16[2048,384]{1,0:T(8,128)(2,1)} %bitcast.130, bf16[2048,384]{1,0:T(8,128)(2,1)} %bitcast.131, f32[8,128]{1,0:T(8,128)} %get-tuple-element.200.refs_4_), custom_call_target="tpu_custom_call" | custom-call | flops 6442450944 | bytes 4718592 | tf_op jit(solution)/shard_map/unpack/pallas_call | solution.py:89
  450.7 13.2 %all-to-all-done.12 = bf16[8,4,128,256]{3,2,1,0:T(8,128)(2,1)S(1)} async-done(((bf16[8,4,128,256]{3,2,1,0:T(8,128)(2,1)}), bf16[8,4,128,256]{3,2,1,0:T(8,128)(2,1)S(1)}, u32[]{:S(2)}, u32[]{:S(2)}) %all-to-all-start.12) | async-done | bytes 2097184 | tf_op jit(solution)/shard_map/all_to_all | solution.py:561
  529.5 11.7 %weight_pass.7 = (f32[4,1024,1024]{2,1,0:T(8,128)}, f32[4,1024,1024]{2,1,0:T(8,128)}, f32[8,128]{1,0:T(8,128)}) custom-call(bf16[1024,1024]{1,0:T(8,128)(2,1)} %bitcast.108, bf16[8,2,128,1024]{3,2,1,0:T(8,128)(2,1)} %all-to-all-done.2.gy_ref, bf16[1024,32]{1,0:T(8,128)(2,1)} %copy.123.router_ref, ...), custom_call_target="tpu_custom_call", output_to_operand_aliasing={{0}: (6, {}), {1}: (7, {})} | custom-call | flops 4294967296 | bytes 16777216 | tf_op jit(solution)/shard_map/weight_pass/pallas_call | solution.py:527
  541.2 25.6 %all-to-all-done.14 = bf16[4,512,256]{2,1,0:T(8,128)(2,1)} async-done(((bf16[4,512,256]{2,1,0:T(8,128)(2,1)}), bf16[4,512,256]{2,1,0:T(8,128)(2,1)}, u32[]{:S(2)}, u32[]{:S(2)}) %all-to-all-start.14) | async-done | bytes 1048608 | tf_op jit(solution)/shard_map/all_to_all | solution.py:561
  570.7 31.4 %attend_backward.1 = bf16[2048,768]{1,0:T(8,128)(2,1)} custom-call(bf16[2048,768]{1,0:T(8,128)(2,1)} %convolution_convert_fusion.1.q_ref.k_ref.v_ref.refs_0_.refs_4_.refs_5_, bf16[2048,256]{1,0:T(8,128)(2,1)} %bitcast.58.refs_1_, bf16[2048,256]{1,0:T(8,128)(2,1)} %get-tuple-element.126.rest_1_.refs_2_, f32[4,2048]{1,0:T(4,128)} %get-tuple-element.207.refs_3_, ...), custom_call_target="tpu_custom_call" | custom-call | flops 21474836480 | bytes 8388608 | tf_op jit(solution)/shard_map/attend_backward/pallas_call | solution.py:286
  640.8 52.0 %reduce-scatter.23.cloned.1.call-done.share_ref = bf16[512,1024]{1,0:T(8,128)(2,1)} async-done(((bf16[2048,1024]{1,0:T(8,128)(2,1)}), bf16[512,1024]{1,0:T(8,128)(2,1)}) %reduce-scatter.23.cloned.1.call-update) | async-done | bytes 1048592 | tf_op jit(solution)/shard_map/reduce_scatter | solution.py:842
  707.4 9.9 %all_to_all.105 = f32[4,4,128]{2,1,0:T(4,128)S(1)} all-to-all(f32[4,4,128]{2,1,0:T(4,128)S(1)} %broadcast_in_dim.16), channel_id=1, replica_groups=mesh['row'=8,'col'=4] {'col'}, dimensions={0} | all-to-all | bytes 16384 | tf_op jit(solution)/shard_map/all_to_all | solution.py:561
  722.6 19.2 %all-to-all-done.17 = bf16[8,128,768]{2,1,0:T(8,128)(2,1)S(1)} async-done(((bf16[8,128,768]{2,1,0:T(8,128)(2,1)}), bf16[8,128,768]{2,1,0:T(8,128)(2,1)S(1)}, u32[]{:S(2)}, u32[]{:S(2)}) %all-to-all-start.17) | async-done | bytes 1572896 | tf_op jit(solution)/shard_map/all_to_all | solution.py:561
  743.2 36.3 %all-gather.12.cloned.1.call-done = bf16[2048,1024]{1,0:T(8,128)(2,1)} async-done(((bf16[512,1024]{1,0:T(8,128)(2,1)}), bf16[2048,1024]{1,0:T(8,128)(2,1)}) %all-gather.12.cloned.1.call-update) | async-done | bytes 4194320 | tf_op jit(solution)/shard_map/all_gather | solution.py:857
  (193 shorter events, 313.1 us)
Async XLA Ops:
  7.2 32.3 %all-gather.8.cloned.1.call-start = ((), (), s32[]{:S(2)}) async-start(), calls=%async_computation.28 | async-start | bytes 1861632 | tf_op jit(solution)/shard_map/all_gather | solution.py:611
  20.3 107.4 %all-gather.10.cloned.1.call-start = ((), (), s32[]{:S(2)}) async-start(), calls=%async_computation.29 | async-start | bytes 2359296 | tf_op jit(solution)/shard_map/all_gather | solution.py:655
  69.2 53.7 %all-to-all-start.1 = ((bf16[8,2,128,1024]{3,2,1,0:T(8,128)(2,1)}), bf16[8,2,128,1024]{3,2,1,0:T(8,128)(2,1)}, u32[]{:S(2)}, u32[]{:S(2)}) async-start(bf16[8,2,128,1024]{3,2,1,0:T(8,128)(2,1)} %bitcast.103), calls=%async_computation.1 | async-start | bytes 8388608 | tf_op jit(solution)/shard_map/all_to_all | solution.py:561
  73.8 85.0 %all-gather.14.cloned.1.call-start = ((), (), s32[]{:S(2)}) async-start(), calls=%async_computation.39 | async-start | bytes 5242880 | tf_op jit(solution)/shard_map/all_gather | solution.py:653
  122.9 53.9 %all-to-all-start.2 = ((bf16[8,2,128,1024]{3,2,1,0:T(8,128)(2,1)}), bf16[8,2,128,1024]{3,2,1,0:T(8,128)(2,1)}, u32[]{:S(2)}, u32[]{:S(2)}) async-start(bf16[8,2,128,1024]{3,2,1,0:T(8,128)(2,1)} %bitcast.104), calls=%async_computation.2 | async-start | bytes 8388608 | tf_op jit(solution)/shard_map/all_to_all | solution.py:561
  199.3 114.0 %reduce-scatter.9.cloned.1.call-start = ((), (), s32[]{:S(2)}) async-start(), calls=%async_computation.30 | async-start | bytes 1310720 | tf_op jit(solution)/shard_map/reduce_scatter | solution.py:694
  214.7 31.0 %all-to-all-start.5 = ((bf16[8,128,1024]{2,1,0:T(8,128)(2,1)}), bf16[8,128,1024]{2,1,0:T(8,128)(2,1)}, u32[]{:S(2)}, u32[]{:S(2)}) async-start(bf16[8,128,1024]{2,1,0:T(8,128)(2,1)} %bitcast.112), calls=%async_computation.5 | async-start | bytes 4194304 | tf_op jit(solution)/shard_map/all_to_all | solution.py:561
  219.0 193.1 %reduce-scatter.13.cloned.1.call-start = ((), (), s32[]{:S(2)}) async-start(), calls=%async_computation.32 | async-start | bytes 1310720 | tf_op jit(solution)/shard_map/reduce_scatter | solution.py:694
  245.7 30.2 %all-to-all-start.6 = ((bf16[8,128,1024]{2,1,0:T(8,128)(2,1)}), bf16[8,128,1024]{2,1,0:T(8,128)(2,1)S(1)}, u32[]{:S(2)}, u32[]{:S(2)}) async-start(bf16[8,128,1024]{2,1,0:T(8,128)(2,1)} %bitcast.115), calls=%async_computation.6 | async-start | bytes 4194304 | tf_op jit(solution)/shard_map/all_to_all | solution.py:561
  249.3 175.5 %reduce-scatter.15.cloned.1.call-start = ((), (), s32[]{:S(2)}) async-start(), calls=%async_computation.33 | async-start | bytes 2621440 | tf_op jit(solution)/shard_map/reduce_scatter | solution.py:694
  277.3 30.2 %all-to-all-start.7 = ((bf16[8,128,1024]{2,1,0:T(8,128)(2,1)}), bf16[8,128,1024]{2,1,0:T(8,128)(2,1)S(1)}, u32[]{:S(2)}, u32[]{:S(2)}) async-start(bf16[8,128,1024]{2,1,0:T(8,128)(2,1)} %bitcast.111), calls=%async_computation.7 | async-start | bytes 4194304 | tf_op jit(solution)/shard_map/all_to_all | solution.py:561
  280.9 143.9 %reduce-scatter.17.cloned.1.call-start = ((), (), s32[]{:S(2)}) async-start(), calls=%async_computation.34 | async-start | bytes 2621440 | tf_op jit(solution)/shard_map/reduce_scatter | solution.py:694
  308.8 36.7 %all-to-all-start.8 = ((bf16[8,2,128,640]{3,2,1,0:T(8,128)(2,1)}), bf16[8,2,128,640]{3,2,1,0:T(8,128)(2,1)}, u32[]{:S(2)}, u32[]{:S(2)}) async-start(bf16[8,2,128,640]{3,2,1,0:T(8,128)(2,1)} %get-tuple-element.179), calls=%async_computation.9 | async-start | bytes 5242880 | tf_op jit(solution)/shard_map/all_to_all | solution.py:561
  313.2 111.6 %reduce-scatter.19.cloned.1.call-start = ((), (), s32[]{:S(2)}) async-start(), calls=%async_computation.35 | async-start | bytes 2621440 | tf_op jit(solution)/shard_map/reduce_scatter | solution.py:775
  345.5 36.8 %all-to-all-start.9 = ((bf16[8,2,128,640]{3,2,1,0:T(8,128)(2,1)}), bf16[8,2,128,640]{3,2,1,0:T(8,128)(2,1)}, u32[]{:S(2)}, u32[]{:S(2)}) async-start(bf16[8,2,128,640]{3,2,1,0:T(8,128)(2,1)} %get-tuple-element.183), calls=%async_computation.10 | async-start | bytes 5242880 | tf_op jit(solution)/shard_map/all_to_all | solution.py:561
  385.9 85.5 %reduce-scatter.11.cloned.1.call-start = ((), (), s32[]{:S(2)}) async-start(), calls=%async_computation.31 | async-start | bytes 3276800 | tf_op jit(solution)/shard_map/reduce_scatter | solution.py:785
  407.1 25.5 %all-to-all-start.11 = ((bf16[8,2,128,384]{3,2,1,0:T(8,128)(2,1)}), bf16[8,2,128,384]{3,2,1,0:T(8,128)(2,1)S(1)}, u32[]{:S(2)}, u32[]{:S(2)}) async-start(bf16[8,2,128,384]{3,2,1,0:T(8,128)(2,1)} %get-tuple-element.190), calls=%async_computation.13 | async-start | bytes 3145728 | tf_op jit(solution)/shard_map/all_to_all | solution.py:561
  433.7 30.2 %all-to-all-start.12 = ((bf16[8,4,128,256]{3,2,1,0:T(8,128)(2,1)}), bf16[8,4,128,256]{3,2,1,0:T(8,128)(2,1)S(1)}, u32[]{:S(2)}, u32[]{:S(2)}) async-start(bf16[8,4,128,256]{3,2,1,0:T(8,128)(2,1)} %pad_maximum_fusion.2), calls=%async_computation.18 | async-start | bytes 4194304 | tf_op jit(solution)/shard_map/all_to_all | solution.py:561
  437.3 65.2 %reduce-scatter.21.cloned.1.call-start = ((), (), s32[]{:S(2)}) async-start(), calls=%async_computation.36 | async-start | bytes 1966080 | tf_op jit(solution)/shard_map/reduce_scatter | solution.py:792
  463.9 146.0 %all-gather.16.cloned.1.call-start = ((), (), s32[]{:S(2)}) async-start(), calls=%async_computation.40 | async-start | bytes 5242880 | tf_op jit(solution)/shard_map/all_gather | solution.py:806
  509.3 57.5 %all-to-all-start.14 = ((bf16[4,512,256]{2,1,0:T(8,128)(2,1)}), bf16[4,512,256]{2,1,0:T(8,128)(2,1)}, u32[]{:S(2)}, u32[]{:S(2)}) async-start(bf16[4,512,256]{2,1,0:T(8,128)(2,1)} %get-tuple-element.206), calls=%async_computation.21 | async-start | bytes 2097152 | tf_op jit(solution)/shard_map/all_to_all | solution.py:561
  566.8 35.3 %all-to-all-start.15 = ((bf16[8,128,1056]{1,2,0:T(8,128)(2,1)}), bf16[8,128,1056]{1,2,0:T(8,128)(2,1)S(1)}, u32[]{:S(2)}, u32[]{:S(2)}) async-start(bf16[8,128,1056]{1,2,0:T(8,128)(2,1)} %copy.139), calls=%async_computation.22 | async-start | bytes 4325376 | tf_op jit(solution)/shard_map/all_to_all | solution.py:561
  570.5 122.3 %reduce-scatter.23.cloned.1.call-start = ((), (), s32[]{:S(2)}) async-start(), calls=%async_computation.37 | async-start | bytes 5242880 | tf_op jit(solution)/shard_map/reduce_scatter | solution.py:842
  616.3 163.1 %all-gather.12.cloned.1.call-start = ((), (), s32[]{:S(2)}) async-start(), calls=%async_computation.38 | async-start | bytes 5242880 | tf_op jit(solution)/shard_map/all_gather | solution.py:857
  (32 other events, 301.3 us)
Sparse Core Ops, SparseCore 0:
  10.5 28.9 all-gather.7
  41.9 27.8 all-gather.9
  76.2 82.5 all-gather.13
  214.8 26.7 reduce-scatter.8
  245.8 26.7 reduce-scatter.12
  276.1 43.4 reduce-scatter.14
  322.0 43.1 reduce-scatter.16
  367.5 43.1 reduce-scatter.18
  413.7 51.3 reduce-scatter.10
  467.4 35.1 reduce-scatter.20
  504.2 101.9 all-gather.15
  610.1 82.6 reduce-scatter.22
  697.6 81.7 all-gather.11

commit v11 on v10

--- a/solution.py
+++ b/solution.py
@@ -210,10 +210,9 @@
     )(projected, projected, projected, *waits)
 
 
-def backward_body(block, first, given, *refs):
-    q_ref, do_ref, o_ref, lse_ref, k_ref, v_ref = refs[:6]
-    outs = refs[6 + given :]
-    out_ref, p_ref, ds_ref, qm_ref, dom_ref, dk_ref, dv_ref = outs[:1] + outs[-6:]
+def backward_body(block, given, *refs):
+    q_ref, do_ref, o_ref, lse_ref, k_ref, v_ref, weight_ref = refs[:7]
+    out_ref, share_ref, p_ref, ds_ref, qm_ref, dom_ref, dk_ref, dv_ref = refs[7 + given :]
     width = q_ref.shape[1]
     heads = width // HEAD_DIM
     count = q_ref.shape[0] // block
@@ -221,10 +220,9 @@
     hidden = lax.broadcasted_iota(jnp.int32, (block, block), 0) > lax.broadcasted_iota(
         jnp.int32, (block, block), 1
     )
-    for at in reversed(range(count)):
-        i = first + at
+    for i in reversed(range(count)):
         span = (i + 1) * block
-        here = pl.ds(at * block, block)
+        here = pl.ds(i * block, block)
 
         def one_head(h, carry, here=here, span=span, i=i):
             mine = (lane >= h * HEAD_DIM) & (lane < (h + 1) * HEAD_DIM)
@@ -260,7 +258,7 @@
         lax.fori_loop(0, heads, one_head, 0, unroll=heads)
         new_v = dot(p_ref[pl.ds(0, span), :], dom_ref[...], NN)
         new_k = dot(ds_ref[pl.ds(0, span), :], qm_ref[...], NN)
-        if at == count - 1:
+        if i == count - 1:
             dv_ref[...] = new_v
             dk_ref[...] = new_k
         else:
@@ -269,34 +267,36 @@
         low = pl.ds(i * block, block)
         out_ref[here, pl.ds(width, width)] = dk_ref[low, :].astype(out_ref.dtype)
         out_ref[here, pl.ds(2 * width, width)] = dv_ref[low, :].astype(out_ref.dtype)
-    if first:
-        outs[1][...] = dk_ref[pl.ds(0, first * block), :]
-        outs[2][...] = dv_ref[pl.ds(0, first * block), :]
-
-
-def attend_backward(projected, grad_context, context, logsum, block, first, waits=()):
-    rows, width = context.shape
+        share_ref[here, :] = dot(out_ref[here, :], weight_ref[...], NT).astype(share_ref.dtype)
+
+
+def attend_backward(projected, grad_context, context, logsum, weights, block, waits=()):
+    length, width = context.shape
     heads = width // HEAD_DIM
-    length = first * block + rows
-    half = lambda j: pl.BlockSpec((rows, width), lambda i: (first * block // rows, j))
-    own = pl.BlockSpec((rows, width), lambda i: (0, 0))
-    low = pl.BlockSpec((first * block, width), lambda i: (0, 0))
-    rest = jax.ShapeDtypeStruct((first * block, width), jnp.float32)
-    more = bool(first)
+    depth = weights.shape[0]
+    third = [pl.BlockSpec((length, width), lambda i, j=j: (0, j)) for j in range(3)]
+    whole = third[0]
     return pl.pallas_call(
-        functools.partial(backward_body, block, first, len(waits)),
-        out_shape=(jax.ShapeDtypeStruct((rows, 3 * width), jnp.bfloat16),) + (rest,) * (2 * more),
+        functools.partial(backward_body, block, len(waits)),
+        out_shape=(
+            jax.ShapeDtypeStruct((length, 3 * width), jnp.bfloat16),
+            jax.ShapeDtypeStruct((length, depth), jnp.bfloat16),
+        ),
         grid=(1,),
         in_specs=[
-            half(0),
-            own,
-            own,
-            pl.BlockSpec((heads, rows), lambda i: (0, 0)),
-            pl.BlockSpec((length, width), lambda i: (0, 1)),
-            pl.BlockSpec((length, width), lambda i: (0, 2)),
+            third[0],
+            whole,
+            whole,
+            pl.BlockSpec((heads, length), lambda i: (0, 0)),
+            third[1],
+            third[2],
+            pl.BlockSpec((depth, 3 * width), lambda i: (0, 0)),
         ]
         + [pl.BlockSpec(memory_space=pl.ANY)] * len(waits),
-        out_specs=(pl.BlockSpec((rows, 3 * width), lambda i: (0, 0)),) + (low,) * (2 * more),
+        out_specs=(
+            pl.BlockSpec((length, 3 * width), lambda i: (0, 0)),
+            pl.BlockSpec((length, depth), lambda i: (0, 0)),
+        ),
         scratch_shapes=[
             pltpu.VMEM((length, heads * block), jnp.bfloat16),
             pltpu.VMEM((length, heads * block), jnp.bfloat16),
@@ -308,9 +308,9 @@
         compiler_params=params("arbitrary"),
         name="attend_backward",
         cost_estimate=cost(
-            20 * rows * length * width, 16 * length * width, rows * length * heads
-        ),
-    )(projected, grad_context, context, logsum, projected, projected, *waits)
+            20 * length * length * width, 16 * length * width, length * length * heads
+        ),
+    )(projected, grad_context, context, logsum, projected, projected, weights, *waits)
 
 
 def normed_rows(values):
@@ -404,7 +404,7 @@
 
 def close_pass(col, shares, tokens, grads, gain):
     part, depth = shares.shape
-    step = min(128, part)
+    step = min(256, part)
     block = pl.BlockSpec((step, depth), lambda i, c: (i, 0))
     mine = pl.BlockSpec((step, depth), lambda i, c: (c[0] * (part // step) + i, 0))
     return pl.pallas_call(
@@ -834,11 +834,12 @@
         *grad_weights, token = weigh(e, waits)
         waits = [token]
     grad_in, grad_back = grad_weights
-    grad_proj = attend_backward(projected, grad_context, context, logsum, block, 0, waits)[0]
-    grad_proj, plane = tie(grad_proj, plane)
-
-    shares = jnp.einsum("tc,dc->td", grad_proj, qkv_full, preferred_element_type=jnp.float32)
-    shares, mixed_full = tie(shares.astype(jnp.bfloat16), mixed_full)
+    grad_proj, shares = attend_backward(
+        projected, grad_context, context, logsum, qkv_full, block, waits
+    )
+    shares, plane = tie(shares, plane)
+
+    shares, mixed_full = tie(shares, mixed_full)
     grad_normal = lax.psum_scatter(shares, "col", scatter_dimension=0, tiled=True)
     mixed_out = mixed_full.transpose(1, 0, 2).reshape(length, depth)
     grad_qkv = jnp.einsum("td,tc->dc", normal_in, grad_proj, preferred_element_type=jnp.float32)

time: 798 us -> 796 us (level)
  transfers between devices with their start and end apart: 31 -> 31, of which waited for: 20 -> 20; matrix products, arithmetic and copies ran while one was open for 11% -> 10% of each run, Pallas kernels for 35% -> 36%
where the time goes in v11:
time: 796 us; the launch traced here: 789 us
  waiting for transfers between devices  294 us (37%)
  Pallas kernels  291 us (37%)
  starting transfers between devices  78 us (10%)
  local copies, waits for them, and re-layouts  34.3 us (4%)
  matrix products  29.8 us (4%)
  other arithmetic  29.1 us (4%)
  blocking collectives  18.2 us (2%)
  between operations  14.7 us (2%)
    all_to_all x18, waiting for transfers between devices, swap(): return lax.all_to_all(blocks, axis, split_axis=0, concat_axis=0, tiled=True)  168 us
    all_to_all x18, starting transfers between devices, swap(): return lax.all_to_all(blocks, axis, split_axis=0, concat_axis=0, tiled=True)  77.3 us
    pallas_call x5, Pallas kernels, expert_pass(): pl.pallas_call(functools.partial(expert_body, len(given) + len(waits)), o...  62.5 us
    pallas_call x7, Pallas kernels, pack(): pl.pallas_call(functools.partial(pack_body, base, step, each, len(rows)),...  61.5 us
    reduce_scatter x1, waiting for transfers between devices, per_device(): lax.psum_scatter(shares, 'col', scatter_dimension=0, tiled=True)  52 us
    pallas_call x4, Pallas kernels, weight_pass(): pl.pallas_call(functools.partial(weight_body, len(sent) + len(waits)), ou...  46.8 us
    pallas_call x3, Pallas kernels, unpack(): pl.pallas_call(functools.partial(unpack_body, len(rows)), out_shape=jax.S...  40.7 us
    pallas_call x1, Pallas kernels, attend_backward(): pl.pallas_call(functools.partial(backward_body, block, len(waits)), out_s...  37.9 us
  transfers between devices with their start and end apart: 31, of which 20 were waited for; matrix products, arithmetic and copies ran while one was open for 10% of the time, Pallas kernels for 36%

profile of v11, /device:TPU:0, one launch (start us, length us, event | category | flops | bytes accessed | tf_op | source)
XLA Modules:
  0.0 788.9 jit_solution(8743934469014744130)
XLA Ops:
  25.9 13.3 %pack.7 = bf16[2048,1024]{1,0:T(8,128)(2,1)} custom-call(s32[1,2048]{1,0:T(1,128)} %bitcast.151, bf16[2048,1024]{1,0:T(8,128)(2,1)} %cot_ref.1), custom_call_target="tpu_custom_call" | custom-call | flops 1 | bytes 1 | tf_op jit(solution)/shard_map/pack/pallas_call | solution.py:55
  49.9 19.3 %attend_forward.1 = (bf16[2048,256]{1,0:T(8,128)(2,1)}, f32[4,2048]{1,0:T(4,128)}) custom-call(bf16[2048,768]{1,0:T(8,128)(2,1)} %convolution_convert_fusion.q_ref.k_ref.v_ref.refs_0_.refs_4_.refs_5_, bf16[2048,768]{1,0:T(8,128)(2,1)} %convolution_convert_fusion.q_ref.k_ref.v_ref.refs_0_.refs_4_.refs_5_, ...), custom_call_target="tpu_custom_call" | custom-call | flops 524288 | bytes 524288 | tf_op jit(solution)/shard_map/attend_forward/pallas_call | solution.py:195
  74.5 12.9 %pack.10 = bf16[2048,1024]{1,0:T(8,128)(2,1)} custom-call(s32[1,2048]{1,0:T(1,128)} %bitcast.152, bf16[2048,1024]{1,0:T(8,128)(2,1)} %cot_ref.1, bf16[2048,256]{1,0:T(8,128)(2,1)} %get-tuple-element.128.rest_1_.refs_2_), custom_call_target="tpu_custom_call" | custom-call | flops 1 | bytes 1 | tf_op jit(solution)/shard_map/pack/pallas_call | solution.py:55
  87.5 35.4 %all-to-all-done.1.gy_ref = bf16[8,2,128,1024]{3,2,1,0:T(8,128)(2,1)} async-done(((bf16[8,2,128,1024]{3,2,1,0:T(8,128)(2,1)}), bf16[8,2,128,1024]{3,2,1,0:T(8,128)(2,1)}, u32[]{:S(2)}, u32[]{:S(2)}) %all-to-all-start.1) | async-done | bytes 4194336 | tf_op jit(solution)/shard_map/all_to_all | solution.py:561
  127.7 31.1 %all-gather.14.cloned.1.call-done = bf16[8192,256]{1,0:T(8,128)(2,1)} async-done(((bf16[2048,256]{1,0:T(8,128)(2,1)}), bf16[8192,256]{1,0:T(8,128)(2,1)}) %all-gather.14.cloned.1.call-update) | async-done | bytes 4194320 | tf_op jit(solution)/shard_map/all_gather | solution.py:653
  158.8 11.5 %middle_pass.1 = (f32[2048,1024]{1,0:T(8,128)}, bf16[2048,1024]{1,0:T(8,128)(2,1)}) custom-call(bf16[4,2048,256]{2,1,0:T(8,128)(2,1)} %bitcast.164, bf16[4,1024,256]{2,1,0:T(8,128)(2,1)} %all-gather.10.cloned.1.call-done.out_ref.weight_ref, bf16[2048,1024]{1,0:T(8,128)(2,1)} %tokens_ref.3, f32[1,1024]{1,0:T(1,128)} %get-tuple-element.283.gain_ref, ...), custom_call_target="tpu_custom_call" | custom-call | flops 4294967296 | bytes 20971520 | tf_op jit(solution)/shard_map/middle_pass/pallas_call | solution.py:126
  249.4 14.5 %expert_pass.7 = (bf16[4,1024,256]{2,1,0:T(8,128)(2,1)}, bf16[8,128,1024]{2,1,0:T(8,128)(2,1)}, bf16[8,128,1024]{2,1,0:T(8,128)(2,1)}, bf16[8,2,128,640]{3,2,1,0:T(8,128)(2,1)}, bf16[8,2,128,384]{3,2,1,0:T(8,128)(2,1)}) custom-call(bf16[1024,1024]{1,0:T(8,128)(2,1)} %bitcast.24.x_ref, ...), custom_call_target="tpu_custom_call", output_to_operand_aliasing={{3}: (4, {}), {4}: (5, {})} | custom-call | flops 8589934592 | bytes 16777216 | tf_op jit(solution)/shard_map/expert_pass/pallas_call | solution.py:475
  281.0 14.6 %expert_pass.8 = (bf16[4,1024,256]{2,1,0:T(8,128)(2,1)}, bf16[8,128,1024]{2,1,0:T(8,128)(2,1)}, bf16[8,128,1024]{2,1,0:T(8,128)(2,1)}, bf16[8,2,128,640]{3,2,1,0:T(8,128)(2,1)}, bf16[8,2,128,384]{3,2,1,0:T(8,128)(2,1)}) custom-call(bf16[1024,1024]{1,0:T(8,128)(2,1)} %bitcast.108, bf16[8,2,128,1024]{3,2,1,0:T(8,128)(2,1)} %all-to-all-done.2.gy_ref, ...), custom_call_target="tpu_custom_call" | custom-call | flops 8589934592 | bytes 16777216 | tf_op jit(solution)/shard_map/expert_pass/pallas_call | solution.py:475
  295.6 11.9 %all-to-all-done.7 = bf16[8,128,1024]{2,1,0:T(8,128)(2,1)S(1)} async-done(((bf16[8,128,1024]{2,1,0:T(8,128)(2,1)}), bf16[8,128,1024]{2,1,0:T(8,128)(2,1)S(1)}, u32[]{:S(2)}, u32[]{:S(2)}) %all-to-all-start.7) | async-done | bytes 2097184 | tf_op jit(solution)/shard_map/all_to_all | solution.py:561
  313.3 14.6 %expert_pass.9 = (bf16[4,1024,256]{2,1,0:T(8,128)(2,1)}, bf16[8,128,1024]{2,1,0:T(8,128)(2,1)}, bf16[8,128,1024]{2,1,0:T(8,128)(2,1)}, bf16[8,2,128,640]{3,2,1,0:T(8,128)(2,1)}, bf16[8,2,128,384]{3,2,1,0:T(8,128)(2,1)}) custom-call(bf16[1024,1024]{1,0:T(8,128)(2,1)} %bitcast.106, ...), custom_call_target="tpu_custom_call", output_to_operand_aliasing={{3}: (4, {}), {4}: (5, {})} | custom-call | flops 8589934592 | bytes 16777216 | tf_op jit(solution)/shard_map/expert_pass/pallas_call | solution.py:475
  327.9 17.6 %all-to-all-done.8 = bf16[8,2,128,640]{3,2,1,0:T(8,128)(2,1)} async-done(((bf16[8,2,128,640]{3,2,1,0:T(8,128)(2,1)}), bf16[8,2,128,640]{3,2,1,0:T(8,128)(2,1)}, u32[]{:S(2)}, u32[]{:S(2)}) %all-to-all-start.8) | async-done | bytes 2621472 | tf_op jit(solution)/shard_map/all_to_all | solution.py:561
  353.6 11.7 %weight_pass.4 = (f32[4,1024,1024]{2,1,0:T(8,128)}, f32[4,1024,1024]{2,1,0:T(8,128)}, f32[8,128]{1,0:T(8,128)}) custom-call(bf16[1024,1024]{1,0:T(8,128)(2,1)} %bitcast.126, bf16[8,2,128,1024]{3,2,1,0:T(8,128)(2,1)} %all-to-all-done.1.gy_ref, bf16[1024,32]{1,0:T(8,128)(2,1)} %copy.127.router_ref, f32[1,32]{1,0:T(1,128)} %compare_convert_fusion.2.pick_ref, ...), custom_call_target="tpu_custom_call" | custom-call | flops 4294967296 | bytes 16777216 | tf_op jit(solution)/shard_map/weight_pass/pallas_call | solution.py:527
  365.3 11.7 %weight_pass.5 = (f32[4,1024,1024]{2,1,0:T(8,128)}, f32[4,1024,1024]{2,1,0:T(8,128)}, f32[8,128]{1,0:T(8,128)}) custom-call(bf16[1024,1024]{1,0:T(8,128)(2,1)} %bitcast.24.x_ref, bf16[8,2,128,1024]{3,2,1,0:T(8,128)(2,1)} %all-to-all-done.1.gy_ref, bf16[1024,32]{1,0:T(8,128)(2,1)} %copy.127.router_ref, ...), custom_call_target="tpu_custom_call", output_to_operand_aliasing={{0}: (6, {}), {1}: (7, {})} | custom-call | flops 4294967296 | bytes 16777216 | tf_op jit(solution)/shard_map/weight_pass/pallas_call | solution.py:527
  388.8 18.3 %unpack.3.rest_2_ = bf16[2048,640]{1,0:T(8,128)(2,1)} custom-call(s32[2048,1]{1,0:T(8,128)} %copy.128.refs_0_, s32[2048,1]{1,0:T(8,128)} %copy.129.refs_1_, bf16[2048,640]{1,0:T(8,128)(2,1)} %bitcast.39.refs_2_, bf16[2048,640]{1,0:T(8,128)(2,1)} %bitcast.40.refs_3_, f32[8,128]{1,0:T(8,128)} %get-tuple-element.189.refs_4_), custom_call_target="tpu_custom_call" | custom-call | flops 10737418240 | bytes 7864320 | tf_op jit(solution)/shard_map/unpack/pallas_call | solution.py:89
  413.2 11.7 %weight_pass.6 = (f32[4,1024,1024]{2,1,0:T(8,128)}, f32[4,1024,1024]{2,1,0:T(8,128)}, f32[8,128]{1,0:T(8,128)}) custom-call(bf16[1024,1024]{1,0:T(8,128)(2,1)} %bitcast.109, bf16[8,2,128,1024]{3,2,1,0:T(8,128)(2,1)} %all-to-all-done.2.gy_ref, bf16[1024,32]{1,0:T(8,128)(2,1)} %copy.127.router_ref, ...), custom_call_target="tpu_custom_call", output_to_operand_aliasing={{0}: (6, {}), {1}: (7, {})} | custom-call | flops 4294967296 | bytes 16777216 | tf_op jit(solution)/shard_map/weight_pass/pallas_call | solution.py:527
  437.5 13.3 %unpack.4 = bf16[2048,384]{1,0:T(8,128)(2,1)} custom-call(s32[2048,1]{1,0:T(8,128)} %copy.128.refs_0_, s32[2048,1]{1,0:T(8,128)} %copy.129.refs_1_, bf16[2048,384]{1,0:T(8,128)(2,1)} %bitcast.129, bf16[2048,384]{1,0:T(8,128)(2,1)} %bitcast.130, f32[8,128]{1,0:T(8,128)} %get-tuple-element.202.refs_4_), custom_call_target="tpu_custom_call" | custom-call | flops 6442450944 | bytes 4718592 | tf_op jit(solution)/shard_map/unpack/pallas_call | solution.py:89
  450.8 13.2 %all-to-all-done.12 = bf16[8,4,128,256]{3,2,1,0:T(8,128)(2,1)S(1)} async-done(((bf16[8,4,128,256]{3,2,1,0:T(8,128)(2,1)}), bf16[8,4,128,256]{3,2,1,0:T(8,128)(2,1)S(1)}, u32[]{:S(2)}, u32[]{:S(2)}) %all-to-all-start.12) | async-done | bytes 2097184 | tf_op jit(solution)/shard_map/all_to_all | solution.py:561
  531.2 11.7 %weight_pass.7 = (f32[4,1024,1024]{2,1,0:T(8,128)}, f32[4,1024,1024]{2,1,0:T(8,128)}, f32[8,128]{1,0:T(8,128)}) custom-call(bf16[1024,1024]{1,0:T(8,128)(2,1)} %bitcast.107, bf16[8,2,128,1024]{3,2,1,0:T(8,128)(2,1)} %all-to-all-done.2.gy_ref, bf16[1024,32]{1,0:T(8,128)(2,1)} %copy.127.router_ref, ...), custom_call_target="tpu_custom_call", output_to_operand_aliasing={{0}: (6, {}), {1}: (7, {})} | custom-call | flops 4294967296 | bytes 16777216 | tf_op jit(solution)/shard_map/weight_pass/pallas_call | solution.py:527
  542.9 24.1 %all-to-all-done.14 = bf16[4,512,256]{2,1,0:T(8,128)(2,1)} async-done(((bf16[4,512,256]{2,1,0:T(8,128)(2,1)}), bf16[4,512,256]{2,1,0:T(8,128)(2,1)}, u32[]{:S(2)}, u32[]{:S(2)}) %all-to-all-start.14) | async-done | bytes 1048608 | tf_op jit(solution)/shard_map/all_to_all | solution.py:561
  570.8 37.9 %attend_backward.1 = (bf16[2048,768]{1,0:T(8,128)(2,1)}, bf16[2048,1024]{1,0:T(8,128)(2,1)}) custom-call(bf16[2048,768]{1,0:T(8,128)(2,1)} %convolution_convert_fusion.q_ref.k_ref.v_ref.refs_0_.refs_4_.refs_5_, bf16[2048,256]{1,0:T(8,128)(2,1)} %bitcast.58.refs_1_, bf16[2048,256]{1,0:T(8,128)(2,1)} %get-tuple-element.128.rest_1_.refs_2_, ...), custom_call_target="tpu_custom_call" | custom-call | flops 21474836480 | bytes 8388608 | tf_op jit(solution)/shard_map/attend_backward/pallas_call | solution.py:279
  639.5 52.0 %reduce-scatter.23.cloned.1.call-done.share_ref = bf16[512,1024]{1,0:T(8,128)(2,1)} async-done(((bf16[2048,1024]{1,0:T(8,128)(2,1)}), bf16[512,1024]{1,0:T(8,128)(2,1)}) %reduce-scatter.23.cloned.1.call-update) | async-done | bytes 1048592 | tf_op jit(solution)/shard_map/reduce_scatter | solution.py:843
  705.6 9.9 %all_to_all.105 = f32[4,4,128]{2,1,0:T(4,128)S(1)} all-to-all(f32[4,4,128]{2,1,0:T(4,128)S(1)} %broadcast_in_dim.16), channel_id=1, replica_groups=mesh['row'=8,'col'=4] {'col'}, dimensions={0} | all-to-all | bytes 16384 | tf_op jit(solution)/shard_map/all_to_all | solution.py:561
  720.7 19.2 %all-to-all-done.17 = bf16[8,128,768]{2,1,0:T(8,128)(2,1)S(1)} async-done(((bf16[8,128,768]{2,1,0:T(8,128)(2,1)}), bf16[8,128,768]{2,1,0:T(8,128)(2,1)S(1)}, u32[]{:S(2)}, u32[]{:S(2)}) %all-to-all-start.17) | async-done | bytes 1572896 | tf_op jit(solution)/shard_map/all_to_all | solution.py:561
  741.3 36.3 %all-gather.12.cloned.1.call-done = bf16[2048,1024]{1,0:T(8,128)(2,1)} async-done(((bf16[512,1024]{1,0:T(8,128)(2,1)}), bf16[2048,1024]{1,0:T(8,128)(2,1)}) %all-gather.12.cloned.1.call-update) | async-done | bytes 4194320 | tf_op jit(solution)/shard_map/all_gather | solution.py:858
  (196 shorter events, 306.3 us)
Async XLA Ops:
  7.2 32.3 %all-gather.8.cloned.1.call-start = ((), (), s32[]{:S(2)}) async-start(), calls=%async_computation.28 | async-start | bytes 1861632 | tf_op jit(solution)/shard_map/all_gather | solution.py:611
  20.3 107.5 %all-gather.10.cloned.1.call-start = ((), (), s32[]{:S(2)}) async-start(), calls=%async_computation.29 | async-start | bytes 2359296 | tf_op jit(solution)/shard_map/all_gather | solution.py:655
  69.2 53.7 %all-to-all-start.1 = ((bf16[8,2,128,1024]{3,2,1,0:T(8,128)(2,1)}), bf16[8,2,128,1024]{3,2,1,0:T(8,128)(2,1)}, u32[]{:S(2)}, u32[]{:S(2)}) async-start(bf16[8,2,128,1024]{3,2,1,0:T(8,128)(2,1)} %bitcast.102), calls=%async_computation.1 | async-start | bytes 8388608 | tf_op jit(solution)/shard_map/all_to_all | solution.py:561
  73.8 85.0 %all-gather.14.cloned.1.call-start = ((), (), s32[]{:S(2)}) async-start(), calls=%async_computation.39 | async-start | bytes 5242880 | tf_op jit(solution)/shard_map/all_gather | solution.py:653
  122.9 53.9 %all-to-all-start.2 = ((bf16[8,2,128,1024]{3,2,1,0:T(8,128)(2,1)}), bf16[8,2,128,1024]{3,2,1,0:T(8,128)(2,1)}, u32[]{:S(2)}, u32[]{:S(2)}) async-start(bf16[8,2,128,1024]{3,2,1,0:T(8,128)(2,1)} %bitcast.103), calls=%async_computation.2 | async-start | bytes 8388608 | tf_op jit(solution)/shard_map/all_to_all | solution.py:561
  199.3 114.0 %reduce-scatter.9.cloned.1.call-start = ((), (), s32[]{:S(2)}) async-start(), calls=%async_computation.30 | async-start | bytes 1310720 | tf_op jit(solution)/shard_map/reduce_scatter | solution.py:694
  214.7 31.1 %all-to-all-start.5 = ((bf16[8,128,1024]{2,1,0:T(8,128)(2,1)}), bf16[8,128,1024]{2,1,0:T(8,128)(2,1)}, u32[]{:S(2)}, u32[]{:S(2)}) async-start(bf16[8,128,1024]{2,1,0:T(8,128)(2,1)} %bitcast.111), calls=%async_computation.5 | async-start | bytes 4194304 | tf_op jit(solution)/shard_map/all_to_all | solution.py:561
  219.1 193.1 %reduce-scatter.13.cloned.1.call-start = ((), (), s32[]{:S(2)}) async-start(), calls=%async_computation.32 | async-start | bytes 1310720 | tf_op jit(solution)/shard_map/reduce_scatter | solution.py:694
  245.8 30.2 %all-to-all-start.6 = ((bf16[8,128,1024]{2,1,0:T(8,128)(2,1)}), bf16[8,128,1024]{2,1,0:T(8,128)(2,1)S(1)}, u32[]{:S(2)}, u32[]{:S(2)}) async-start(bf16[8,128,1024]{2,1,0:T(8,128)(2,1)} %bitcast.114), calls=%async_computation.6 | async-start | bytes 4194304 | tf_op jit(solution)/shard_map/all_to_all | solution.py:561
  249.4 175.5 %reduce-scatter.15.cloned.1.call-start = ((), (), s32[]{:S(2)}) async-start(), calls=%async_computation.33 | async-start | bytes 2621440 | tf_op jit(solution)/shard_map/reduce_scatter | solution.py:694
  277.3 30.2 %all-to-all-start.7 = ((bf16[8,128,1024]{2,1,0:T(8,128)(2,1)}), bf16[8,128,1024]{2,1,0:T(8,128)(2,1)S(1)}, u32[]{:S(2)}, u32[]{:S(2)}) async-start(bf16[8,128,1024]{2,1,0:T(8,128)(2,1)} %bitcast.110), calls=%async_computation.7 | async-start | bytes 4194304 | tf_op jit(solution)/shard_map/all_to_all | solution.py:561
  280.9 144.0 %reduce-scatter.17.cloned.1.call-start = ((), (), s32[]{:S(2)}) async-start(), calls=%async_computation.34 | async-start | bytes 2621440 | tf_op jit(solution)/shard_map/reduce_scatter | solution.py:694
  308.8 36.7 %all-to-all-start.8 = ((bf16[8,2,128,640]{3,2,1,0:T(8,128)(2,1)}), bf16[8,2,128,640]{3,2,1,0:T(8,128)(2,1)}, u32[]{:S(2)}, u32[]{:S(2)}) async-start(bf16[8,2,128,640]{3,2,1,0:T(8,128)(2,1)} %get-tuple-element.181), calls=%async_computation.9 | async-start | bytes 5242880 | tf_op jit(solution)/shard_map/all_to_all | solution.py:561
  313.3 111.7 %reduce-scatter.19.cloned.1.call-start = ((), (), s32[]{:S(2)}) async-start(), calls=%async_computation.35 | async-start | bytes 2621440 | tf_op jit(solution)/shard_map/reduce_scatter | solution.py:775
  345.6 36.8 %all-to-all-start.9 = ((bf16[8,2,128,640]{3,2,1,0:T(8,128)(2,1)}), bf16[8,2,128,640]{3,2,1,0:T(8,128)(2,1)}, u32[]{:S(2)}, u32[]{:S(2)}) async-start(bf16[8,2,128,640]{3,2,1,0:T(8,128)(2,1)} %get-tuple-element.185), calls=%async_computation.10 | async-start | bytes 5242880 | tf_op jit(solution)/shard_map/all_to_all | solution.py:561
  386.0 85.5 %reduce-scatter.11.cloned.1.call-start = ((), (), s32[]{:S(2)}) async-start(), calls=%async_computation.31 | async-start | bytes 3276800 | tf_op jit(solution)/shard_map/reduce_scatter | solution.py:785
  407.2 25.5 %all-to-all-start.11 = ((bf16[8,2,128,384]{3,2,1,0:T(8,128)(2,1)}), bf16[8,2,128,384]{3,2,1,0:T(8,128)(2,1)S(1)}, u32[]{:S(2)}, u32[]{:S(2)}) async-start(bf16[8,2,128,384]{3,2,1,0:T(8,128)(2,1)} %get-tuple-element.192), calls=%async_computation.13 | async-start | bytes 3145728 | tf_op jit(solution)/shard_map/all_to_all | solution.py:561
  433.8 30.2 %all-to-all-start.12 = ((bf16[8,4,128,256]{3,2,1,0:T(8,128)(2,1)}), bf16[8,4,128,256]{3,2,1,0:T(8,128)(2,1)S(1)}, u32[]{:S(2)}, u32[]{:S(2)}) async-start(bf16[8,4,128,256]{3,2,1,0:T(8,128)(2,1)} %pad_maximum_fusion.2), calls=%async_computation.18 | async-start | bytes 4194304 | tf_op jit(solution)/shard_map/all_to_all | solution.py:561
  437.4 65.2 %reduce-scatter.21.cloned.1.call-start = ((), (), s32[]{:S(2)}) async-start(), calls=%async_computation.36 | async-start | bytes 1966080 | tf_op jit(solution)/shard_map/reduce_scatter | solution.py:792
  464.0 144.7 %all-gather.16.cloned.1.call-start = ((), (), s32[]{:S(2)}) async-start(), calls=%async_computation.40 | async-start | bytes 5242880 | tf_op jit(solution)/shard_map/all_gather | solution.py:806
  509.3 57.6 %all-to-all-start.14 = ((bf16[4,512,256]{2,1,0:T(8,128)(2,1)}), bf16[4,512,256]{2,1,0:T(8,128)(2,1)}, u32[]{:S(2)}, u32[]{:S(2)}) async-start(bf16[4,512,256]{2,1,0:T(8,128)(2,1)} %get-tuple-element.208), calls=%async_computation.21 | async-start | bytes 2097152 | tf_op jit(solution)/shard_map/all_to_all | solution.py:561
  566.9 41.8 %all-to-all-start.15 = ((bf16[8,128,1056]{1,2,0:T(8,128)(2,1)}), bf16[8,128,1056]{1,2,0:T(8,128)(2,1)S(1)}, u32[]{:S(2)}, u32[]{:S(2)}) async-start(bf16[8,128,1056]{1,2,0:T(8,128)(2,1)} %copy.144), calls=%async_computation.22 | async-start | bytes 4325376 | tf_op jit(solution)/shard_map/all_to_all | solution.py:561
  570.6 121.0 %reduce-scatter.23.cloned.1.call-start = ((), (), s32[]{:S(2)}) async-start(), calls=%async_computation.37 | async-start | bytes 5242880 | tf_op jit(solution)/shard_map/reduce_scatter | solution.py:843
  615.0 162.5 %all-gather.12.cloned.1.call-start = ((), (), s32[]{:S(2)}) async-start(), calls=%async_computation.38 | async-start | bytes 5242880 | tf_op jit(solution)/shard_map/all_gather | solution.py:858
  (33 other events, 292.2 us)
Sparse Core Ops, SparseCore 0:
  10.5 28.9 all-gather.7
  41.9 27.8 all-gather.9
  76.2 82.5 all-gather.13
  214.8 26.7 reduce-scatter.8
  245.9 26.7 reduce-scatter.12
  276.1 43.4 reduce-scatter.14
  322.0 43.1 reduce-scatter.16
  367.5 43.1 reduce-scatter.18
  413.7 51.4 reduce-scatter.10
  467.4 35.1 reduce-scatter.20
  504.2 101.9 all-gather.15
  609.1 82.4 reduce-scatter.22
  695.7 81.7 all-gather.11

commit v12 on v11

--- a/solution.py
+++ b/solution.py
@@ -423,6 +423,32 @@
         name="close_pass",
         cost_estimate=cost(30 * part * depth, 12 * part * depth),
     )(col, shares, tokens, grads, gain)
+
+
+def move_body(source_ref, target_ref, sems):
+    rows = source_ref.shape[0] // sems.shape[0]
+    copies = []
+    for j in range(sems.shape[0]):
+        part = pl.ds(j * rows, rows)
+        copies.append(
+            pltpu.make_async_copy(source_ref.at[part], target_ref.at[part], sems.at[j])
+        )
+    for copy in copies:
+        copy.start()
+    for copy in copies:
+        copy.wait()
+
+
+def move(values):
+    return pl.pallas_call(
+        move_body,
+        out_shape=jax.ShapeDtypeStruct(values.shape, values.dtype),
+        in_specs=[pl.BlockSpec(memory_space=pl.ANY)],
+        out_specs=pl.BlockSpec(memory_space=pl.ANY),
+        scratch_shapes=[pltpu.SemaphoreType.DMA((8,))],
+        compiler_params=params(),
+        name="move",
+    )(values)
 
 
 ROOT = math.sqrt(2.0 / math.pi)
@@ -855,7 +881,7 @@
     )
 
     grad_tokens, sums_one = close_pass(place, grad_normal, tokens, grad_middle, gains[0:1])
-    grad_tokens = lax.all_gather(grad_tokens, "col", axis=0, tiled=True)
+    grad_tokens = move(lax.all_gather(grad_tokens, "col", axis=0, tiled=True))
     small = jnp.concatenate([sums_one[0:2], sums_two[0:2]], axis=0)
     small = swap(small.reshape(4, rows_all, share).transpose(1, 0, 2), "row")
     small = jnp.sum(small, axis=0)

time: 796 us -> 920 us (1.16)
  Pallas kernels: 291 us -> 419 us
    pallas_call x0 -> x1, Pallas kernels: none -> 128 us  [move(): pl.pallas_call(move_body, out_shape=jax.ShapeDtypeStruct(values.shape, va...]
  transfers between devices with their start and end apart: 31 -> 31, of which waited for: 20 -> 20; matrix products, arithmetic and copies ran while one was open for 10% -> 9% of each run, Pallas kernels for 36% -> 31%
where the time goes in v12:
time: 920 us; the launch traced here: 913 us
  Pallas kernels  419 us (46%)
  waiting for transfers between devices  294 us (32%)
  starting transfers between devices  78 us (8%)
  matrix products  29.8 us (3%)
  local copies, waits for them, and re-layouts  29.7 us (3%)
  other arithmetic  29.1 us (3%)
  blocking collectives  18.2 us (2%)
  between operations  14.7 us (2%)
    all_to_all x18, waiting for transfers between devices, swap(): return lax.all_to_all(blocks, axis, split_axis=0, concat_axis=0, tiled=True)  168 us
    pallas_call x1, Pallas kernels, move(): pl.pallas_call(move_body, out_shape=jax.ShapeDtypeStruct(values.shape, va...  128 us
    all_to_all x18, starting transfers between devices, swap(): return lax.all_to_all(blocks, axis, split_axis=0, concat_axis=0, tiled=True)  77.3 us
    pallas_call x5, Pallas kernels, expert_pass(): pl.pallas_call(functools.partial(expert_body, len(given) + len(waits)), o...  62.5 us
    pallas_call x7, Pallas kernels, pack(): pl.pallas_call(functools.partial(pack_body, base, step, each, len(rows)),...  61.5 us
    reduce_scatter x1, waiting for transfers between devices, per_device(): lax.psum_scatter(shares, 'col', scatter_dimension=0, tiled=True)  52 us
    pallas_call x4, Pallas kernels, weight_pass(): pl.pallas_call(functools.partial(weight_body, len(sent) + len(waits)), ou...  46.8 us
    pallas_call x3, Pallas kernels, unpack(): pl.pallas_call(functools.partial(unpack_body, len(rows)), out_shape=jax.S...  40.7 us
  transfers between devices with their start and end apart: 31, of which 20 were waited for; matrix products, arithmetic and copies ran while one was open for 9% of the time, Pallas kernels for 31%

profile of v12, /device:TPU:0, one launch (start us, length us, event | category | flops | bytes accessed | tf_op | source)
XLA Modules:
  0.0 912.5 jit_solution(15524572164800559628)
XLA Ops:
  25.9 13.3 %pack.7 = bf16[2048,1024]{1,0:T(8,128)(2,1)} custom-call(s32[1,2048]{1,0:T(1,128)} %bitcast.151, bf16[2048,1024]{1,0:T(8,128)(2,1)} %cot_ref.1), custom_call_target="tpu_custom_call" | custom-call | flops 1 | bytes 1 | tf_op jit(solution)/shard_map/pack/pallas_call | solution.py:55
  49.9 19.3 %attend_forward.1 = (bf16[2048,256]{1,0:T(8,128)(2,1)}, f32[4,2048]{1,0:T(4,128)}) custom-call(bf16[2048,768]{1,0:T(8,128)(2,1)} %convolution_convert_fusion.q_ref.k_ref.v_ref.refs_0_.refs_4_.refs_5_, bf16[2048,768]{1,0:T(8,128)(2,1)} %convolution_convert_fusion.q_ref.k_ref.v_ref.refs_0_.refs_4_.refs_5_, ...), custom_call_target="tpu_custom_call" | custom-call | flops 524288 | bytes 524288 | tf_op jit(solution)/shard_map/attend_forward/pallas_call | solution.py:195
  74.5 12.9 %pack.10 = bf16[2048,1024]{1,0:T(8,128)(2,1)} custom-call(s32[1,2048]{1,0:T(1,128)} %bitcast.152, bf16[2048,1024]{1,0:T(8,128)(2,1)} %cot_ref.1, bf16[2048,256]{1,0:T(8,128)(2,1)} %get-tuple-element.128.rest_1_.refs_2_), custom_call_target="tpu_custom_call" | custom-call | flops 1 | bytes 1 | tf_op jit(solution)/shard_map/pack/pallas_call | solution.py:55
  87.5 35.4 %all-to-all-done.1.gy_ref = bf16[8,2,128,1024]{3,2,1,0:T(8,128)(2,1)} async-done(((bf16[8,2,128,1024]{3,2,1,0:T(8,128)(2,1)}), bf16[8,2,128,1024]{3,2,1,0:T(8,128)(2,1)}, u32[]{:S(2)}, u32[]{:S(2)}) %all-to-all-start.1) | async-done | bytes 4194336 | tf_op jit(solution)/shard_map/all_to_all | solution.py:587
  127.7 31.1 %all-gather.14.cloned.1.call-done = bf16[8192,256]{1,0:T(8,128)(2,1)} async-done(((bf16[2048,256]{1,0:T(8,128)(2,1)}), bf16[8192,256]{1,0:T(8,128)(2,1)}) %all-gather.14.cloned.1.call-update) | async-done | bytes 4194320 | tf_op jit(solution)/shard_map/all_gather | solution.py:679
  158.8 11.5 %middle_pass.1 = (f32[2048,1024]{1,0:T(8,128)}, bf16[2048,1024]{1,0:T(8,128)(2,1)}) custom-call(bf16[4,2048,256]{2,1,0:T(8,128)(2,1)} %bitcast.164, bf16[4,1024,256]{2,1,0:T(8,128)(2,1)} %all-gather.10.cloned.1.call-done.out_ref.weight_ref, bf16[2048,1024]{1,0:T(8,128)(2,1)} %tokens_ref.3, f32[1,1024]{1,0:T(1,128)} %get-tuple-element.283.gain_ref, ...), custom_call_target="tpu_custom_call" | custom-call | flops 4294967296 | bytes 20971520 | tf_op jit(solution)/shard_map/middle_pass/pallas_call | solution.py:126
  249.4 14.5 %expert_pass.7 = (bf16[4,1024,256]{2,1,0:T(8,128)(2,1)}, bf16[8,128,1024]{2,1,0:T(8,128)(2,1)}, bf16[8,128,1024]{2,1,0:T(8,128)(2,1)}, bf16[8,2,128,640]{3,2,1,0:T(8,128)(2,1)}, bf16[8,2,128,384]{3,2,1,0:T(8,128)(2,1)}) custom-call(bf16[1024,1024]{1,0:T(8,128)(2,1)} %bitcast.24.x_ref, ...), custom_call_target="tpu_custom_call", output_to_operand_aliasing={{3}: (4, {}), {4}: (5, {})} | custom-call | flops 8589934592 | bytes 16777216 | tf_op jit(solution)/shard_map/expert_pass/pallas_call | solution.py:501
  281.0 14.6 %expert_pass.8 = (bf16[4,1024,256]{2,1,0:T(8,128)(2,1)}, bf16[8,128,1024]{2,1,0:T(8,128)(2,1)}, bf16[8,128,1024]{2,1,0:T(8,128)(2,1)}, bf16[8,2,128,640]{3,2,1,0:T(8,128)(2,1)}, bf16[8,2,128,384]{3,2,1,0:T(8,128)(2,1)}) custom-call(bf16[1024,1024]{1,0:T(8,128)(2,1)} %bitcast.108, bf16[8,2,128,1024]{3,2,1,0:T(8,128)(2,1)} %all-to-all-done.2.gy_ref, ...), custom_call_target="tpu_custom_call" | custom-call | flops 8589934592 | bytes 16777216 | tf_op jit(solution)/shard_map/expert_pass/pallas_call | solution.py:501
  295.6 11.9 %all-to-all-done.7 = bf16[8,128,1024]{2,1,0:T(8,128)(2,1)S(1)} async-done(((bf16[8,128,1024]{2,1,0:T(8,128)(2,1)}), bf16[8,128,1024]{2,1,0:T(8,128)(2,1)S(1)}, u32[]{:S(2)}, u32[]{:S(2)}) %all-to-all-start.7) | async-done | bytes 2097184 | tf_op jit(solution)/shard_map/all_to_all | solution.py:587
  313.3 14.6 %expert_pass.9 = (bf16[4,1024,256]{2,1,0:T(8,128)(2,1)}, bf16[8,128,1024]{2,1,0:T(8,128)(2,1)}, bf16[8,128,1024]{2,1,0:T(8,128)(2,1)}, bf16[8,2,128,640]{3,2,1,0:T(8,128)(2,1)}, bf16[8,2,128,384]{3,2,1,0:T(8,128)(2,1)}) custom-call(bf16[1024,1024]{1,0:T(8,128)(2,1)} %bitcast.106, ...), custom_call_target="tpu_custom_call", output_to_operand_aliasing={{3}: (4, {}), {4}: (5, {})} | custom-call | flops 8589934592 | bytes 16777216 | tf_op jit(solution)/shard_map/expert_pass/pallas_call | solution.py:501
  327.9 17.6 %all-to-all-done.8 = bf16[8,2,128,640]{3,2,1,0:T(8,128)(2,1)} async-done(((bf16[8,2,128,640]{3,2,1,0:T(8,128)(2,1)}), bf16[8,2,128,640]{3,2,1,0:T(8,128)(2,1)}, u32[]{:S(2)}, u32[]{:S(2)}) %all-to-all-start.8) | async-done | bytes 2621472 | tf_op jit(solution)/shard_map/all_to_all | solution.py:587
  353.6 11.7 %weight_pass.4 = (f32[4,1024,1024]{2,1,0:T(8,128)}, f32[4,1024,1024]{2,1,0:T(8,128)}, f32[8,128]{1,0:T(8,128)}) custom-call(bf16[1024,1024]{1,0:T(8,128)(2,1)} %bitcast.126, bf16[8,2,128,1024]{3,2,1,0:T(8,128)(2,1)} %all-to-all-done.1.gy_ref, bf16[1024,32]{1,0:T(8,128)(2,1)} %copy.127.router_ref, f32[1,32]{1,0:T(1,128)} %compare_convert_fusion.2.pick_ref, ...), custom_call_target="tpu_custom_call" | custom-call | flops 4294967296 | bytes 16777216 | tf_op jit(solution)/shard_map/weight_pass/pallas_call | solution.py:553
  365.3 11.7 %weight_pass.5 = (f32[4,1024,1024]{2,1,0:T(8,128)}, f32[4,1024,1024]{2,1,0:T(8,128)}, f32[8,128]{1,0:T(8,128)}) custom-call(bf16[1024,1024]{1,0:T(8,128)(2,1)} %bitcast.24.x_ref, bf16[8,2,128,1024]{3,2,1,0:T(8,128)(2,1)} %all-to-all-done.1.gy_ref, bf16[1024,32]{1,0:T(8,128)(2,1)} %copy.127.router_ref, ...), custom_call_target="tpu_custom_call", output_to_operand_aliasing={{0}: (6, {}), {1}: (7, {})} | custom-call | flops 4294967296 | bytes 16777216 | tf_op jit(solution)/shard_map/weight_pass/pallas_call | solution.py:553
  388.8 18.3 %unpack.3.rest_2_ = bf16[2048,640]{1,0:T(8,128)(2,1)} custom-call(s32[2048,1]{1,0:T(8,128)} %copy.128.refs_0_, s32[2048,1]{1,0:T(8,128)} %copy.129.refs_1_, bf16[2048,640]{1,0:T(8,128)(2,1)} %bitcast.39.refs_2_, bf16[2048,640]{1,0:T(8,128)(2,1)} %bitcast.40.refs_3_, f32[8,128]{1,0:T(8,128)} %get-tuple-element.189.refs_4_), custom_call_target="tpu_custom_call" | custom-call | flops 10737418240 | bytes 7864320 | tf_op jit(solution)/shard_map/unpack/pallas_call | solution.py:89
  413.2 11.7 %weight_pass.6 = (f32[4,1024,1024]{2,1,0:T(8,128)}, f32[4,1024,1024]{2,1,0:T(8,128)}, f32[8,128]{1,0:T(8,128)}) custom-call(bf16[1024,1024]{1,0:T(8,128)(2,1)} %bitcast.109, bf16[8,2,128,1024]{3,2,1,0:T(8,128)(2,1)} %all-to-all-done.2.gy_ref, bf16[1024,32]{1,0:T(8,128)(2,1)} %copy.127.router_ref, ...), custom_call_target="tpu_custom_call", output_to_operand_aliasing={{0}: (6, {}), {1}: (7, {})} | custom-call | flops 4294967296 | bytes 16777216 | tf_op jit(solution)/shard_map/weight_pass/pallas_call | solution.py:553
  437.5 13.3 %unpack.4 = bf16[2048,384]{1,0:T(8,128)(2,1)} custom-call(s32[2048,1]{1,0:T(8,128)} %copy.128.refs_0_, s32[2048,1]{1,0:T(8,128)} %copy.129.refs_1_, bf16[2048,384]{1,0:T(8,128)(2,1)} %bitcast.129, bf16[2048,384]{1,0:T(8,128)(2,1)} %bitcast.130, f32[8,128]{1,0:T(8,128)} %get-tuple-element.202.refs_4_), custom_call_target="tpu_custom_call" | custom-call | flops 6442450944 | bytes 4718592 | tf_op jit(solution)/shard_map/unpack/pallas_call | solution.py:89
  450.8 13.2 %all-to-all-done.12 = bf16[8,4,128,256]{3,2,1,0:T(8,128)(2,1)S(1)} async-done(((bf16[8,4,128,256]{3,2,1,0:T(8,128)(2,1)}), bf16[8,4,128,256]{3,2,1,0:T(8,128)(2,1)S(1)}, u32[]{:S(2)}, u32[]{:S(2)}) %all-to-all-start.12) | async-done | bytes 2097184 | tf_op jit(solution)/shard_map/all_to_all | solution.py:587
  531.2 11.7 %weight_pass.7 = (f32[4,1024,1024]{2,1,0:T(8,128)}, f32[4,1024,1024]{2,1,0:T(8,128)}, f32[8,128]{1,0:T(8,128)}) custom-call(bf16[1024,1024]{1,0:T(8,128)(2,1)} %bitcast.107, bf16[8,2,128,1024]{3,2,1,0:T(8,128)(2,1)} %all-to-all-done.2.gy_ref, bf16[1024,32]{1,0:T(8,128)(2,1)} %copy.127.router_ref, ...), custom_call_target="tpu_custom_call", output_to_operand_aliasing={{0}: (6, {}), {1}: (7, {})} | custom-call | flops 4294967296 | bytes 16777216 | tf_op jit(solution)/shard_map/weight_pass/pallas_call | solution.py:553
  542.9 24.1 %all-to-all-done.14 = bf16[4,512,256]{2,1,0:T(8,128)(2,1)} async-done(((bf16[4,512,256]{2,1,0:T(8,128)(2,1)}), bf16[4,512,256]{2,1,0:T(8,128)(2,1)}, u32[]{:S(2)}, u32[]{:S(2)}) %all-to-all-start.14) | async-done | bytes 1048608 | tf_op jit(solution)/shard_map/all_to_all | solution.py:587
  570.8 37.9 %attend_backward.1 = (bf16[2048,768]{1,0:T(8,128)(2,1)}, bf16[2048,1024]{1,0:T(8,128)(2,1)}) custom-call(bf16[2048,768]{1,0:T(8,128)(2,1)} %convolution_convert_fusion.q_ref.k_ref.v_ref.refs_0_.refs_4_.refs_5_, bf16[2048,256]{1,0:T(8,128)(2,1)} %bitcast.58.refs_1_, bf16[2048,256]{1,0:T(8,128)(2,1)} %get-tuple-element.128.rest_1_.refs_2_, ...), custom_call_target="tpu_custom_call" | custom-call | flops 21474836480 | bytes 8388608 | tf_op jit(solution)/shard_map/attend_backward/pallas_call | solution.py:279
  639.5 52.0 %reduce-scatter.23.cloned.1.call-done.share_ref = bf16[512,1024]{1,0:T(8,128)(2,1)} async-done(((bf16[2048,1024]{1,0:T(8,128)(2,1)}), bf16[512,1024]{1,0:T(8,128)(2,1)}) %reduce-scatter.23.cloned.1.call-update) | async-done | bytes 1048592 | tf_op jit(solution)/shard_map/reduce_scatter | solution.py:869
  720.7 19.2 %all-to-all-done.17 = bf16[8,128,768]{2,1,0:T(8,128)(2,1)S(1)} async-done(((bf16[8,128,768]{2,1,0:T(8,128)(2,1)}), bf16[8,128,768]{2,1,0:T(8,128)(2,1)S(1)}, u32[]{:S(2)}, u32[]{:S(2)}) %all-to-all-start.17) | async-done | bytes 1572896 | tf_op jit(solution)/shard_map/all_to_all | solution.py:587
  741.3 36.3 %all-gather.12.cloned.1.call-done.source_ref = bf16[2048,1024]{1,0:T(8,128)(2,1)} async-done(((bf16[512,1024]{1,0:T(8,128)(2,1)}), bf16[2048,1024]{1,0:T(8,128)(2,1)}) %all-gather.12.cloned.1.call-update) | async-done | bytes 4194320 | tf_op jit(solution)/shard_map/all_gather | solution.py:884
  777.5 128.2 %move.1 = bf16[2048,1024]{1,0:T(8,128)(2,1)} custom-call(bf16[2048,1024]{1,0:T(8,128)(2,1)} %all-gather.12.cloned.1.call-done.source_ref), custom_call_target="tpu_custom_call" | custom-call | tf_op jit(solution)/shard_map/move/pallas_call | solution.py:443
  (196 shorter events, 311.5 us)
Async XLA Ops:
  7.2 32.3 %all-gather.8.cloned.1.call-start = ((), (), s32[]{:S(2)}) async-start(), calls=%async_computation.28 | async-start | bytes 1861632 | tf_op jit(solution)/shard_map/all_gather | solution.py:637
  20.3 107.5 %all-gather.10.cloned.1.call-start = ((), (), s32[]{:S(2)}) async-start(), calls=%async_computation.29 | async-start | bytes 2359296 | tf_op jit(solution)/shard_map/all_gather | solution.py:681
  69.2 53.7 %all-to-all-start.1 = ((bf16[8,2,128,1024]{3,2,1,0:T(8,128)(2,1)}), bf16[8,2,128,1024]{3,2,1,0:T(8,128)(2,1)}, u32[]{:S(2)}, u32[]{:S(2)}) async-start(bf16[8,2,128,1024]{3,2,1,0:T(8,128)(2,1)} %bitcast.102), calls=%async_computation.1 | async-start | bytes 8388608 | tf_op jit(solution)/shard_map/all_to_all | solution.py:587
  73.8 85.0 %all-gather.14.cloned.1.call-start = ((), (), s32[]{:S(2)}) async-start(), calls=%async_computation.39 | async-start | bytes 5242880 | tf_op jit(solution)/shard_map/all_gather | solution.py:679
  122.9 53.9 %all-to-all-start.2 = ((bf16[8,2,128,1024]{3,2,1,0:T(8,128)(2,1)}), bf16[8,2,128,1024]{3,2,1,0:T(8,128)(2,1)}, u32[]{:S(2)}, u32[]{:S(2)}) async-start(bf16[8,2,128,1024]{3,2,1,0:T(8,128)(2,1)} %bitcast.103), calls=%async_computation.2 | async-start | bytes 8388608 | tf_op jit(solution)/shard_map/all_to_all | solution.py:587
  199.3 114.0 %reduce-scatter.9.cloned.1.call-start = ((), (), s32[]{:S(2)}) async-start(), calls=%async_computation.30 | async-start | bytes 1310720 | tf_op jit(solution)/shard_map/reduce_scatter | solution.py:720
  214.7 31.1 %all-to-all-start.5 = ((bf16[8,128,1024]{2,1,0:T(8,128)(2,1)}), bf16[8,128,1024]{2,1,0:T(8,128)(2,1)}, u32[]{:S(2)}, u32[]{:S(2)}) async-start(bf16[8,128,1024]{2,1,0:T(8,128)(2,1)} %bitcast.111), calls=%async_computation.5 | async-start | bytes 4194304 | tf_op jit(solution)/shard_map/all_to_all | solution.py:587
  219.1 193.1 %reduce-scatter.13.cloned.1.call-start = ((), (), s32[]{:S(2)}) async-start(), calls=%async_computation.32 | async-start | bytes 1310720 | tf_op jit(solution)/shard_map/reduce_scatter | solution.py:720
  245.8 30.2 %all-to-all-start.6 = ((bf16[8,128,1024]{2,1,0:T(8,128)(2,1)}), bf16[8,128,1024]{2,1,0:T(8,128)(2,1)S(1)}, u32[]{:S(2)}, u32[]{:S(2)}) async-start(bf16[8,128,1024]{2,1,0:T(8,128)(2,1)} %bitcast.114), calls=%async_computation.6 | async-start | bytes 4194304 | tf_op jit(solution)/shard_map/all_to_all | solution.py:587
  249.4 175.5 %reduce-scatter.15.cloned.1.call-start = ((), (), s32[]{:S(2)}) async-start(), calls=%async_computation.33 | async-start | bytes 2621440 | tf_op jit(solution)/shard_map/reduce_scatter | solution.py:720
  277.3 30.2 %all-to-all-start.7 = ((bf16[8,128,1024]{2,1,0:T(8,128)(2,1)}), bf16[8,128,1024]{2,1,0:T(8,128)(2,1)S(1)}, u32[]{:S(2)}, u32[]{:S(2)}) async-start(bf16[8,128,1024]{2,1,0:T(8,128)(2,1)} %bitcast.110), calls=%async_computation.7 | async-start | bytes 4194304 | tf_op jit(solution)/shard_map/all_to_all | solution.py:587
  280.9 144.0 %reduce-scatter.17.cloned.1.call-start = ((), (), s32[]{:S(2)}) async-start(), calls=%async_computation.34 | async-start | bytes 2621440 | tf_op jit(solution)/shard_map/reduce_scatter | solution.py:720
  308.8 36.7 %all-to-all-start.8 = ((bf16[8,2,128,640]{3,2,1,0:T(8,128)(2,1)}), bf16[8,2,128,640]{3,2,1,0:T(8,128)(2,1)}, u32[]{:S(2)}, u32[]{:S(2)}) async-start(bf16[8,2,128,640]{3,2,1,0:T(8,128)(2,1)} %get-tuple-element.181), calls=%async_computation.9 | async-start | bytes 5242880 | tf_op jit(solution)/shard_map/all_to_all | solution.py:587
  313.3 111.7 %reduce-scatter.19.cloned.1.call-start = ((), (), s32[]{:S(2)}) async-start(), calls=%async_computation.35 | async-start | bytes 2621440 | tf_op jit(solution)/shard_map/reduce_scatter | solution.py:801
  345.6 36.8 %all-to-all-start.9 = ((bf16[8,2,128,640]{3,2,1,0:T(8,128)(2,1)}), bf16[8,2,128,640]{3,2,1,0:T(8,128)(2,1)}, u32[]{:S(2)}, u32[]{:S(2)}) async-start(bf16[8,2,128,640]{3,2,1,0:T(8,128)(2,1)} %get-tuple-element.185), calls=%async_computation.10 | async-start | bytes 5242880 | tf_op jit(solution)/shard_map/all_to_all | solution.py:587
  386.0 85.5 %reduce-scatter.11.cloned.1.call-start = ((), (), s32[]{:S(2)}) async-start(), calls=%async_computation.31 | async-start | bytes 3276800 | tf_op jit(solution)/shard_map/reduce_scatter | solution.py:811
  407.2 25.5 %all-to-all-start.11 = ((bf16[8,2,128,384]{3,2,1,0:T(8,128)(2,1)}), bf16[8,2,128,384]{3,2,1,0:T(8,128)(2,1)S(1)}, u32[]{:S(2)}, u32[]{:S(2)}) async-start(bf16[8,2,128,384]{3,2,1,0:T(8,128)(2,1)} %get-tuple-element.192), calls=%async_computation.13 | async-start | bytes 3145728 | tf_op jit(solution)/shard_map/all_to_all | solution.py:587
  433.8 30.2 %all-to-all-start.12 = ((bf16[8,4,128,256]{3,2,1,0:T(8,128)(2,1)}), bf16[8,4,128,256]{3,2,1,0:T(8,128)(2,1)S(1)}, u32[]{:S(2)}, u32[]{:S(2)}) async-start(bf16[8,4,128,256]{3,2,1,0:T(8,128)(2,1)} %pad_maximum_fusion.2), calls=%async_computation.18 | async-start | bytes 4194304 | tf_op jit(solution)/shard_map/all_to_all | solution.py:587
  437.4 65.2 %reduce-scatter.21.cloned.1.call-start = ((), (), s32[]{:S(2)}) async-start(), calls=%async_computation.36 | async-start | bytes 1966080 | tf_op jit(solution)/shard_map/reduce_scatter | solution.py:818
  464.0 144.7 %all-gather.16.cloned.1.call-start = ((), (), s32[]{:S(2)}) async-start(), calls=%async_computation.40 | async-start | bytes 5242880 | tf_op jit(solution)/shard_map/all_gather | solution.py:832
  509.3 57.6 %all-to-all-start.14 = ((bf16[4,512,256]{2,1,0:T(8,128)(2,1)}), bf16[4,512,256]{2,1,0:T(8,128)(2,1)}, u32[]{:S(2)}, u32[]{:S(2)}) async-start(bf16[4,512,256]{2,1,0:T(8,128)(2,1)} %get-tuple-element.208), calls=%async_computation.21 | async-start | bytes 2097152 | tf_op jit(solution)/shard_map/all_to_all | solution.py:587
  566.9 41.8 %all-to-all-start.15 = ((bf16[8,128,1056]{1,2,0:T(8,128)(2,1)}), bf16[8,128,1056]{1,2,0:T(8,128)(2,1)S(1)}, u32[]{:S(2)}, u32[]{:S(2)}) async-start(bf16[8,128,1056]{1,2,0:T(8,128)(2,1)} %copy.144), calls=%async_computation.22 | async-start | bytes 4325376 | tf_op jit(solution)/shard_map/all_to_all | solution.py:587
  570.6 121.0 %reduce-scatter.23.cloned.1.call-start = ((), (), s32[]{:S(2)}) async-start(), calls=%async_computation.37 | async-start | bytes 5242880 | tf_op jit(solution)/shard_map/reduce_scatter | solution.py:869
  615.0 162.5 %all-gather.12.cloned.1.call-start = ((), (), s32[]{:S(2)}) async-start(), calls=%async_computation.38 | async-start | bytes 5242880 | tf_op jit(solution)/shard_map/all_gather | solution.py:884
  (33 other events, 292.2 us)
Sparse Core Ops, SparseCore 0:
  10.5 28.9 all-gather.7
  41.9 27.8 all-gather.9
  76.2 82.5 all-gather.13
  214.8 26.7 reduce-scatter.8
  245.9 26.7 reduce-scatter.12
  276.1 43.4 reduce-scatter.14
  322.0 43.1 reduce-scatter.16
  367.5 43.1 reduce-scatter.18
  413.7 51.4 reduce-scatter.10
  467.4 35.1 reduce-scatter.20
  504.2 101.9 all-gather.15
  609.1 82.4 reduce-scatter.22
  695.7 81.7 all-gather.11
